TPU v7x, 32 devices: a whole 2x2x4 slice. The times are simulated.
32 devices in a mesh: expert: 8 (over z, y), tensor: 4 (over x, core).
Axes of the slice: x: 2, y: 2, z: 4, core: 2. Of those that a mesh axis runs over, the one named last changes fastest.
Arguments:
- hidden_in: bfloat16 [2048, 2048], P('expert'), may hold values from -6 to 6
- cotangent: bfloat16 [2048, 2048], P('expert'), may hold values from -6 to 6
- layout: int32 [2048], P('expert'), may hold values from 0 to 2047, each once
- seq_lengths: int32 [3], replicated, may hold values from 1 to 960, 1920 in all
- expert_ids: int32 [2048, 8], P('expert'), may hold values from 0 to 15, all different within a row; in each aligned block of 256 rows (0 to 255, 256 to 511, ...) at most 256 rows name the same one
- drop_rank: int32 [2048], P('expert'), may hold values from 0 to 2047, each once
- norm1_gain: float32 [2048], replicated, may hold values from 0.5 to 1.5
- w_query: bfloat16 [2048, 4096], P(None, 'tensor'), may hold values from -0.125 to 0.125
- key_weight: bfloat16 [2048, 512], P(None, 'tensor'), may hold values from -0.125 to 0.125
- value_weight: bfloat16 [2048, 512], P(None, 'tensor'), may hold values from -0.125 to 0.125
- query_gain: float32 [128], replicated, may hold values from 0.5 to 1.5
- key_gain: float32 [128], replicated, may hold values from 0.5 to 1.5
- w_out: bfloat16 [4096, 2048], P('tensor'), may hold values from -1.5 to 1.5
- norm2_gain: float32 [2048], replicated, may hold values from 0.5 to 1.5
- w_router: bfloat16 [2048, 16], replicated, may hold values from -0.0625 to 0.0625
- w_gate: bfloat16 [16, 2048, 768], P('expert', None, 'tensor'), may hold values from -0.125 to 0.125
- w_up: bfloat16 [16, 2048, 768], P('expert', None, 'tensor'), may hold values from -0.125 to 0.125
- w_down: bfloat16 [16, 768, 2048], P('expert', 'tensor'), may hold values from -0.875 to 0.875
Outputs:
- out_hidden: bfloat16 [2048, 2048], P('expert')
- grad_hidden: bfloat16 [2048, 2048], P('expert')
- grad_norm1: float32 [2048], replicated
- grad_query: float32 [2048, 4096], P(None, 'tensor')
- grad_key: float32 [2048, 512], P(None, 'tensor')
- grad_value: float32 [2048, 512], P(None, 'tensor')
- grad_query_gain: float32 [128], replicated
- grad_key_gain: float32 [128], replicated
- grad_out: float32 [4096, 2048], P('tensor')
- grad_norm2: float32 [2048], replicated
- grad_router: float32 [2048, 16], replicated
- grad_gate: float32 [16, 2048, 768], P('expert', None, 'tensor')
- grad_up: float32 [16, 2048, 768], P('expert', None, 'tensor')
- grad_down: float32 [16, 768, 2048], P('expert', 'tensor')
Inputs may be any that keep to these rules, and one draw needn't show every extreme that they name: `layout`: each place of the packed order is held by exactly one row. `seq_lengths`: the sequences lie one after another from place 0 and their lengths add up to 1920; places from 1920 on are padding; the longest has exactly 960. `expert_ids`: each row names 8 different experts; the 256 rows of one device name one expert at most 256 times, a bound that some block reaches. `drop_rank`: each value appears once.
All inputs are finite; a program needn't handle non-finite values.
Results may differ from a plain program's by a relative error of at most 0.024.
Values may be sent and summed in bfloat16 or wider, within the bound.
A program may use at most 320 MiB of HBM per device.

v0:
```python
from functools import partial
import math

import jax
import jax.numpy as jnp
from jax import lax
from jax.sharding import PartitionSpec as P

TOPK = 8
CAP = 1280


EPS = 1e-06
THETA = 1000000.0
NEG = -1e30


def norm_rows(value_matrix, gain):
    return (
        value_matrix
        * lax.rsqrt(jnp.mean(value_matrix * value_matrix, axis=-1, keepdims=True) + EPS)
        * gain
    )


def rotary(value_matrix, position):
    half_dim = value_matrix.shape[-1] // 2
    inverse = THETA ** (-(jnp.arange(half_dim, dtype=jnp.float32) * 2.0) / value_matrix.shape[-1])
    angles = position.astype(jnp.float32)[:, None] * inverse[None, :]
    cosine_table = jnp.concatenate([jnp.cos(angles), jnp.cos(angles)], axis=-1)[:, None, :]
    sine_table = jnp.concatenate([jnp.sin(angles), jnp.sin(angles)], axis=-1)[:, None, :]
    turned = jnp.concatenate([-value_matrix[..., half_dim:], value_matrix[..., :half_dim]], axis=-1)
    return value_matrix * cosine_table + turned * sine_table


def shape_queries(linear, gain, position):
    head_dim = gain.shape[0]
    shaped = linear.reshape(linear.shape[0], linear.shape[1] // head_dim, head_dim)
    return rotary(norm_rows(shaped, gain), position) * head_dim ** (-0.5)


def shape_keys(linear, gain, position):
    head_dim = gain.shape[0]
    shaped = linear.reshape(linear.shape[0], linear.shape[1] // head_dim, head_dim)
    return rotary(norm_rows(shaped, gain), position)


def token_tables(token_position, seq_lengths):
    bounds = jnp.cumsum(seq_lengths)
    passed = token_position[:, None] >= bounds[None, :]
    segment_ids = jnp.sum(passed.astype(jnp.int32), axis=1)
    opening = jnp.max(jnp.where(passed, bounds[None, :], 0), axis=1)
    return (segment_ids, (token_position - opening).astype(jnp.int32))


def visible(query_segment, query_place, key_segment, key_place):
    return (query_segment[:, None] == key_segment[None, :]) & (
        key_place[None, :] <= query_place[:, None]
    )


def deliver(payload, slot_ids):
    return (
        lax.all_to_all(payload, "expert", split_axis=0, concat_axis=0, tiled=True),
        lax.all_to_all(slot_ids, "expert", split_axis=0, concat_axis=0, tiled=True),
    )


def bring_back(payload):
    return lax.all_to_all(payload, "expert", split_axis=0, concat_axis=0, tiled=True)


def expert_forward(entry_rows, w_gate, w_up, w_down):
    gate_lin = jnp.einsum("gesd,edf->gesf", entry_rows, w_gate, preferred_element_type=jnp.float32)
    up_lin = jnp.einsum("gesd,edf->gesf", entry_rows, w_up, preferred_element_type=jnp.float32)
    activation = (jax.nn.silu(gate_lin) * up_lin).astype(jnp.bfloat16)
    expert_out = jnp.einsum(
        "gesf,efd->gesd", activation, w_down, preferred_element_type=jnp.float32
    ).astype(jnp.bfloat16)
    return (gate_lin, up_lin, activation, expert_out)


def expert_backward(entry_rows, gate_lin, up_lin, activation, grad_in, w_gate, w_up, w_down):
    grad_down = jnp.einsum(
        "gesf,gesd->efd", activation, grad_in, preferred_element_type=jnp.float32
    )
    grad_act = jnp.einsum("gesd,efd->gesf", grad_in, w_down, preferred_element_type=jnp.float32)
    sigmoid = jax.nn.sigmoid(gate_lin)
    grad_gate_lin = (grad_act * up_lin * sigmoid * (1.0 + gate_lin * (1.0 - sigmoid))).astype(
        jnp.bfloat16
    )
    grad_up_lin = (grad_act * gate_lin * sigmoid).astype(jnp.bfloat16)
    grad_w_gate = jnp.einsum(
        "gesd,gesf->edf", entry_rows, grad_gate_lin, preferred_element_type=jnp.float32
    )
    grad_w_up = jnp.einsum(
        "gesd,gesf->edf", entry_rows, grad_up_lin, preferred_element_type=jnp.float32
    )
    grad_entry = jnp.einsum(
        "gesf,edf->gesd", grad_gate_lin, w_gate, preferred_element_type=jnp.float32
    )
    grad_entry = (
        grad_entry
        + jnp.einsum("gesf,edf->gesd", grad_up_lin, w_up, preferred_element_type=jnp.float32)
    ).astype(jnp.bfloat16)
    return (grad_entry, grad_w_gate, grad_w_up, grad_down)


def per_device(
    hidden_in,
    cotangent,
    layout,
    seq_lengths,
    expert_ids,
    drop_rank,
    norm1_gain,
    w_query,
    key_weight,
    value_weight,
    query_gain,
    key_gain,
    w_out,
    norm2_gain,
    w_router,
    w_gate,
    w_up,
    w_down,
):
    tok_rows = hidden_in.shape[0]
    model_width = hidden_in.shape[1]
    head_dim = query_gain.shape[0]
    local_heads = w_query.shape[1] // head_dim
    expert_count = w_router.shape[1]
    local_count = w_gate.shape[0]
    group_count = lax.axis_size("expert")
    slot_count = 2 * tok_rows * TOPK // expert_count
    seq_count = seq_lengths.shape[0]
    expert_range = jnp.arange(expert_count, dtype=jnp.int32)
    hidden = hidden_in.astype(jnp.float32)
    segment_ids, position = token_tables(layout, seq_lengths)
    valid = segment_ids < seq_count
    first_normalized = norm_rows(hidden, norm1_gain)
    normed1_low = first_normalized.astype(jnp.bfloat16)
    query_lin = jnp.dot(normed1_low, w_query, preferred_element_type=jnp.float32)
    key_lin = jnp.dot(normed1_low, key_weight, preferred_element_type=jnp.float32)
    value_lin = jnp.dot(normed1_low, value_weight, preferred_element_type=jnp.float32)
    query_shaped = shape_queries(query_lin, query_gain, position).astype(jnp.bfloat16)
    query_total = local_heads * tok_rows
    query_rows = jnp.transpose(query_shaped, (1, 0, 2)).reshape(query_total, head_dim)
    key_rows = (
        shape_keys(key_lin, key_gain, position).astype(jnp.bfloat16).reshape(tok_rows, head_dim)
    )
    value_rows = value_lin.astype(jnp.bfloat16)
    all_keys, all_values, all_place, all_ids, all_rank = (
        lax.all_gather(key_rows, "expert", axis=0, tiled=True),
        lax.all_gather(value_rows, "expert", axis=0, tiled=True),
        lax.all_gather(layout, "expert", axis=0, tiled=True),
        lax.all_gather(expert_ids, "expert", axis=0, tiled=True),
        lax.all_gather(drop_rank, "expert", axis=0, tiled=True),
    )
    all_segment = token_tables(all_place, seq_lengths)[0]
    rows_per_block = math.gcd(512, query_total)
    count_of_blocks = query_total // rows_per_block
    query_segment = jnp.tile(segment_ids, local_heads)
    query_place = jnp.tile(layout, local_heads)

    def attend_block(operands):
        query_block, segment_block, place_block = operands
        scores = jnp.einsum("qd,kd->qk", query_block, all_keys, preferred_element_type=jnp.float32)
        scores = jnp.where(visible(segment_block, place_block, all_segment, all_place), scores, NEG)
        highest = jnp.max(scores, axis=1, keepdims=True)
        weights = jnp.exp(scores - highest)
        totals = jnp.sum(weights, axis=1, keepdims=True)
        probability = (weights / totals).astype(jnp.bfloat16)
        mixed_out = jnp.dot(probability, all_values, preferred_element_type=jnp.float32)
        return (mixed_out, (highest + jnp.log(totals))[:, 0])

    attention_output, log_totals = lax.map(
        attend_block,
        (
            query_rows.reshape(count_of_blocks, rows_per_block, head_dim),
            query_segment.reshape(count_of_blocks, rows_per_block),
            query_place.reshape(count_of_blocks, rows_per_block),
        ),
    )
    attention_output = attention_output.reshape(local_heads, tok_rows, head_dim).astype(
        jnp.bfloat16
    )
    att_cat = jnp.transpose(attention_output, (1, 0, 2)).reshape(tok_rows, local_heads * head_dim)
    branch_part = jnp.dot(att_cat, w_out, preferred_element_type=jnp.float32)
    branch = lax.psum(branch_part, "tensor")
    residual = hidden + branch
    normed2 = norm_rows(residual, norm2_gain)
    normed2_low = normed2.astype(jnp.bfloat16)
    logits = jnp.dot(normed2_low, w_router, preferred_element_type=jnp.float32)
    soft_gate = jax.nn.softmax(jnp.take_along_axis(logits, expert_ids, axis=1), axis=1)
    picks = jnp.any(expert_ids[:, :, None] == expert_range, axis=1) & valid[:, None]
    all_valid = all_segment < seq_count
    all_picks = jnp.any(all_ids[:, :, None] == expert_range, axis=1) & all_valid[:, None]
    earlier = (all_rank[None, :] < drop_rank[:, None]).astype(jnp.bfloat16)
    before_counts = jnp.dot(
        earlier, all_picks.astype(jnp.bfloat16), preferred_element_type=jnp.float32
    )
    global_slot = jnp.take_along_axis(before_counts, expert_ids, axis=1).astype(jnp.int32)
    kept_mask = (global_slot < CAP) & valid[:, None]
    gate_weight = soft_gate * kept_mask.astype(jnp.float32)
    lower_rows = (jnp.arange(tok_rows)[None, :] < jnp.arange(tok_rows)[:, None]).astype(
        jnp.bfloat16
    )
    local_counts = jnp.dot(
        lower_rows, picks.astype(jnp.bfloat16), preferred_element_type=jnp.float32
    )
    local_slot = jnp.take_along_axis(local_counts, expert_ids, axis=1).astype(jnp.int32)
    pair_count = tok_rows * TOPK
    dump_index = expert_count * slot_count
    target = jnp.where(kept_mask, expert_ids * slot_count + local_slot, dump_index)
    pair_index = jnp.arange(pair_count, dtype=jnp.int32)
    slot_pair = (
        jnp.full((dump_index,), pair_count, jnp.int32)
        .at[target.reshape(-1)]
        .set(pair_index, mode="drop")
    )
    slot_token = jnp.where(slot_pair < pair_count, slot_pair // TOPK, tok_rows)
    slot_global = (
        jnp.full((dump_index,), -1, jnp.int32)
        .at[target.reshape(-1)]
        .set(global_slot.reshape(-1), mode="drop")
    )
    padded_rows = jnp.concatenate([normed2_low, jnp.zeros((1, model_width), jnp.bfloat16)], axis=0)
    send_rows = padded_rows[slot_token].reshape(group_count, local_count, slot_count, model_width)
    send_slot = slot_global.reshape(group_count, local_count, slot_count)
    received, received_slot = deliver(send_rows, send_slot)
    gate_lin, up_lin, activation, expert_out = expert_forward(received, w_gate, w_up, w_down)
    returned = bring_back(expert_out)
    returned_flat = jnp.concatenate(
        [returned.reshape(dump_index, model_width), jnp.zeros((1, model_width), returned.dtype)],
        axis=0,
    )
    pair_out = returned_flat[target]
    moe_part = jnp.sum(gate_weight[:, :, None] * pair_out, axis=1)
    moe_branch = lax.psum(moe_part.astype(jnp.bfloat16), "tensor").astype(jnp.float32)
    out_hidden = (residual + moe_branch).astype(jnp.bfloat16)
    grad_y = cotangent.astype(jnp.float32)
    gate_dot = jnp.sum(grad_y[:, None, :] * pair_out, axis=2)
    pair_grads = (
        (gate_weight[:, :, None] * grad_y[:, None, :])
        .astype(jnp.bfloat16)
        .reshape(pair_count, model_width)
    )
    pair_grads = jnp.concatenate([pair_grads, jnp.zeros((1, model_width), jnp.bfloat16)], axis=0)
    send_grad = pair_grads[slot_pair].reshape(group_count, local_count, slot_count, model_width)
    grad_received, grad_slot = deliver(send_grad, send_slot)
    grad_entry, grad_w_gate, grad_w_up, grad_w_down = expert_backward(
        received, gate_lin, up_lin, activation, grad_received, w_gate, w_up, w_down
    )
    grad_returned = bring_back(grad_entry)
    grad_flat = jnp.concatenate(
        [
            grad_returned.reshape(dump_index, model_width),
            jnp.zeros((1, model_width), grad_returned.dtype),
        ],
        axis=0,
    )
    grad_normed2_part = jnp.sum(grad_flat[target], axis=1, dtype=jnp.float32)
    grad_normed2_exp, gate_dot = lax.psum((grad_normed2_part, gate_dot), "tensor")
    grad_soft = gate_dot * kept_mask.astype(jnp.float32)
    grad_chosen = soft_gate * (grad_soft - jnp.sum(soft_gate * grad_soft, axis=1, keepdims=True))
    grad_logits = jnp.sum(
        grad_chosen[:, :, None] * (expert_ids[:, :, None] == expert_range).astype(jnp.float32),
        axis=1,
    ).astype(jnp.bfloat16)
    grad_w_router = jnp.einsum(
        "td,te->de", normed2_low, grad_logits, preferred_element_type=jnp.float32
    )
    grad_normed2 = grad_normed2_exp + jnp.einsum(
        "te,de->td", grad_logits, w_router, preferred_element_type=jnp.float32
    )
    norm2_pull = jax.vjp(norm_rows, residual, norm2_gain)[1]
    grad_resid_norm, grad_norm2 = norm2_pull(grad_normed2)
    grad_residual = grad_y + grad_resid_norm
    grad_residual_low = grad_residual.astype(jnp.bfloat16)
    grad_w_out = jnp.einsum(
        "tc,td->cd", att_cat, grad_residual_low, preferred_element_type=jnp.float32
    )
    grad_att_cat = jnp.einsum(
        "td,cd->tc", grad_residual_low, w_out, preferred_element_type=jnp.float32
    ).astype(jnp.bfloat16)
    grad_att_rows = jnp.transpose(
        grad_att_cat.reshape(tok_rows, local_heads, head_dim), (1, 0, 2)
    ).reshape(query_total, head_dim)

    def query_grad_block(operands):
        query_block, segment_block, place_block, grad_block, log_block = operands
        scores = jnp.einsum("qd,kd->qk", query_block, all_keys, preferred_element_type=jnp.float32)
        scores = jnp.where(visible(segment_block, place_block, all_segment, all_place), scores, NEG)
        probability = jnp.exp(scores - log_block[:, None])
        grad_prob = jnp.einsum(
            "qd,kd->qk", grad_block, all_values, preferred_element_type=jnp.float32
        )
        delta_row = jnp.sum(probability * grad_prob, axis=1)
        grad_scores = (probability * (grad_prob - delta_row[:, None])).astype(jnp.bfloat16)
        return (jnp.dot(grad_scores, all_keys, preferred_element_type=jnp.float32), delta_row)

    grad_query_rows, deltas = lax.map(
        query_grad_block,
        (
            query_rows.reshape(count_of_blocks, rows_per_block, head_dim),
            query_segment.reshape(count_of_blocks, rows_per_block),
            query_place.reshape(count_of_blocks, rows_per_block),
            grad_att_rows.reshape(count_of_blocks, rows_per_block, head_dim),
            log_totals,
        ),
    )
    log_flat = log_totals.reshape(query_total)
    delta_flat = deltas.reshape(query_total)
    key_block = math.gcd(lax.axis_size("expert") * tok_rows, 2048)

    def one_block(offset):
        key_part = lax.dynamic_slice_in_dim(all_keys, offset, key_block, 0)
        value_part = lax.dynamic_slice_in_dim(all_values, offset, key_block, 0)
        segment_part = lax.dynamic_slice_in_dim(all_segment, offset, key_block, 0)
        place_part = lax.dynamic_slice_in_dim(all_place, offset, key_block, 0)
        scores = jnp.einsum("qd,kd->qk", query_rows, key_part, preferred_element_type=jnp.float32)
        scores = jnp.where(
            visible(query_segment, query_place, segment_part, place_part), scores, NEG
        )
        probability = jnp.exp(scores - log_flat[:, None])
        grad_value = jnp.einsum(
            "qk,qd->kd",
            probability.astype(jnp.bfloat16),
            grad_att_rows,
            preferred_element_type=jnp.float32,
        )
        grad_prob = jnp.einsum(
            "qd,kd->qk", grad_att_rows, value_part, preferred_element_type=jnp.float32
        )
        grad_scores = (probability * (grad_prob - delta_flat[:, None])).astype(jnp.bfloat16)
        grad_key = jnp.einsum(
            "qk,qd->kd", grad_scores, query_rows, preferred_element_type=jnp.float32
        )
        return jnp.concatenate([grad_key, grad_value], axis=1)

    stacked = lax.map(
        one_block,
        jnp.arange(lax.axis_size("expert") * tok_rows // key_block, dtype=jnp.int32) * key_block,
    )
    key_value_grad = lax.psum_scatter(
        stacked.reshape(lax.axis_size("expert") * tok_rows, 2 * head_dim).astype(jnp.bfloat16),
        "expert",
        scatter_dimension=0,
        tiled=True,
    ).astype(jnp.float32)
    grad_key_post = key_value_grad[:, :head_dim].reshape(tok_rows, 1, head_dim)
    grad_values_low = key_value_grad[:, head_dim:].astype(jnp.bfloat16)
    grad_query_tok = jnp.transpose(
        grad_query_rows.reshape(local_heads, tok_rows, head_dim), (1, 0, 2)
    )
    query_pull = jax.vjp(partial(shape_queries, position=position), query_lin, query_gain)[1]
    grad_query_lin, grad_qgain_part = query_pull(grad_query_tok)
    key_pull = jax.vjp(partial(shape_keys, position=position), key_lin, key_gain)[1]
    grad_key_lin, grad_kgain_part = key_pull(grad_key_post)
    grad_query_low = grad_query_lin.astype(jnp.bfloat16)
    grad_key_low = grad_key_lin.astype(jnp.bfloat16)
    grad_w_query = jnp.einsum(
        "td,tc->dc", normed1_low, grad_query_low, preferred_element_type=jnp.float32
    )
    grad_w_key = jnp.einsum(
        "td,tc->dc", normed1_low, grad_key_low, preferred_element_type=jnp.float32
    )
    grad_w_value = jnp.einsum(
        "td,tc->dc", normed1_low, grad_values_low, preferred_element_type=jnp.float32
    )
    grad_normed1_part = jnp.einsum(
        "tc,dc->td", grad_query_low, w_query, preferred_element_type=jnp.float32
    )
    grad_normed1_part = grad_normed1_part + jnp.einsum(
        "tc,dc->td", grad_key_low, key_weight, preferred_element_type=jnp.float32
    )
    grad_normed1_part = grad_normed1_part + jnp.einsum(
        "tc,dc->td", grad_values_low, value_weight, preferred_element_type=jnp.float32
    )
    grad_normed1, grad_qgain_part, grad_kgain_part = (
        lax.psum(grad_normed1_part.astype(jnp.bfloat16), "tensor").astype(jnp.float32),
        lax.psum(grad_qgain_part.astype(jnp.bfloat16), "tensor").astype(jnp.float32),
        lax.psum(grad_kgain_part.astype(jnp.bfloat16), "tensor").astype(jnp.float32),
    )
    norm1_pull = jax.vjp(norm_rows, hidden, norm1_gain)[1]
    grad_hidden_norm, grad_norm1 = norm1_pull(grad_normed1)
    grad_hidden = (grad_residual + grad_hidden_norm).astype(jnp.bfloat16)
    summed = (
        lax.psum(grad_norm1.astype(jnp.bfloat16), "expert").astype(jnp.float32),
        lax.psum(grad_w_query.astype(jnp.bfloat16), "expert").astype(jnp.float32),
        lax.psum(grad_w_key.astype(jnp.bfloat16), "expert").astype(jnp.float32),
        lax.psum(grad_w_value.astype(jnp.bfloat16), "expert").astype(jnp.float32),
        lax.psum(grad_qgain_part.astype(jnp.bfloat16), "expert").astype(jnp.float32),
        lax.psum(grad_kgain_part.astype(jnp.bfloat16), "expert").astype(jnp.float32),
        lax.psum(grad_w_out.astype(jnp.bfloat16), "expert").astype(jnp.float32),
        lax.psum(grad_norm2.astype(jnp.bfloat16), "expert").astype(jnp.float32),
        lax.psum(grad_w_router.astype(jnp.bfloat16), "expert").astype(jnp.float32),
    )
    return (
        out_hidden,
        grad_hidden,
        summed[0],
        summed[1],
        summed[2],
        summed[3],
        summed[4],
        summed[5],
        summed[6],
        summed[7],
        summed[8],
        grad_w_gate,
        grad_w_up,
        grad_w_down,
    )


def solution(mesh):
    return jax.shard_map(
        per_device,
        mesh=mesh,
        in_specs=(
            P("expert", None),
            P("expert", None),
            P("expert"),
            P(),
            P("expert", None),
            P("expert"),
            P(),
            P(None, "tensor"),
            P(None, "tensor"),
            P(None, "tensor"),
            P(),
            P(),
            P("tensor", None),
            P(),
            P(),
            P("expert", None, "tensor"),
            P("expert", None, "tensor"),
            P("expert", "tensor", None),
        ),
        out_specs=(
            P("expert", None),
            P("expert", None),
            P(),
            P(None, "tensor"),
            P(None, "tensor"),
            P(None, "tensor"),
            P(),
            P(),
            P("tensor", None),
            P(),
            P(),
            P("expert", None, "tensor"),
            P("expert", None, "tensor"),
            P("expert", "tensor", None),
        ),
        check_vma=False,
    )
```

profile of v0, /device:TPU:0, one launch (start us, length us, event | category | flops | bytes accessed | tf_op | source)
XLA Modules:
  0.0 2397.1 jit_solution(16629170171599714229)
XLA Ops:
  12.7 22.5 all-gather
  39.9 31.7 %all_gather.17 = bf16[2048,128]{1,0:T(8,128)(2,1)S(1)} all-gather(bf16[256,128]{1,0:T(8,128)(2,1)} %convolution_convert_fusion.7), channel_id=1, replica_groups=mesh['expert'=8,'tensor'=4] {'expert'}, dimensions={0}, use_global_device_ids=true | all-gather | bytes 589824 | tf_op jit(solution)/shard_map/all_gather | solution.py:156
  71.6 33.2 %all_gather.16 = bf16[2048,128]{0,1:T(8,128)(2,1)} all-gather(bf16[256,128]{0,1:T(8,128)(2,1)S(1)} %get-tuple-element.469), channel_id=1, replica_groups=mesh['expert'=8,'tensor'=4] {'expert'}, dimensions={0}, use_global_device_ids=true | all-gather | bytes 589824 | tf_op jit(solution)/shard_map/all_gather | solution.py:155
  117.0 20.0 while.30
  144.8 16.8 gather_fusion.6
  161.6 16.6 all-gather.1
  178.3 30.7 %all_gather.19 = s32[2048,8]{0,1:T(8,128)S(1)} all-gather(s32[256,8]{0,1:T(8,128)S(1)} %copy-done.43), channel_id=1, replica_groups=mesh['expert'=8,'tensor'=4] {'expert'}, dimensions={0}, use_global_device_ids=true | all-gather | bytes 73728 | tf_op jit(solution)/shard_map/all_gather | solution.py:158
  209.7 16.8 gather_fusion.4
  231.7 16.8 gather_fusion.5
  259.7 20.9 gather_fusion
  302.4 35.8 %gather_fusion.2 = bf16[4096,2048]{1,0:T(8,128)(2,1)} fusion(bf16[2049,2048]{1,0:T(8,128)(2,1)} %concatenate.48, s32[4096]{0:T(1024)S(1)} %get-tuple-element.472), kind=kCustom, calls=%fused_computation.5 | custom fusion | bytes 33570816 | tf_op jit(solution)/shard_map/gather | solution.py:251
  338.3 285.7 %all-to-all-done = bf16[8,2,256,2048]{3,2,1,0:T(8,128)(2,1)} async-done(((bf16[8,2,256,2048]{3,2,1,0:T(8,128)(2,1)}), bf16[8,2,256,2048]{3,2,1,0:T(8,128)(2,1)}, u32[]{:S(2)}, u32[]{:S(2)}) %all-to-all-start) | async-done | bytes 16777248 | tf_op jit(solution)/shard_map/all_to_all | solution.py:64
  651.2 339.8 %all-to-all-done.2 = bf16[8,2,256,2048]{3,2,1,0:T(8,128)(2,1)} async-done(((bf16[8,2,256,2048]{3,2,1,0:T(8,128)(2,1)}), bf16[8,2,256,2048]{3,2,1,0:T(8,128)(2,1)}, u32[]{:S(2)}, u32[]{:S(2)}) %all-to-all-start.2) | async-done | bytes 16777248 | tf_op jit(solution)/shard_map/all_to_all | solution.py:64
  991.0 12.1 fusion.37
  1013.3 14.1 copy.324
  1033.4 14.8 fusion.63
  1048.2 12.6 fusion.20
  1067.5 326.9 %all-to-all-done.1 = bf16[8,2,256,2048]{3,2,1,0:T(8,128)(2,1)} async-done(((bf16[8,2,256,2048]{3,2,1,0:T(8,128)(2,1)}), bf16[8,2,256,2048]{3,2,1,0:T(8,128)(2,1)}, u32[]{:S(2)}, u32[]{:S(2)}) %all-to-all-start.1) | async-done | bytes 16777248 | tf_op jit(solution)/shard_map/all_to_all | solution.py:70
  1408.7 13.9 concatenate.47
  1422.6 339.4 %all-to-all-done.3 = bf16[8,2,256,2048]{3,2,1,0:T(8,128)(2,1)} async-done(((bf16[8,2,256,2048]{3,2,1,0:T(8,128)(2,1)}), bf16[8,2,256,2048]{3,2,1,0:T(8,128)(2,1)}, u32[]{:S(2)}, u32[]{:S(2)}) %all-to-all-start.3) | async-done | bytes 16777248 | tf_op jit(solution)/shard_map/all_to_all | solution.py:70
  1762.0 13.9 concatenate.49
  1776.0 24.3 %gather_fusion.1 = bf16[2048,2048]{1,0:T(8,128)(2,1)} fusion(bf16[4097,2048]{1,0:T(8,128)(2,1)} %concatenate.47, s32[2048]{0:T(1024)S(1)} %broadcast_clamp_fusion), kind=kCustom, calls=%fused_computation.4 | custom fusion | bytes 16785408 | tf_op jit(solution)/shard_map/gather | solution.py:239
  1800.2 24.6 %gather_fusion.3 = bf16[2048,2048]{1,0:T(8,128)(2,1)} fusion(bf16[4097,2048]{1,0:T(8,128)(2,1)} %concatenate.49, s32[2048]{0:T(1024)S(1)} %broadcast_clamp_fusion), kind=kCustom, calls=%fused_computation.6 | custom fusion | bytes 16785408 | tf_op jit(solution)/shard_map/gather | solution.py:264
  1824.9 11.3 convert_reduce_fusion
  1852.9 35.1 %all-reduce.19.cloned.1.call-done = f32[256,2048]{1,0:T(8,128)} async-done(((f32[256,2048]{1,0:T(8,128)}), f32[256,2048]{1,0:T(8,128)}) %all-reduce.19.cloned.1.call-update) | async-done | bytes 2097168 | tf_op jit(solution)/shard_map/psum | solution.py:265
  1895.4 16.2 while.31
  1921.3 13.4 convolution_convert_fusion.2
  1938.2 63.1 %reduce-scatter.2.cloned.1.call-done = bf16[256,256]{0,1:T(8,128)(2,1)} async-done(((bf16[2048,256]{0,1:T(8,128)(2,1)}), bf16[256,256]{0,1:T(8,128)(2,1)}) %reduce-scatter.2.cloned.1.call-update) | async-done | bytes 131088 | tf_op jit(solution)/shard_map/reduce_scatter | solution.py:347
  2025.5 11.2 fusion.43
  2047.8 11.3 convolution_bitcast_fusion.1
  2067.0 21.3 all-reduce.8
  2095.8 277.5 %all-reduce.21.cloned.1.call-done = (bf16[2048,1024]{1,0:T(8,128)(2,1)}, bf16[2048,128]{1,0:T(8,128)(2,1)}, bf16[2048,128]{1,0:T(8,128)(2,1)}, bf16[1024,2048]{1,0:T(8,128)(2,1)}, bf16[2048,16]{0,1:T(8,128)(2,1)}) async-done(((bf16[2048,1024]{1,0:T(8,128)(2,1)}, bf16[2048,128]{1,0:T(8,128)(2,1)}, bf16[2048,128]{1,0:T(8,128)(2,1)}, bf16[1024,2048]{1,0:T(8,128)(2,1)}, bf16[2048,16]{0,1:T(8,128)(2,1)}), ...) | async-done | bytes 9502736 | tf_op jit(solution)/shard_map/psum | solution.py:392
  (400 shorter events, 272.8 us)
Async XLA Ops:
  7.2 983.8 %copy-start = (bf16[2,192,2048]{2,1,0:T(8,128)(2,1)S(1)}, bf16[2,192,2048]{2,1,0:T(8,128)(2,1)}, u32[]{:S(2)}) copy-start(bf16[2,192,2048]{2,1,0:T(8,128)(2,1)} %param.41) | copy-start | bytes 4718596
  7.2 219.6 %all-reduce.17.cloned.1.call-start = ((), (), s32[]{:S(2)}) async-start(), calls=%async_computation.5 | async-start | bytes 4194304 | tf_op jit(solution)/shard_map/psum | solution.py:191
  10.5 96.4 %copy-start.70 = (f32[256]{0:T(256)}, f32[256]{0:T(256)S(1)}, u32[]{:S(2)}) copy-start(f32[256]{0:T(256)S(1)} %fusion.121) | copy-start | bytes 3076
  11.9 132.7 %copy-start.83 = (s32[256]{0:T(256)}, s32[256]{0:T(256)S(1)}, u32[]{:S(2)}) copy-start(s32[256]{0:T(256)S(1)} %get-tuple-element.380) | copy-start | bytes 3076
  38.4 72.0 %copy-start.72 = (f32[256]{0:T(256)}, f32[256]{0:T(256)S(1)}, u32[]{:S(2)}) copy-start(f32[256]{0:T(256)S(1)} %fusion.122) | copy-start | bytes 3076
  137.1 72.1 %copy-start.63 = (s32[2048]{0:T(1024)}, s32[2048]{0:T(1024)S(1)}, u32[]{:S(2)}) copy-start(s32[2048]{0:T(1024)S(1)} %get-tuple-element.815) | copy-start | bytes 24580
  249.3 31.2 %copy-start.68 = (pred[256,8]{0,1:T(8,128)(4,1)}, pred[256,8]{0,1:T(8,128)(4,1)S(1)}, u32[]{:S(2)}) copy-start(pred[256,8]{0,1:T(8,128)(4,1)S(1)} %get-tuple-element.440) | copy-start | bytes 6148
  280.5 343.4 %all-to-all-start = ((bf16[8,2,256,2048]{3,2,1,0:T(8,128)(2,1)}), bf16[8,2,256,2048]{3,2,1,0:T(8,128)(2,1)}, u32[]{:S(2)}, u32[]{:S(2)}) async-start(bf16[8,2,256,2048]{3,2,1,0:T(8,128)(2,1)} %bitcast.323), calls=%async_computation | async-start | bytes 33554432 | tf_op jit(solution)/shard_map/all_to_all | solution.py:64
  624.0 367.1 %all-to-all-start.2 = ((bf16[8,2,256,2048]{3,2,1,0:T(8,128)(2,1)}), bf16[8,2,256,2048]{3,2,1,0:T(8,128)(2,1)}, u32[]{:S(2)}, u32[]{:S(2)}) async-start(bf16[8,2,256,2048]{3,2,1,0:T(8,128)(2,1)} %bitcast.324), calls=%async_computation.2 | async-start | bytes 33554432 | tf_op jit(solution)/shard_map/all_to_all | solution.py:64
  1027.4 366.9 %all-to-all-start.1 = ((bf16[8,2,256,2048]{3,2,1,0:T(8,128)(2,1)}), bf16[8,2,256,2048]{3,2,1,0:T(8,128)(2,1)}, u32[]{:S(2)}, u32[]{:S(2)}) async-start(bf16[8,2,256,2048]{3,2,1,0:T(8,128)(2,1)} %copy.324), calls=%async_computation.1 | async-start | bytes 33554432 | tf_op jit(solution)/shard_map/all_to_all | solution.py:70
  1067.4 332.7 %copy-start.84 = (s32[256]{0:T(256)S(1)}, s32[256]{0:T(256)}, u32[]{:S(2)}) copy-start(s32[256]{0:T(256)} %copy-done.83) | copy-start | bytes 3076
  1067.4 332.8 %copy-start.74 = (s32[256]{0:T(256)S(1)}, s32[256]{0:T(256)}, u32[]{:S(2)}) copy-start(s32[256]{0:T(256)} %param.26) | copy-start | bytes 3076
  1067.4 332.8 %copy-start.56 = (f32[4,512]{1,0:T(4,128)S(1)}, f32[4,512]{1,0:T(4,128)}, u32[]{:S(2)}) copy-start(f32[4,512]{1,0:T(4,128)} %copy-done.55) | copy-start | bytes 24580
  1067.4 332.8 %copy-start.19 = (bf16[2048,128]{0,1:T(8,128)(2,1)S(1)}, bf16[2048,128]{0,1:T(8,128)(2,1)}, u32[]{:S(2)}) copy-start(bf16[2048,128]{0,1:T(8,128)(2,1)} %all_gather.16) | copy-start | bytes 1572868
  1067.5 332.8 %copy-start.24 = (bf16[4,512,128]{2,1,0:T(8,128)(2,1)S(1)}, bf16[4,512,128]{2,1,0:T(8,128)(2,1)}, u32[]{:S(2)}) copy-start(bf16[4,512,128]{2,1,0:T(8,128)(2,1)} %get-tuple-element.799) | copy-start | bytes 1572868
  1394.4 367.7 %all-to-all-start.3 = ((bf16[8,2,256,2048]{3,2,1,0:T(8,128)(2,1)}), bf16[8,2,256,2048]{3,2,1,0:T(8,128)(2,1)}, u32[]{:S(2)}, u32[]{:S(2)}) async-start(bf16[8,2,256,2048]{3,2,1,0:T(8,128)(2,1)} %copy.328), calls=%async_computation.3 | async-start | bytes 33554432 | tf_op jit(solution)/shard_map/all_to_all | solution.py:70
  1400.1 487.9 %all-reduce.19.cloned.1.call-start = ((), (), s32[]{:S(2)}) async-start(), calls=%async_computation.6 | async-start | bytes 4194304 | tf_op jit(solution)/shard_map/psum | solution.py:265
  1836.3 51.8 %copy-start.48 = (bf16[2048,16]{0,1:T(8,128)(2,1)S(1)}, bf16[2048,16]{0,1:T(8,128)(2,1)}, u32[]{:S(2)}) copy-start(bf16[2048,16]{0,1:T(8,128)(2,1)} %param.38) | copy-start | bytes 196612
  1836.3 51.8 %copy-start.58 = (f32[2048]{0:T(1024)S(1)}, f32[2048]{0:T(1024)}, u32[]{:S(2)}) copy-start(f32[2048]{0:T(1024)} %param.37) | copy-start | bytes 24580
  1836.3 51.8 %copy-start.78 = (f32[256]{0:T(256)S(1)}, f32[256]{0:T(256)}, u32[]{:S(2)}) copy-start(f32[256]{0:T(256)} %copy-done.77) | copy-start | bytes 3076
  1836.3 165.0 %reduce-scatter.2.cloned.1.call-start = ((), (), s32[]{:S(2)}) async-start(), calls=%async_computation.7 | async-start | bytes 1179648 | tf_op jit(solution)/shard_map/reduce_scatter | solution.py:347
  1852.9 38.3 %copy-start.86 = (f32[256]{0:T(256)S(1)}, f32[256]{0:T(256)}, u32[]{:S(2)}) copy-start(f32[256]{0:T(256)} %copy-done.85) | copy-start | bytes 3076
  1852.9 38.3 %copy-start.22 = (bf16[256,2048]{1,0:T(8,128)(2,1)S(1)}, bf16[256,2048]{1,0:T(8,128)(2,1)}, u32[]{:S(2)}) copy-start(bf16[256,2048]{1,0:T(8,128)(2,1)} %param.25) | copy-start | bytes 3145732
  1934.7 66.7 %copy-start.37 = (f32[256,64]{0,1:T(8,128)S(1)}, f32[256,64]{0,1:T(8,128)}, u32[]{:S(2)}) copy-start(f32[256,64]{0,1:T(8,128)} %copy-done.36) | copy-start | bytes 196612
  1934.7 67.5 %copy-start.28 = (f32[256,128]{0,1:T(8,128)S(1)}, f32[256,128]{0,1:T(8,128)}, u32[]{:S(2)}) copy-start(f32[256,128]{0,1:T(8,128)} %copy-done.27) | copy-start | bytes 393220
  1934.7 67.6 %copy-start.35 = (f32[256,64]{0,1:T(8,128)S(1)}, f32[256,64]{0,1:T(8,128)}, u32[]{:S(2)}) copy-start(f32[256,64]{0,1:T(8,128)} %copy-done.34) | copy-start | bytes 196612
  1934.7 67.6 %copy-start.73 = (f32[256]{0:T(256)S(1)}, f32[256]{0:T(256)}, u32[]{:S(2)}) copy-start(f32[256]{0:T(256)} %copy-done.72) | copy-start | bytes 3076
  1934.7 67.6 %copy-start.88 = (f32[128]{0:T(128)S(1)}, f32[128]{0:T(128)}, u32[]{:S(2)}) copy-start(f32[128]{0:T(128)} %param.35) | copy-start | bytes 1540
  1934.7 68.5 %copy-start.92 = (f32[256]{0:T(256)S(1)}, f32[256]{0:T(256)}, u32[]{:S(2)}) copy-start(f32[256]{0:T(256)} %copy-done.91) | copy-start | bytes 3076
  1937.1 127.6 %all-reduce.23.cloned.1.call-start = ((), (), s32[]{:S(2)}) async-start(), calls=%async_computation.9 | async-start | bytes 4194304 | tf_op jit(solution)/shard_map/psum | solution.py:241
  2012.7 360.6 %all-reduce.21.cloned.1.call-start = ((), (), s32[]{:S(2)}) async-start(), calls=%async_computation.8 | async-start | bytes 19005440 | tf_op jit(solution)/shard_map/psum | solution.py:392
  2047.8 42.8 %copy-start.82 = (f32[256]{0:T(256)S(1)}, f32[256]{0:T(256)}, u32[]{:S(2)}) copy-start(f32[256]{0:T(256)} %copy-done.81) | copy-start | bytes 3076
  (78 other events, 538.5 us)
Sparse Core Ops, SparseCore 0:
  144.5 48.6 all-reduce.16
  1836.3 51.6 all-reduce.18
  1937.3 64.0 reduce-scatter.1
  2012.7 50.5 all-reduce.22
  2069.2 304.0 all-reduce.20
where the time goes:
time: 2410 us; the launch traced here: 2400 us
  waiting for transfers between devices  1670 us (69%)
  local copies, waits for them, and re-layouts  247 us (10%)
  matrix products  195 us (8%)
  blocking collectives  169 us (7%)
  other arithmetic  78.2 us (3%)
  starting transfers between devices  24.3 us (1%)
    all_to_all x2, waiting for transfers between devices, bring_back(): lax.all_to_all(payload, 'expert', split_axis=0, concat_axis=0, tiled=True)  666 us
    all_to_all x2, waiting for transfers between devices, deliver(): lax.all_to_all(payload, 'expert', split_axis=0, concat_axis=0, tiled=True)  626 us
    psum x1, waiting for transfers between devices, per_device(): lax.psum(grad_w_query.astype(jnp.bfloat16), 'expert').astype(jnp.float32)  277 us
    reduce_scatter x1, waiting for transfers between devices, per_device(): lax.psum_scatter(stacked.reshape(lax.axis_size('expert') * tok_rows, 2 *...  63.1 us
  transfers between devices with their start and end apart: 9, of which 7 were waited for; matrix products, arithmetic and copies ran while one was open for 10% of the time, Pallas kernels for 0%

commit v1 on v0

--- a/solution.py
+++ b/solution.py
@@ -416,9 +416,223 @@
     )
 
 
+def all_tokens(layout, expert_ids, drop_rank):
+    packed = jnp.concatenate([layout[None], drop_rank[None], expert_ids.T], axis=0)
+    gathered = lax.all_gather(packed, "expert", axis=1, tiled=True)
+    return gathered[0], gathered[1], gathered[2:]
+
+
+BOTH = ("expert", "tensor")
+
+
+def gather_rows(rows):
+    return lax.all_gather(rows, BOTH, axis=0, tiled=True)
+
+
+def scatter_rows(partial_rows):
+    return lax.psum_scatter(partial_rows, BOTH, scatter_dimension=0, tiled=True)
+
+
+def head_device(
+    hidden_in,
+    cotangent,
+    layout,
+    seq_lengths,
+    expert_ids,
+    drop_rank,
+    norm1_gain,
+    w_query,
+    key_weight,
+    value_weight,
+    query_gain,
+    key_gain,
+    w_out,
+    norm2_gain,
+    w_router,
+    w_gate,
+    w_up,
+    w_down,
+):
+    f32, bf16 = jnp.float32, jnp.bfloat16
+    tok_rows, model_width = hidden_in.shape
+    head_dim = query_gain.shape[0]
+    expert_count = w_router.shape[1]
+    local_count, _, ff_local = w_gate.shape
+    groups = lax.axis_size("expert")
+    tensor_size = lax.axis_size("tensor")
+    total_rows = groups * tok_rows
+    own_rows = tok_rows // tensor_size
+    seq_count = seq_lengths.shape[0]
+    group = lax.axis_index("expert")
+    part = lax.axis_index("tensor")
+
+    def own(rows):
+        return lax.dynamic_slice_in_dim(rows, part * own_rows, own_rows, 0)
+
+    place, rank, ids_t = all_tokens(layout, expert_ids, drop_rank)
+    segment, position = token_tables(place, seq_lengths)
+    valid = segment < seq_count
+    hidden_all = gather_rows(own(hidden_in))
+    grad_y_all = gather_rows(own(cotangent))
+
+    head_query = lax.dynamic_slice_in_dim(w_query, group * head_dim, head_dim, 1)
+    head_out = lax.dynamic_slice_in_dim(w_out, group * head_dim, head_dim, 0)
+    qkv_weight = jnp.concatenate([head_query, key_weight, value_weight], axis=1)
+    normed1 = norm_rows(hidden_all.astype(f32), norm1_gain).astype(bf16)
+    lin = jnp.dot(normed1, qkv_weight, preferred_element_type=f32)
+    query_lin, key_lin = lin[:, :head_dim], lin[:, head_dim : 2 * head_dim]
+    values = lin[:, 2 * head_dim :].astype(bf16)
+    queries, query_pull = jax.vjp(
+        lambda v, g: shape_queries(v, g, position)[:, 0], query_lin, query_gain
+    )
+    keys, key_pull = jax.vjp(lambda v, g: shape_keys(v, g, position)[:, 0], key_lin, key_gain)
+    queries, keys = queries.astype(bf16), keys.astype(bf16)
+    allowed = visible(segment, place, segment, place)
+    scores = jnp.einsum("qd,kd->qk", queries, keys, preferred_element_type=f32)
+    scores = jnp.where(allowed, scores, NEG)
+    probability = jax.nn.softmax(scores, axis=1)
+    attended = jnp.dot(probability.astype(bf16), values, preferred_element_type=f32).astype(bf16)
+    att_rows = lax.all_to_all(attended, "expert", split_axis=0, concat_axis=0, tiled=True)
+    att_rows = jnp.transpose(att_rows.reshape(groups, tok_rows, head_dim), (1, 0, 2)).reshape(
+        tok_rows, groups * head_dim
+    )
+    branch_part = jnp.dot(att_rows, w_out, preferred_element_type=f32)
+    branch = lax.psum_scatter(
+        branch_part.astype(bf16), "tensor", scatter_dimension=0, tiled=True
+    ).astype(f32)
+    residual = own(hidden_in).astype(f32) + branch
+    normed2, norm2_pull = jax.vjp(norm_rows, residual, norm2_gain)
+    normed2 = normed2.astype(bf16)
+    normed2_all = gather_rows(normed2)
+
+    expert_range = jnp.arange(expert_count, dtype=jnp.int32)
+    chosen = jnp.any(ids_t[:, :, None] == expert_range, axis=0)
+    picks = (chosen & valid[:, None]).astype(bf16)
+    earlier = (rank[None, :] < rank[:, None]).astype(bf16)
+    slot = jnp.dot(earlier, picks, preferred_element_type=f32)
+    kept = chosen & valid[:, None] & (slot < CAP)
+
+    def gates(rows, picked):
+        logits = jnp.dot(rows, w_router, preferred_element_type=f32)
+        return jax.nn.softmax(jnp.where(picked, logits, -jnp.inf), axis=1)
+
+    gate_weight = jnp.where(kept, gates(normed2_all, chosen), 0.0)
+    gate_local = lax.dynamic_slice_in_dim(gate_weight, group * local_count, local_count, 1)
+    kept_local = lax.dynamic_slice_in_dim(kept, group * local_count, local_count, 1)
+
+    weight_in = jnp.concatenate([w_gate, w_up], axis=0)
+    weight_in = jnp.transpose(weight_in, (1, 0, 2)).reshape(model_width, -1)
+    weight_down = w_down.reshape(local_count * ff_local, model_width)
+    wide = local_count * ff_local
+    lin2 = jnp.dot(normed2_all, weight_in, preferred_element_type=f32)
+    gate_lin, up_lin = lin2[:, :wide], lin2[:, wide:]
+    sigmoid = jax.nn.sigmoid(gate_lin)
+    silu = gate_lin * sigmoid
+    spread = jnp.repeat(gate_local, ff_local, axis=1)
+    activation = (silu * up_lin).astype(bf16).astype(f32)
+    weighted = (activation * spread).astype(bf16)
+    out_part = jnp.dot(weighted, weight_down, preferred_element_type=f32)
+    grad_down = jnp.einsum("rf,rd->fd", weighted, grad_y_all, preferred_element_type=f32)
+    grad_mid = jnp.einsum("rd,fd->rf", grad_y_all, weight_down, preferred_element_type=f32)
+    dots = jnp.sum((activation * grad_mid).reshape(total_rows, local_count, ff_local), axis=2)
+    dots = jnp.where(kept_local, dots, 0.0)
+    grad_act = grad_mid * spread
+    grad_gate_lin = (grad_act * up_lin * sigmoid * (1.0 + gate_lin * (1.0 - sigmoid))).astype(bf16)
+    grad_up_lin = (grad_act * silu).astype(bf16)
+    grad_lin2 = jnp.concatenate([grad_gate_lin, grad_up_lin], axis=1)
+    grad_in = jnp.einsum("rd,rf->df", normed2_all, grad_lin2, preferred_element_type=f32)
+    grad_in = jnp.transpose(
+        grad_in.reshape(model_width, 2 * local_count, ff_local), (1, 0, 2)
+    )
+    grad_normed2_part = jnp.einsum(
+        "rf,df->rd", grad_lin2, weight_in, preferred_element_type=f32
+    )
+    dots_wide = jnp.zeros((total_rows, head_dim), f32)
+    dots_wide = lax.dynamic_update_slice(dots_wide, dots, (0, group * local_count))
+    back = scatter_rows(
+        jnp.concatenate([grad_normed2_part, dots_wide], axis=1).astype(bf16)
+    ).astype(f32)
+    moe_branch = scatter_rows(out_part.astype(bf16)).astype(f32)
+    out_own = (residual + moe_branch).astype(bf16)
+
+    start = group * tok_rows + part * own_rows
+    chosen_own = lax.dynamic_slice_in_dim(chosen, start, own_rows, 0)
+    soft_own = gates(normed2, chosen_own)
+    grad_soft = back[:, model_width : model_width + expert_count]
+    grad_logits = (
+        soft_own * (grad_soft - jnp.sum(soft_own * grad_soft, axis=1, keepdims=True))
+    ).astype(bf16)
+    grad_router = jnp.einsum("td,te->de", normed2, grad_logits, preferred_element_type=f32)
+    grad_normed2 = back[:, :model_width] + jnp.einsum(
+        "te,de->td", grad_logits, w_router, preferred_element_type=f32
+    )
+    grad_resid_norm, grad_norm2 = norm2_pull(grad_normed2)
+    grad_residual = own(cotangent).astype(f32) + grad_resid_norm
+    grad_residual_all = gather_rows(grad_residual.astype(bf16))
+
+    grad_out = jnp.einsum("rc,rd->cd", attended, grad_residual_all, preferred_element_type=f32)
+    grad_att = jnp.einsum(
+        "rd,cd->rc", grad_residual_all, head_out, preferred_element_type=f32
+    ).astype(bf16)
+    grad_prob = jnp.einsum("qd,kd->qk", grad_att, values, preferred_element_type=f32)
+    delta = jnp.sum(probability * grad_prob, axis=1, keepdims=True)
+    grad_scores = (probability * (grad_prob - delta)).astype(bf16)
+    grad_queries = jnp.dot(grad_scores, keys, preferred_element_type=f32)
+    grad_keys = jnp.einsum("qk,qd->kd", grad_scores, queries, preferred_element_type=f32)
+    grad_values = jnp.einsum(
+        "qk,qd->kd", probability.astype(bf16), grad_att, preferred_element_type=f32
+    )
+    grad_query_lin, grad_qgain = query_pull(grad_queries)
+    grad_key_lin, grad_kgain = key_pull(grad_keys)
+    grad_lin = jnp.concatenate([grad_query_lin, grad_key_lin, grad_values], axis=1).astype(bf16)
+    grad_qkv = jnp.einsum("td,tc->dc", normed1, grad_lin, preferred_element_type=f32)
+    grad_normed1_part = jnp.einsum(
+        "tc,dc->td", grad_lin, qkv_weight, preferred_element_type=f32
+    )
+    grad_normed1 = scatter_rows(grad_normed1_part.astype(bf16)).astype(f32)
+    norm1_pull = jax.vjp(norm_rows, own(hidden_in).astype(f32), norm1_gain)[1]
+    grad_hidden_norm, grad_norm1 = norm1_pull(grad_normed1)
+    grad_hidden_own = (grad_residual + grad_hidden_norm).astype(bf16)
+    ends = lax.all_gather(
+        jnp.concatenate([out_own, grad_hidden_own], axis=1), "tensor", axis=0, tiled=True
+    )
+    grad_query = lax.all_gather(
+        grad_qkv[:, :head_dim].astype(bf16), "expert", axis=1, tiled=True
+    ).astype(f32)
+    grad_out = lax.all_gather(grad_out.astype(bf16), "expert", axis=0, tiled=True).astype(f32)
+    grad_kv = lax.psum(grad_qkv[:, head_dim:].astype(bf16), "expert").astype(f32)
+    grad_norm1, grad_norm2, grad_qgain, grad_kgain, grad_router = lax.psum(
+        (grad_norm1, grad_norm2, grad_qgain, grad_kgain, grad_router), BOTH
+    )
+    grad_down = grad_down.reshape(local_count, ff_local, model_width)
+    return (
+        ends[:, :model_width],
+        ends[:, model_width:],
+        grad_norm1,
+        grad_query,
+        grad_kv[:, :head_dim],
+        grad_kv[:, head_dim:],
+        grad_qgain,
+        grad_kgain,
+        grad_out,
+        grad_norm2,
+        grad_router,
+        grad_in[:local_count],
+        grad_in[local_count:],
+        grad_down,
+    )
+
+
 def solution(mesh):
+    groups = mesh.shape["expert"]
+
+    def device_fn(*operands):
+        heads = operands[7].shape[1] // operands[10].shape[0]
+        one_head = heads == groups and operands[8].shape[1] == operands[10].shape[0]
+        return (head_device if one_head else per_device)(*operands)
+
     return jax.shard_map(
-        per_device,
+        device_fn,
         mesh=mesh,
         in_specs=(
             P("expert", None),

time: 2410 us -> 1380 us (0.57)
  waiting for transfers between devices: 1670 us -> 978 us
  local copies, waits for them, and re-layouts: 247 us -> 44 us
  blocking collectives: 169 us -> 90.6 us
  matrix products: 195 us -> 155 us
    all_to_all x4 -> x0, waiting for transfers between devices: 1290 us -> none  [the longest x2 666 us: bring_back(): lax.all_to_all(payload, 'expert', split_axis=0, concat_axis=0, tiled=True)]
    all_gather x0 -> x7, waiting for transfers between devices: none -> 386 us  [the longest x4 244 us: gather_rows(): return lax.all_gather(rows, BOTH, axis=0, tiled=True)]
    reduce_scatter x1 -> x4, waiting for transfers between devices: 63.1 us -> 436 us  [the longest x3 413 us: scatter_rows(): return lax.psum_scatter(partial_rows, BOTH, scatter_dimension=0, tiled=True)]
    psum x4 -> x2, waiting for transfers between devices: 313 us -> 156 us  [the longest x1 104 us: head_device(): lax.psum((grad_norm1, grad_norm2, grad_qgain, grad_kgain, grad_router), B...]
    gather x15 -> x0, local copies, waits for them, and re-layouts: 157 us -> none  [the longest x1 35.8 us: per_device(): pair_grads[slot_pair]]
    all_gather x5 -> x1, blocking collectives: 135 us -> 32.6 us  [all_tokens(): gathered = lax.all_gather(packed, 'expert', axis=1, tiled=True)]
    dot_general x49 -> x23, matrix products: 195 us -> 155 us  [the longest x1 14.7 us: head_device(): scores = jnp.einsum('qd,kd->qk', queries, keys, preferred_element_type=f32)]
    concatenate x6 -> x0, local copies, waits for them, and re-layouts: 37.6 us -> none  [the longest x1 13.9 us: per_device(): jnp.concatenate([grad_returned.reshape(dump_index, model_width), jnp.zero...]
  transfers between devices with their start and end apart: 9 -> 13, of which waited for: 7 -> 12; matrix products, arithmetic and copies ran while one was open for 10% -> 8% of each run, Pallas kernels for 0% -> 0%
where the time goes in v1:
time: 1380 us
  waiting for transfers between devices  978 us (71%)
  matrix products  155 us (11%)
  other arithmetic  93.3 us (7%)
  blocking collectives  90.6 us (7%)
  local copies, waits for them, and re-layouts  44 us (3%)
  between operations  15 us (1%)
    reduce_scatter x3, waiting for transfers between devices, scatter_rows(): return lax.psum_scatter(partial_rows, BOTH, scatter_dimension=0, tiled=True)  413 us
    all_gather x4, waiting for transfers between devices, gather_rows(): return lax.all_gather(rows, BOTH, axis=0, tiled=True)  244 us
    psum x1, waiting for transfers between devices, head_device(): lax.psum((grad_norm1, grad_norm2, grad_qgain, grad_kgain, grad_router), B...  104 us
    all_gather x1, waiting for transfers between devices, head_device(): lax.all_gather(grad_qkv[:, :head_dim].astype(bf16), 'expert', axis=1, til...  74.7 us
    all_gather x1, waiting for transfers between devices, head_device(): lax.all_gather(grad_out.astype(bf16), 'expert', axis=0, tiled=True)  67.3 us
    psum x1, waiting for transfers between devices, head_device(): lax.psum(grad_qkv[:, head_dim:].astype(bf16), 'expert').astype(f32)  51.6 us
    psum x1, blocking collectives, head_device(): lax.psum((grad_norm1, grad_norm2, grad_qgain, grad_kgain, grad_router), B...  39.2 us
    all_gather x1, blocking collectives, all_tokens(): gathered = lax.all_gather(packed, 'expert', axis=1, tiled=True)  32.6 us
  transfers between devices with their start and end apart: 13, of which 12 were waited for; matrix products, arithmetic and copies ran while one was open for 8% of the time, Pallas kernels for 0%

profile of v1, /device:TPU:0, one launch (start us, length us, event | category | flops | bytes accessed | tf_op | source)
XLA Modules:
  0.0 1376.4 jit_solution(9442896550912258059)
XLA Ops:
  10.7 32.6 %all_gather.24 = s32[10,2048]{1,0:T(8,128)S(1)} all-gather(s32[10,256]{1,0:T(8,128)S(1)} %pad_add_fusion), channel_id=1, replica_groups=mesh['expert'=8,'tensor'=4] {'expert'}, dimensions={1}, use_global_device_ids=true | all-gather | bytes 92160 | tf_op jit(solution)/shard_map/all_gather | solution.py:421
  47.1 44.6 %all-gather.8.cloned.1.call-done = bf16[2048,2048]{1,0:T(8,128)(2,1)} async-done(((bf16[64,2048]{1,0:T(8,128)(2,1)}), bf16[2048,2048]{1,0:T(8,128)(2,1)}) %all-gather.8.cloned.1.call-update) | async-done | bytes 8388624 | tf_op jit(solution)/shard_map/all_gather | solution.py:429
  104.5 14.7 %fusion.7 = (f32[2048]{0:T(1024)S(1)}, f32[2048,2048]{0,1:T(8,128)S(1)}) fusion(s32[2048]{0:T(1024)S(1)} %bitcast.127, s32[2048]{0:T(1024)S(1)} %get-tuple-element.27, bf16[2048,128]{0,1:T(8,128)(2,1)S(1)} %get-tuple-element.46, bf16[2048,128]{0,1:T(8,128)(2,1)S(1)} %get-tuple-element.45), kind=kOutput, calls=%fused_computation.14 | convolution fusion | flops 1094711296 | bytes 17850368 | tf_op jit(solution)/shard_map/qd,kd->qk/dot_general | solution.py:491
  131.2 10.2 fusion.5
  147.4 18.8 %all_to_all.9 = bf16[8,256,128]{1,2,0:T(8,128)(2,1)S(1)} all-to-all(bf16[8,256,128]{1,2,0:T(8,128)(2,1)S(1)} %copy.50), channel_id=1, replica_groups=mesh['expert'=8,'tensor'=4] {'expert'}, dimensions={0} | all-to-all | bytes 1048576 | tf_op jit(solution)/shard_map/all_to_all | solution.py:495
  170.8 23.1 %reduce-scatter.5.cloned.1.call-done = bf16[64,2048]{1,0:T(8,128)(2,1)} async-done(((bf16[256,2048]{1,0:T(8,128)(2,1)}), bf16[64,2048]{1,0:T(8,128)(2,1)}) %reduce-scatter.5.cloned.1.call-update) | async-done | bytes 262160 | tf_op jit(solution)/shard_map/reduce_scatter | solution.py:500
  206.2 68.5 %all-gather.10.cloned.1.call-done = bf16[2048,2048]{1,0:T(8,128)(2,1)} async-done(((bf16[64,2048]{1,0:T(8,128)(2,1)}), bf16[2048,2048]{1,0:T(8,128)(2,1)}) %all-gather.10.cloned.1.call-update) | async-done | bytes 8388624 | tf_op jit(solution)/shard_map/all_gather | solution.py:429
  284.5 12.2 fusion.102
  296.8 57.4 %all-gather.12.cloned.1.call-done = bf16[2048,2048]{1,0:T(8,128)(2,1)} async-done(((bf16[64,2048]{1,0:T(8,128)(2,1)}), bf16[2048,2048]{1,0:T(8,128)(2,1)}) %all-gather.12.cloned.1.call-update) | async-done | bytes 8388624 | tf_op jit(solution)/shard_map/all_gather | solution.py:429
  354.2 12.0 multiply_convert_fusion.2
  372.9 11.4 convolution_convert_fusion.1
  390.3 8.1 pad_maximum_fusion
  400.5 147.0 %reduce-scatter.9.cloned.1.call-done = bf16[64,2176]{1,0:T(8,128)(2,1)} async-done(((bf16[2048,2176]{1,0:T(8,128)(2,1)}), bf16[64,2176]{1,0:T(8,128)(2,1)}) %reduce-scatter.9.cloned.1.call-update) | async-done | bytes 278544 | tf_op jit(solution)/shard_map/reduce_scatter | solution.py:433
  553.9 73.4 %all-gather.14.cloned.1.call-done = bf16[2048,2048]{1,0:T(8,128)(2,1)} async-done(((bf16[64,2048]{1,0:T(8,128)(2,1)}), bf16[2048,2048]{1,0:T(8,128)(2,1)}) %all-gather.14.cloned.1.call-update) | async-done | bytes 8388624 | tf_op jit(solution)/shard_map/all_gather | solution.py:429
  627.4 6.7 convolution_convert_fusion.6
  634.1 9.7 fusion.22
  643.8 10.2 multiply_reduce_fusion
  654.1 20.9 %multiply_convert_fusion = bf16[2048,2048]{0,1:T(8,128)(2,1)S(1)} fusion(f32[2048,2048]{0,1:T(8,128)} %get-tuple-element.80, f32[2048]{0:T(1024)} %get-tuple-element.79, f32[2048]{0:T(1024)} %copy-done.33, f32[2048]{0:T(1024)} %copy-done.32, f32[2048,2048]{0,1:T(8,128)} %copy-done.2, s32[2048]{0:T(1024)S(1)} %bitcast.130, s32[2048]{0:T(1024)S(1)} %get-tuple-element.27), kind=kLoop, calls=%fused_computation.5 | loop fusion | flops 37748736 | bytes 41984000 | tf_op jit(solution)/shard_map/convert_element_type | solution.py:579
  683.6 6.8 convolution_convert_fusion
  690.5 8.6 convolution_convert_fusion.2
  699.8 8.7 convolution_convert_fusion.3
  718.5 119.7 %reduce-scatter.11.cloned.1.call-done = bf16[64,2048]{1,0:T(8,128)(2,1)} async-done(((bf16[2048,2048]{1,0:T(8,128)(2,1)}), bf16[64,2048]{1,0:T(8,128)(2,1)}) %reduce-scatter.11.cloned.1.call-update) | async-done | bytes 262160 | tf_op jit(solution)/shard_map/reduce_scatter | solution.py:433
  839.6 146.2 %reduce-scatter.7.cloned.1.call-done = bf16[64,2048]{1,0:T(8,128)(2,1)} async-done(((bf16[2048,2048]{1,0:T(8,128)(2,1)}), bf16[64,2048]{1,0:T(8,128)(2,1)}) %reduce-scatter.7.cloned.1.call-update) | async-done | bytes 262160 | tf_op jit(solution)/shard_map/reduce_scatter | solution.py:433
  988.4 10.4 fusion.31
  1002.0 8.6 fusion.104
  1012.3 51.6 %all-reduce.8.cloned.1.call-done = bf16[2048,256]{1,0:T(8,128)(2,1)} async-done(((bf16[2048,256]{1,0:T(8,128)(2,1)}), bf16[2048,256]{1,0:T(8,128)(2,1)}) %all-reduce.8.cloned.1.call-update) | async-done | bytes 1048592 | tf_op jit(solution)/shard_map/psum | solution.py:603
  1066.5 74.7 %all-gather.18.cloned.1.call-done = bf16[2048,1024]{1,0:T(8,128)(2,1)} async-done(((bf16[2048,128]{1,0:T(8,128)(2,1)}), bf16[2048,1024]{1,0:T(8,128)(2,1)}) %all-gather.18.cloned.1.call-update) | async-done | bytes 4194320 | tf_op jit(solution)/shard_map/all_gather | solution.py:599
  1141.2 6.6 convert_element_type.146
  1147.8 67.3 %all-gather.20.cloned.1.call-done = bf16[1024,2048]{1,0:T(8,128)(2,1)} async-done(((bf16[128,2048]{1,0:T(8,128)(2,1)}), bf16[1024,2048]{1,0:T(8,128)(2,1)}) %all-gather.20.cloned.1.call-update) | async-done | bytes 4194320 | tf_op jit(solution)/shard_map/all_gather | solution.py:602
  1215.1 6.7 convert_element_type.149
  1221.8 39.2 %all-reduce.4 = (f32[2048]{0:T(1024)}, f32[128]{0:T(128)}, f32[128]{0:T(128)}, f32[2048]{0:T(1024)}) all-reduce(f32[2048]{0:T(1024)S(1)} %get-tuple-element.24, f32[128]{0:T(128)S(1)} %get-tuple-element.19, f32[128]{0:T(128)S(1)} %get-tuple-element.14, ...), channel_id=1, replica_groups=mesh['expert'=8,'tensor'=4] {'expert','tensor'}, use_global_device_ids=true, to_apply=%region_27.28 | all-reduce | flops 4352 | bytes 34816 | tf_op jit(solution)/shard_map/psum | solution.py:604
  1264.1 104.1 %all-reduce.10.cloned.1.call-done = f32[2048,16]{0,1:T(8,128)} async-done(((f32[2048,16]{0,1:T(8,128)}), f32[2048,16]{0,1:T(8,128)}) %all-reduce.10.cloned.1.call-update) | async-done | bytes 131088 | tf_op jit(solution)/shard_map/psum | solution.py:604
  (239 shorter events, 120.8 us)
Async XLA Ops:
  7.2 347.0 %copy-start = (bf16[2,192,2048]{2,1,0:T(8,128)(2,1)S(1)}, bf16[2,192,2048]{2,1,0:T(8,128)(2,1)}, u32[]{:S(2)}) copy-start(bf16[2,192,2048]{2,1,0:T(8,128)(2,1)} %param.35) | copy-start | bytes 4718596
  7.2 84.4 %all-gather.8.cloned.1.call-start = ((), (), s32[]{:S(2)}) async-start(), calls=%async_computation.5 | async-start | bytes 8650752 | tf_op jit(solution)/shard_map/all_gather | solution.py:429
  9.1 184.8 %reduce-scatter.5.cloned.1.call-start = ((), (), s32[]{:S(2)}) async-start(), calls=%async_computation.6 | async-start | bytes 1310720 | tf_op jit(solution)/shard_map/reduce_scatter | solution.py:500
  45.1 51.7 %copy-start.23 = (bf16[2048,128]{1,0:T(8,128)(2,1)}, bf16[2048,128]{1,0:T(8,128)(2,1)S(1)}, u32[]{:S(2)}) copy-start(bf16[2048,128]{1,0:T(8,128)(2,1)S(1)} %constant_dynamic-slice_fusion.1) | copy-start | bytes 1572868
  47.0 56.5 %copy-start.6 = (f32[2048,64]{0,1:T(8,128)}, f32[2048,64]{0,1:T(8,128)S(1)}, u32[]{:S(2)}) copy-start(f32[2048,64]{0,1:T(8,128)S(1)} %get-tuple-element.69) | copy-start | bytes 1572868
  47.1 49.8 %copy-start.41 = (f32[2048]{0:T(1024)S(1)}, f32[2048]{0:T(1024)}, u32[]{:S(2)}) copy-start(f32[2048]{0:T(1024)} %param.24) | copy-start | bytes 24580
  102.6 38.9 %copy-start.3 = (f32[2048,384]{0,1:T(8,128)}, f32[2048,384]{0,1:T(8,128)S(1)}, u32[]{:S(2)}) copy-start(f32[2048,384]{0,1:T(8,128)S(1)} %fusion.17) | copy-start | bytes 9437188
  170.7 103.9 %all-gather.10.cloned.1.call-start = ((), (), s32[]{:S(2)}) async-start(), calls=%async_computation.7 | async-start | bytes 8650752 | tf_op jit(solution)/shard_map/all_gather | solution.py:429
  197.0 157.1 %all-gather.12.cloned.1.call-start = ((), (), s32[]{:S(2)}) async-start(), calls=%async_computation.9 | async-start | bytes 8650752 | tf_op jit(solution)/shard_map/all_gather | solution.py:429
  198.8 348.7 %reduce-scatter.9.cloned.1.call-start = ((), (), s32[]{:S(2)}) async-start(), calls=%async_computation.10 | async-start | bytes 9191424 | tf_op jit(solution)/shard_map/reduce_scatter | solution.py:433
  199.3 75.3 %copy-start.29 = (pred[2048,16]{1,0:T(32,128)(4,1)}, pred[2048,16]{1,0:T(32,128)(4,1)S(1)}, u32[]{:S(2)}) copy-start(pred[2048,16]{1,0:T(32,128)(4,1)S(1)} %copy.51) | copy-start | bytes 98308
  203.3 71.4 %copy-start.40 = (bf16[2048,16]{0,1:T(8,128)(2,1)S(1)}, bf16[2048,16]{0,1:T(8,128)(2,1)}, u32[]{:S(2)}) copy-start(bf16[2048,16]{0,1:T(8,128)(2,1)} %param.32) | copy-start | bytes 196612
  398.3 150.9 %copy-start.8 = (bf16[64,2048]{1,0:T(8,128)(2,1)S(1)}, bf16[64,2048]{1,0:T(8,128)(2,1)}, u32[]{:S(2)}) copy-start(bf16[64,2048]{1,0:T(8,128)(2,1)} %reduce-scatter.5.cloned.1.call-done) | copy-start | bytes 786436
  398.3 150.9 %copy-start.54 = (f32[64]{0:T(128)S(1)}, f32[64]{0:T(128)}, u32[]{:S(2)}) copy-start(f32[64]{0:T(128)} %copy-done.53) | copy-start | bytes 772
  398.3 229.0 %all-gather.14.cloned.1.call-start = ((), (), s32[]{:S(2)}) async-start(), calls=%async_computation.11 | async-start | bytes 8650752 | tf_op jit(solution)/shard_map/all_gather | solution.py:429
  400.3 227.1 %copy-start.21 = (f32[64,16]{1,0:T(8,128)}, f32[64,16]{1,0:T(8,128)S(1)}, u32[]{:S(2)}) copy-start(f32[64,16]{1,0:T(8,128)S(1)} %get-tuple-element.77) | copy-start | bytes 12292
  400.3 227.1 %copy-start.47 = (f32[64]{0:T(128)}, f32[64]{0:T(128)S(1)}, u32[]{:S(2)}) copy-start(f32[64]{0:T(128)S(1)} %get-tuple-element.76) | copy-start | bytes 772
  400.5 226.9 %copy-start.56 = (f32[64]{0:T(128)}, f32[64]{0:T(128)S(1)}, u32[]{:S(2)}) copy-start(f32[64]{0:T(128)S(1)} %fusion.78) | copy-start | bytes 772
  551.8 75.5 %copy-start.58 = (f32[64]{0:T(128)}, f32[64]{0:T(128)S(1)}, u32[]{:S(2)}) copy-start(f32[64]{0:T(128)S(1)} %multiply_multiply_fusion.3) | copy-start | bytes 772
  553.8 284.4 %reduce-scatter.11.cloned.1.call-start = ((), (), s32[]{:S(2)}) async-start(), calls=%async_computation.12 | async-start | bytes 8650752 | tf_op jit(solution)/shard_map/reduce_scatter | solution.py:433
  690.4 295.3 %reduce-scatter.7.cloned.1.call-start = ((), (), s32[]{:S(2)}) async-start(), calls=%async_computation.8 | async-start | bytes 8650752 | tf_op jit(solution)/shard_map/reduce_scatter | solution.py:433
  699.1 364.7 %all-reduce.8.cloned.1.call-start = ((), (), s32[]{:S(2)}) async-start(), calls=%async_computation.15 | async-start | bytes 2097152 | tf_op jit(solution)/shard_map/psum | solution.py:603
  710.7 430.5 %all-gather.18.cloned.1.call-start = ((), (), s32[]{:S(2)}) async-start(), calls=%async_computation.14 | async-start | bytes 4718592 | tf_op jit(solution)/shard_map/all_gather | solution.py:599
  712.7 273.1 %copy-start.9 = (bf16[64,2048]{1,0:T(8,128)(2,1)S(1)}, bf16[64,2048]{1,0:T(8,128)(2,1)}, u32[]{:S(2)}) copy-start(bf16[64,2048]{1,0:T(8,128)(2,1)} %reduce-scatter.5.cloned.1.call-done) | copy-start | bytes 786436
  712.7 273.1 %copy-start.15 = (f32[64,2048]{1,0:T(8,128)S(1)}, f32[64,2048]{1,0:T(8,128)}, u32[]{:S(2)}) copy-start(f32[64,2048]{1,0:T(8,128)} %copy-done.14) | copy-start | bytes 1572868
  712.7 273.1 %copy-start.35 = (f32[2048]{0:T(1024)S(1)}, f32[2048]{0:T(1024)}, u32[]{:S(2)}) copy-start(f32[2048]{0:T(1024)} %param.31) | copy-start | bytes 24580
  712.7 273.1 %copy-start.55 = (f32[64]{0:T(128)S(1)}, f32[64]{0:T(128)}, u32[]{:S(2)}) copy-start(f32[64]{0:T(128)} %copy-done.53) | copy-start | bytes 772
  712.7 273.1 %copy-start.59 = (f32[64]{0:T(128)S(1)}, f32[64]{0:T(128)}, u32[]{:S(2)}) copy-start(f32[64]{0:T(128)} %copy-done.58) | copy-start | bytes 772
  712.7 502.4 %all-gather.20.cloned.1.call-start = ((), (), s32[]{:S(2)}) async-start(), calls=%async_computation.16 | async-start | bytes 4718592 | tf_op jit(solution)/shard_map/all_gather | solution.py:602
  718.4 542.5 %all-gather.16.cloned.1.call-start = ((), (), s32[]{:S(2)}) async-start(), calls=%async_computation.13 | async-start | bytes 2621440 | tf_op jit(solution)/shard_map/all_gather | solution.py:596
  988.3 379.8 %all-reduce.10.cloned.1.call-start = ((), (), s32[]{:S(2)}) async-start(), calls=%async_computation.17 | async-start | bytes 262144 | tf_op jit(solution)/shard_map/psum | solution.py:604
  1147.8 74.0 %copy-start.45 = (f32[2048]{0:T(1024)S(1)}, f32[2048]{0:T(1024)}, u32[]{:S(2)}) copy-start(f32[2048]{0:T(1024)} %get-tuple-element.22) | copy-start | bytes 24580
  (51 other events, 314.0 us)
Sparse Core Ops, SparseCore 0:
  11.5 80.1 all-gather.7
  170.8 22.9 reduce-scatter.4
  197.1 77.4 all-gather.9
  278.4 75.7 all-gather.11
  398.5 148.9 reduce-scatter.8
  554.0 73.3 all-gather.13
  690.6 147.6 reduce-scatter.10
  841.1 144.6 reduce-scatter.6
  989.9 73.9 all-reduce.7
  1066.5 74.5 all-gather.17
  1143.5 71.5 all-gather.19
  1217.2 21.5 all-gather.15
  1245.8 122.2 all-reduce.9

commit v2 on v1

--- a/solution.py
+++ b/solution.py
@@ -4,6 +4,8 @@
 import jax
 import jax.numpy as jnp
 from jax import lax
+from jax.experimental import pallas as pl
+from jax.experimental.pallas import tpu as pltpu
 from jax.sharding import PartitionSpec as P
 
 TOPK = 8
@@ -425,12 +427,316 @@
 BOTH = ("expert", "tensor")
 
 
+MESH = pl.DeviceIdType.MESH
+FAR_FIRST = (3, -3, 2, -2, 1, -1, 0)
+
+
+class Spot:
+    def __init__(self):
+        group, part = lax.axis_index("expert"), lax.axis_index("tensor")
+        self.z, self.y = group // 2, group % 2
+        self.x, self.c = part // 2, part % 2
+
+    def has(self, dz):
+        return (self.z + dz >= 0) & (self.z + dz <= 3)
+
+    def device(self, dz=0, dy=0, dx=0, dc=0):
+        y = 1 - self.y if dy else self.y
+        x = 1 - self.x if dx else self.x
+        c = 1 - self.c if dc else self.c
+        return ((self.z + dz) * 2 + y, x * 2 + c)
+
+    def rows(self, dz, dy, dx, dc, count):
+        group, part = self.device(dz, dy, dx, dc)
+        return pl.ds(pl.multiple_of((group * 4 + part) * count, count), count)
+
+    def greet(self):
+        barrier = pltpu.get_barrier_semaphore()
+        for step in ((0, 1, 0, 0), (0, 0, 1, 0), (0, 0, 0, 1)):
+            pl.semaphore_signal(barrier, inc=1, device_id=self.device(*step), device_id_type=MESH)
+        for dz in (1, -1):
+
+            @pl.when(self.has(dz))
+            def _(dz=dz):
+                pl.semaphore_signal(
+                    barrier, inc=1, device_id=self.device(dz), device_id_type=MESH
+                )
+
+        inner = jnp.where((self.z > 0) & (self.z < 3), 1, 0)
+        pl.semaphore_wait(barrier, 4 + inner)
+
+
+def when_has(spot, dz, action):
+    if dz == 0:
+        action()
+    else:
+        pl.when(spot.has(dz))(action)
+
+
+def gather_kernel(src, out, recv, z_send, y_send, x_send, c_send, c_recv, local_sem):
+    count, width = src.shape
+    half = width // 2
+    first, second, whole = pl.ds(0, half), pl.ds(half, half), pl.ds(0, width)
+    spot = Spot()
+    local = pltpu.make_async_copy(src, out.at[spot.rows(0, 0, 0, 0, count), :], local_sem)
+    local.start()
+    spot.greet()
+
+    def send(dz, dy, dx, columns, send_sem, recv_sem, device):
+        place = out.at[spot.rows(dz, dy, dx, 0, count), columns]
+        own = dz == 0 and dy == 0 and dx == 0
+        copy = pltpu.make_async_remote_copy(
+            src_ref=src.at[:, columns] if own else place,
+            dst_ref=place,
+            send_sem=send_sem,
+            recv_sem=recv_sem,
+            device_id=device,
+            device_id_type=MESH,
+        )
+        copy.start()
+
+    def await_bytes(rows, columns, sem):
+        view = out.at[pl.ds(0, rows), columns]
+        pltpu.make_async_copy(view, view, sem).wait()
+
+    to_y, to_x, to_c = spot.device(0, 1), spot.device(0, 0, 1), spot.device(0, 0, 0, 1)
+
+    def spread(dz):
+        if dz <= 0:
+
+            @pl.when(spot.has(1))
+            def _():
+                send(dz, 0, 0, whole, z_send.at[dz + 3, 0], recv.at[0, dz + 2], spot.device(1))
+
+        if dz >= 0:
+
+            @pl.when(spot.has(-1))
+            def _():
+                send(dz, 0, 0, whole, z_send.at[dz + 3, 1], recv.at[0, dz + 4], spot.device(-1))
+
+        send(dz, 0, 0, whole, y_send, recv.at[1, dz + 3], to_y)
+        send(dz, 0, 0, whole, x_send, recv.at[2, dz + 3], to_x)
+        send(dz, 0, 0, whole, c_send, c_recv, to_c)
+
+    def take_z(dz):
+        def action():
+            await_bytes(count, whole, recv.at[0, dz + 3])
+            spread(dz)
+
+        when_has(spot, dz, action)
+
+    def take_yx(dz):
+        def action():
+            await_bytes(count, whole, recv.at[1, dz + 3])
+            send(dz, 1, 0, first, x_send, recv.at[3, dz + 3], to_x)
+            send(dz, 1, 0, whole, c_send, c_recv, to_c)
+            await_bytes(count, whole, recv.at[2, dz + 3])
+            send(dz, 0, 1, second, y_send, recv.at[4, dz + 3], to_y)
+            send(dz, 0, 1, whole, c_send, c_recv, to_c)
+
+        when_has(spot, dz, action)
+
+    def take_diagonal(dz):
+        def action():
+            await_bytes(count, first, recv.at[3, dz + 3])
+            await_bytes(count, second, recv.at[4, dz + 3])
+            send(dz, 1, 1, whole, c_send, c_recv, to_c)
+
+        when_has(spot, dz, action)
+
+    spread(0)
+    for dz in (1, -1):
+        take_z(dz)
+    take_yx(0)
+    for dz in (2, -2):
+        take_z(dz)
+    for dz in (1, -1):
+        take_yx(dz)
+    take_diagonal(0)
+    for dz in (3, -3):
+        take_z(dz)
+    for dz in (2, -2):
+        take_yx(dz)
+    for dz in (1, -1):
+        take_diagonal(dz)
+    for dz in (3, -3):
+        take_yx(dz)
+    for dz in (2, -2, 3, -3):
+        take_diagonal(dz)
+
+    await_bytes(16 * count, whole, c_recv)
+    await_bytes(16 * count, whole, c_send)
+    await_bytes(6 * count, whole, y_send)
+    await_bytes(6 * count, whole, x_send)
+    for dz in range(-3, 4):
+        for side, step in ((0, 1), (1, -1)):
+            if dz * step <= 0:
+
+                @pl.when(spot.has(dz) & spot.has(step))
+                def _(dz=dz, side=side):
+                    await_bytes(count, whole, z_send.at[dz + 3, side])
+
+    local.wait()
+
+
 def gather_rows(rows):
-    return lax.all_gather(rows, BOTH, axis=0, tiled=True)
-
-
-def scatter_rows(partial_rows):
-    return lax.psum_scatter(partial_rows, BOTH, scatter_dimension=0, tiled=True)
+    count, width = rows.shape
+    dma = pltpu.SemaphoreType.DMA
+    return pl.pallas_call(
+        gather_kernel,
+        out_shape=jax.ShapeDtypeStruct((32 * count, width), rows.dtype),
+        in_specs=[pl.BlockSpec(memory_space=pl.ANY)],
+        out_specs=pl.BlockSpec(memory_space=pl.ANY),
+        scratch_shapes=[dma((5, 7)), dma((7, 2)), dma, dma, dma, dma, dma],
+        compiler_params=pltpu.CompilerParams(collective_id=0, has_side_effects=True),
+        name="gather_rows",
+    )(rows)
+
+
+def scatter_kernel(
+    part, out, held, from_a, from_b, from_y, from_x, from_below, from_above,
+    c_recv, recv, z_send, y_send, x_send, c_send,
+):
+    count, width = out.shape
+    half = 1024
+    first, second, whole = pl.ds(0, half), pl.ds(half, width - half), pl.ds(0, width)
+    spot = Spot()
+    spot.greet()
+    to_y, to_x, to_c = spot.device(0, 1), spot.device(0, 0, 1), spot.device(0, 0, 0, 1)
+
+    def send(src, dst, send_sem, recv_sem, device):
+        pltpu.make_async_remote_copy(
+            src_ref=src, dst_ref=dst, send_sem=send_sem, recv_sem=recv_sem,
+            device_id=device, device_id_type=MESH,
+        ).start()
+
+    def arrive(view, sem):
+        pltpu.make_async_copy(view, view, sem).wait()
+
+    def add(into, *terms):
+        @pl.loop(0, count // 16)
+        def _(step):
+            rows = pl.ds(pl.multiple_of(step * 16, 16), 16)
+            total = into[rows, :].astype(jnp.float32)
+            for term in terms:
+                total = total + term[rows, :].astype(jnp.float32)
+            into[rows, :] = total.astype(into.dtype)
+
+    groups = ((1, 1), (1, 0), (0, 1), (0, 0))
+    for dy, dx in groups:
+        for dz in FAR_FIRST:
+
+            def action(dz=dz, dy=dy, dx=dx):
+                send(
+                    part.at[spot.rows(dz, dy, dx, 1, count), :],
+                    held.at[spot.z + dz, dy, dx],
+                    c_send, c_recv.at[dz + 3, dy, dx], to_c,
+                )
+
+            when_has(spot, dz, action)
+
+    def merge(dz, dy, dx, *terms):
+        mine = held.at[spot.z + dz, dy, dx]
+        arrive(mine, c_recv.at[dz + 3, dy, dx])
+        add(mine, part.at[spot.rows(dz, dy, dx, 0, count), :])
+        return mine
+
+    for dz in FAR_FIRST:
+
+        def action(dz=dz):
+            far = spot.z + dz
+            mine = merge(dz, 1, 1)
+            send(mine.at[:, first], from_a.at[far], x_send, recv.at[0, dz + 3], to_x)
+            send(mine.at[:, second], from_b.at[far], y_send, recv.at[1, dz + 3], to_y)
+
+        when_has(spot, dz, action)
+    for dz in FAR_FIRST:
+
+        def action(dz=dz):
+            far = spot.z + dz
+            mine = merge(dz, 1, 0)
+            arrive(from_a.at[far], recv.at[0, dz + 3])
+            add(mine.at[:, first], from_a.at[far])
+            send(mine, from_y.at[far], y_send, recv.at[2, dz + 3], to_y)
+            mine = merge(dz, 0, 1)
+            arrive(from_b.at[far], recv.at[1, dz + 3])
+            add(mine.at[:, second], from_b.at[far])
+            send(mine, from_x.at[far], x_send, recv.at[3, dz + 3], to_x)
+
+        when_has(spot, dz, action)
+    for dz in FAR_FIRST:
+
+        def action(dz=dz):
+            far = spot.z + dz
+            mine = merge(dz, 0, 0)
+            arrive(from_y.at[far], recv.at[2, dz + 3])
+            arrive(from_x.at[far], recv.at[3, dz + 3])
+            add(mine, from_y.at[far], from_x.at[far])
+            if dz >= 0:
+
+                @pl.when(spot.has(-1))
+                def _():
+                    arrive(from_below.at[far], recv.at[4, dz + 3])
+                    add(mine, from_below.at[far])
+
+            if dz <= 0:
+
+                @pl.when(spot.has(1))
+                def _():
+                    arrive(from_above.at[far], recv.at[5, dz + 3])
+                    add(mine, from_above.at[far])
+
+            if dz > 0:
+                send(mine, from_below.at[far], z_send.at[dz + 3], recv.at[4, dz + 2],
+                     spot.device(1))
+            if dz < 0:
+                send(mine, from_above.at[far], z_send.at[dz + 3], recv.at[5, dz + 4],
+                     spot.device(-1))
+            if dz == 0:
+                out[...] = mine[...].astype(out.dtype)
+
+        when_has(spot, dz, action)
+
+    def await_rows(rows, sem):
+        view = part.at[pl.ds(0, rows), :]
+        pltpu.make_async_copy(view, view, sem).wait()
+
+    await_rows(16 * count, c_send)
+    for columns, other, sem in ((second, first, y_send), (first, second, x_send)):
+        view = part.at[pl.ds(0, 4 * count), columns]
+        whole_view = part.at[pl.ds(0, 4 * count), :]
+        pltpu.make_async_copy(view, view, sem).wait()
+        pltpu.make_async_copy(whole_view, whole_view, sem).wait()
+    for dz in FAR_FIRST[:-1]:
+
+        def action(dz=dz):
+            await_rows(count, z_send.at[dz + 3])
+
+        when_has(spot, dz, action)
+
+
+def scatter_rows(partial_rows, ident):
+    total, width = partial_rows.shape
+    count = total // 32
+    dma, bf16 = pltpu.SemaphoreType.DMA, jnp.bfloat16
+    line = pltpu.VMEM((4, count, width), bf16)
+    return pl.pallas_call(
+        scatter_kernel,
+        out_shape=jax.ShapeDtypeStruct((count, width), jnp.float32),
+        in_specs=[pl.BlockSpec(memory_space=pltpu.VMEM)],
+        out_specs=pl.BlockSpec(memory_space=pltpu.VMEM),
+        scratch_shapes=[
+            pltpu.VMEM((4, 2, 2, count, width), bf16),
+            pltpu.VMEM((4, count, 1024), bf16),
+            pltpu.VMEM((4, count, width - 1024), bf16),
+            line, line, line, line,
+            dma((7, 2, 2)), dma((6, 7)), dma((7,)), dma, dma, dma,
+        ],
+        compiler_params=pltpu.CompilerParams(
+            collective_id=ident, has_side_effects=True, vmem_limit_bytes=40 << 20
+        ),
+        name="scatter_rows",
+    )(partial_rows)
 
 
 def head_device(
@@ -550,9 +856,10 @@
     dots_wide = jnp.zeros((total_rows, head_dim), f32)
     dots_wide = lax.dynamic_update_slice(dots_wide, dots, (0, group * local_count))
     back = scatter_rows(
-        jnp.concatenate([grad_normed2_part, dots_wide], axis=1).astype(bf16)
-    ).astype(f32)
-    moe_branch = scatter_rows(out_part.astype(bf16)).astype(f32)
+        jnp.concatenate([grad_normed2_part, dots_wide], axis=1).astype(bf16),
+        1,
+    )
+    moe_branch = scatter_rows(out_part.astype(bf16), 2)
     out_own = (residual + moe_branch).astype(bf16)
 
     start = group * tok_rows + part * own_rows
@@ -589,7 +896,7 @@
     grad_normed1_part = jnp.einsum(
         "tc,dc->td", grad_lin, qkv_weight, preferred_element_type=f32
     )
-    grad_normed1 = scatter_rows(grad_normed1_part.astype(bf16)).astype(f32)
+    grad_normed1 = scatter_rows(grad_normed1_part.astype(bf16), 2)
     norm1_pull = jax.vjp(norm_rows, own(hidden_in).astype(f32), norm1_gain)[1]
     grad_hidden_norm, grad_norm1 = norm1_pull(grad_normed1)
     grad_hidden_own = (grad_residual + grad_hidden_norm).astype(bf16)
@@ -628,7 +935,8 @@
 
     def device_fn(*operands):
         heads = operands[7].shape[1] // operands[10].shape[0]
-        one_head = heads == groups and operands[8].shape[1] == operands[10].shape[0]
+        one_head = heads == groups == 8 and operands[8].shape[1] == operands[10].shape[0]
+        one_head = one_head and mesh.shape["tensor"] == 4
         return (head_device if one_head else per_device)(*operands)
 
     return jax.shard_map(

time: 1380 us -> 903 us (0.65)
  waiting for transfers between devices: 978 us -> 211 us
  Pallas kernels: 0 us -> 309 us
  matrix products: 155 us -> 131 us
    reduce_scatter x3 -> x0, waiting for transfers between devices: 413 us -> none  [scatter_rows(): return lax.psum_scatter(partial_rows, BOTH, scatter_dimension=0, tiled=True)]
    pallas_call x0 -> x7, Pallas kernels: none -> 309 us  [the longest x4 166 us: gather_rows(): pl.pallas_call(gather_kernel, out_shape=jax.ShapeDtypeStruct((32 * count,...]
    all_gather x4 -> x0, waiting for transfers between devices: 244 us -> none  [gather_rows(): return lax.all_gather(rows, BOTH, axis=0, tiled=True)]
    psum x1, waiting for transfers between devices: 51.6 us -> 0.01 us  [head_device(): lax.psum(grad_qkv[:, head_dim:].astype(bf16), 'expert').astype(f32)]
    all_gather x1, waiting for transfers between devices: 74.7 us -> 23.9 us  [head_device(): lax.all_gather(grad_qkv[:, :head_dim].astype(bf16), 'expert', axis=1, til...]
    reduce_scatter x1, waiting for transfers between devices: 23.1 us -> 0.02 us  [head_device(): lax.psum_scatter(branch_part.astype(bf16), 'tensor', scatter_dimension=0,...]
    psum x1, waiting for transfers between devices: 104 us -> 120 us  [head_device(): lax.psum((grad_norm1, grad_norm2, grad_qgain, grad_kgain, grad_router), B...]
  transfers between devices with their start and end apart: 13 -> 6, of which waited for: 12 -> 3; matrix products, arithmetic and copies ran while one was open for 8% -> 7% of each run, Pallas kernels for 0% -> 16%
where the time goes in v2:
time: 903 us; the launch traced here: 899 us
  Pallas kernels  309 us (34%)
  waiting for transfers between devices  211 us (23%)
  matrix products  131 us (15%)
  blocking collectives  95 us (11%)
  other arithmetic  91.5 us (10%)
  local copies, waits for them, and re-layouts  45.9 us (5%)
  between operations  15.4 us (2%)
    pallas_call x4, Pallas kernels, gather_rows(): pl.pallas_call(gather_kernel, out_shape=jax.ShapeDtypeStruct((32 * count,...  166 us
    pallas_call x3, Pallas kernels, scatter_rows(): pl.pallas_call(scatter_kernel, out_shape=jax.ShapeDtypeStruct((count, wid...  143 us
    psum x1, waiting for transfers between devices, head_device(): lax.psum((grad_norm1, grad_norm2, grad_qgain, grad_kgain, grad_router), B...  120 us
    all_gather x1, waiting for transfers between devices, head_device(): lax.all_gather(grad_out.astype(bf16), 'expert', axis=0, tiled=True)  67 us
    psum x1, blocking collectives, head_device(): lax.psum((grad_norm1, grad_norm2, grad_qgain, grad_kgain, grad_router), B...  41.6 us
    all_gather x1, blocking collectives, all_tokens(): gathered = lax.all_gather(packed, 'expert', axis=1, tiled=True)  32.3 us
    all_gather x1, waiting for transfers between devices, head_device(): lax.all_gather(grad_qkv[:, :head_dim].astype(bf16), 'expert', axis=1, til...  23.9 us
    convert_element_type x1, other arithmetic, head_device(): grad_scores = (probability * (grad_prob - delta)).astype(bf16)  21.1 us
  transfers between devices with their start and end apart: 6, of which 3 were waited for; matrix products, arithmetic and copies ran while one was open for 7% of the time, Pallas kernels for 16%

profile of v2, /device:TPU:0, one launch (start us, length us, event | category | flops | bytes accessed | tf_op | source)
XLA Modules:
  0.0 899.3 jit_solution(3774085452454880846)
XLA Ops:
  8.9 32.3 %all_gather.12 = s32[10,2048]{1,0:T(8,128)S(1)} all-gather(s32[10,256]{1,0:T(8,128)S(1)} %pad_add_fusion), channel_id=1, replica_groups=mesh['expert'=8,'tensor'=4] {'expert'}, dimensions={1}, use_global_device_ids=true | all-gather | bytes 92160 | tf_op jit(solution)/shard_map/all_gather | solution.py:423
  43.1 39.4 %gather_rows.4 = bf16[2048,2048]{1,0:T(8,128)(2,1)} custom-call(bf16[64,2048]{1,0:T(8,128)(2,1)} %constant_dynamic-slice_fusion.2.src), custom_call_target="tpu_custom_call" | custom-call | tf_op jit(solution)/shard_map/gather_rows/pallas_call | solution.py:585
  88.9 6.4 fusion.17
  102.9 5.7 copy-done.4
  108.6 5.7 fusion.6
  114.3 10.7 %fusion.5 = f32[2048,2048]{0,1:T(8,128)S(1)} fusion(f32[2048,2048]{0,1:T(8,128)} %copy-done.4, f32[2048]{0:T(1024)S(1)} %fusion.6, f32[2048]{0:T(1024)S(1)} %get-tuple-element.71, s32[2048]{0:T(1024)S(1)} %bitcast.129, s32[2048]{0:T(1024)S(1)} %get-tuple-element.27), kind=kLoop, calls=%fused_computation.11 | loop fusion | flops 25165824 | bytes 33587200 | tf_op jit(solution)/shard_map/div | solution.py:799
  131.0 21.1 %all_to_all.9 = bf16[8,256,128]{1,2,0:T(8,128)(2,1)S(1)} all-to-all(bf16[8,256,128]{1,2,0:T(8,128)(2,1)S(1)} %copy.50), channel_id=1, replica_groups=mesh['expert'=8,'tensor'=4] {'expert'}, dimensions={0} | all-to-all | bytes 1048576 | tf_op jit(solution)/shard_map/all_to_all | solution.py:801
  158.8 44.5 %gather_rows.6 = bf16[2048,2048]{1,0:T(8,128)(2,1)} custom-call(bf16[64,2048]{1,0:T(8,128)(2,1)} %constant_dynamic-slice_fusion.src), custom_call_target="tpu_custom_call" | custom-call | tf_op jit(solution)/shard_map/gather_rows/pallas_call | solution.py:585
  213.2 42.0 %gather_rows.5 = bf16[2048,2048]{1,0:T(8,128)(2,1)} custom-call(bf16[64,2048]{1,0:T(8,128)(2,1)} %multiply_convert_fusion.4.src), custom_call_target="tpu_custom_call" | custom-call | tf_op jit(solution)/shard_map/gather_rows/pallas_call | solution.py:585
  256.4 5.8 fusion.100
  266.3 10.3 %fusion.102 = f32[2048,768]{0,1:T(8,128)S(1)} fusion(bf16[2048,2048]{1,0:T(8,128)(2,1)} %gather_rows.5, bf16[2048,768]{0,1:T(8,128)(2,1)} %bitcast.123), kind=kOutput, calls=%fused_computation.179 | convolution fusion | flops 6442450944 | bytes 17825792 | tf_op jit(solution)/shard_map/dot_general | solution.py:833
  276.6 10.2 %multiply_convert_fusion.2 = (bf16[2048,384]{0,1:T(8,128)(2,1)}, bf16[2048,384]{0,1:T(8,128)(2,1)}, bf16[2048,384]{0,1:T(8,128)(2,1)}, bf16[2048,384]{0,1:T(8,128)(2,1)S(1)}, f32[2048,384]{0,1:T(8,128)S(1)}) fusion(f32[2048,768]{0,1:T(8,128)S(1)} %fusion.102, f32[2048,2]{0,1:T(2,128)S(1)} %copy.55, bf16[2048,2048]{1,0:T(8,128)(2,1)} %gather_rows.6, ...), kind=kOutput, calls=%fused_computation.31 | convolution fusion | flops 3236167680 | bytes 25706496 | tf_op jit(solution)/shard_map/rd,fd->rf/dot_general | solution.py:842
  293.6 11.4 %convolution_convert_fusion.1 = bf16[2048,2048]{1,0:T(8,128)(2,1)} fusion(bf16[2048,768]{0,1:T(8,128)(2,1)} %bitcast.124, bf16[2048,384]{0,1:T(8,128)(2,1)} %get-tuple-element.40, bf16[2048,384]{0,1:T(8,128)(2,1)} %get-tuple-element.39), kind=kOutput, calls=%fused_computation.18 | convolution fusion | flops 6452936704 | bytes 14680064 | tf_op jit(solution)/shard_map/rf,df->rd/dot_general | solution.py:853
  310.9 8.0 pad_maximum_fusion.part
  322.5 46.0 %scatter_rows.4 = f32[64,2176]{1,0:T(8,128)S(1)} custom-call(bf16[2048,2176]{1,0:T(8,128)(2,1)S(1)} %copy-done.1), custom_call_target="tpu_custom_call" | custom-call | tf_op jit(solution)/shard_map/scatter_rows/pallas_call | solution.py:723
  372.6 40.3 %gather_rows.7 = bf16[2048,2048]{1,0:T(8,128)(2,1)} custom-call(bf16[64,2048]{1,0:T(8,128)(2,1)} %fusion.90.src), custom_call_target="tpu_custom_call" | custom-call | tf_op jit(solution)/shard_map/gather_rows/pallas_call | solution.py:585
  412.9 5.8 convolution_convert_fusion.6
  418.7 8.8 fusion.22
  427.5 10.5 %multiply_reduce_fusion = (f32[2048]{0:T(1024)S(1)}, f32[2048,2048]{0,1:T(8,128)}) fusion(f32[2048,2048]{0,1:T(8,128)} %copy-done.3, bf16[2048,128]{1,0:T(8,128)(2,1)S(1)} %convolution_convert_fusion.6, f32[2048,384]{0,1:T(8,128)S(1)} %copy-done.6), kind=kOutput, calls=%fused_computation.6 | convolution fusion | flops 1082128384 | bytes 34611200 | tf_op jit(solution)/shard_map/qd,kd->qk/dot_general | solution.py:884
  438.0 21.1 %multiply_convert_fusion = bf16[2048,2048]{0,1:T(8,128)(2,1)S(1)} fusion(f32[2048,2048]{0,1:T(8,128)} %get-tuple-element.80, f32[2048]{0:T(1024)S(1)} %get-tuple-element.79, f32[2048]{0:T(1024)S(1)} %fusion.6, f32[2048]{0:T(1024)S(1)} %get-tuple-element.71, f32[2048,2048]{0,1:T(8,128)} %copy-done.4, s32[2048]{0:T(1024)S(1)} %bitcast.130, ...), kind=kLoop, calls=%fused_computation.5 | loop fusion | flops 37748736 | bytes 41984000 | tf_op jit(solution)/shard_map/convert_element_type | solution.py:886
  467.3 5.5 convolution_convert_fusion.3
  472.9 7.0 convolution_convert_fusion.part
  484.4 49.6 %scatter_rows.5 = f32[64,2048]{1,0:T(8,128)S(1)} custom-call(bf16[2048,2048]{1,0:T(8,128)(2,1)S(1)} %copy-done.2), custom_call_target="tpu_custom_call" | custom-call | tf_op jit(solution)/shard_map/scatter_rows/pallas_call | solution.py:723
  539.2 47.2 %scatter_rows.3 = f32[64,2048]{1,0:T(8,128)S(1)} custom-call(bf16[2048,2048]{1,0:T(8,128)(2,1)S(1)} %convolution_convert_fusion.2.part), custom_call_target="tpu_custom_call" | custom-call | tf_op jit(solution)/shard_map/scatter_rows/pallas_call | solution.py:723
  597.2 10.2 %fusion.31 = f32[2048,768]{0,1:T(8,128)S(1)} fusion(bf16[2048,2048]{1,0:T(8,128)(2,1)} %gather_rows.5, bf16[2048,384]{0,1:T(8,128)(2,1)} %get-tuple-element.40, bf16[2048,384]{0,1:T(8,128)(2,1)} %get-tuple-element.39), kind=kOutput, calls=%fused_computation.47 | convolution fusion | flops 6448742400 | bytes 17825792 | tf_op jit(solution)/shard_map/rd,rf->df/dot_general | solution.py:849
  610.5 8.5 fusion.104
  619.1 41.6 %all-reduce.4 = (f32[2048]{0:T(1024)}, f32[128]{0:T(128)}, f32[128]{0:T(128)}, f32[2048]{0:T(1024)}) all-reduce(f32[2048]{0:T(1024)S(1)} %get-tuple-element.24, f32[128]{0:T(128)S(1)} %copy-done.42, f32[128]{0:T(128)S(1)} %copy-done.41, f32[2048]{0:T(1024)S(1)} %get-tuple-element.22), channel_id=1, replica_groups=mesh['expert'=8,'tensor'=4] {'expert','tensor'}, use_global_device_ids=true, to_apply=%region_24.25 | all-reduce | flops 4352 | bytes 34816 | tf_op jit(solution)/shard_map/psum | solution.py:911
  666.4 23.9 %all-gather.6.cloned.1.call-done = bf16[2048,1024]{1,0:T(8,128)(2,1)} async-done(((bf16[2048,128]{1,0:T(8,128)(2,1)}), bf16[2048,1024]{1,0:T(8,128)(2,1)}) %all-gather.6.cloned.1.call-update) | async-done | bytes 4194320 | tf_op jit(solution)/shard_map/all_gather | solution.py:906
  690.4 6.6 convert_element_type.134
  697.0 67.0 %all-gather.8.cloned.1.call-done = bf16[1024,2048]{1,0:T(8,128)(2,1)} async-done(((bf16[128,2048]{1,0:T(8,128)(2,1)}), bf16[1024,2048]{1,0:T(8,128)(2,1)}) %all-gather.8.cloned.1.call-update) | async-done | bytes 4194320 | tf_op jit(solution)/shard_map/all_gather | solution.py:909
  764.0 6.7 convert_element_type.137
  770.6 120.0 %all-reduce.10.cloned.1.call-done = f32[2048,16]{0,1:T(8,128)} async-done(((f32[2048,16]{0,1:T(8,128)}), f32[2048,16]{0,1:T(8,128)}) %all-reduce.10.cloned.1.call-update) | async-done | bytes 131088 | tf_op jit(solution)/shard_map/psum | solution.py:911
  (196 shorter events, 104.1 us)
Async XLA Ops:
  7.2 269.4 %copy-start = (bf16[2,192,2048]{2,1,0:T(8,128)(2,1)S(1)}, bf16[2,192,2048]{2,1,0:T(8,128)(2,1)}, u32[]{:S(2)}) copy-start(bf16[2,192,2048]{2,1,0:T(8,128)(2,1)} %param.35) | copy-start | bytes 4718596
  7.2 202.8 %reduce-scatter.2.cloned.1.call-start = ((), (), s32[]{:S(2)}) async-start(), calls=%async_computation.2 | async-start | bytes 1310720 | tf_op jit(solution)/shard_map/reduce_scatter | solution.py:806
  82.5 6.3 copy-start.32
  88.9 6.5 copy-start.22
  88.9 6.7 copy-start.36
  88.9 6.7 copy-start.37
  95.3 29.7 %copy-start.5 = (f32[2048,384]{0,1:T(8,128)}, f32[2048,384]{0,1:T(8,128)S(1)}, u32[]{:S(2)}) copy-start(f32[2048,384]{0,1:T(8,128)S(1)} %fusion.17) | copy-start | bytes 9437188
  156.5 504.1 %all-reduce.8.cloned.1.call-start = ((), (), s32[]{:S(2)}) async-start(), calls=%async_computation.5 | async-start | bytes 2097152 | tf_op jit(solution)/shard_map/psum | solution.py:910
  210.0 52.9 %copy-start.21 = (pred[2048,16]{1,0:T(8,128)(4,1)}, pred[2048,16]{1,0:T(8,128)(4,1)S(1)}, u32[]{:S(2)}) copy-start(pred[2048,16]{1,0:T(8,128)(4,1)S(1)} %fusion.28) | copy-start | bytes 98308
  211.3 43.9 %copy-start.47 = (f32[64]{0:T(128)}, f32[64]{0:T(128)S(1)}, u32[]{:S(2)}) copy-start(f32[64]{0:T(128)S(1)} %multiply_reduce_fusion.5) | copy-start | bytes 772
  211.3 43.9 %copy-start.38 = (f32[64]{0:T(128)}, f32[64]{0:T(128)S(1)}, u32[]{:S(2)}) copy-start(f32[64]{0:T(128)S(1)} %fusion.82) | copy-start | bytes 772
  213.2 42.1 %copy-start.9 = (bf16[64,2048]{1,0:T(8,128)(2,1)S(1)}, bf16[64,2048]{1,0:T(8,128)(2,1)}, u32[]{:S(2)}) copy-start(bf16[64,2048]{1,0:T(8,128)(2,1)} %multiply_convert_fusion.4.src) | copy-start | bytes 786436
  322.5 46.4 %copy-start.10 = (bf16[64,2048]{1,0:T(8,128)(2,1)S(1)}, bf16[64,2048]{1,0:T(8,128)(2,1)}, u32[]{:S(2)}) copy-start(bf16[64,2048]{1,0:T(8,128)(2,1)} %reduce-scatter.2.cloned.1.call-done) | copy-start | bytes 786436
  322.5 46.4 %copy-start.20 = (bf16[64,2048]{1,0:T(8,128)(2,1)S(1)}, bf16[64,2048]{1,0:T(8,128)(2,1)}, u32[]{:S(2)}) copy-start(bf16[64,2048]{1,0:T(8,128)(2,1)} %constant_dynamic-slice_fusion.2.src) | copy-start | bytes 786436
  322.5 46.4 %copy-start.31 = (bf16[2048,16]{0,1:T(8,128)(2,1)S(1)}, bf16[2048,16]{0,1:T(8,128)(2,1)}, u32[]{:S(2)}) copy-start(bf16[2048,16]{0,1:T(8,128)(2,1)} %param.32) | copy-start | bytes 196612
  322.5 46.4 %copy-start.39 = (f32[64]{0:T(128)S(1)}, f32[64]{0:T(128)}, u32[]{:S(2)}) copy-start(f32[64]{0:T(128)} %copy-done.38) | copy-start | bytes 772
  322.5 47.3 %copy-start.48 = (f32[64]{0:T(128)S(1)}, f32[64]{0:T(128)}, u32[]{:S(2)}) copy-start(f32[64]{0:T(128)} %copy-done.47) | copy-start | bytes 772
  418.7 8.8 copy-start.6
  438.0 21.1 %copy-start.25 = (bf16[2048,128]{0,1:T(8,128)(2,1)S(1)}, bf16[2048,128]{0,1:T(8,128)(2,1)}, u32[]{:S(2)}) copy-start(bf16[2048,128]{0,1:T(8,128)(2,1)} %copy-done.24) | copy-start | bytes 1572868
  472.9 7.0 copy-start.17
  472.9 7.0 copy-start.53
  481.0 182.4 %all-gather.4.cloned.1.call-start = ((), (), s32[]{:S(2)}) async-start(), calls=%async_computation.3 | async-start | bytes 2621440 | tf_op jit(solution)/shard_map/all_gather | solution.py:903
  484.4 49.6 %copy-start.18 = (bf16[2048,384]{0,1:T(8,128)(2,1)S(1)}, bf16[2048,384]{0,1:T(8,128)(2,1)}, u32[]{:S(2)}) copy-start(bf16[2048,384]{0,1:T(8,128)(2,1)} %get-tuple-element.41) | copy-start | bytes 4718596
  539.1 47.2 %copy-start.11 = (bf16[64,2048]{1,0:T(8,128)(2,1)S(1)}, bf16[64,2048]{1,0:T(8,128)(2,1)}, u32[]{:S(2)}) copy-start(bf16[64,2048]{1,0:T(8,128)(2,1)} %reduce-scatter.2.cloned.1.call-done) | copy-start | bytes 786436
  539.1 47.3 %copy-start.16 = (f32[64,2048]{1,0:T(8,128)S(1)}, f32[64,2048]{1,0:T(8,128)}, u32[]{:S(2)}) copy-start(f32[64,2048]{1,0:T(8,128)} %copy-done.15) | copy-start | bytes 1572868
  539.1 47.3 %copy-start.40 = (f32[64]{0:T(128)S(1)}, f32[64]{0:T(128)}, u32[]{:S(2)}) copy-start(f32[64]{0:T(128)} %copy-done.38) | copy-start | bytes 772
  539.1 47.2 %copy-start.46 = (f32[64]{0:T(128)S(1)}, f32[64]{0:T(128)}, u32[]{:S(2)}) copy-start(f32[64]{0:T(128)} %copy-done.45) | copy-start | bytes 772
  588.7 101.7 %all-gather.6.cloned.1.call-start = ((), (), s32[]{:S(2)}) async-start(), calls=%async_computation.4 | async-start | bytes 4718592 | tf_op jit(solution)/shard_map/all_gather | solution.py:906
  590.6 173.4 %all-gather.8.cloned.1.call-start = ((), (), s32[]{:S(2)}) async-start(), calls=%async_computation.6 | async-start | bytes 4718592 | tf_op jit(solution)/shard_map/all_gather | solution.py:909
  596.2 294.5 %all-reduce.10.cloned.1.call-start = ((), (), s32[]{:S(2)}) async-start(), calls=%async_computation.7 | async-start | bytes 262144 | tf_op jit(solution)/shard_map/psum | solution.py:911
  610.5 8.5 copy-start.41
  610.5 8.5 copy-start.42
  (30 other events, 99.5 us)
Sparse Core Ops, SparseCore 0:
  156.7 28.7 reduce-scatter.1
  481.1 84.3 all-reduce.7
  588.8 22.0 all-gather.3
  613.4 76.9 all-gather.5
  692.3 71.5 all-gather.7
  769.9 120.6 all-reduce.9

commit v3 on v2

--- a/solution.py
+++ b/solution.py
@@ -418,15 +418,6 @@
     )
 
 
-def all_tokens(layout, expert_ids, drop_rank):
-    packed = jnp.concatenate([layout[None], drop_rank[None], expert_ids.T], axis=0)
-    gathered = lax.all_gather(packed, "expert", axis=1, tiled=True)
-    return gathered[0], gathered[1], gathered[2:]
-
-
-BOTH = ("expert", "tensor")
-
-
 MESH = pl.DeviceIdType.MESH
 FAR_FIRST = (3, -3, 2, -2, 1, -1, 0)
 
@@ -473,14 +464,14 @@
         pl.when(spot.has(dz))(action)
 
 
-def gather_kernel(src, out, recv, z_send, y_send, x_send, c_send, c_recv, local_sem):
+def gather_body(
+    spot, src, out, recv, z_send, y_send, x_send, c_send, c_recv, local_sem, also=lambda *_: None
+):
     count, width = src.shape
     half = width // 2
     first, second, whole = pl.ds(0, half), pl.ds(half, half), pl.ds(0, width)
-    spot = Spot()
     local = pltpu.make_async_copy(src, out.at[spot.rows(0, 0, 0, 0, count), :], local_sem)
     local.start()
-    spot.greet()
 
     def send(dz, dy, dx, columns, send_sem, recv_sem, device):
         place = out.at[spot.rows(dz, dy, dx, 0, count), columns]
@@ -502,6 +493,7 @@
     to_y, to_x, to_c = spot.device(0, 1), spot.device(0, 0, 1), spot.device(0, 0, 0, 1)
 
     def spread(dz):
+        also("spread", dz)
         if dz <= 0:
 
             @pl.when(spot.has(1))
@@ -521,6 +513,7 @@
     def take_z(dz):
         def action():
             await_bytes(count, whole, recv.at[0, dz + 3])
+            also("take", dz)
             spread(dz)
 
         when_has(spot, dz, action)
@@ -579,66 +572,169 @@
     local.wait()
 
 
-def gather_rows(rows):
+GATHER_SEMS = ((5, 7), (7, 2), None, None, None, None, None)
+
+
+def dma_sems(shapes):
+    return [pltpu.SemaphoreType.DMA(shape) if shape else pltpu.SemaphoreType.DMA for shape in shapes]
+
+
+def gather_kernel(src, out, *sems):
+    spot = Spot()
+    spot.greet()
+    gather_body(spot, src, out, *sems)
+
+
+def gather_tagged_kernel(src, tag, out, tag_out, *refs):
+    sems, (tag_z, tag_y, tag_z_send, tag_y_send, tag_local) = refs[:7], refs[7:]
+    spot = Spot()
+
+    def place(dz, dy):
+        return tag_out.at[spot.device(dz, dy)[0]]
+
+    own = pltpu.make_async_copy(tag, place(0, 0), tag_local)
+    own.start()
+    spot.greet()
+
+    def also(what, dz):
+        here = place(dz, 0)
+        source = tag if dz == 0 else here
+        if what == "take":
+            arrive(here, tag_z.at[dz + 3])
+            return
+        if dz <= 0:
+
+            @pl.when(spot.has(1))
+            def _():
+                push(source, here, tag_z_send.at[dz + 3, 0], tag_z.at[dz + 2], spot.device(1))
+
+        if dz >= 0:
+
+            @pl.when(spot.has(-1))
+            def _():
+                push(source, here, tag_z_send.at[dz + 3, 1], tag_z.at[dz + 4], spot.device(-1))
+
+        push(source, here, tag_y_send.at[dz + 3], tag_y.at[dz + 3], spot.device(0, 1))
+
+    gather_body(spot, src, out, *sems, also=also)
+    for dz in range(-3, 4):
+
+        def action(dz=dz):
+            arrive(place(dz, 1), tag_y.at[dz + 3])
+            arrive(place(dz, 0), tag_y_send.at[dz + 3])
+            for side, step in ((0, 1), (1, -1)):
+                if dz * step <= 0:
+
+                    @pl.when(spot.has(step))
+                    def _():
+                        arrive(place(dz, 0), tag_z_send.at[dz + 3, side])
+
+        when_has(spot, dz, action)
+    own.wait()
+
+
+def gather_rows(rows, tag=None):
     count, width = rows.shape
-    dma = pltpu.SemaphoreType.DMA
+    hbm = pl.BlockSpec(memory_space=pl.ANY)
+    shape = jax.ShapeDtypeStruct((32 * count, width), rows.dtype)
+    if tag is None:
+        return pl.pallas_call(
+            gather_kernel,
+            out_shape=shape,
+            in_specs=[hbm],
+            out_specs=hbm,
+            scratch_shapes=dma_sems(GATHER_SEMS),
+            compiler_params=pltpu.CompilerParams(collective_id=0, has_side_effects=True),
+            name="gather_rows",
+        )(rows)
     return pl.pallas_call(
-        gather_kernel,
-        out_shape=jax.ShapeDtypeStruct((32 * count, width), rows.dtype),
-        in_specs=[pl.BlockSpec(memory_space=pl.ANY)],
-        out_specs=pl.BlockSpec(memory_space=pl.ANY),
-        scratch_shapes=[dma((5, 7)), dma((7, 2)), dma, dma, dma, dma, dma],
-        compiler_params=pltpu.CompilerParams(collective_id=0, has_side_effects=True),
-        name="gather_rows",
-    )(rows)
-
-
-def scatter_kernel(
-    part, out, held, from_a, from_b, from_y, from_x, from_below, from_above,
-    c_recv, recv, z_send, y_send, x_send, c_send,
-):
+        gather_tagged_kernel,
+        out_shape=(shape, jax.ShapeDtypeStruct((8,) + tag.shape, tag.dtype)),
+        in_specs=[hbm, hbm],
+        out_specs=(hbm, hbm),
+        scratch_shapes=dma_sems(GATHER_SEMS + ((7,), (7,), (7, 2), (7,), None)),
+        compiler_params=pltpu.CompilerParams(collective_id=1, has_side_effects=True),
+        name="gather_tagged",
+    )(rows, tag)
+
+
+def add_into(into, chunk, *terms):
+    @pl.loop(0, into.shape[0] // chunk)
+    def _(step):
+        rows = pl.ds(pl.multiple_of(step * chunk, chunk), chunk)
+        total = into[rows, :].astype(jnp.float32)
+        for term in terms:
+            total = total + term[rows, :].astype(jnp.float32)
+        into[rows, :] = total.astype(into.dtype)
+
+
+def push(src, dst, send_sem, recv_sem, device):
+    pltpu.make_async_remote_copy(
+        src_ref=src,
+        dst_ref=dst,
+        send_sem=send_sem,
+        recv_sem=recv_sem,
+        device_id=device,
+        device_id_type=MESH,
+    ).start()
+
+
+def arrive(view, sem):
+    pltpu.make_async_copy(view, view, sem).wait()
+
+
+def scatter_kernel(split, with_kv, *refs):
+    refs = list(refs)
+    part = refs.pop(0)
+    kv_part = refs.pop(0) if with_kv else None
+    out = refs.pop(0)
+    kv_out = refs.pop(0) if with_kv else None
+    held, from_a, from_b, from_y, from_x, from_below, from_above = refs[:7]
+    c_recv, recv, z_send, half_send, y_send, x_send, c_send = refs[7:14]
+    if with_kv:
+        kv_held, kv_y, kv_below, kv_above, kv_recv, kv_z_send, kv_send = refs[14:]
     count, width = out.shape
-    half = 1024
-    first, second, whole = pl.ds(0, half), pl.ds(half, width - half), pl.ds(0, width)
+    first, second, whole = pl.ds(0, split), pl.ds(split, width - split), pl.ds(0, width)
     spot = Spot()
     spot.greet()
     to_y, to_x, to_c = spot.device(0, 1), spot.device(0, 0, 1), spot.device(0, 0, 0, 1)
-
-    def send(src, dst, send_sem, recv_sem, device):
-        pltpu.make_async_remote_copy(
-            src_ref=src, dst_ref=dst, send_sem=send_sem, recv_sem=recv_sem,
-            device_id=device, device_id_type=MESH,
-        ).start()
-
-    def arrive(view, sem):
-        pltpu.make_async_copy(view, view, sem).wait()
-
-    def add(into, *terms):
-        @pl.loop(0, count // 16)
-        def _(step):
-            rows = pl.ds(pl.multiple_of(step * 16, 16), 16)
-            total = into[rows, :].astype(jnp.float32)
-            for term in terms:
-                total = total + term[rows, :].astype(jnp.float32)
-            into[rows, :] = total.astype(into.dtype)
-
     groups = ((1, 1), (1, 0), (0, 1), (0, 0))
     for dy, dx in groups:
         for dz in FAR_FIRST:
 
             def action(dz=dz, dy=dy, dx=dx):
-                send(
+                push(
                     part.at[spot.rows(dz, dy, dx, 1, count), :],
                     held.at[spot.z + dz, dy, dx],
-                    c_send, c_recv.at[dz + 3, dy, dx], to_c,
+                    c_send,
+                    c_recv.at[dz + 3, dy, dx],
+                    to_c,
                 )
 
             when_has(spot, dz, action)
 
-    def merge(dz, dy, dx, *terms):
+    def kv_rows(dz, dy):
+        group, _ = spot.device(dz, dy)
+        return pl.ds(pl.multiple_of(group * 256, 256), 256)
+
+    if with_kv:
+        for dz in FAR_FIRST:
+
+            def action(dz=dz):
+                push(
+                    kv_part.at[kv_rows(dz, 1), :],
+                    kv_y.at[spot.z + dz],
+                    kv_send,
+                    kv_recv.at[0, dz + 3],
+                    to_y,
+                )
+
+            when_has(spot, dz, action)
+
+    def merge(dz, dy, dx):
         mine = held.at[spot.z + dz, dy, dx]
         arrive(mine, c_recv.at[dz + 3, dy, dx])
-        add(mine, part.at[spot.rows(dz, dy, dx, 0, count), :])
+        add_into(mine, 16, part.at[spot.rows(dz, dy, dx, 0, count), :])
         return mine
 
     for dz in FAR_FIRST:
@@ -646,22 +742,53 @@
         def action(dz=dz):
             far = spot.z + dz
             mine = merge(dz, 1, 1)
-            send(mine.at[:, first], from_a.at[far], x_send, recv.at[0, dz + 3], to_x)
-            send(mine.at[:, second], from_b.at[far], y_send, recv.at[1, dz + 3], to_y)
+            push(mine.at[:, first], from_a.at[far], half_send.at[0], recv.at[0, dz + 3], to_x)
+            push(mine.at[:, second], from_b.at[far], half_send.at[1], recv.at[1, dz + 3], to_y)
 
         when_has(spot, dz, action)
+
+    def line(dz, mine, chunk, below, above, sems, sends):
+        far = spot.z + dz
+        if dz >= 0:
+
+            @pl.when(spot.has(-1))
+            def _():
+                arrive(below.at[far], sems[0].at[dz + 3])
+                add_into(mine, chunk, below.at[far])
+
+        if dz <= 0:
+
+            @pl.when(spot.has(1))
+            def _():
+                arrive(above.at[far], sems[1].at[dz + 3])
+                add_into(mine, chunk, above.at[far])
+
+        if dz > 0:
+            push(mine, below.at[far], sends.at[dz + 3], sems[0].at[dz + 2], spot.device(1))
+        if dz < 0:
+            push(mine, above.at[far], sends.at[dz + 3], sems[1].at[dz + 4], spot.device(-1))
+
     for dz in FAR_FIRST:
 
         def action(dz=dz):
             far = spot.z + dz
             mine = merge(dz, 1, 0)
             arrive(from_a.at[far], recv.at[0, dz + 3])
-            add(mine.at[:, first], from_a.at[far])
-            send(mine, from_y.at[far], y_send, recv.at[2, dz + 3], to_y)
+            add_into(mine.at[:, first], 16, from_a.at[far])
+            push(mine, from_y.at[far], y_send, recv.at[2, dz + 3], to_y)
             mine = merge(dz, 0, 1)
             arrive(from_b.at[far], recv.at[1, dz + 3])
-            add(mine.at[:, second], from_b.at[far])
-            send(mine, from_x.at[far], x_send, recv.at[3, dz + 3], to_x)
+            add_into(mine.at[:, second], 16, from_b.at[far])
+            push(mine, from_x.at[far], x_send, recv.at[3, dz + 3], to_x)
+            if with_kv:
+                kv_mine = kv_held.at[far]
+                kv_mine[...] = kv_part[kv_rows(dz, 0), :]
+                arrive(kv_y.at[far], kv_recv.at[0, dz + 3])
+                add_into(kv_mine, 64, kv_y.at[far])
+                line(
+                    dz, kv_mine, 64, kv_below, kv_above,
+                    (kv_recv.at[1], kv_recv.at[2]), kv_z_send,
+                )
 
         when_has(spot, dz, action)
     for dz in FAR_FIRST:
@@ -671,72 +798,511 @@
             mine = merge(dz, 0, 0)
             arrive(from_y.at[far], recv.at[2, dz + 3])
             arrive(from_x.at[far], recv.at[3, dz + 3])
-            add(mine, from_y.at[far], from_x.at[far])
-            if dz >= 0:
-
-                @pl.when(spot.has(-1))
-                def _():
-                    arrive(from_below.at[far], recv.at[4, dz + 3])
-                    add(mine, from_below.at[far])
-
-            if dz <= 0:
-
-                @pl.when(spot.has(1))
-                def _():
-                    arrive(from_above.at[far], recv.at[5, dz + 3])
-                    add(mine, from_above.at[far])
-
-            if dz > 0:
-                send(mine, from_below.at[far], z_send.at[dz + 3], recv.at[4, dz + 2],
-                     spot.device(1))
-            if dz < 0:
-                send(mine, from_above.at[far], z_send.at[dz + 3], recv.at[5, dz + 4],
-                     spot.device(-1))
+            add_into(mine, 16, from_y.at[far], from_x.at[far])
+            line(dz, mine, 16, from_below, from_above, (recv.at[4], recv.at[5]), z_send)
             if dz == 0:
                 out[...] = mine[...].astype(out.dtype)
+                if with_kv:
+                    kv_out[...] = kv_held[far].astype(kv_out.dtype)
 
         when_has(spot, dz, action)
 
-    def await_rows(rows, sem):
-        view = part.at[pl.ds(0, rows), :]
+    def await_view(rows, columns, sem):
+        view = part.at[pl.ds(0, rows), columns]
         pltpu.make_async_copy(view, view, sem).wait()
 
-    await_rows(16 * count, c_send)
-    for columns, other, sem in ((second, first, y_send), (first, second, x_send)):
-        view = part.at[pl.ds(0, 4 * count), columns]
-        whole_view = part.at[pl.ds(0, 4 * count), :]
-        pltpu.make_async_copy(view, view, sem).wait()
-        pltpu.make_async_copy(whole_view, whole_view, sem).wait()
+    await_view(16 * count, whole, c_send)
+    await_view(4 * count, whole, y_send)
+    await_view(4 * count, whole, x_send)
+    arrive(from_a, half_send.at[0])
+    arrive(from_b, half_send.at[1])
+    if with_kv:
+        view = kv_part.at[pl.ds(0, 1024), :]
+        pltpu.make_async_copy(view, view, kv_send).wait()
     for dz in FAR_FIRST[:-1]:
 
         def action(dz=dz):
-            await_rows(count, z_send.at[dz + 3])
+            await_view(count, whole, z_send.at[dz + 3])
+            if with_kv:
+                view = kv_part.at[pl.ds(0, 256), :]
+                pltpu.make_async_copy(view, view, kv_z_send.at[dz + 3]).wait()
 
         when_has(spot, dz, action)
 
 
-def scatter_rows(partial_rows, ident):
+def scatter_rows(partial_rows, ident, kv_partial=None):
     total, width = partial_rows.shape
     count = total // 32
+    with_kv = kv_partial is not None
     dma, bf16 = pltpu.SemaphoreType.DMA, jnp.bfloat16
+    split = 1536 if with_kv else 1024
     line = pltpu.VMEM((4, count, width), bf16)
+    scratch = [
+        pltpu.VMEM((4, 2, 2, count, width), bf16),
+        pltpu.VMEM((4, count, split), bf16),
+        pltpu.VMEM((4, count, width - split), bf16),
+        line, line, line, line,
+        dma((7, 2, 2)), dma((6, 7)), dma((7,)), dma((2,)), dma, dma, dma,
+    ]
+    vmem = pl.BlockSpec(memory_space=pltpu.VMEM)
+    out_shape = jax.ShapeDtypeStruct((count, width), jnp.float32)
+    if with_kv:
+        kv_line = pltpu.VMEM((4, 256, kv_partial.shape[1]), bf16)
+        scratch += [kv_line, kv_line, kv_line, kv_line, dma((3, 7)), dma((7,)), dma]
+        out_shape = (out_shape, jax.ShapeDtypeStruct((256, kv_partial.shape[1]), bf16))
     return pl.pallas_call(
-        scatter_kernel,
-        out_shape=jax.ShapeDtypeStruct((count, width), jnp.float32),
-        in_specs=[pl.BlockSpec(memory_space=pltpu.VMEM)],
-        out_specs=pl.BlockSpec(memory_space=pltpu.VMEM),
+        partial(scatter_kernel, split, with_kv),
+        out_shape=out_shape,
+        in_specs=[vmem] * (2 if with_kv else 1),
+        out_specs=(vmem, vmem) if with_kv else vmem,
+        scratch_shapes=scratch,
+        compiler_params=pltpu.CompilerParams(
+            collective_id=ident, has_side_effects=True, vmem_limit_bytes=48 << 20
+        ),
+        name="scatter_rows_kv" if with_kv else "scatter_rows",
+    )(*((partial_rows, kv_partial) if with_kv else (partial_rows,)))
+
+
+def finish_kernel(
+    query, kv, small, ends, query_out, kv_out, small_out, ends_out,
+    z_recv, y_recv, x_recv, z_send, total_send, total_recv, local_sem,
+):
+    spot = Spot()
+    dim = query.shape[1]
+    few, many = small.shape[0], ends.shape[0]
+
+    def query_at(dz, dy):
+        group, _ = spot.device(dz, dy)
+        return query_out.at[:, pl.ds(pl.multiple_of(group * dim, dim), dim)]
+
+    def kv_at(dz, dy):
+        group, _ = spot.device(dz, dy)
+        return kv_out.at[pl.ds(pl.multiple_of(group * 256, 256), 256), :]
+
+    def small_at(dz, dy, dx, dc):
+        return small_out.at[spot.rows(dz, dy, dx, dc, few), :]
+
+    def ends_at(dx, dc):
+        _, part = spot.device(0, 0, dx, dc)
+        return ends_out.at[pl.ds(pl.multiple_of(part * many, many), many), :]
+
+    locals_ = [
+        pltpu.make_async_copy(query, query_at(0, 0), local_sem.at[0]),
+        pltpu.make_async_copy(kv, kv_at(0, 0), local_sem.at[1]),
+        pltpu.make_async_copy(small, small_at(0, 0, 0, 0), local_sem.at[2]),
+        pltpu.make_async_copy(ends, ends_at(0, 0), local_sem.at[3]),
+    ]
+    for copy in locals_:
+        copy.start()
+    spot.greet()
+    to_y, to_x, to_c = spot.device(0, 1), spot.device(0, 0, 1), spot.device(0, 0, 0, 1)
+
+    def spread(dz):
+        own = dz == 0
+        goods = (
+            (small if own else small_at(dz, 0, 0, 0), small_at(dz, 0, 0, 0)),
+            (kv if own else kv_at(dz, 0), kv_at(dz, 0)),
+            (query if own else query_at(dz, 0), query_at(dz, 0)),
+        )
+        for kind, (src, dst) in enumerate(goods):
+            if dz <= 0:
+
+                @pl.when(spot.has(1))
+                def _(kind=kind, src=src, dst=dst):
+                    push(src, dst, z_send.at[kind, dz + 3, 0], z_recv.at[kind, dz + 2],
+                         spot.device(1))
+
+            if dz >= 0:
+
+                @pl.when(spot.has(-1))
+                def _(kind=kind, src=src, dst=dst):
+                    push(src, dst, z_send.at[kind, dz + 3, 1], z_recv.at[kind, dz + 4],
+                         spot.device(-1))
+
+            push(src, dst, total_send.at[kind], y_recv.at[kind, dz + 3], to_y)
+        src, dst = goods[0]
+        push(src, dst, total_send.at[3], x_recv.at[dz + 3, 0], to_x)
+        push(src, dst, total_send.at[4], total_recv.at[0], to_c)
+
+    push(ends, ends_at(0, 0), total_send.at[5], total_recv.at[1], to_x)
+    push(ends, ends_at(0, 0), total_send.at[6], total_recv.at[2], to_c)
+    spread(0)
+    for step in (1, 2, 3):
+        for dz in (step, -step):
+
+            def action(dz=dz):
+                for kind, dst in enumerate((small_at(dz, 0, 0, 0), kv_at(dz, 0), query_at(dz, 0))):
+                    arrive(dst, z_recv.at[kind, dz + 3])
+                spread(dz)
+
+            when_has(spot, dz, action)
+    arrive(ends_at(1, 0), total_recv.at[1])
+    push(ends_at(1, 0), ends_at(1, 0), total_send.at[6], total_recv.at[2], to_c)
+    for dz in (0, 1, -1, 2, -2, 3, -3):
+
+        def action(dz=dz):
+            place = small_at(dz, 1, 0, 0)
+            arrive(place, y_recv.at[0, dz + 3])
+            push(place, place, total_send.at[3], x_recv.at[dz + 3, 1], to_x)
+            push(place, place, total_send.at[4], total_recv.at[0], to_c)
+            place = small_at(dz, 0, 1, 0)
+            arrive(place, x_recv.at[dz + 3, 0])
+            push(place, place, total_send.at[4], total_recv.at[0], to_c)
+
+        when_has(spot, dz, action)
+    for dz in (0, 1, -1, 2, -2, 3, -3):
+
+        def action(dz=dz):
+            place = small_at(dz, 1, 1, 0)
+            arrive(place, x_recv.at[dz + 3, 1])
+            push(place, place, total_send.at[4], total_recv.at[0], to_c)
+            arrive(kv_at(dz, 1), y_recv.at[1, dz + 3])
+            arrive(query_at(dz, 1), y_recv.at[2, dz + 3])
+
+        when_has(spot, dz, action)
+
+    def drain(ref, rows, sem):
+        view = ref.at[pl.ds(0, rows), :]
+        pltpu.make_async_copy(view, view, sem).wait()
+
+    drain(small_out, 16 * few, total_recv.at[0])
+    drain(ends_out, 2 * many, total_recv.at[2])
+    drain(small_out, 4 * few, total_send.at[0])
+    drain(kv_out, 4 * 256, total_send.at[1])
+    half = query_out.at[:, pl.ds(0, 4 * dim)]
+    pltpu.make_async_copy(half, half, total_send.at[2]).wait()
+    drain(small_out, 8 * few, total_send.at[3])
+    drain(small_out, 16 * few, total_send.at[4])
+    drain(ends_out, many, total_send.at[5])
+    drain(ends_out, 2 * many, total_send.at[6])
+    for dz in range(-3, 4):
+        for side, step in ((0, 1), (1, -1)):
+            if dz * step <= 0:
+
+                @pl.when(spot.has(dz) & spot.has(step))
+                def _(dz=dz, side=side):
+                    places = (small_at(dz, 0, 0, 0), kv_at(dz, 0), query_at(dz, 0))
+                    for kind, place in enumerate(places):
+                        arrive(place, z_send.at[kind, dz + 3, side])
+
+    for copy in locals_:
+        copy.wait()
+
+
+def finish(query, kv, small, ends, ident):
+    dma, shape = pltpu.SemaphoreType.DMA, jax.ShapeDtypeStruct
+    hbm = pl.BlockSpec(memory_space=pl.ANY)
+    return pl.pallas_call(
+        finish_kernel,
+        out_shape=(
+            shape((query.shape[0], 8 * query.shape[1]), query.dtype),
+            shape((8 * kv.shape[0], kv.shape[1]), kv.dtype),
+            shape((32 * small.shape[0], small.shape[1]), small.dtype),
+            shape((4 * ends.shape[0], ends.shape[1]), ends.dtype),
+        ),
+        in_specs=[hbm] * 4,
+        out_specs=(hbm,) * 4,
         scratch_shapes=[
-            pltpu.VMEM((4, 2, 2, count, width), bf16),
-            pltpu.VMEM((4, count, 1024), bf16),
-            pltpu.VMEM((4, count, width - 1024), bf16),
-            line, line, line, line,
-            dma((7, 2, 2)), dma((6, 7)), dma((7,)), dma, dma, dma,
+            dma((3, 7)), dma((3, 7)), dma((7, 2)), dma((3, 7, 2)), dma((7,)), dma((3,)), dma((4,)),
         ],
+        compiler_params=pltpu.CompilerParams(collective_id=ident, has_side_effects=True),
+        name="finish",
+    )(query, kv, small, ends)
+
+
+F32, BF16 = jnp.float32, jnp.bfloat16
+VMEM_SPEC = pl.BlockSpec(memory_space=pltpu.VMEM)
+HBM_SPEC = pl.BlockSpec(memory_space=pl.ANY)
+
+
+def mxu(left, right, left_dim=1, right_dim=0):
+    return lax.dot_general(
+        left, right, (((left_dim,), (right_dim,)), ((), ())), preferred_element_type=F32
+    )
+
+
+def head_norm(lin):
+    root = lax.rsqrt(jnp.mean(lin * lin, axis=-1, keepdims=True) + EPS)
+    return lin * root, root
+
+
+def project_kernel(
+    which, hidden, gain, w_query, w_key, w_value, q_gain, k_gain, cosine, sine,
+    normed, queries, keys, values, lin_out, weight,
+):
+    dim = w_query.shape[1]
+
+    @pl.when(pl.program_id(0) == 0)
+    def _():
+        weight[:, :dim] = w_query[...]
+        weight[:, dim : 2 * dim] = w_key[...]
+        weight[:, 2 * dim :] = w_value[...]
+
+    rows = hidden[...].astype(F32)
+    scaled = rows * lax.rsqrt(jnp.mean(rows * rows, axis=-1, keepdims=True) + EPS) * gain[...]
+    normed[...] = scaled.astype(BF16)
+    lin = mxu(normed[...], weight[...])
+    lin_out[...] = lin[:, : 2 * dim]
+    values[...] = lin[:, 2 * dim :].astype(BF16)
+    for at, head_gain, scale, out in ((0, q_gain, dim**-0.5, queries), (dim, k_gain, 1.0, keys)):
+        plain, _ = head_norm(lin[:, at : at + dim])
+        plain = plain * head_gain[...]
+        turned = pltpu.roll(plain, dim // 2, 1)
+        out[...] = ((plain * cosine[...] + turned * sine[...]) * scale).astype(BF16)
+
+
+def project(group, hidden, gain, w_query, w_key, w_value, q_gain, k_gain, cosine, sine):
+    total, width = hidden.shape
+    dim = w_key.shape[1]
+    rows = 256
+    block = lambda columns: pl.BlockSpec((rows, columns), lambda i, _: (i, 0))
+    fixed = lambda shape: pl.BlockSpec(shape, lambda i, _: (0, 0))
+    shape = jax.ShapeDtypeStruct
+    return pl.pallas_call(
+        project_kernel,
+        grid_spec=pltpu.PrefetchScalarGridSpec(
+            num_scalar_prefetch=1,
+            grid=(total // rows,),
+            in_specs=[
+                block(width), fixed((1, width)),
+                pl.BlockSpec((width, dim), lambda i, which: (0, which[0])),
+                fixed((width, dim)), fixed((width, dim)), fixed((1, dim)), fixed((1, dim)),
+                block(dim), block(dim),
+            ],
+            out_specs=[block(width), block(dim), block(dim), block(dim), block(2 * dim)],
+            scratch_shapes=[pltpu.VMEM((width, 3 * dim), BF16)],
+        ),
+        out_shape=[
+            shape((total, width), BF16), shape((total, dim), BF16), shape((total, dim), BF16),
+            shape((total, dim), BF16), shape((total, 2 * dim), F32),
+        ],
+        compiler_params=pltpu.CompilerParams(vmem_limit_bytes=40 << 20),
+        name="project",
+    )(group, hidden, gain, w_query, w_key, w_value, q_gain, k_gain, cosine, sine)
+
+
+def attend_kernel(
+    queries, keys, values, place_column, place_row, open_row,
+    attended, log_total, att_rows, send_sem, recv_sem, local_sem,
+):
+    group, part = lax.axis_index("expert"), lax.axis_index("tensor")
+    dim = queries.shape[1]
+    rows = 256
+    barrier = pltpu.get_barrier_semaphore()
+
+    @pl.loop(1, 8)
+    def _(step):
+        pl.semaphore_signal(
+            barrier, inc=1, device_id=((group + step) % 8, part), device_id_type=MESH
+        )
+
+    pl.semaphore_wait(barrier, 7)
+    mine = att_rows.at[:, pl.ds(pl.multiple_of(group * dim, dim), dim)]
+
+    def copy_of(step):
+        target = (group + step) % 8
+        block = attended.at[pl.ds(pl.multiple_of(target * rows, rows), rows), :]
+        return pltpu.make_async_remote_copy(
+            src_ref=block,
+            dst_ref=mine,
+            send_sem=send_sem.at[step],
+            recv_sem=recv_sem.at[step],
+            device_id=(target, part),
+            device_id_type=MESH,
+        )
+
+    def block_of(step):
+        at = pl.multiple_of((group + step) % 8 * rows, rows)
+        here = pl.ds(at, rows)
+        scores = mxu(keys[...], queries[here, :], 1, 1)
+        seen = (place_column[...] <= place_row[:, here]) & (place_column[...] >= open_row[:, here])
+        scores = jnp.where(seen, scores, NEG)
+        highest = jnp.max(scores, axis=0, keepdims=True)
+        weights = jnp.exp(scores - highest)
+        totals = jnp.sum(weights, axis=0, keepdims=True)
+        probability = (weights * (1.0 / totals)).astype(BF16)
+        mixed = mxu(values[...], probability, 0, 0)
+        attended[here, :] = mixed.T.astype(BF16)
+        log_total[:, here] = highest + jnp.log(totals)
+
+    @pl.loop(1, 8)
+    def _(step):
+        block_of(step)
+        copy_of(step).start()
+
+    block_of(0)
+    own = attended.at[pl.ds(pl.multiple_of(group * rows, rows), rows), :]
+    local = pltpu.make_async_copy(own, mine, local_sem)
+    local.start()
+
+    @pl.loop(1, 8)
+    def _(step):
+        copy_of(step).wait_send()
+        source = (group + 8 - step) % 8
+        there = att_rows.at[:, pl.ds(pl.multiple_of(source * dim, dim), dim)]
+        pltpu.make_async_copy(there, there, recv_sem.at[step]).wait()
+
+    local.wait()
+
+
+def attend(queries, keys, values, place_column, place_row, open_row):
+    total, dim = queries.shape
+    shape = jax.ShapeDtypeStruct
+    return pl.pallas_call(
+        attend_kernel,
+        out_shape=(
+            shape((total, dim), BF16), shape((1, total), F32), shape((total // 8, 8 * dim), BF16),
+        ),
+        in_specs=[VMEM_SPEC] * 6,
+        out_specs=(VMEM_SPEC, VMEM_SPEC, HBM_SPEC),
+        scratch_shapes=dma_sems(((8,), (8,), None)),
         compiler_params=pltpu.CompilerParams(
-            collective_id=ident, has_side_effects=True, vmem_limit_bytes=40 << 20
+            collective_id=6, has_side_effects=True, vmem_limit_bytes=40 << 20
         ),
-        name="scatter_rows",
-    )(partial_rows)
+        name="attend",
+    )(queries, keys, values, place_column, place_row, open_row)
+
+
+def branch_kernel(
+    att_rows, w_out, hidden, gain, residual, normed, normed_all,
+    partial_sum, from_core, to_x_sum, from_x, tensor_sems, *sems,
+):
+    count, width = hidden.shape
+    spot = Spot()
+
+    @pl.loop(0, width // 256)
+    def _(step):
+        columns = pl.ds(pl.multiple_of(step * 256, 256), 256)
+        partial_sum[:, columns] = mxu(att_rows[...], w_out[:, columns]).astype(BF16)
+
+    spot.greet()
+
+    def rows(dx, dc):
+        _, part = spot.device(0, 0, dx, dc)
+        return partial_sum.at[pl.ds(pl.multiple_of(part * count, count), count), :]
+
+    to_x, to_c = spot.device(0, 0, 1), spot.device(0, 0, 0, 1)
+    for dx in (1, 0):
+        push(rows(dx, 1), from_core.at[dx], tensor_sems.at[dx], tensor_sems.at[2 + dx], to_c)
+    arrive(from_core.at[1], tensor_sems.at[3])
+    to_x_sum[...] = (rows(1, 0)[...].astype(F32) + from_core[1].astype(F32)).astype(BF16)
+    push(to_x_sum, from_x, tensor_sems.at[4], tensor_sems.at[5], to_x)
+    arrive(from_core.at[0], tensor_sems.at[2])
+    arrive(from_x, tensor_sems.at[5])
+    branch = rows(0, 0)[...].astype(F32) + from_core[0].astype(F32) + from_x[...].astype(F32)
+    total = hidden[...].astype(F32) + branch
+    residual[...] = total
+    root = lax.rsqrt(jnp.mean(total * total, axis=-1, keepdims=True) + EPS)
+    normed[...] = (total * root * gain[...]).astype(BF16)
+    for at, view in ((0, from_core.at[0]), (1, from_core.at[1]), (4, from_x)):
+        arrive(view, tensor_sems.at[at])
+    gather_body(spot, normed, normed_all, *sems)
+
+
+def branch_rows(att_rows, w_out, hidden, gain):
+    count, width = hidden.shape
+    shape = jax.ShapeDtypeStruct
+    return pl.pallas_call(
+        branch_kernel,
+        out_shape=(
+            shape((count, width), F32), shape((count, width), BF16),
+            shape((32 * count, width), BF16),
+        ),
+        in_specs=[VMEM_SPEC] * 4,
+        out_specs=(VMEM_SPEC, VMEM_SPEC, HBM_SPEC),
+        scratch_shapes=[
+            pltpu.VMEM((4 * count, width), BF16), pltpu.VMEM((2, count, width), BF16),
+            pltpu.VMEM((count, width), BF16), pltpu.VMEM((count, width), BF16),
+        ]
+        + dma_sems(((6,),) + GATHER_SEMS),
+        compiler_params=pltpu.CompilerParams(
+            collective_id=7, has_side_effects=True, vmem_limit_bytes=40 << 20
+        ),
+        name="branch",
+    )(att_rows, w_out, hidden, gain)
+
+
+def attend_back_kernel(
+    which, grad_rows, w_out, queries, query_lin, cosine, sine, place_row, open_row, log_total,
+    keys, values, place_column, lin, k_gain, q_gain, cosine_all, sine_all,
+    grad_lin, grad_q_gain, grad_k_gain, grad_keys, grad_values,
+):
+    step = pl.program_id(0)
+    rows, dim = queries.shape
+    here = pl.ds(pl.multiple_of(step * rows, rows), rows)
+
+    @pl.when(step == 0)
+    def _():
+        grad_keys[...] = jnp.zeros_like(grad_keys)
+        grad_values[...] = jnp.zeros_like(grad_values)
+        grad_q_gain[...] = jnp.zeros_like(grad_q_gain)
+
+    def unshape(grad, plain, gain, cos, sin):
+        grad = grad * cos + pltpu.roll(grad * sin, dim // 2, 1)
+        normed, root = head_norm(plain)
+        gain_part = jnp.sum(grad * normed, axis=0, keepdims=True)
+        grad = grad * gain
+        return root * (grad - normed * jnp.mean(grad * normed, axis=-1, keepdims=True)), gain_part
+
+    grad_att = mxu(grad_rows[...], w_out[...], 1, 1).astype(BF16)
+    scores = mxu(keys[...], queries[...], 1, 1)
+    seen = (place_column[...] <= place_row[...]) & (place_column[...] >= open_row[...])
+    probability = jnp.exp(jnp.where(seen, scores - log_total[...], NEG))
+    grad_prob = mxu(values[...], grad_att, 1, 1)
+    delta = jnp.sum(probability * grad_prob, axis=0, keepdims=True)
+    grad_scores = (probability * (grad_prob - delta)).astype(BF16)
+    grad_values[...] += mxu(probability.astype(BF16), grad_att)
+    grad_keys[...] += mxu(grad_scores, queries[...])
+    grad_query = mxu(grad_scores, keys[...], 0, 0) * dim**-0.5
+    grad_query, gain_part = unshape(
+        grad_query, query_lin[...], q_gain[...], cosine[...], sine[...]
+    )
+    grad_q_gain[...] += gain_part
+    grad_lin[here, :dim] = grad_query.astype(BF16)
+
+    @pl.when(step == pl.num_programs(0) - 1)
+    def _():
+        grad_key, key_part = unshape(
+            grad_keys[...], lin[:, dim:], k_gain[...], cosine_all[...], sine_all[...]
+        )
+        grad_lin[:, dim : 2 * dim] = grad_key.astype(BF16)
+        grad_lin[:, 2 * dim :] = grad_values[...].astype(BF16)
+        grad_k_gain[...] = key_part
+
+
+def attend_back(
+    group, grad_rows, w_out, queries, lin, cosine, sine, place_row, open_row, log_total,
+    keys, values, place_column, k_gain, q_gain,
+):
+    total, width = grad_rows.shape
+    dim = keys.shape[1]
+    rows = 256
+    block = lambda columns: pl.BlockSpec((rows, columns), lambda i, _: (i, 0))
+    across = pl.BlockSpec((1, rows), lambda i, _: (0, i))
+    fixed = lambda shape: pl.BlockSpec(shape, lambda i, _: (0, 0))
+    shape = jax.ShapeDtypeStruct
+    return pl.pallas_call(
+        attend_back_kernel,
+        grid_spec=pltpu.PrefetchScalarGridSpec(
+            num_scalar_prefetch=1,
+            grid=(total // rows,),
+            in_specs=[
+                block(width), pl.BlockSpec((dim, width), lambda i, which: (which[0], 0)),
+                block(dim), block(dim), block(dim), block(dim), across, across, across,
+                fixed((total, dim)), fixed((total, dim)), fixed((total, 1)),
+                fixed((total, 2 * dim)), fixed((1, dim)), fixed((1, dim)),
+                fixed((total, dim)), fixed((total, dim)),
+            ],
+            out_specs=[fixed((total, 3 * dim)), fixed((1, dim)), fixed((1, dim))],
+            scratch_shapes=[pltpu.VMEM((total, dim), F32), pltpu.VMEM((total, dim), F32)],
+        ),
+        out_shape=[shape((total, 3 * dim), BF16), shape((1, dim), F32), shape((1, dim), F32)],
+        compiler_params=pltpu.CompilerParams(vmem_limit_bytes=48 << 20),
+        name="attend_back",
+    )(
+        group, grad_rows, w_out, queries, lin, cosine, sine, place_row, open_row, log_total,
+        keys, values, place_column, lin, k_gain, q_gain, cosine, sine,
+    )
 
 
 def head_device(
@@ -775,41 +1341,37 @@
     def own(rows):
         return lax.dynamic_slice_in_dim(rows, part * own_rows, own_rows, 0)
 
-    place, rank, ids_t = all_tokens(layout, expert_ids, drop_rank)
+    which = jnp.reshape(group, (1,))
+    tag = jnp.concatenate(
+        [layout[None], drop_rank[None], expert_ids.T, jnp.zeros((6, tok_rows), jnp.int32)], axis=0
+    )
+    hidden_all, tags = gather_rows(own(hidden_in), tag)
+    tags = jnp.transpose(tags, (1, 0, 2)).reshape(16, total_rows)
+    place, rank, ids_t = tags[0], tags[1], tags[2:10]
     segment, position = token_tables(place, seq_lengths)
     valid = segment < seq_count
-    hidden_all = gather_rows(own(hidden_in))
-    grad_y_all = gather_rows(own(cotangent))
-
-    head_query = lax.dynamic_slice_in_dim(w_query, group * head_dim, head_dim, 1)
-    head_out = lax.dynamic_slice_in_dim(w_out, group * head_dim, head_dim, 0)
-    qkv_weight = jnp.concatenate([head_query, key_weight, value_weight], axis=1)
-    normed1 = norm_rows(hidden_all.astype(f32), norm1_gain).astype(bf16)
-    lin = jnp.dot(normed1, qkv_weight, preferred_element_type=f32)
-    query_lin, key_lin = lin[:, :head_dim], lin[:, head_dim : 2 * head_dim]
-    values = lin[:, 2 * head_dim :].astype(bf16)
-    queries, query_pull = jax.vjp(
-        lambda v, g: shape_queries(v, g, position)[:, 0], query_lin, query_gain
-    )
-    keys, key_pull = jax.vjp(lambda v, g: shape_keys(v, g, position)[:, 0], key_lin, key_gain)
-    queries, keys = queries.astype(bf16), keys.astype(bf16)
-    allowed = visible(segment, place, segment, place)
-    scores = jnp.einsum("qd,kd->qk", queries, keys, preferred_element_type=f32)
-    scores = jnp.where(allowed, scores, NEG)
-    probability = jax.nn.softmax(scores, axis=1)
-    attended = jnp.dot(probability.astype(bf16), values, preferred_element_type=f32).astype(bf16)
-    att_rows = lax.all_to_all(attended, "expert", split_axis=0, concat_axis=0, tiled=True)
-    att_rows = jnp.transpose(att_rows.reshape(groups, tok_rows, head_dim), (1, 0, 2)).reshape(
-        tok_rows, groups * head_dim
-    )
-    branch_part = jnp.dot(att_rows, w_out, preferred_element_type=f32)
-    branch = lax.psum_scatter(
-        branch_part.astype(bf16), "tensor", scatter_dimension=0, tiled=True
-    ).astype(f32)
-    residual = own(hidden_in).astype(f32) + branch
-    normed2, norm2_pull = jax.vjp(norm_rows, residual, norm2_gain)
-    normed2 = normed2.astype(bf16)
-    normed2_all = gather_rows(normed2)
+    cotangent_late, _ = lax.optimization_barrier((own(cotangent), tags))
+    grad_y_all = lax.all_gather(cotangent_late, ("expert", "tensor"), axis=0, tiled=True)
+
+    half_dim = head_dim // 2
+    inverse = THETA ** (-(jnp.arange(half_dim, dtype=f32) * 2.0) / head_dim)
+    angles = position.astype(f32)[:, None] * inverse[None, :]
+    cosine, sine = jnp.cos(angles), jnp.sin(angles)
+    cosine = jnp.concatenate([cosine, cosine], axis=1)
+    sine = jnp.concatenate([-sine, sine], axis=1)
+    q_gain, k_gain = query_gain[None], key_gain[None]
+    normed1, queries, keys, values, lin = project(
+        which, hidden_all, norm1_gain[None], w_query, key_weight, value_weight, q_gain, k_gain,
+        cosine, sine,
+    )
+    place_row, open_row = place[None], (place - position)[None]
+    place_column = place[:, None]
+    attended, log_total, att_rows = attend(
+        queries, keys, values, place_column, place_row, open_row
+    )
+    residual, normed2, normed2_all = branch_rows(
+        att_rows, w_out, own(hidden_in), norm2_gain[None]
+    )
 
     expert_range = jnp.arange(expert_count, dtype=jnp.int32)
     chosen = jnp.any(ids_t[:, :, None] == expert_range, axis=0)
@@ -857,9 +1419,9 @@
     dots_wide = lax.dynamic_update_slice(dots_wide, dots, (0, group * local_count))
     back = scatter_rows(
         jnp.concatenate([grad_normed2_part, dots_wide], axis=1).astype(bf16),
-        1,
-    )
-    moe_branch = scatter_rows(out_part.astype(bf16), 2)
+        2,
+    )
+    moe_branch = scatter_rows(out_part.astype(bf16), 4)
     out_own = (residual + moe_branch).astype(bf16)
 
     start = group * tok_rows + part * own_rows
@@ -873,44 +1435,60 @@
     grad_normed2 = back[:, :model_width] + jnp.einsum(
         "te,de->td", grad_logits, w_router, preferred_element_type=f32
     )
+    norm2_pull = jax.vjp(norm_rows, residual, norm2_gain)[1]
     grad_resid_norm, grad_norm2 = norm2_pull(grad_normed2)
     grad_residual = own(cotangent).astype(f32) + grad_resid_norm
     grad_residual_all = gather_rows(grad_residual.astype(bf16))
 
-    grad_out = jnp.einsum("rc,rd->cd", attended, grad_residual_all, preferred_element_type=f32)
-    grad_att = jnp.einsum(
-        "rd,cd->rc", grad_residual_all, head_out, preferred_element_type=f32
+    grad_out = jnp.einsum(
+        "rc,rd->cd", attended, grad_residual_all, preferred_element_type=f32
     ).astype(bf16)
-    grad_prob = jnp.einsum("qd,kd->qk", grad_att, values, preferred_element_type=f32)
-    delta = jnp.sum(probability * grad_prob, axis=1, keepdims=True)
-    grad_scores = (probability * (grad_prob - delta)).astype(bf16)
-    grad_queries = jnp.dot(grad_scores, keys, preferred_element_type=f32)
-    grad_keys = jnp.einsum("qk,qd->kd", grad_scores, queries, preferred_element_type=f32)
-    grad_values = jnp.einsum(
-        "qk,qd->kd", probability.astype(bf16), grad_att, preferred_element_type=f32
-    )
-    grad_query_lin, grad_qgain = query_pull(grad_queries)
-    grad_key_lin, grad_kgain = key_pull(grad_keys)
-    grad_lin = jnp.concatenate([grad_query_lin, grad_key_lin, grad_values], axis=1).astype(bf16)
-    grad_qkv = jnp.einsum("td,tc->dc", normed1, grad_lin, preferred_element_type=f32)
+    grad_out_all = lax.all_gather(grad_out, "expert", axis=0, tiled=True)
+    grad_residual_all, _ = lax.optimization_barrier((grad_residual_all, grad_out))
+    grad_lin, grad_qgain, grad_kgain = attend_back(
+        which, grad_residual_all, w_out, queries, lin, cosine, sine, place_row, open_row,
+        log_total, keys, values, place_column, k_gain, q_gain,
+    )
+    head_query = lax.dynamic_slice_in_dim(w_query, group * head_dim, head_dim, 1)
+    qkv_weight = jnp.concatenate([head_query, key_weight, value_weight], axis=1)
     grad_normed1_part = jnp.einsum(
         "tc,dc->td", grad_lin, qkv_weight, preferred_element_type=f32
     )
-    grad_normed1 = scatter_rows(grad_normed1_part.astype(bf16), 2)
+    grad_qkv = jnp.einsum(
+        "td,tc->dc", normed1, grad_lin, preferred_element_type=f32
+    ).astype(bf16)
+    extra = jnp.zeros((model_width, head_dim), f32)
+    router_rows = lax.dynamic_update_slice(extra, grad_router, (0, 0))
+    extra = lax.dynamic_update_slice(router_rows, grad_norm2[:, None], (0, expert_count))
+    extra = lax.dynamic_update_slice(extra, grad_qgain.T, (0, expert_count + 1))
+    extra = lax.dynamic_update_slice(extra, grad_kgain.T, (0, expert_count + 2))
+    reduced, kv_own = scatter_rows(
+        jnp.concatenate([grad_normed1_part, extra], axis=1).astype(bf16),
+        3,
+        grad_qkv[:, head_dim:],
+    )
     norm1_pull = jax.vjp(norm_rows, own(hidden_in).astype(f32), norm1_gain)[1]
-    grad_hidden_norm, grad_norm1 = norm1_pull(grad_normed1)
+    grad_hidden_norm, grad_norm1 = norm1_pull(reduced[:, :model_width])
     grad_hidden_own = (grad_residual + grad_hidden_norm).astype(bf16)
-    ends = lax.all_gather(
-        jnp.concatenate([out_own, grad_hidden_own], axis=1), "tensor", axis=0, tiled=True
-    )
-    grad_query = lax.all_gather(
-        grad_qkv[:, :head_dim].astype(bf16), "expert", axis=1, tiled=True
-    ).astype(f32)
-    grad_out = lax.all_gather(grad_out.astype(bf16), "expert", axis=0, tiled=True).astype(f32)
-    grad_kv = lax.psum(grad_qkv[:, head_dim:].astype(bf16), "expert").astype(f32)
-    grad_norm1, grad_norm2, grad_qgain, grad_kgain, grad_router = lax.psum(
-        (grad_norm1, grad_norm2, grad_qgain, grad_kgain, grad_router), BOTH
-    )
+    extra_rows = own_rows * head_dim // model_width
+    small = jnp.concatenate(
+        [
+            grad_norm1[None],
+            reduced[:, model_width:].reshape(extra_rows, model_width),
+            jnp.zeros((15 - extra_rows, model_width), f32),
+        ],
+        axis=0,
+    ).astype(bf16)
+    grad_query, grad_kv, small, ends = finish(
+        grad_qkv[:, :head_dim], kv_own, small, jnp.concatenate([out_own, grad_hidden_own], axis=1), 5
+    )
+    grad_query, grad_kv, grad_out = (v.astype(f32) for v in (grad_query, grad_kv, grad_out_all))
+    small = small.reshape(groups * tensor_size, 16, model_width).astype(f32)
+    grad_norm1 = jnp.sum(small[:, 0], axis=0)
+    extra = small[:, 1 : 1 + extra_rows].reshape(model_width, head_dim)
+    grad_router = extra[:, :expert_count]
+    grad_norm2 = extra[:, expert_count]
+    grad_qgain, grad_kgain = extra[:head_dim, expert_count + 1], extra[:head_dim, expert_count + 2]
     grad_down = grad_down.reshape(local_count, ff_local, model_width)
     return (
         ends[:, :model_width],

time: 903 us -> 655 us (0.73)
  waiting for transfers between devices: 211 us -> 0.06 us
  Pallas kernels: 309 us -> 427 us
  blocking collectives: 95 us -> 0 us
  matrix products: 131 us -> 89.2 us
  other arithmetic: 91.5 us -> 61.2 us
    psum x2 -> x0, waiting for transfers between devices: 120 us -> none  [the longest x1 120 us: head_device(): lax.psum((grad_norm1, grad_norm2, grad_qgain, grad_kgain, grad_router), B...]
    pallas_call x7 -> x10, Pallas kernels: 309 us -> 427 us  [the longest x3 155 us: scatter_rows(): pl.pallas_call(partial(scatter_kernel, split, with_kv), out_shape=out_sha...]
    all_gather x3 -> x2, waiting for transfers between devices: 90.9 us -> 0.02 us  [the longest x1 0.02 us: head_device(): lax.all_gather(cotangent_late, ('expert', 'tensor'), axis=0, tiled=True)]
    dot_general x9 -> x0, matrix products: 46.3 us -> none  [the longest x1 10.5 us: head_device(): jnp.einsum('qd,kd->qk', grad_att, values, preferred_element_type=f32)]
    psum x1 -> x0, blocking collectives: 41.6 us -> none  [head_device(): lax.psum((grad_norm1, grad_norm2, grad_qgain, grad_kgain, grad_router), B...]
    all_gather x1 -> x0, blocking collectives: 32.3 us -> none  [all_tokens(): gathered = lax.all_gather(packed, 'expert', axis=1, tiled=True)]
    convert_element_type x7 -> x5, other arithmetic: 38.4 us -> 15.4 us  [the longest x2 13.6 us: head_device(): v.astype(f32)]
    all_to_all x1 -> x0, blocking collectives: 21.1 us -> none  [head_device(): lax.all_to_all(attended, 'expert', split_axis=0, concat_axis=0, tiled=True)]
  transfers between devices with their start and end apart: 6 -> 2, of which waited for: 3 -> 0; matrix products, arithmetic and copies ran while one was open for 7% -> 18% of each run, Pallas kernels for 16% -> 45%
where the time goes in v3:
time: 655 us; the launch traced here: 645 us
  Pallas kernels  427 us (65%)
  matrix products  89.2 us (14%)
  other arithmetic  61.2 us (9%)
  local copies, waits for them, and re-layouts  53.1 us (8%)
  between operations  15.2 us (2%)
    pallas_call x3, Pallas kernels, scatter_rows(): pl.pallas_call(partial(scatter_kernel, split, with_kv), out_shape=out_sha...  155 us
    pallas_call x1, Pallas kernels, finish(): pl.pallas_call(finish_kernel, out_shape=(shape((query.shape[0], 8 * query...  64.9 us
    pallas_call x1, Pallas kernels, gather_rows(): pl.pallas_call(gather_tagged_kernel, out_shape=(shape, jax.ShapeDtypeStru...  55.4 us
    pallas_call x1, Pallas kernels, branch_rows(): pl.pallas_call(branch_kernel, out_shape=(shape((count, width), F32), shap...  52.9 us
    pallas_call x1, Pallas kernels, gather_rows(): pl.pallas_call(gather_kernel, out_shape=shape, in_specs=[hbm], out_specs=...  40.7 us
    pallas_call x1, Pallas kernels, attend_back(): pl.pallas_call(attend_back_kernel, grid_spec=pltpu.PrefetchScalarGridSpec...  26.2 us
    pallas_call x1, Pallas kernels, attend(): pl.pallas_call(attend_kernel, out_shape=(shape((total, dim), BF16), shape...  18.6 us
    unnamed x115, local copies, waits for them, and re-layouts  16.2 us
  transfers between devices with their start and end apart: 2, of which 0 were waited for; matrix products, arithmetic and copies ran while one was open for 18% of the time, Pallas kernels for 45%

profile of v3, /device:TPU:0, one launch (start us, length us, event | category | flops | bytes accessed | tf_op | source)
XLA Modules:
  0.0 645.4 jit_solution(6644606470842882846)
XLA Ops:
  10.0 2.3 fusion.24
  13.7 55.4 %gather_tagged.1 = (bf16[2048,2048]{1,0:T(8,128)(2,1)}, s32[8,16,256]{2,1,0:T(8,128)}) custom-call(bf16[64,2048]{1,0:T(8,128)(2,1)} %get-tuple-element.127.src.hidden, s32[16,256]{1,0:T(8,128)} %add_add_fusion.2.tag), custom_call_target="tpu_custom_call" | custom-call | tf_op jit(solution)/shard_map/gather_tagged/pallas_call | solution.py:650
  73.7 3.7 fusion.29
  80.3 13.1 %project.1 = (bf16[2048,2048]{1,0:T(8,128)(2,1)}, bf16[2048,128]{1,0:T(8,128)(2,1)S(1)}, bf16[2048,128]{1,0:T(8,128)(2,1)S(1)}, bf16[2048,128]{1,0:T(8,128)(2,1)S(1)}, f32[2048,256]{1,0:T(8,128)S(1)}) custom-call(s32[1]{0:T(128)} %bitcast.which, bf16[2048,2048]{1,0:T(8,128)(2,1)} %get-tuple-element.37.hidden, f32[1,2048]{1,0:T(1,128)S(1)} %bitcast.73, ...), custom_call_target="tpu_custom_call" | custom-call | tf_op jit(solution)/shard_map/project/pallas_call | solution.py:1061
  93.5 18.6 %attend.1 = (bf16[2048,128]{1,0:T(8,128)(2,1)S(1)}, f32[1,2048]{1,0:T(1,128)S(1)}, bf16[256,1024]{1,0:T(8,128)(2,1)S(1)}) custom-call(bf16[2048,128]{1,0:T(8,128)(2,1)S(1)} %get-tuple-element.40.queries, bf16[2048,128]{1,0:T(8,128)(2,1)S(1)} %get-tuple-element.41.keys, bf16[2048,128]{1,0:T(8,128)(2,1)S(1)} %get-tuple-element.42.values, ...), custom_call_target="tpu_custom_call" | custom-call | tf_op jit(solution)/shard_map/attend/pallas_call | solution.py:1151
  114.6 52.9 %branch.1 = (f32[64,2048]{1,0:T(8,128)S(1)}, bf16[64,2048]{1,0:T(8,128)(2,1)S(1)}, bf16[2048,2048]{1,0:T(8,128)(2,1)S(1)}) custom-call(bf16[256,1024]{1,0:T(8,128)(2,1)S(1)} %get-tuple-element.43.att_rows, bf16[1024,2048]{1,0:T(8,128)(2,1)S(1)} %copy-done.4, bf16[64,2048]{1,0:T(8,128)(2,1)S(1)} %copy-done.8, f32[1,2048]{1,0:T(1,128)S(1)} %bitcast.70), custom_call_target="tpu_custom_call" | custom-call | tf_op jit(solution)/shard_map/branch/pallas_call | solution.py:1205
  167.5 2.4 fusion.46
  171.5 2.9 fusion.9
  190.0 11.1 %fusion.48 = f32[2048,768]{0,1:T(8,128)} fusion(bf16[2048,2048]{1,0:T(8,128)(2,1)} %copy-done.26, bf16[2048,768]{0,1:T(8,128)(2,1)S(1)} %bitcast.85), kind=kOutput, calls=%fused_computation.105 | convolution fusion | flops 6442450944 | bytes 17825792 | tf_op jit(solution)/shard_map/dot_general | solution.py:1395
  201.1 11.9 %multiply_convert_fusion.2 = (bf16[2048,384]{0,1:T(8,128)(2,1)}, bf16[2048,384]{0,1:T(8,128)(2,1)}, bf16[2048,384]{0,1:T(8,128)(2,1)}, bf16[2048,384]{0,1:T(8,128)(2,1)S(1)}, f32[2048,384]{0,1:T(8,128)S(1)}) fusion(f32[2048,768]{0,1:T(8,128)} %fusion.48, f32[2048,2]{0,1:T(2,128)} %copy.86, bf16[2048,2048]{1,0:T(8,128)(2,1)} %all-gather.3.cloned.1.call-done, ...), kind=kOutput, calls=%fused_computation.17 | convolution fusion | flops 3236167680 | bytes 25706496 | tf_op jit(solution)/shard_map/rd,fd->rf/dot_general | solution.py:1404
  213.1 2.3 convert_multiply_fusion
  215.3 2.7 reduce_sum.107
  222.0 11.3 %convolution_convert_fusion.2 = bf16[2048,2048]{1,0:T(8,128)(2,1)} fusion(bf16[2048,768]{0,1:T(8,128)(2,1)} %bitcast.86, bf16[2048,384]{0,1:T(8,128)(2,1)} %get-tuple-element.131, bf16[2048,384]{0,1:T(8,128)(2,1)} %get-tuple-element.130), kind=kOutput, calls=%fused_computation.8 | convolution fusion | flops 6452936704 | bytes 14680064 | tf_op jit(solution)/shard_map/rf,df->rd/dot_general | solution.py:1415
  234.2 5.2 dynamic_update_slice.15
  239.4 8.1 %pad_maximum_fusion.refs_0_ = bf16[2048,2176]{1,0:T(8,128)(2,1)} fusion(bf16[2048,128]{1,0:T(8,128)(2,1)} %dynamic_update_slice.15, bf16[2048,2048]{1,0:T(8,128)(2,1)} %convolution_convert_fusion.2), kind=kLoop, calls=%fused_computation.2 | loop fusion | flops 17825792 | bytes 17825792 | tf_op jit(solution)/shard_map/concatenate | solution.py:1421
  247.5 49.7 %scatter_rows.2 = f32[64,2176]{1,0:T(8,128)S(1)} custom-call(bf16[2048,2176]{1,0:T(8,128)(2,1)} %pad_maximum_fusion.refs_0_), custom_call_target="tpu_custom_call" | custom-call | tf_op jit(solution)/shard_map/scatter_rows/pallas_call | solution.py:853
  297.2 7.0 %convolution_convert_fusion.refs_0_ = bf16[2048,2048]{1,0:T(8,128)(2,1)} fusion(bf16[2048,384]{0,1:T(8,128)(2,1)S(1)} %copy-done.36, bf16[384,2048]{1,0:T(8,128)(2,1)S(1)} %bitcast.64), kind=kOutput, calls=%fused_computation.6 | convolution fusion | flops 3225419776 | bytes 11534336 | tf_op jit(solution)/shard_map/dot_general | solution.py:1402
  304.2 47.6 %scatter_rows.3 = f32[64,2048]{1,0:T(8,128)S(1)} custom-call(bf16[2048,2048]{1,0:T(8,128)(2,1)} %convolution_convert_fusion.refs_0_), custom_call_target="tpu_custom_call" | custom-call | tf_op jit(solution)/shard_map/scatter_rows/pallas_call | solution.py:853
  356.9 40.7 %gather_rows.1.grad_rows = bf16[2048,2048]{1,0:T(8,128)(2,1)} custom-call(bf16[64,2048]{1,0:T(8,128)(2,1)} %fusion.40.src), custom_call_target="tpu_custom_call" | custom-call | tf_op jit(solution)/shard_map/gather_rows/pallas_call | solution.py:641
  397.7 5.7 convolution_convert_fusion.4
  409.8 26.2 %attend_back.1 = (bf16[2048,384]{1,0:T(8,128)(2,1)}, f32[1,128]{1,0:T(1,128)S(1)}, f32[1,128]{1,0:T(1,128)S(1)}) custom-call(s32[1]{0:T(128)} %bitcast.which, bf16[2048,2048]{1,0:T(8,128)(2,1)} %gather_rows.1.grad_rows, bf16[1024,2048]{1,0:T(8,128)(2,1)} %w_out.3, bf16[2048,128]{1,0:T(8,128)(2,1)S(1)} %copy-done.11, f32[2048,256]{1,0:T(8,128)} %copy-done.7, ...), custom_call_target="tpu_custom_call" | custom-call | tf_op jit(solution)/shard_map/attend_back/pallas_call | solution.py:1284
  436.3 9.9 %convolution_convert_fusion.1 = bf16[2048,2048]{1,0:T(8,128)(2,1)} fusion(bf16[2048,384]{1,0:T(8,128)(2,1)} %get-tuple-element.51, bf16[2048,128]{1,0:T(8,128)(2,1)} %w_value.1, bf16[2048,128]{1,0:T(8,128)(2,1)} %w_key.1, bf16[2048,128]{1,0:T(8,128)(2,1)} %constant_dynamic-slice_fusion), kind=kOutput, calls=%fused_computation.7 | convolution fusion | flops 3230138368 | bytes 11534336 | tf_op jit(solution)/shard_map/tc,dc->td/dot_general | solution.py:1454
  449.3 7.9 %pad_maximum_fusion.1.refs_0_ = bf16[2048,2176]{1,0:T(8,128)(2,1)} fusion(bf16[2048,128]{1,0:T(8,128)(2,1)S(1)} %dynamic_update_slice.19, bf16[2048,2048]{1,0:T(8,128)(2,1)} %convolution_convert_fusion.1), kind=kLoop, calls=%fused_computation.3 | loop fusion | flops 17825792 | bytes 17825792 | tf_op jit(solution)/shard_map/concatenate | solution.py:1466
  457.3 8.4 %convolution_convert_fusion.3 = bf16[2048,384]{1,0:T(8,128)(2,1)S(1)} fusion(bf16[2048,2048]{1,0:T(8,128)(2,1)} %get-tuple-element.39, bf16[2048,384]{1,0:T(8,128)(2,1)} %get-tuple-element.51), kind=kOutput, calls=%fused_computation.20 | convolution fusion | flops 3222011904 | bytes 11534336 | tf_op jit(solution)/shard_map/td,tc->dc/dot_general | solution.py:1457
  466.6 57.3 %scatter_rows_kv.1 = (f32[64,2176]{1,0:T(8,128)S(1)}, bf16[256,256]{1,0:T(8,128)(2,1)S(1)}) custom-call(bf16[2048,2176]{1,0:T(8,128)(2,1)} %pad_maximum_fusion.1.refs_0_, bf16[2048,256]{1,0:T(8,128)(2,1)S(1)} %slice.105.refs_1_), custom_call_target="tpu_custom_call" | custom-call | tf_op jit(solution)/shard_map/scatter_rows_kv/pallas_call | solution.py:853
  527.1 64.9 %finish.1 = (bf16[2048,1024]{1,0:T(8,128)(2,1)}, bf16[2048,256]{1,0:T(8,128)(2,1)}, bf16[512,2048]{1,0:T(8,128)(2,1)}, bf16[256,4096]{1,0:T(8,128)(2,1)}) custom-call(bf16[2048,128]{1,0:T(8,128)(2,1)} %slice.104.query, bf16[256,256]{1,0:T(8,128)(2,1)} %copy-done.22, bf16[16,2048]{1,0:T(8,128)(2,1)} %maximum_maximum_fusion.small, ...), custom_call_target="tpu_custom_call" | custom-call | tf_op jit(solution)/shard_map/finish/pallas_call | solution.py:995
  592.0 6.8 %convert_element_type.90 = f32[2048,1024]{1,0:T(8,128)} convert(bf16[2048,1024]{1,0:T(8,128)(2,1)} %get-tuple-element.58) | non-fusion elementwise | flops 2097152 | bytes 12582912 | tf_op jit(solution)/shard_map/convert_element_type | solution.py:1485
  607.3 2.3 slice_reduce_fusion.1
  613.7 9.3 %fusion.12 = f32[2048,768]{0,1:T(8,128)S(1)} fusion(bf16[2048,2048]{1,0:T(8,128)(2,1)} %copy-done.26, bf16[2048,384]{0,1:T(8,128)(2,1)S(1)} %copy-done.39, bf16[2048,384]{0,1:T(8,128)(2,1)S(1)} %copy-done.38), kind=kOutput, calls=%fused_computation.26 | convolution fusion | flops 6448742400 | bytes 17825792 | tf_op jit(solution)/shard_map/rd,rf->df/dot_general | solution.py:1411
  623.0 3.1 fusion.42
  626.2 5.2 fusion.49
  631.3 6.8 %convert_element_type.92 = f32[1024,2048]{1,0:T(8,128)} convert(bf16[1024,2048]{1,0:T(8,128)(2,1)} %all-gather.5.cloned.1.call-done) | non-fusion elementwise | flops 2097152 | bytes 12582912 | tf_op jit(solution)/shard_map/convert_element_type | solution.py:1485
  (181 shorter events, 67.4 us)
Async XLA Ops:
  7.2 194.0 %copy-start = (bf16[2,192,2048]{2,1,0:T(8,128)(2,1)S(1)}, bf16[2,192,2048]{2,1,0:T(8,128)(2,1)}, u32[]{:S(2)}) copy-start(bf16[2,192,2048]{2,1,0:T(8,128)(2,1)} %param.35) | copy-start | bytes 4718596
  7.2 193.9 %all-gather.3.cloned.1.call-start = ((), (), s32[]{:S(2)}) async-start(), calls=%async_computation | async-start | bytes 8650752 | tf_op jit(solution)/shard_map/all_gather | solution.py:1354
  9.1 622.3 %all-gather.5.cloned.1.call-start = ((), (), s32[]{:S(2)}) async-start(), calls=%async_computation.1 | async-start | bytes 4718592 | tf_op jit(solution)/shard_map/all_gather | solution.py:1446
  78.1 15.3 %copy-start.2 = (f32[2048,128]{1,0:T(8,128)}, f32[2048,128]{1,0:T(8,128)S(1)}, u32[]{:S(2)}) copy-start(f32[2048,128]{1,0:T(8,128)S(1)} %get-tuple-element.153.sine.sine_all) | copy-start | bytes 3145732
  80.3 13.2 %copy-start.5 = (s32[2048,1]{1,0:T(8,128)S(1)}, s32[2048,1]{1,0:T(8,128)}, u32[]{:S(2)}) copy-start(s32[2048,1]{1,0:T(8,128)} %copy.83.place_column) | copy-start | bytes 24580
  80.3 34.2 %copy-start.4 = (bf16[1024,2048]{1,0:T(8,128)(2,1)S(1)}, bf16[1024,2048]{1,0:T(8,128)(2,1)}, u32[]{:S(2)}) copy-start(bf16[1024,2048]{1,0:T(8,128)(2,1)} %w_out.3) | copy-start | bytes 12582916
  80.3 34.2 %copy-start.8 = (bf16[64,2048]{1,0:T(8,128)(2,1)S(1)}, bf16[64,2048]{1,0:T(8,128)(2,1)}, u32[]{:S(2)}) copy-start(bf16[64,2048]{1,0:T(8,128)(2,1)} %get-tuple-element.127.src.hidden) | copy-start | bytes 786436
  80.3 34.2 %copy-start.21 = (f32[2048]{0:T(1024)S(1)}, f32[2048]{0:T(1024)}, u32[]{:S(2)}) copy-start(f32[2048]{0:T(1024)} %param.31) | copy-start | bytes 24580
  93.4 21.1 %copy-start.10 = (bf16[2048,128]{1,0:T(8,128)(2,1)}, bf16[2048,128]{1,0:T(8,128)(2,1)S(1)}, u32[]{:S(2)}) copy-start(bf16[2048,128]{1,0:T(8,128)(2,1)S(1)} %get-tuple-element.40.queries) | copy-start | bytes 1572868
  93.4 74.0 %copy-start.7 = (f32[2048,256]{1,0:T(8,128)}, f32[2048,256]{1,0:T(8,128)S(1)}, u32[]{:S(2)}) copy-start(f32[2048,256]{1,0:T(8,128)S(1)} %get-tuple-element.49.query_lin.lin) | copy-start | bytes 6291460
  114.5 53.0 %copy-start.42 = (pred[2048,16]{1,0:T(32,128)(4,1)S(1)}, pred[2048,16]{1,0:T(32,128)(4,1)}, u32[]{:S(2)}) copy-start(pred[2048,16]{1,0:T(32,128)(4,1)} %copy.81) | copy-start | bytes 98308
  114.5 53.0 %copy-start.43 = (bf16[2048,16]{0,1:T(8,128)(2,1)S(1)}, bf16[2048,16]{0,1:T(8,128)(2,1)}, u32[]{:S(2)}) copy-start(bf16[2048,16]{0,1:T(8,128)(2,1)} %param.32) | copy-start | bytes 196612
  247.5 49.7 %copy-start.36 = (bf16[2048,384]{0,1:T(8,128)(2,1)S(1)}, bf16[2048,384]{0,1:T(8,128)(2,1)}, u32[]{:S(2)}) copy-start(bf16[2048,384]{0,1:T(8,128)(2,1)} %get-tuple-element.132) | copy-start | bytes 4718596
  304.2 47.6 %copy-start.46 = (f32[64]{0:T(128)S(1)}, f32[64]{0:T(128)}, u32[]{:S(2)}) copy-start(f32[64]{0:T(128)} %copy-done.45) | copy-start | bytes 772
  304.2 47.6 %copy-start.47 = (f32[64]{0:T(128)S(1)}, f32[64]{0:T(128)}, u32[]{:S(2)}) copy-start(f32[64]{0:T(128)} %fusion.33) | copy-start | bytes 772
  304.2 47.8 %copy-start.18 = (bf16[64,2048]{1,0:T(8,128)(2,1)S(1)}, bf16[64,2048]{1,0:T(8,128)(2,1)}, u32[]{:S(2)}) copy-start(bf16[64,2048]{1,0:T(8,128)(2,1)} %copy-done.17) | copy-start | bytes 786436
  304.2 49.0 %copy-start.48 = (f32[64]{0:T(128)S(1)}, f32[64]{0:T(128)}, u32[]{:S(2)}) copy-start(f32[64]{0:T(128)} %fusion.34) | copy-start | bytes 772
  304.2 50.6 %copy-start.53 = (f32[64]{0:T(128)S(1)}, f32[64]{0:T(128)}, u32[]{:S(2)}) copy-start(f32[64]{0:T(128)} %copy-done.52) | copy-start | bytes 772
  354.8 42.8 %copy-start.28 = (f32[64,2048]{1,0:T(8,128)}, f32[64,2048]{1,0:T(8,128)S(1)}, u32[]{:S(2)}) copy-start(f32[64,2048]{1,0:T(8,128)S(1)} %get-tuple-element.151) | copy-start | bytes 1572868
  397.6 7.7 %copy-start.44 = (f32[2048]{0:T(1024)S(1)}, f32[2048]{0:T(1024)}, u32[]{:S(2)}) copy-start(f32[2048]{0:T(1024)} %get-tuple-element.118) | copy-start | bytes 24580
  397.7 8.8 %copy-start.3 = (f32[2048,128]{1,0:T(8,128)S(1)}, f32[2048,128]{1,0:T(8,128)}, u32[]{:S(2)}) copy-start(f32[2048,128]{1,0:T(8,128)} %copy-done.2) | copy-start | bytes 3145732
  397.7 8.8 %copy-start.11 = (bf16[2048,128]{1,0:T(8,128)(2,1)S(1)}, bf16[2048,128]{1,0:T(8,128)(2,1)}, u32[]{:S(2)}) copy-start(bf16[2048,128]{1,0:T(8,128)(2,1)} %copy-done.10) | copy-start | bytes 1572868
  436.3 9.9 %copy-start.33 = (bf16[2048,128]{1,0:T(8,128)(2,1)S(1)}, bf16[2048,128]{1,0:T(8,128)(2,1)}, u32[]{:S(2)}) copy-start(bf16[2048,128]{1,0:T(8,128)(2,1)} %dynamic_update_slice.16) | copy-start | bytes 1572868
  436.3 9.9 %copy-start.34 = (bf16[2048,1]{1,0:T(8,128)(2,1)S(1)}, bf16[2048,1]{1,0:T(8,128)(2,1)}, u32[]{:S(2)}) copy-start(bf16[2048,1]{1,0:T(8,128)(2,1)} %copy.94) | copy-start | bytes 12292
  466.5 57.4 %copy-start.50 = (f32[64]{0:T(128)S(1)}, f32[64]{0:T(128)}, u32[]{:S(2)}) copy-start(f32[64]{0:T(128)} %fusion.35) | copy-start | bytes 772
  466.5 57.7 %copy-start.54 = (f32[64]{0:T(128)S(1)}, f32[64]{0:T(128)}, u32[]{:S(2)}) copy-start(f32[64]{0:T(128)} %get-tuple-element.126) | copy-start | bytes 772
  466.5 57.7 %copy-start.51 = (bf16[16]{0:T(256)(128)(2,1)S(1)}, bf16[16]{0:T(256)(128)(2,1)}, u32[]{:S(2)}) copy-start(bf16[16]{0:T(256)(128)(2,1)} %pad.5.clone) | copy-start | bytes 100
  466.6 58.4 %copy-start.29 = (f32[64,2048]{1,0:T(8,128)S(1)}, f32[64,2048]{1,0:T(8,128)}, u32[]{:S(2)}) copy-start(f32[64,2048]{1,0:T(8,128)} %copy-done.28) | copy-start | bytes 1572868
  466.6 58.4 %copy-start.49 = (f32[64]{0:T(128)S(1)}, f32[64]{0:T(128)}, u32[]{:S(2)}) copy-start(f32[64]{0:T(128)} %fusion.34) | copy-start | bytes 772
  601.4 8.2 %copy-start.30 = (bf16[2048,256]{1,0:T(8,128)(2,1)S(1)}, bf16[2048,256]{1,0:T(8,128)(2,1)}, u32[]{:S(2)}) copy-start(bf16[2048,256]{1,0:T(8,128)(2,1)} %get-tuple-element.59) | copy-start | bytes 3145732
  611.0 15.1 %slice-start = ((s8[8388608]{0:T(1024)(128)(4,1)}), s8[4194304]{0:T(1024)(128)(4,1)S(1)}, s32[]{:S(2)}) async-start(s8[8388608]{0:T(1024)(128)(4,1)} %bitcast.82), calls=%async_computation.2 | async-start | bytes 8388608
  613.7 12.5 %slice-start.1 = ((s8[8388608]{0:T(1024)(128)(4,1)}), s8[4194304]{0:T(1024)(128)(4,1)S(1)}, s32[]{:S(2)}) async-start(s8[8388608]{0:T(1024)(128)(4,1)} %bitcast.82), calls=%async_computation.3 | async-start | bytes 8388608
  (27 other events, 67.7 us)
Sparse Core Ops, SparseCore 0:
  11.5 88.8 all-gather.2
  403.6 71.4 all-gather.4

commit v4 on v3

--- a/solution.py
+++ b/solution.py
@@ -1164,8 +1164,8 @@
 
 
 def branch_kernel(
-    att_rows, w_out, hidden, gain, residual, normed, normed_all,
-    partial_sum, from_core, to_x_sum, from_x, tensor_sems, *sems,
+    att_rows, w_out, hidden, gain, residual, normed,
+    partial_sum, from_core, to_x_sum, from_x, tensor_sems,
 ):
     count, width = hidden.shape
     spot = Spot()
@@ -1196,7 +1196,6 @@
     normed[...] = (total * root * gain[...]).astype(BF16)
     for at, view in ((0, from_core.at[0]), (1, from_core.at[1]), (4, from_x)):
         arrive(view, tensor_sems.at[at])
-    gather_body(spot, normed, normed_all, *sems)
 
 
 def branch_rows(att_rows, w_out, hidden, gain):
@@ -1206,15 +1205,14 @@
         branch_kernel,
         out_shape=(
             shape((count, width), F32), shape((count, width), BF16),
-            shape((32 * count, width), BF16),
         ),
         in_specs=[VMEM_SPEC] * 4,
-        out_specs=(VMEM_SPEC, VMEM_SPEC, HBM_SPEC),
+        out_specs=(VMEM_SPEC, VMEM_SPEC),
         scratch_shapes=[
             pltpu.VMEM((4 * count, width), BF16), pltpu.VMEM((2, count, width), BF16),
             pltpu.VMEM((count, width), BF16), pltpu.VMEM((count, width), BF16),
         ]
-        + dma_sems(((6,),) + GATHER_SEMS),
+        + dma_sems(((6,),)),
         compiler_params=pltpu.CompilerParams(
             collective_id=7, has_side_effects=True, vmem_limit_bytes=40 << 20
         ),
@@ -1305,6 +1303,407 @@
     )
 
 
+def near_first(step, z):
+    high = z // 2
+    folded = z + high * (3 - 2 * z)
+    place = (step + folded * (1 - step // 2)) % 2 + 2 * (step // 2)
+    return place + high * (3 - 2 * place)
+
+
+class Gather:
+    SEMS = ((5, 7), (7, 2), (4,), (7, 2, 2), None)
+
+    def __init__(self, spot, src, out, recv, z_send, sends, c_recv, local_sem):
+        self.spot, self.src, self.out = spot, src, out
+        self.recv, self.z_send, self.sends, self.c_recv = recv, z_send, sends, c_recv
+        self.count, self.width = src.shape
+        half = self.width // 2
+        self.first, self.second = pl.ds(0, half), pl.ds(half, half)
+        self.whole = pl.ds(0, self.width)
+        self.local = pltpu.make_async_copy(src, self.place(0, 0, 0), local_sem)
+
+    def place(self, dz, dy, dx, dc=0, columns=None):
+        rows = self.spot.rows(dz, dy, dx, dc, self.count)
+        return self.out.at[rows, self.whole if columns is None else columns]
+
+    def send(self, dz, dy, dx, columns, send_sem, recv_sem, device):
+        here = self.place(dz, dy, dx, 0, columns)
+        own = dz == 0 and dy == 0 and dx == 0
+        push(self.src.at[:, columns] if own else here, here, send_sem, recv_sem, device)
+
+    def to_core(self, dz, dy, dx):
+        self.send(
+            dz, dy, dx, self.whole, self.sends.at[0], self.c_recv.at[dz + 3, dy, dx],
+            self.spot.device(0, 0, 0, 1),
+        )
+
+    def spread(self, dz):
+        spot = self.spot
+        for side, step in ((0, 1), (1, -1)):
+            if dz * step <= 0:
+
+                @pl.when(spot.has(step))
+                def _(side=side, step=step):
+                    self.send(
+                        dz, 0, 0, self.whole, self.z_send.at[dz + 3, side],
+                        self.recv.at[0, dz + 3 - step], spot.device(step),
+                    )
+
+        self.send(dz, 0, 0, self.whole, self.sends.at[1], self.recv.at[1, dz + 3], spot.device(0, 1))
+        self.send(
+            dz, 0, 0, self.whole, self.sends.at[2], self.recv.at[2, dz + 3], spot.device(0, 0, 1)
+        )
+        self.to_core(dz, 0, 0)
+
+    def start(self):
+        self.local.start()
+        self.spread(0)
+
+    def take_z(self, dz):
+        def action():
+            arrive(self.place(dz, 0, 0), self.recv.at[0, dz + 3])
+            self.spread(dz)
+
+        when_has(self.spot, dz, action)
+
+    def take_yx(self, dz):
+        spot = self.spot
+
+        def action():
+            arrive(self.place(dz, 1, 0), self.recv.at[1, dz + 3])
+            self.send(
+                dz, 1, 0, self.first, self.sends.at[3], self.recv.at[3, dz + 3],
+                spot.device(0, 0, 1),
+            )
+            self.to_core(dz, 1, 0)
+            arrive(self.place(dz, 0, 1), self.recv.at[2, dz + 3])
+            self.send(
+                dz, 0, 1, self.second, self.sends.at[3], self.recv.at[4, dz + 3],
+                spot.device(0, 1),
+            )
+            self.to_core(dz, 0, 1)
+
+        when_has(spot, dz, action)
+
+    def take_diagonal(self, dz):
+        def action():
+            arrive(self.place(dz, 1, 1, 0, self.first), self.recv.at[3, dz + 3])
+            arrive(self.place(dz, 1, 1, 0, self.second), self.recv.at[4, dz + 3])
+            self.to_core(dz, 1, 1)
+
+        when_has(self.spot, dz, action)
+
+    def take_core(self, far, dy, dx):
+        view = self.out.at[pl.ds(0, self.count), :]
+        arrive(view, self.c_recv.at[far - self.spot.z + 3, dy, dx])
+
+    def drain(self):
+        count, spot = self.count, self.spot
+        for at, pieces in ((0, 16), (1, 4), (2, 4), (3, 4)):
+            arrive(self.out.at[pl.ds(0, pieces * count), :], self.sends.at[at])
+        for dz in range(-3, 4):
+            for side, step in ((0, 1), (1, -1)):
+                if dz * step <= 0:
+
+                    @pl.when(spot.has(dz) & spot.has(step))
+                    def _(dz=dz, side=side):
+                        arrive(self.place(0, 0, 0), self.z_send.at[dz + 3, side])
+
+
+def experts_kernel(
+    normed, grad_y, w_gate, w_up, w_down, router, chosen, kept,
+    reduced, out_part, grad_gate, grad_up, grad_down,
+    rows_all, weight, staged, grad_in, grad_in_down, y_block, out_block, back_block,
+    mine, other, from_a, from_b, from_y, from_x, from_z,
+    weight_sem, y_sem, out_sem, flush_sem, core_send, core_recv, half_send, yx_send, recv,
+    line_send, line_recv, *gather_sems,
+):
+    spot = Spot()
+    count, width = normed.shape
+    wide = reduced.shape[1]
+    local_count, _, ff = w_gate.shape
+    both = local_count * ff
+    block = 4 * count
+    split = 1024
+    first, second = pl.ds(0, split), pl.ds(split, wide - split)
+    group = lax.axis_index("expert")
+    to_y, to_x, to_c = spot.device(0, 1), spot.device(0, 0, 1), spot.device(0, 0, 0, 1)
+
+    def dy_of(step):
+        return (step + step // 4) % 2
+
+    def place_of(step):
+        return near_first(step // 2, spot.z), dy_of(step)
+
+    def group_rows(step):
+        far, dy = place_of(step)
+        y = spot.y + dy * (1 - 2 * spot.y)
+        return pl.ds(pl.multiple_of((far * 2 + y) * block, block), block)
+
+    def y_copy(step):
+        slot = step % 2
+        return pltpu.make_async_copy(
+            grad_y.at[group_rows(step), :], y_block.at[slot], y_sem.at[slot]
+        )
+
+    def out_copy(step):
+        slot = step % 2
+        return pltpu.make_async_copy(
+            out_block.at[slot], out_part.at[group_rows(step), :], out_sem.at[slot]
+        )
+
+    sources = [ref.at[at] for ref in (w_gate, w_up) for at in range(local_count)]
+
+    def weight_copy(at):
+        return pltpu.make_async_copy(sources[at], staged.at[at % 2], weight_sem.at[at % 2])
+
+    weight_copy(0).start()
+    weight_copy(1).start()
+    y_copy(0).start()
+    gather = Gather(spot, normed, rows_all, *gather_sems)
+    spot.greet()
+    gather.start()
+    for at in range(len(sources)):
+        weight_copy(at).wait()
+        weight[:, at * ff : (at + 1) * ff] = staged[at % 2]
+        if at + 2 < len(sources):
+            weight_copy(at + 2).start()
+    grad_in[...] = jnp.zeros_like(grad_in)
+    grad_in_down[...] = jnp.zeros_like(grad_in_down)
+    gather.local.wait()
+
+    def piece(dx, dc):
+        _, part = spot.device(0, 0, dx, dc)
+        return pl.ds(pl.multiple_of(part * count, count), count)
+
+    def core_copy(step, dx):
+        far, dy = place_of(step)
+        slot = step % 2
+        return pltpu.make_async_remote_copy(
+            src_ref=back_block.at[slot, piece(dx, 1), :],
+            dst_ref=other.at[far, dy, dx],
+            send_sem=core_send.at[slot, dx],
+            recv_sem=core_recv.at[far, dy, dx],
+            device_id=to_c,
+            device_id_type=MESH,
+        )
+
+    def merge(far, dy, dx):
+        into = mine.at[far, dy, dx]
+        arrive(other.at[far, dy, dx], core_recv.at[far, dy, dx])
+        return into
+
+    def merge_diagonal(k):
+        far = near_first(k, spot.z)
+        into = merge(far, 1, 1)
+        add_into(into, 16, other.at[far, 1, 1])
+        push(into.at[:, first], from_a.at[far], half_send.at[0], recv.at[0, far], to_x)
+        push(into.at[:, second], from_b.at[far], half_send.at[1], recv.at[1, far], to_y)
+
+    def merge_yx(k):
+        far = near_first(k, spot.z)
+        into = merge(far, 1, 0)
+        add_into(into, 16, other.at[far, 1, 0])
+        arrive(from_a.at[far], recv.at[0, far])
+        add_into(into.at[:, first], 16, from_a.at[far])
+        push(into, from_y.at[far], yx_send.at[0], recv.at[2, far], to_y)
+        into = merge(far, 0, 1)
+        add_into(into, 16, other.at[far, 0, 1])
+        arrive(from_b.at[far], recv.at[1, far])
+        add_into(into.at[:, second], 16, from_b.at[far])
+        push(into, from_x.at[far], yx_send.at[1], recv.at[3, far], to_x)
+
+    def merge_line(k):
+        far = near_first(k, spot.z)
+        into = merge(far, 0, 0)
+        arrive(from_y.at[far], recv.at[2, far])
+        arrive(from_x.at[far], recv.at[3, far])
+        add_into(into, 16, other.at[far, 0, 0], from_y.at[far], from_x.at[far])
+        if k > 0:
+            push(
+                into, from_z.at[spot.z], line_send.at[k], line_recv.at[spot.z],
+                (far * 2 + spot.y, spot.x * 2 + spot.c),
+            )
+
+    def both_ways(take, distance):
+        for dz in (distance, -distance) if distance else (0,):
+            take(dz)
+
+    columns = lax.broadcasted_iota(jnp.int32, (block, both), 1)
+    lower = columns < ff
+    lanes = lax.broadcasted_iota(jnp.int32, (block, 128), 1)
+    names = lax.broadcasted_iota(jnp.int32, (router.shape[0], block), 0)
+
+    def compute(step):
+        slot = step % 2
+        here = group_rows(step)
+        rows = rows_all[here, :]
+        lin = mxu(rows, weight[...])
+        gate, up = lin[:, :both], lin[:, both:]
+        logits = mxu(router[...], rows, 1, 1)
+        picked = chosen[:, here] > 0.0
+        top = jnp.max(jnp.where(picked, logits, NEG), axis=0, keepdims=True)
+        exps = jnp.where(picked, jnp.exp(logits - top), 0.0)
+        soft = exps / jnp.sum(exps, axis=0, keepdims=True)
+        keep = kept[:, here]
+        soft = jnp.where(keep > 0.0, soft, 0.0)
+        lines = []
+        for table in (soft, keep):
+            for at in range(local_count):
+                lines.append(
+                    jnp.sum(
+                        jnp.where(names == group * local_count + at, table, 0.0),
+                        axis=0, keepdims=True,
+                    )
+                )
+        stack = jnp.concatenate(lines + [jnp.zeros((8 - len(lines), block), F32)], axis=0).T
+        spread = jnp.where(lower, stack[:, 0:1], stack[:, 1:2])
+        sigmoid = 1.0 / (1.0 + jnp.exp(-gate))
+        silu = gate * sigmoid
+        act = (silu * up).astype(BF16).astype(F32)
+        weighted = (act * spread).astype(BF16)
+        y_copy(step).wait()
+
+        @pl.when(step >= 2)
+        def _():
+            out_copy(step - 2).wait()
+            for dx in (0, 1):
+                core_copy(step - 2, dx).wait_send()
+
+        out_block[slot] = mxu(weighted, w_down[...]).astype(BF16)
+        out_copy(step).start()
+        y_rows = y_block[slot]
+        mid = mxu(y_rows, w_down[...], 1, 1)
+        dots = act * mid
+        low = jnp.sum(jnp.where(lower, dots, 0.0), axis=1, keepdims=True) * stack[:, 2:3]
+        high = jnp.sum(jnp.where(lower, 0.0, dots), axis=1, keepdims=True) * stack[:, 3:4]
+        mine_at = group * local_count
+        tail = jnp.where(lanes == mine_at, low, jnp.where(lanes == mine_at + 1, high, 0.0))
+        grad_act = mid * spread
+        grad_up_lin = (grad_act * silu).astype(BF16)
+        grad_gate_lin = (grad_act * up * sigmoid * (1.0 + gate * (1.0 - sigmoid))).astype(BF16)
+        grad_lin = jnp.concatenate([grad_gate_lin, grad_up_lin], axis=1)
+        back_block[slot, :, :width] = mxu(grad_lin, weight[...], 1, 1).astype(BF16)
+        back_block[slot, :, width:] = tail.astype(BF16)
+        far, dy = place_of(step)
+        for dx in (1, 0):
+            core_copy(step, dx).start()
+            mine[far, dy, dx] = back_block[slot, piece(dx, 0), :]
+        for at in range(2 * local_count):
+            grad_in[at] += mxu(rows, grad_lin[:, at * ff : (at + 1) * ff], 0, 0)
+        grad_in_down[...] += mxu(weighted, y_rows, 0, 0)
+
+    plans = {
+        0: lambda: (both_ways(gather.take_yx, 0), both_ways(gather.take_z, 1)),
+        1: lambda: (both_ways(gather.take_z, 2), both_ways(gather.take_diagonal, 0)),
+        2: lambda: (
+            both_ways(gather.take_yx, 1), both_ways(gather.take_z, 3), merge_diagonal(0),
+        ),
+        3: lambda: (
+            both_ways(gather.take_diagonal, 1), both_ways(gather.take_yx, 2), merge_yx(0),
+        ),
+        4: lambda: (
+            both_ways(gather.take_diagonal, 2), both_ways(gather.take_yx, 3),
+            merge_diagonal(1), merge_line(0),
+        ),
+        5: lambda: (both_ways(gather.take_diagonal, 3), merge_diagonal(2), merge_yx(1)),
+        6: lambda: (merge_yx(2), merge_line(1)),
+        7: lambda: (merge_diagonal(3), merge_line(2)),
+    }
+
+    @pl.loop(0, 8)
+    def _(step):
+        for at, plan in plans.items():
+
+            @pl.when(step == at)
+            def _(plan=plan):
+                plan()
+
+        @pl.when(step < 7)
+        def _():
+            y_copy(step + 1).start()
+
+        far, dy = place_of(step)
+        for dx in (0, 1):
+            gather.take_core(far, dy, dx)
+        compute(step)
+
+    flush = [
+        pltpu.make_async_copy(
+            grad_in.at[at], (grad_gate, grad_up)[at // local_count].at[at % local_count],
+            flush_sem.at[at],
+        )
+        for at in range(2 * local_count)
+    ]
+    flush.append(pltpu.make_async_copy(grad_in_down, grad_down, flush_sem.at[2 * local_count]))
+    for copy in flush:
+        copy.start()
+    merge_yx(3)
+    merge_line(3)
+    total = mine[spot.z, 0, 0].astype(F32)
+    for k in (1, 2, 3):
+        source = near_first(k, spot.z)
+        arrive(from_z.at[source], line_recv.at[source])
+        total = total + from_z[source].astype(F32)
+    reduced[...] = total
+    gather.drain()
+    for step in (6, 7):
+        out_copy(step).wait()
+        for dx in (0, 1):
+            core_copy(step, dx).wait_send()
+    arrive(from_a, half_send.at[0])
+    arrive(from_b, half_send.at[1])
+    arrive(from_y, yx_send.at[0])
+    arrive(from_x, yx_send.at[1])
+    for k in (1, 2, 3):
+        arrive(from_z.at[0], line_send.at[k])
+    for copy in flush:
+        copy.wait()
+
+
+def experts(normed, grad_y, w_gate, w_up, w_down, router, chosen, kept):
+    count, width = normed.shape
+    wide = width + 128
+    total = grad_y.shape[0]
+    local_count, _, ff = w_gate.shape
+    both = local_count * ff
+    shape, vmem, dma = jax.ShapeDtypeStruct, pltpu.VMEM, pltpu.SemaphoreType.DMA
+    line = vmem((4, count, wide), BF16)
+    return pl.pallas_call(
+        experts_kernel,
+        out_shape=(
+            shape((count, wide), F32), shape((total, width), BF16),
+            shape(w_gate.shape, F32), shape(w_up.shape, F32), shape((both, width), F32),
+        ),
+        in_specs=[VMEM_SPEC, HBM_SPEC, HBM_SPEC, HBM_SPEC] + [VMEM_SPEC] * 4,
+        out_specs=(VMEM_SPEC,) + (HBM_SPEC,) * 4,
+        scratch_shapes=[
+            vmem((total, width), BF16),
+            vmem((width, 2 * both), BF16),
+            vmem((2, width, ff), BF16),
+            vmem((2 * local_count, width, ff), F32),
+            vmem((both, width), F32),
+            vmem((2, 4 * count, width), BF16),
+            vmem((2, 4 * count, width), BF16),
+            vmem((2, 4 * count, wide), BF16),
+            vmem((4, 2, 2, count, wide), BF16),
+            vmem((4, 2, 2, count, wide), BF16),
+            vmem((4, count, 1024), BF16),
+            vmem((4, count, wide - 1024), BF16),
+            line, line, line,
+        ]
+        + dma_sems(
+            ((2,), (2,), (2,), (2 * local_count + 1,), (2, 2), (4, 2, 2), (2,), (2,), (4, 4),
+             (4,), (4,))
+            + Gather.SEMS
+        ),
+        compiler_params=pltpu.CompilerParams(
+            collective_id=8, has_side_effects=True, vmem_limit_bytes=62 << 20
+        ),
+        name="experts",
+    )(normed, grad_y, w_gate, w_up, w_down, router, chosen, kept)
+
+
 def head_device(
     hidden_in,
     cotangent,
@@ -1369,64 +1768,26 @@
     attended, log_total, att_rows = attend(
         queries, keys, values, place_column, place_row, open_row
     )
-    residual, normed2, normed2_all = branch_rows(
-        att_rows, w_out, own(hidden_in), norm2_gain[None]
-    )
+    residual, normed2 = branch_rows(att_rows, w_out, own(hidden_in), norm2_gain[None])
 
     expert_range = jnp.arange(expert_count, dtype=jnp.int32)
-    chosen = jnp.any(ids_t[:, :, None] == expert_range, axis=0)
-    picks = (chosen & valid[:, None]).astype(bf16)
-    earlier = (rank[None, :] < rank[:, None]).astype(bf16)
-    slot = jnp.dot(earlier, picks, preferred_element_type=f32)
-    kept = chosen & valid[:, None] & (slot < CAP)
-
-    def gates(rows, picked):
-        logits = jnp.dot(rows, w_router, preferred_element_type=f32)
-        return jax.nn.softmax(jnp.where(picked, logits, -jnp.inf), axis=1)
-
-    gate_weight = jnp.where(kept, gates(normed2_all, chosen), 0.0)
-    gate_local = lax.dynamic_slice_in_dim(gate_weight, group * local_count, local_count, 1)
-    kept_local = lax.dynamic_slice_in_dim(kept, group * local_count, local_count, 1)
-
-    weight_in = jnp.concatenate([w_gate, w_up], axis=0)
-    weight_in = jnp.transpose(weight_in, (1, 0, 2)).reshape(model_width, -1)
-    weight_down = w_down.reshape(local_count * ff_local, model_width)
-    wide = local_count * ff_local
-    lin2 = jnp.dot(normed2_all, weight_in, preferred_element_type=f32)
-    gate_lin, up_lin = lin2[:, :wide], lin2[:, wide:]
-    sigmoid = jax.nn.sigmoid(gate_lin)
-    silu = gate_lin * sigmoid
-    spread = jnp.repeat(gate_local, ff_local, axis=1)
-    activation = (silu * up_lin).astype(bf16).astype(f32)
-    weighted = (activation * spread).astype(bf16)
-    out_part = jnp.dot(weighted, weight_down, preferred_element_type=f32)
-    grad_down = jnp.einsum("rf,rd->fd", weighted, grad_y_all, preferred_element_type=f32)
-    grad_mid = jnp.einsum("rd,fd->rf", grad_y_all, weight_down, preferred_element_type=f32)
-    dots = jnp.sum((activation * grad_mid).reshape(total_rows, local_count, ff_local), axis=2)
-    dots = jnp.where(kept_local, dots, 0.0)
-    grad_act = grad_mid * spread
-    grad_gate_lin = (grad_act * up_lin * sigmoid * (1.0 + gate_lin * (1.0 - sigmoid))).astype(bf16)
-    grad_up_lin = (grad_act * silu).astype(bf16)
-    grad_lin2 = jnp.concatenate([grad_gate_lin, grad_up_lin], axis=1)
-    grad_in = jnp.einsum("rd,rf->df", normed2_all, grad_lin2, preferred_element_type=f32)
-    grad_in = jnp.transpose(
-        grad_in.reshape(model_width, 2 * local_count, ff_local), (1, 0, 2)
-    )
-    grad_normed2_part = jnp.einsum(
-        "rf,df->rd", grad_lin2, weight_in, preferred_element_type=f32
-    )
-    dots_wide = jnp.zeros((total_rows, head_dim), f32)
-    dots_wide = lax.dynamic_update_slice(dots_wide, dots, (0, group * local_count))
-    back = scatter_rows(
-        jnp.concatenate([grad_normed2_part, dots_wide], axis=1).astype(bf16),
-        2,
-    )
-    moe_branch = scatter_rows(out_part.astype(bf16), 4)
+    chosen = jnp.any(ids_t[:, None, :] == expert_range[:, None], axis=0)
+    picks = (chosen & valid).astype(bf16)
+    earlier = (rank[:, None] < rank[None, :]).astype(bf16)
+    slot = jnp.dot(picks, earlier, preferred_element_type=f32)
+    kept = chosen & valid & (slot < CAP)
+
+    back, out_part, grad_gate, grad_up, grad_down = experts(
+        normed2, grad_y_all, w_gate, w_up, w_down.reshape(-1, model_width), w_router.T,
+        chosen.astype(f32), kept.astype(f32),
+    )
+    moe_branch = scatter_rows(out_part, 4)
     out_own = (residual + moe_branch).astype(bf16)
 
     start = group * tok_rows + part * own_rows
-    chosen_own = lax.dynamic_slice_in_dim(chosen, start, own_rows, 0)
-    soft_own = gates(normed2, chosen_own)
+    chosen_own = lax.dynamic_slice_in_dim(chosen, start, own_rows, 1).T
+    logits = jnp.dot(normed2, w_router, preferred_element_type=f32)
+    soft_own = jax.nn.softmax(jnp.where(chosen_own, logits, -jnp.inf), axis=1)
     grad_soft = back[:, model_width : model_width + expert_count]
     grad_logits = (
         soft_own * (grad_soft - jnp.sum(soft_own * grad_soft, axis=1, keepdims=True))
@@ -1502,8 +1863,8 @@
         grad_out,
         grad_norm2,
         grad_router,
-        grad_in[:local_count],
-        grad_in[local_count:],
+        grad_gate,
+        grad_up,
         grad_down,
     )
 

time: 655 us -> 589 us (0.90)
  matrix products: 89.2 us -> 30.7 us
  other arithmetic: 61.2 us -> 40.2 us
  Pallas kernels: 427 us -> 443 us
    pallas_call x0 -> x1, Pallas kernels: none -> 102 us  [experts(): pl.pallas_call(experts_kernel, out_shape=(shape((count, wide), F32), shap...]
    dot_general x9 -> x2, matrix products: 62.4 us -> 3.62 us  [the longest x1 3.32 us: head_device(): slot = jnp.dot(picks, earlier, preferred_element_type=f32)]
    pallas_call x3 -> x2, Pallas kernels: 155 us -> 107 us  [scatter_rows(): pl.pallas_call(partial(scatter_kernel, split, with_kv), out_shape=out_sha...]
    pallas_call x1, Pallas kernels: 52.9 us -> 12.5 us  [branch_rows(): pl.pallas_call(branch_kernel, out_shape=(shape((count, width), F32), shap...]
    unnamed x115 -> x81, local copies, waits for them, and re-layouts: 16.2 us -> 27.8 us
    concatenate x2 -> x0, other arithmetic: 10.2 us -> none  [the longest x1 8.08 us: head_device(): jnp.concatenate([grad_normed2_part, dots_wide], axis=1).astype(bf16)]
  transfers between devices with their start and end apart: 2 -> 2, of which waited for: 0 -> 0; matrix products, arithmetic and copies ran while one was open for 18% -> 16% of each run, Pallas kernels for 45% -> 43%
where the time goes in v4:
time: 589 us; the launch traced here: 580 us
  Pallas kernels  443 us (75%)
  local copies, waits for them, and re-layouts  50.2 us (9%)
  other arithmetic  40.2 us (7%)
  matrix products  30.7 us (5%)
  between operations  15.1 us (3%)
    pallas_call x2, Pallas kernels, scatter_rows(): pl.pallas_call(partial(scatter_kernel, split, with_kv), out_shape=out_sha...  107 us
    pallas_call x1, Pallas kernels, experts(): pl.pallas_call(experts_kernel, out_shape=(shape((count, wide), F32), shap...  102 us
    pallas_call x1, Pallas kernels, finish(): pl.pallas_call(finish_kernel, out_shape=(shape((query.shape[0], 8 * query...  69.4 us
    pallas_call x1, Pallas kernels, gather_rows(): pl.pallas_call(gather_tagged_kernel, out_shape=(shape, jax.ShapeDtypeStru...  55.3 us
    pallas_call x1, Pallas kernels, gather_rows(): pl.pallas_call(gather_kernel, out_shape=shape, in_specs=[hbm], out_specs=...  39.2 us
    unnamed x81, local copies, waits for them, and re-layouts  27.8 us
    pallas_call x1, Pallas kernels, attend_back(): pl.pallas_call(attend_back_kernel, grid_spec=pltpu.PrefetchScalarGridSpec...  26.2 us
    pallas_call x1, Pallas kernels, attend(): pl.pallas_call(attend_kernel, out_shape=(shape((total, dim), BF16), shape...  18.6 us
  transfers between devices with their start and end apart: 2, of which 0 were waited for; matrix products, arithmetic and copies ran while one was open for 16% of the time, Pallas kernels for 43%

profile of v4, /device:TPU:0, one launch (start us, length us, event | category | flops | bytes accessed | tf_op | source)
XLA Modules:
  0.0 579.6 jit_solution(8390668895419285542)
XLA Ops:
  7.2 1.8 constant_dynamic-slice_fusion.2
  10.0 1.8 fusion.22
  13.2 55.3 %gather_tagged.1 = (bf16[2048,2048]{1,0:T(8,128)(2,1)}, s32[8,16,256]{2,1,0:T(8,128)}) custom-call(bf16[64,2048]{1,0:T(8,128)(2,1)} %get-tuple-element.133.src.hidden, s32[16,256]{1,0:T(8,128)} %add_add_fusion.2.tag), custom_call_target="tpu_custom_call" | custom-call | tf_op jit(solution)/shard_map/gather_tagged/pallas_call | solution.py:650
  71.9 2.4 copy.68.w_gate
  74.3 3.7 copy.69.w_up
  78.3 3.7 fusion.26
  82.7 13.3 %project.1 = (bf16[2048,2048]{1,0:T(8,128)(2,1)}, bf16[2048,128]{1,0:T(8,128)(2,1)S(1)}, bf16[2048,128]{1,0:T(8,128)(2,1)S(1)}, bf16[2048,128]{1,0:T(8,128)(2,1)S(1)}, f32[2048,256]{1,0:T(8,128)S(1)}) custom-call(s32[1]{0:T(128)} %bitcast.which, bf16[2048,2048]{1,0:T(8,128)(2,1)} %get-tuple-element.41.hidden, f32[1,2048]{1,0:T(1,128)S(1)} %bitcast.46, ...), custom_call_target="tpu_custom_call" | custom-call | tf_op jit(solution)/shard_map/project/pallas_call | solution.py:1061
  96.1 18.6 %attend.1 = (bf16[2048,128]{1,0:T(8,128)(2,1)S(1)}, f32[1,2048]{1,0:T(1,128)S(1)}, bf16[256,1024]{1,0:T(8,128)(2,1)S(1)}) custom-call(bf16[2048,128]{1,0:T(8,128)(2,1)S(1)} %get-tuple-element.44.queries, bf16[2048,128]{1,0:T(8,128)(2,1)S(1)} %get-tuple-element.45.keys, bf16[2048,128]{1,0:T(8,128)(2,1)S(1)} %get-tuple-element.46.values, ...), custom_call_target="tpu_custom_call" | custom-call | tf_op jit(solution)/shard_map/attend/pallas_call | solution.py:1151
  115.5 12.5 %branch.1 = (f32[64,2048]{1,0:T(8,128)S(1)}, bf16[64,2048]{1,0:T(8,128)(2,1)S(1)}) custom-call(bf16[256,1024]{1,0:T(8,128)(2,1)S(1)} %get-tuple-element.47.att_rows, bf16[1024,2048]{1,0:T(8,128)(2,1)S(1)} %copy-done.2, bf16[64,2048]{1,0:T(8,128)(2,1)S(1)} %copy-done.6, f32[1,2048]{1,0:T(1,128)S(1)} %bitcast.43), custom_call_target="tpu_custom_call" | custom-call | tf_op jit(solution)/shard_map/branch/pallas_call | solution.py:1204
  128.8 3.3 fusion.10.kept
  132.1 102.0 %experts.1 = (f32[64,2176]{1,0:T(8,128)}, bf16[2048,2048]{1,0:T(8,128)(2,1)}, f32[2,2048,192]{2,1,0:T(8,128)}, f32[2,2048,192]{2,1,0:T(8,128)}, f32[384,2048]{1,0:T(8,128)}) custom-call(bf16[64,2048]{1,0:T(8,128)(2,1)} %copy-done.8, bf16[2048,2048]{1,0:T(8,128)(2,1)} %all-gather.3.cloned.1.call-done.grad_y, bf16[2,2048,192]{2,1,0:T(8,128)(2,1)} %copy.68.w_gate, ...), custom_call_target="tpu_custom_call" | custom-call | tf_op jit(solution)/shard_map/experts/pallas_call | solution.py:1672
  234.1 50.7 %scatter_rows.1 = f32[64,2048]{1,0:T(8,128)S(1)} custom-call(bf16[2048,2048]{1,0:T(8,128)(2,1)} %get-tuple-element.60.refs_0_), custom_call_target="tpu_custom_call" | custom-call | tf_op jit(solution)/shard_map/scatter_rows/pallas_call | solution.py:853
  285.8 2.2 multiply_reduce_fusion
  288.8 1.8 fusion.37.src
  290.7 39.2 %gather_rows.1.grad_rows = bf16[2048,2048]{1,0:T(8,128)(2,1)} custom-call(bf16[64,2048]{1,0:T(8,128)(2,1)} %fusion.37.src), custom_call_target="tpu_custom_call" | custom-call | tf_op jit(solution)/shard_map/gather_rows/pallas_call | solution.py:641
  329.9 5.7 convolution_convert_fusion.2
  335.8 1.9 constant_dynamic-slice_fusion
  342.0 26.2 %attend_back.1 = (bf16[2048,384]{1,0:T(8,128)(2,1)}, f32[1,128]{1,0:T(1,128)S(1)}, f32[1,128]{1,0:T(1,128)S(1)}) custom-call(s32[1]{0:T(128)} %bitcast.which, bf16[2048,2048]{1,0:T(8,128)(2,1)} %gather_rows.1.grad_rows, bf16[1024,2048]{1,0:T(8,128)(2,1)} %w_out.3, bf16[2048,128]{1,0:T(8,128)(2,1)S(1)} %copy-done.11, f32[2048,256]{1,0:T(8,128)} %copy-done.5, ...), custom_call_target="tpu_custom_call" | custom-call | tf_op jit(solution)/shard_map/attend_back/pallas_call | solution.py:1282
  368.2 8.6 %convolution_convert_fusion.1 = bf16[2048,384]{1,0:T(8,128)(2,1)S(1)} fusion(bf16[2048,2048]{1,0:T(8,128)(2,1)} %get-tuple-element.43, bf16[2048,384]{1,0:T(8,128)(2,1)} %get-tuple-element.55), kind=kOutput, calls=%fused_computation.6 | convolution fusion | flops 3222011904 | bytes 11534336 | tf_op jit(solution)/shard_map/td,tc->dc/dot_general | solution.py:1818
  381.1 4.0 dynamic_update_slice.13
  385.0 1.7 dynamic_update_slice.14
  386.7 1.9 dynamic_update_slice.15
  388.6 9.5 %convolution_convert_fusion = bf16[2048,2048]{1,0:T(8,128)(2,1)} fusion(bf16[2048,384]{1,0:T(8,128)(2,1)} %get-tuple-element.55, bf16[2048,128]{1,0:T(8,128)(2,1)S(1)} %copy-done.20, bf16[2048,128]{1,0:T(8,128)(2,1)S(1)} %copy-done.18, bf16[2048,128]{1,0:T(8,128)(2,1)} %constant_dynamic-slice_fusion), kind=kOutput, calls=%fused_computation.5 | convolution fusion | flops 3230138368 | bytes 11534336 | tf_op jit(solution)/shard_map/tc,dc->td/dot_general | solution.py:1815
  398.1 8.1 %pad_maximum_fusion.refs_0_ = bf16[2048,2176]{1,0:T(8,128)(2,1)} fusion(bf16[2048,128]{1,0:T(8,128)(2,1)} %dynamic_update_slice.15, bf16[2048,2048]{1,0:T(8,128)(2,1)} %convolution_convert_fusion), kind=kLoop, calls=%fused_computation.2 | loop fusion | flops 17825792 | bytes 17825792 | tf_op jit(solution)/shard_map/concatenate | solution.py:1827
  406.2 56.0 %scatter_rows_kv.1 = (f32[64,2176]{1,0:T(8,128)S(1)}, bf16[256,256]{1,0:T(8,128)(2,1)S(1)}) custom-call(bf16[2048,2176]{1,0:T(8,128)(2,1)} %pad_maximum_fusion.refs_0_, bf16[2048,256]{1,0:T(8,128)(2,1)S(1)} %slice.87.refs_1_), custom_call_target="tpu_custom_call" | custom-call | tf_op jit(solution)/shard_map/scatter_rows_kv/pallas_call | solution.py:853
  465.3 69.4 %finish.1 = (bf16[2048,1024]{1,0:T(8,128)(2,1)}, bf16[2048,256]{1,0:T(8,128)(2,1)}, bf16[512,2048]{1,0:T(8,128)(2,1)}, bf16[256,4096]{1,0:T(8,128)(2,1)}) custom-call(bf16[2048,128]{1,0:T(8,128)(2,1)} %slice.86.query, bf16[256,256]{1,0:T(8,128)(2,1)} %copy-done.22, bf16[16,2048]{1,0:T(8,128)(2,1)} %maximum_maximum_fusion.small, ...), custom_call_target="tpu_custom_call" | custom-call | tf_op jit(solution)/shard_map/finish/pallas_call | solution.py:995
  534.7 6.8 %convert_element_type.73 = f32[2048,1024]{1,0:T(8,128)} convert(bf16[2048,1024]{1,0:T(8,128)(2,1)} %get-tuple-element.63) | non-fusion elementwise | flops 2097152 | bytes 12582912 | tf_op jit(solution)/shard_map/convert_element_type | solution.py:1846
  542.1 2.0 copy-done.26
  545.9 5.5 copy.79
  551.3 5.3 copy.80
  558.6 2.3 slice_reduce_fusion.1
  563.8 6.8 %convert_element_type.75 = f32[1024,2048]{1,0:T(8,128)} convert(bf16[1024,2048]{1,0:T(8,128)(2,1)} %all-gather.5.cloned.1.call-done) | non-fusion elementwise | flops 2097152 | bytes 12582912 | tf_op jit(solution)/shard_map/convert_element_type | solution.py:1846
  (128 shorter events, 30.5 us)
Async XLA Ops:
  7.2 64.7 %copy-start.33 = (bf16[2,2048,192]{1,2,0:T(8,128)(2,1)S(1)}, bf16[2,2048,192]{1,2,0:T(8,128)(2,1)}, u32[]{:S(2)}) copy-start(bf16[2,2048,192]{1,2,0:T(8,128)(2,1)} %param.33) | copy-start | bytes 4718596
  7.2 124.9 %all-gather.3.cloned.1.call-start = ((), (), s32[]{:S(2)}) async-start(), calls=%async_computation | async-start | bytes 8650752 | tf_op jit(solution)/shard_map/all_gather | solution.py:1753
  9.0 554.8 %all-gather.5.cloned.1.call-start = ((), (), s32[]{:S(2)}) async-start(), calls=%async_computation.1 | async-start | bytes 4718592 | tf_op jit(solution)/shard_map/all_gather | solution.py:1807
  70.8 25.3 %copy-start.3 = (s32[2048,1]{1,0:T(8,128)}, s32[2048,1]{1,0:T(8,128)S(1)}, u32[]{:S(2)}) copy-start(s32[2048,1]{1,0:T(8,128)S(1)} %copy.67.place_column) | copy-start | bytes 24580
  78.2 4.4 copy-start.7
  78.2 4.4 copy-start.17
  78.2 4.4 copy-start.19
  78.3 4.4 copy-start.23
  78.3 4.4 copy-start.24
  78.3 4.4 copy-start.25
  82.6 13.4 %copy-start = (f32[2048,128]{1,0:T(8,128)}, f32[2048,128]{1,0:T(8,128)S(1)}, u32[]{:S(2)}) copy-start(f32[2048,128]{1,0:T(8,128)S(1)} %get-tuple-element.148.sine.sine_all) | copy-start | bytes 3145732
  82.7 32.8 %copy-start.2 = (bf16[1024,2048]{1,0:T(8,128)(2,1)S(1)}, bf16[1024,2048]{1,0:T(8,128)(2,1)}, u32[]{:S(2)}) copy-start(bf16[1024,2048]{1,0:T(8,128)(2,1)} %w_out.3) | copy-start | bytes 12582916
  82.7 32.8 %copy-start.6 = (bf16[64,2048]{1,0:T(8,128)(2,1)S(1)}, bf16[64,2048]{1,0:T(8,128)(2,1)}, u32[]{:S(2)}) copy-start(bf16[64,2048]{1,0:T(8,128)(2,1)} %get-tuple-element.133.src.hidden) | copy-start | bytes 786436
  82.7 32.8 %copy-start.21 = (f32[2048]{0:T(1024)S(1)}, f32[2048]{0:T(1024)}, u32[]{:S(2)}) copy-start(f32[2048]{0:T(1024)} %param.31) | copy-start | bytes 24580
  96.0 32.7 %copy-start.5 = (f32[2048,256]{1,0:T(8,128)}, f32[2048,256]{1,0:T(8,128)S(1)}, u32[]{:S(2)}) copy-start(f32[2048,256]{1,0:T(8,128)S(1)} %get-tuple-element.53.query_lin.lin) | copy-start | bytes 6291460
  96.0 32.7 %copy-start.10 = (bf16[2048,128]{1,0:T(8,128)(2,1)}, bf16[2048,128]{1,0:T(8,128)(2,1)S(1)}, u32[]{:S(2)}) copy-start(bf16[2048,128]{1,0:T(8,128)(2,1)S(1)} %get-tuple-element.44.queries) | copy-start | bytes 1572868
  96.0 32.7 %copy-start.12 = (bf16[2048,128]{1,0:T(8,128)(2,1)}, bf16[2048,128]{1,0:T(8,128)(2,1)S(1)}, u32[]{:S(2)}) copy-start(bf16[2048,128]{1,0:T(8,128)(2,1)S(1)} %get-tuple-element.45.keys) | copy-start | bytes 1572868
  96.1 32.7 %copy-start.14 = (bf16[2048,128]{1,0:T(8,128)(2,1)}, bf16[2048,128]{1,0:T(8,128)(2,1)S(1)}, u32[]{:S(2)}) copy-start(bf16[2048,128]{1,0:T(8,128)(2,1)S(1)} %get-tuple-element.46.values) | copy-start | bytes 1572868
  96.1 32.0 %copy-start.35 = (bf16[2048,16]{0,1:T(8,128)(2,1)S(1)}, bf16[2048,16]{0,1:T(8,128)(2,1)}, u32[]{:S(2)}) copy-start(bf16[2048,16]{0,1:T(8,128)(2,1)} %param.32) | copy-start | bytes 196612
  234.1 51.7 %copy-start.36 = (bf16[2048,16]{0,1:T(8,128)(2,1)S(1)}, bf16[2048,16]{0,1:T(8,128)(2,1)}, u32[]{:S(2)}) copy-start(bf16[2048,16]{0,1:T(8,128)(2,1)} %param.32) | copy-start | bytes 196612
  329.9 7.7 %copy-start.1 = (f32[2048,128]{1,0:T(8,128)S(1)}, f32[2048,128]{1,0:T(8,128)}, u32[]{:S(2)}) copy-start(f32[2048,128]{1,0:T(8,128)} %copy-done) | copy-start | bytes 3145732
  368.2 9.5 %copy-start.9 = (bf16[64,2048]{1,0:T(8,128)(2,1)S(1)}, bf16[64,2048]{1,0:T(8,128)(2,1)}, u32[]{:S(2)}) copy-start(bf16[64,2048]{1,0:T(8,128)(2,1)} %copy-done.8) | copy-start | bytes 786436
  376.8 11.8 %copy-start.18 = (bf16[2048,128]{1,0:T(8,128)(2,1)S(1)}, bf16[2048,128]{1,0:T(8,128)(2,1)}, u32[]{:S(2)}) copy-start(bf16[2048,128]{1,0:T(8,128)(2,1)} %w_key.1) | copy-start | bytes 1572868
  376.8 11.8 %copy-start.20 = (bf16[2048,128]{1,0:T(8,128)(2,1)S(1)}, bf16[2048,128]{1,0:T(8,128)(2,1)}, u32[]{:S(2)}) copy-start(bf16[2048,128]{1,0:T(8,128)(2,1)} %w_value.1) | copy-start | bytes 1572868
  406.2 57.0 %copy-start.28 = (f32[64,2048]{1,0:T(8,128)S(1)}, f32[64,2048]{1,0:T(8,128)}, u32[]{:S(2)}) copy-start(f32[64,2048]{1,0:T(8,128)} %copy-done.27) | copy-start | bytes 1572868
  406.2 58.3 %copy-start.34 = (bf16[64,2048]{1,0:T(8,128)(2,1)S(1)}, bf16[64,2048]{1,0:T(8,128)(2,1)}, u32[]{:S(2)}) copy-start(bf16[64,2048]{1,0:T(8,128)(2,1)} %get-tuple-element.138) | copy-start | bytes 786436
  462.2 3.2 copy-start.22
  534.7 6.8 %copy-start.31 = (bf16[512,2048]{1,0:T(8,128)(2,1)S(1)}, bf16[512,2048]{1,0:T(8,128)(2,1)}, u32[]{:S(2)}) copy-start(bf16[512,2048]{1,0:T(8,128)(2,1)} %get-tuple-element.62) | copy-start | bytes 6291460
  542.0 2.0 copy-start.26
  551.3 9.5 %copy-start.29 = (bf16[2048,256]{1,0:T(8,128)(2,1)S(1)}, bf16[2048,256]{1,0:T(8,128)(2,1)}, u32[]{:S(2)}) copy-start(bf16[2048,256]{1,0:T(8,128)(2,1)} %get-tuple-element.64) | copy-start | bytes 3145732
  556.7 5.7 copy-start.32
  563.8 6.8 %copy-start.30 = (f32[384,2048]{1,0:T(8,128)S(1)}, f32[384,2048]{1,0:T(8,128)}, u32[]{:S(2)}) copy-start(f32[384,2048]{1,0:T(8,128)} %get-tuple-element.67) | copy-start | bytes 9437188
  (7 other events, 6.7 us)
Sparse Core Ops, SparseCore 0:
  10.9 88.8 all-gather.2
  335.8 72.1 all-gather.4

commit v5 on v0

--- a/solution.py
+++ b/solution.py
@@ -4,6 +4,8 @@
 import jax
 import jax.numpy as jnp
 from jax import lax
+from jax.experimental import pallas as pl
+from jax.experimental.pallas import tpu as pltpu
 from jax.sharding import PartitionSpec as P
 
 TOPK = 8
@@ -416,9 +418,1604 @@
     )
 
 
+MESH = pl.DeviceIdType.MESH
+FAR_FIRST = (3, -3, 2, -2, 1, -1, 0)
+
+
+class Spot:
+    def __init__(self):
+        group, part = lax.axis_index("expert"), lax.axis_index("tensor")
+        self.z, self.y = group // 2, group % 2
+        self.x, self.c = part // 2, part % 2
+
+    def has(self, dz):
+        return (self.z + dz >= 0) & (self.z + dz <= 3)
+
+    def device(self, dz=0, dy=0, dx=0, dc=0):
+        y = 1 - self.y if dy else self.y
+        x = 1 - self.x if dx else self.x
+        c = 1 - self.c if dc else self.c
+        return ((self.z + dz) * 2 + y, x * 2 + c)
+
+    def rows(self, dz, dy, dx, dc, count):
+        group, part = self.device(dz, dy, dx, dc)
+        return pl.ds(pl.multiple_of((group * 4 + part) * count, count), count)
+
+    def greet(self, line=False):
+        barrier = pltpu.get_barrier_semaphore()
+        for step in ((0, 1, 0, 0), (0, 0, 1, 0), (0, 0, 0, 1)):
+            pl.semaphore_signal(barrier, inc=1, device_id=self.device(*step), device_id_type=MESH)
+        for dz in (1, -1, 2, -2, 3, -3) if line else (1, -1):
+
+            @pl.when(self.has(dz))
+            def _(dz=dz):
+                pl.semaphore_signal(
+                    barrier, inc=1, device_id=self.device(dz), device_id_type=MESH
+                )
+
+        if line:
+            pl.semaphore_wait(barrier, 6)
+        else:
+            inner = jnp.where((self.z > 0) & (self.z < 3), 1, 0)
+            pl.semaphore_wait(barrier, 4 + inner)
+
+
+def when_has(spot, dz, action):
+    if dz == 0:
+        action()
+    else:
+        pl.when(spot.has(dz))(action)
+
+
+def dma_sems(shapes):
+    return [pltpu.SemaphoreType.DMA(shape) if shape else pltpu.SemaphoreType.DMA for shape in shapes]
+
+
+def add_into(into, chunk, *terms):
+    @pl.loop(0, into.shape[0] // chunk)
+    def _(step):
+        rows = pl.ds(pl.multiple_of(step * chunk, chunk), chunk)
+        for at in range(0, into.shape[1], 1024):
+            columns = pl.ds(at, min(1024, into.shape[1] - at))
+            total = into[rows, columns].astype(jnp.float32)
+            for term in terms:
+                total = total + term[rows, columns].astype(jnp.float32)
+            into[rows, columns] = total.astype(into.dtype)
+
+
+def push(src, dst, send_sem, recv_sem, device):
+    pltpu.make_async_remote_copy(
+        src_ref=src,
+        dst_ref=dst,
+        send_sem=send_sem,
+        recv_sem=recv_sem,
+        device_id=device,
+        device_id_type=MESH,
+    ).start()
+
+
+def arrive(view, sem):
+    pltpu.make_async_copy(view, view, sem).wait()
+
+
+F32, BF16 = jnp.float32, jnp.bfloat16
+VMEM_SPEC = pl.BlockSpec(memory_space=pltpu.VMEM)
+HBM_SPEC = pl.BlockSpec(memory_space=pl.ANY)
+
+
+def cost(flops, microseconds):
+    return pl.CostEstimate(
+        flops=flops, bytes_accessed=microseconds * 3_000_000, transcendentals=0
+    )
+
+
+def mxu(left, right, left_dim=1, right_dim=0):
+    return lax.dot_general(
+        left, right, (((left_dim,), (right_dim,)), ((), ())), preferred_element_type=F32
+    )
+
+
+def head_norm(lin):
+    root = lax.rsqrt(jnp.mean(lin * lin, axis=-1, keepdims=True) + EPS)
+    return lin * root, root
+
+
+def near_first(step, z):
+    high = z // 2
+    folded = z + high * (3 - 2 * z)
+    place = (step + folded * (1 - step // 2)) % 2 + 2 * (step // 2)
+    return place + high * (3 - 2 * place)
+
+
+class Gather:
+    SEMS = ((5, 7), (7, 2), (6,), (7, 2, 2), None, (7, 2), (7, 2, 2))
+
+    def __init__(
+        self, spot, src, out, recv, z_send, sends, c_recv, local_sem, late_recv, late_send, full=None
+    ):
+        self.spot, self.src, self.out, self.full = spot, src, out, full
+        self.recv, self.z_send, self.sends, self.c_recv = recv, z_send, sends, c_recv
+        self.late_recv, self.late_send = late_recv, late_send
+        self.count, self.width = src.shape
+        width, late = self.width, self.width * 5 // 16
+        half = width * 5 // 8 if full is not None else width // 2
+        self.first, self.second = pl.ds(0, half), pl.ds(half, width - half)
+        self.whole = pl.ds(0, width)
+        self.early = (pl.ds(0, width - late), pl.ds(late, width - late))
+        self.late = (pl.ds(width - late, late), pl.ds(0, late))
+        if full is None:
+            self.local = pltpu.make_async_copy(src, self.place(0, 0, 0), local_sem)
+        else:
+            group, _ = spot.device()
+            rows = pl.ds(pl.multiple_of(group * 4 * self.count, 4 * self.count), 4 * self.count)
+            self.local = pltpu.make_async_copy(full, out.at[rows, :], local_sem)
+
+    def place(self, dz, dy, dx, dc=0, columns=None):
+        rows = self.spot.rows(dz, dy, dx, dc, self.count)
+        return self.out.at[rows, self.whole if columns is None else columns]
+
+    def source(self, dz, dy, dx, columns):
+        if dz == 0 and dy == 0 and dx == 0:
+            return self.src.at[:, columns]
+        if dz == 0 and dy == 0 and self.full is not None:
+            _, part = self.spot.device(0, 0, 1)
+            rows = pl.ds(pl.multiple_of(part * self.count, self.count), self.count)
+            return self.full.at[rows, columns]
+        return self.place(dz, dy, dx, 0, columns)
+
+    def send(self, dz, dy, dx, columns, send_sem, recv_sem, device):
+        push(
+            self.source(dz, dy, dx, columns), self.place(dz, dy, dx, 0, columns), send_sem,
+            recv_sem, device,
+        )
+
+    def to_core(self, dz, dy, dx):
+        if dz == 0 and dy == 0 and self.full is not None:
+            return
+        self.send(
+            dz, dy, dx, self.whole, self.sends.at[0], self.c_recv.at[dz + 3, dy, dx],
+            self.spot.device(0, 0, 0, 1),
+        )
+
+    def along_z(self, dz, dy, dx, columns, send_sem, recv_sem):
+        for side, step in ((0, 1), (1, -1)):
+            if dz * step <= 0:
+
+                @pl.when(self.spot.has(step))
+                def _(side=side, step=step):
+                    self.send(
+                        dz, dy, dx, columns, send_sem(side), recv_sem(dz + 3 - step),
+                        self.spot.device(step),
+                    )
+
+    def spread(self, dz):
+        spot = self.spot
+        self.along_z(
+            dz, 0, 0, self.whole, lambda side: self.z_send.at[dz + 3, side],
+            lambda at: self.recv.at[0, at],
+        )
+        if dz == 0:
+            columns, at = (self.whole, self.whole), 0
+        else:
+            columns, at = self.early, 3
+        self.send(
+            dz, 0, 0, columns[0], self.sends.at[1 + at], self.recv.at[1, dz + 3], spot.device(0, 1)
+        )
+        if dz != 0 or self.full is None:
+            self.send(
+                dz, 0, 0, columns[1], self.sends.at[2 + at], self.recv.at[2, dz + 3],
+                spot.device(0, 0, 1),
+            )
+        self.to_core(dz, 0, 0)
+
+    def start(self):
+        self.local.start()
+        self.spread(0)
+
+    def take_z(self, dz):
+        def action():
+            arrive(self.place(dz, 0, 0), self.recv.at[0, dz + 3])
+            self.spread(dz)
+
+        when_has(self.spot, dz, action)
+
+    def take_yx(self, dz):
+        spot = self.spot
+
+        def action():
+            columns = self.early if dz else (self.whole, self.whole)
+            arrive(self.place(dz, 1, 0, 0, columns[0]), self.recv.at[1, dz + 3])
+            self.send(
+                dz, 1, 0, self.first, self.sends.at[3], self.recv.at[3, dz + 3],
+                spot.device(0, 0, 1),
+            )
+            if dz != 0 or self.full is None:
+                arrive(self.place(dz, 0, 1, 0, columns[1]), self.recv.at[2, dz + 3])
+            self.send(
+                dz, 0, 1, self.second, self.sends.at[3], self.recv.at[4, dz + 3],
+                spot.device(0, 1),
+            )
+
+        when_has(spot, dz, action)
+
+    def take_late(self, dz):
+        def action():
+            for dy, dx in ((1, 0), (0, 1)):
+                columns = self.late[dx]
+                if dz != 0:
+                    arrive(self.place(dz, dy, dx, 0, columns), self.late_recv.at[dz + 3, dx])
+                self.along_z(
+                    dz, dy, dx, columns, lambda side: self.late_send.at[dz + 3, side, dx],
+                    lambda at: self.late_recv.at[at, dx],
+                )
+                self.to_core(dz, dy, dx)
+
+        when_has(self.spot, dz, action)
+
+    def take_diagonal(self, dz):
+        def action():
+            arrive(self.place(dz, 1, 1, 0, self.first), self.recv.at[3, dz + 3])
+            arrive(self.place(dz, 1, 1, 0, self.second), self.recv.at[4, dz + 3])
+            self.to_core(dz, 1, 1)
+
+        when_has(self.spot, dz, action)
+
+    def take_core(self, far, dy, dx):
+        view = self.out.at[pl.ds(0, self.count), :]
+        arrive(view, self.c_recv.at[far - self.spot.z + 3, dy, dx])
+
+    def drain(self):
+        count, spot = self.count, self.spot
+        replicated = self.full is not None
+        for at, pieces, columns in (
+            (0, 14 if replicated else 16, self.whole), (1, 1, self.whole), (2, 1, self.whole),
+            (3, 4, self.whole), (4, 3, self.early[0]), (5, 3, self.early[1]),
+        ):
+            if at != 2 or not replicated:
+                arrive(self.out.at[pl.ds(0, pieces * count), columns], self.sends.at[at])
+        for dz in range(-3, 4):
+            for side, step in ((0, 1), (1, -1)):
+                if dz * step <= 0:
+
+                    @pl.when(spot.has(dz) & spot.has(step))
+                    def _(dz=dz, side=side):
+                        arrive(self.place(0, 0, 0), self.z_send.at[dz + 3, side])
+                        for at in (0, 1):
+                            arrive(
+                                self.place(0, 0, 0, 0, self.late[at]),
+                                self.late_send.at[dz + 3, side, at],
+                            )
+
+
+def experts_kernel(
+    normed, grad_y, w_gate, w_up, w_down, router, chosen, kept,
+    reduced, grad_gate, grad_up, grad_down,
+    rows_all, weight, grad_in, grad_in_down, y_block, back_block,
+    mine, other, from_a, from_b, from_y, from_x, from_z,
+    weight_sem, y_sem, flush_sem, core_send, core_recv, half_send, yx_send, recv,
+    line_send, line_recv, *gather_sems,
+):
+    spot = Spot()
+    count, width = normed.shape
+    wide = reduced.shape[1]
+    local_count, ff, _ = w_gate.shape
+    both = local_count * ff
+    block = 4 * count
+    split = from_a.shape[2]
+    first, second = pl.ds(0, split), pl.ds(split, wide - split)
+    group = lax.axis_index("expert")
+    to_y, to_x, to_c = spot.device(0, 1), spot.device(0, 0, 1), spot.device(0, 0, 0, 1)
+
+    def place_of(step):
+        return near_first((step // 2 + 1) % 4, spot.z), (step + (step + 6) // 8) % 2
+
+    def group_rows(step):
+        far, dy = place_of(step)
+        y = spot.y + dy * (1 - 2 * spot.y)
+        return pl.ds(pl.multiple_of((far * 2 + y) * block, block), block)
+
+    def y_copy(step):
+        slot = step % 2
+        return pltpu.make_async_copy(
+            grad_y.at[group_rows(step), :], y_block.at[slot], y_sem.at[slot]
+        )
+
+    sources = [ref.at[at] for ref in (w_gate, w_up) for at in range(local_count)]
+    weights = [
+        pltpu.make_async_copy(source, weight.at[pl.ds(at * ff, ff), :], weight_sem.at[at])
+        for at, source in enumerate(sources)
+    ]
+    for copy in weights:
+        copy.start()
+    y_copy(0).start()
+    gather = Gather(spot, normed, rows_all, *gather_sems)
+    spot.greet()
+    gather.start()
+    grad_in[...] = jnp.zeros_like(grad_in)
+    grad_in_down[...] = jnp.zeros_like(grad_in_down)
+    gather.local.wait()
+    for copy in weights:
+        copy.wait()
+
+    def piece(dx, dc):
+        _, part = spot.device(0, 0, dx, dc)
+        return pl.ds(pl.multiple_of(part * count, count), count)
+
+    def core_copy(step, dx):
+        far, dy = place_of(step)
+        slot = step % 2
+        return pltpu.make_async_remote_copy(
+            src_ref=back_block.at[slot, piece(dx, 1), :],
+            dst_ref=other.at[far, dy, dx],
+            send_sem=core_send.at[slot, dx],
+            recv_sem=core_recv.at[far, dy, dx],
+            device_id=to_c,
+            device_id_type=MESH,
+        )
+
+    def merge(far, dy, dx):
+        into = mine.at[far, dy, dx]
+        arrive(other.at[far, dy, dx], core_recv.at[far, dy, dx])
+        return into
+
+    def merge_diagonal(k):
+        far = near_first(k, spot.z)
+        into = merge(far, 1, 1)
+        add_into(into, 16, other.at[far, 1, 1])
+        push(into.at[:, first], from_a.at[far], half_send.at[0], recv.at[0, far], to_x)
+        push(into.at[:, second], from_b.at[far], half_send.at[1], recv.at[1, far], to_y)
+
+    def merge_yx(k):
+        far = near_first(k, spot.z)
+        into = merge(far, 1, 0)
+        add_into(into, 16, other.at[far, 1, 0])
+        arrive(from_a.at[far], recv.at[0, far])
+        add_into(into.at[:, first], 16, from_a.at[far])
+        push(into, from_y.at[far], yx_send.at[0], recv.at[2, far], to_y)
+        into = merge(far, 0, 1)
+        add_into(into, 16, other.at[far, 0, 1])
+        arrive(from_b.at[far], recv.at[1, far])
+        add_into(into.at[:, second], 16, from_b.at[far])
+        push(into, from_x.at[far], yx_send.at[1], recv.at[3, far], to_x)
+
+    def merge_line(k):
+        far = near_first(k, spot.z)
+        into = merge(far, 0, 0)
+        arrive(from_y.at[far], recv.at[2, far])
+        arrive(from_x.at[far], recv.at[3, far])
+        add_into(into, 16, other.at[far, 0, 0], from_y.at[far], from_x.at[far])
+        if k > 0:
+            push(
+                into, from_z.at[spot.z], line_send.at[k], line_recv.at[spot.z],
+                (far * 2 + spot.y, spot.x * 2 + spot.c),
+            )
+
+    def both_ways(take, distance):
+        for dz in (distance, -distance) if distance else (0,):
+            take(dz)
+
+    columns = lax.broadcasted_iota(jnp.int32, (block, both), 1)
+    lower = columns < ff
+    lanes = lax.broadcasted_iota(jnp.int32, (block, 128), 1)
+    names = lax.broadcasted_iota(jnp.int32, (router.shape[0], block), 0)
+
+    def compute(step):
+        slot = step % 2
+        here = group_rows(step)
+        rows = rows_all[here, :]
+        lin = mxu(rows, weight[...], 1, 1)
+        gate, up = lin[:, :both], lin[:, both:]
+        logits = mxu(router[...], rows, 1, 1)
+        picked = chosen[:, here] > 0.0
+        top = jnp.max(jnp.where(picked, logits, NEG), axis=0, keepdims=True)
+        exps = jnp.where(picked, jnp.exp(logits - top), 0.0)
+        soft = exps / jnp.sum(exps, axis=0, keepdims=True)
+        keep = kept[:, here]
+        soft = jnp.where(keep > 0.0, soft, 0.0)
+        lines = []
+        for table in (soft, keep):
+            for at in range(local_count):
+                lines.append(
+                    jnp.sum(
+                        jnp.where(names == group * local_count + at, table, 0.0),
+                        axis=0, keepdims=True,
+                    )
+                )
+        stack = jnp.concatenate(lines + [jnp.zeros((8 - len(lines), block), F32)], axis=0).T
+        spread = jnp.where(lower, stack[:, 0:1], stack[:, 1:2])
+        sigmoid = 1.0 / (1.0 + jnp.exp(-gate))
+        silu = gate * sigmoid
+        act = (silu * up).astype(BF16).astype(F32)
+        weighted = (act * spread).astype(BF16)
+        y_copy(step).wait()
+
+        @pl.when(step >= 2)
+        def _():
+            for dx in (0, 1):
+                core_copy(step - 2, dx).wait_send()
+
+        back_block[slot, :, :width] = mxu(weighted, w_down[...]).astype(BF16)
+        pass_on(step, 1)
+        y_rows = y_block[slot]
+        mid = mxu(y_rows, w_down[...], 1, 1)
+        dots = act * mid
+        low = jnp.sum(jnp.where(lower, dots, 0.0), axis=1, keepdims=True) * stack[:, 2:3]
+        high = jnp.sum(jnp.where(lower, 0.0, dots), axis=1, keepdims=True) * stack[:, 3:4]
+        mine_at = group * local_count
+        tail = jnp.where(lanes == mine_at, low, jnp.where(lanes == mine_at + 1, high, 0.0))
+        grad_act = mid * spread
+        grad_up_lin = (grad_act * silu).astype(BF16)
+        grad_gate_lin = (grad_act * up * sigmoid * (1.0 + gate * (1.0 - sigmoid))).astype(BF16)
+        grad_lin = jnp.concatenate([grad_gate_lin, grad_up_lin], axis=1)
+        back_block[slot, :, width : 2 * width] = mxu(grad_lin, weight[...]).astype(BF16)
+        back_block[slot, :, 2 * width :] = tail.astype(BF16)
+        far, dy = place_of(step)
+        for dx in (1, 0):
+            core_copy(step, dx).start()
+            mine[far, dy, dx] = back_block[slot, piece(dx, 0), :]
+        grad_in[...] += mxu(grad_lin, rows, 0, 0)
+        grad_in_down[...] += mxu(weighted, y_rows, 0, 0)
+
+    plans = {
+        0: lambda: (
+            both_ways(gather.take_yx, 0), both_ways(gather.take_z, 1),
+            both_ways(gather.take_z, 2), both_ways(gather.take_diagonal, 0),
+            both_ways(gather.take_late, 0), both_ways(gather.take_yx, 1),
+            both_ways(gather.take_z, 3), both_ways(gather.take_late, 1),
+        ),
+        1: lambda: both_ways(gather.take_yx, 2),
+        2: lambda: (both_ways(gather.take_diagonal, 1), both_ways(gather.take_late, 2)),
+        3: lambda: both_ways(gather.take_yx, 3),
+        4: lambda: (both_ways(gather.take_diagonal, 2), both_ways(gather.take_late, 3)),
+        5: lambda: merge_diagonal(1),
+        6: lambda: both_ways(gather.take_diagonal, 3),
+        7: lambda: merge_diagonal(2),
+        9: lambda: merge_yx(1),
+        11: lambda: (merge_diagonal(3), merge_yx(2)),
+        13: lambda: merge_line(1),
+        15: lambda: (merge_diagonal(0), merge_yx(3)),
+    }
+
+    def pass_on(step, middle):
+        for at, plan in plans.items():
+            if at % 2 == middle:
+
+                @pl.when(step == at // 2)
+                def _(plan=plan):
+                    plan()
+
+    @pl.loop(0, 8)
+    def _(step):
+        pass_on(step, 0)
+
+        @pl.when(step < 7)
+        def _():
+            y_copy(step + 1).start()
+
+        far, dy = place_of(step)
+        for dx in (0, 1):
+            gather.take_core(far, dy, dx)
+        compute(step)
+
+    flush = [
+        pltpu.make_async_copy(
+            grad_in.at[pl.ds(at * ff, ff), :],
+            (grad_gate, grad_up)[at // local_count].at[at % local_count],
+            flush_sem.at[at],
+        )
+        for at in range(2 * local_count)
+    ]
+    flush.append(pltpu.make_async_copy(grad_in_down, grad_down, flush_sem.at[2 * local_count]))
+    for copy in flush:
+        copy.start()
+    merge_line(2)
+    merge_yx(0)
+    merge_line(3)
+    merge_line(0)
+    total = mine[spot.z, 0, 0].astype(F32)
+    for k in (1, 2, 3):
+        source = near_first(k, spot.z)
+        arrive(from_z.at[source], line_recv.at[source])
+        total = total + from_z[source].astype(F32)
+    reduced[...] = total
+    gather.drain()
+    for step in (6, 7):
+        for dx in (0, 1):
+            core_copy(step, dx).wait_send()
+    arrive(from_a, half_send.at[0])
+    arrive(from_b, half_send.at[1])
+    arrive(from_y, yx_send.at[0])
+    arrive(from_x, yx_send.at[1])
+    for k in (1, 2, 3):
+        arrive(from_z.at[0], line_send.at[k])
+    for copy in flush:
+        copy.wait()
+
+
+def experts(normed, grad_y, w_gate, w_up, w_down, router, chosen, kept):
+    count, width = normed.shape
+    wide = 2 * width + 128
+    total = grad_y.shape[0]
+    local_count, ff, _ = w_gate.shape
+    both = local_count * ff
+    shape, vmem, dma = jax.ShapeDtypeStruct, pltpu.VMEM, pltpu.SemaphoreType.DMA
+    line = vmem((4, count, wide), BF16)
+    return pl.pallas_call(
+        experts_kernel,
+        out_shape=(
+            shape((count, wide), F32),
+            shape(w_gate.shape, F32), shape(w_up.shape, F32), shape((both, width), F32),
+        ),
+        in_specs=[VMEM_SPEC, HBM_SPEC, HBM_SPEC, HBM_SPEC] + [VMEM_SPEC] * 4,
+        out_specs=(VMEM_SPEC,) + (HBM_SPEC,) * 3,
+        scratch_shapes=[
+            vmem((total, width), BF16),
+            vmem((2 * both, width), BF16),
+            vmem((2 * both, width), F32),
+            vmem((both, width), F32),
+            vmem((2, 4 * count, width), BF16),
+            vmem((2, 4 * count, wide), BF16),
+            vmem((4, 2, 2, count, wide), BF16),
+            vmem((4, 2, 2, count, wide), BF16),
+            vmem((4, count, width), BF16),
+            vmem((4, count, wide - width), BF16),
+            line, line, line,
+        ]
+        + dma_sems(
+            ((2 * local_count,), (2,), (2 * local_count + 1,), (2, 2), (4, 2, 2), (2,), (2,), (4, 4),
+             (4,), (4,))
+            + Gather.SEMS
+        ),
+        compiler_params=pltpu.CompilerParams(
+            collective_id=8, has_side_effects=True, vmem_limit_bytes=63 << 20
+        ),
+        name="experts",
+        cost_estimate=cost(29_000_000_000, 120),
+    )(normed, grad_y, w_gate, w_up, w_down, router, chosen, kept)
+
+
+def attend_back_kernel(
+    own_rows, w_out, queries, keys, values, attended, lin, cosine, sine, place_column,
+    place_row, open_row, log_total, k_gain, q_gain,
+    grad_lin, grad_out, grad_q_gain, grad_k_gain,
+    rows_all, head_out, grad_keys, grad_values, out_sum, head_sem, *gather_sems,
+):
+    spot = Spot()
+    count = own_rows.shape[0]
+    block = 4 * count
+    dim = queries.shape[1]
+    group = lax.axis_index("expert")
+    head_copy = pltpu.make_async_copy(
+        w_out.at[pl.ds(pl.multiple_of(group * dim, dim), dim), :], head_out, head_sem
+    )
+    head_copy.start()
+    gather = Gather(spot, own_rows, rows_all, *gather_sems)
+    spot.greet()
+    gather.start()
+    grad_keys[...] = jnp.zeros_like(grad_keys)
+    grad_values[...] = jnp.zeros_like(grad_values)
+    out_sum[...] = jnp.zeros_like(out_sum)
+    grad_q_gain[...] = jnp.zeros_like(grad_q_gain)
+    gather.local.wait()
+    head_copy.wait()
+
+    def unshape(grad, plain, gain, cos, sin):
+        grad = grad * cos + pltpu.roll(grad * sin, dim // 2, 1)
+        normed, root = head_norm(plain)
+        gain_part = jnp.sum(grad * normed, axis=0, keepdims=True)
+        grad = grad * gain
+        return root * (grad - normed * jnp.mean(grad * normed, axis=-1, keepdims=True)), gain_part
+
+    def compute(far, dy):
+        y = spot.y + dy * (1 - 2 * spot.y)
+        here = pl.ds(pl.multiple_of((far * 2 + y) * block, block), block)
+        rows = rows_all[here, :]
+        query = queries[here, :]
+        grad_att = mxu(rows, head_out[...], 1, 1).astype(BF16)
+        scores = mxu(keys[...], query, 1, 1)
+        seen = (place_column[...] <= place_row[:, here]) & (place_column[...] >= open_row[:, here])
+        probability = jnp.exp(jnp.where(seen, scores - log_total[:, here], NEG))
+        grad_prob = mxu(values[...], grad_att, 1, 1)
+        delta = jnp.sum(probability * grad_prob, axis=0, keepdims=True)
+        grad_scores = (probability * (grad_prob - delta)).astype(BF16)
+        grad_values[...] += mxu(probability.astype(BF16), grad_att)
+        grad_keys[...] += mxu(grad_scores, query)
+        grad_query = mxu(grad_scores, keys[...], 0, 0) * dim**-0.5
+        grad_query, gain_part = unshape(
+            grad_query, lin[here, :dim], q_gain[...], cosine[here, :], sine[here, :]
+        )
+        grad_q_gain[...] += gain_part
+        grad_lin[here, :dim] = grad_query.astype(BF16)
+        out_sum[...] += mxu(attended[here, :], rows, 0, 0)
+
+    def both_ways(take, distance):
+        for dz in (distance, -distance) if distance else (0,):
+            take(dz)
+
+    plans = {
+        0: lambda: (both_ways(gather.take_yx, 0), both_ways(gather.take_z, 1),
+                    both_ways(gather.take_late, 0)),
+        1: lambda: (both_ways(gather.take_diagonal, 0), both_ways(gather.take_z, 2)),
+        2: lambda: (both_ways(gather.take_yx, 1), both_ways(gather.take_z, 3),
+                    both_ways(gather.take_late, 1)),
+        3: lambda: (both_ways(gather.take_yx, 2), both_ways(gather.take_diagonal, 1),
+                    both_ways(gather.take_late, 2)),
+        4: lambda: (both_ways(gather.take_yx, 3), both_ways(gather.take_late, 3)),
+        5: lambda: both_ways(gather.take_diagonal, 2),
+        7: lambda: both_ways(gather.take_diagonal, 3),
+    }
+
+    @pl.loop(0, 8)
+    def _(step):
+        for at, plan in plans.items():
+
+            @pl.when(step == at)
+            def _(plan=plan):
+                plan()
+
+        far, dy = near_first(step // 2, spot.z), step % 2
+        for dx in (0, 1):
+            gather.take_core(far, dy, dx)
+        compute(far, dy)
+
+    grad_out[...] = out_sum[...].astype(BF16)
+    grad_key, key_part = unshape(grad_keys[...], lin[:, dim:], k_gain[...], cosine[...], sine[...])
+    grad_lin[:, dim : 2 * dim] = grad_key.astype(BF16)
+    grad_lin[:, 2 * dim :] = grad_values[...].astype(BF16)
+    grad_k_gain[...] = key_part
+    gather.drain()
+
+
+def attend_back(
+    own_rows, w_out, queries, keys, values, attended, lin, cosine, sine, place_column,
+    place_row, open_row, log_total, k_gain, q_gain,
+):
+    count, width = own_rows.shape
+    total, dim = keys.shape
+    shape, vmem = jax.ShapeDtypeStruct, pltpu.VMEM
+    return pl.pallas_call(
+        attend_back_kernel,
+        out_shape=[
+            shape((total, 3 * dim), BF16), shape((dim, width), BF16),
+            shape((1, dim), F32), shape((1, dim), F32),
+        ],
+        in_specs=[VMEM_SPEC, HBM_SPEC] + [VMEM_SPEC] * 13,
+        out_specs=[VMEM_SPEC] * 4,
+        scratch_shapes=[
+            vmem((total, width), BF16), vmem((dim, width), BF16),
+            vmem((total, dim), F32), vmem((total, dim), F32), vmem((dim, width), F32),
+        ]
+        + dma_sems((None,) + Gather.SEMS),
+        compiler_params=pltpu.CompilerParams(
+            collective_id=9, has_side_effects=True, vmem_limit_bytes=60 << 20
+        ),
+        name="attend_back",
+        cost_estimate=cost(9_000_000_000, 50),
+    )(
+        own_rows, w_out, queries, keys, values, attended, lin, cosine, sine, place_column,
+        place_row, open_row, log_total, k_gain, q_gain,
+    )
+
+
+class LineGather:
+    SEMS = ((7,), (7,), (7, 2), None, None, (7, 2), (7, 2, 2), None)
+
+    def __init__(self, spot, place, own, sems):
+        self.spot, self.place, self.own = spot, place, own
+        self.z_recv, self.y_recv, self.z_send, self.y_send = sems[:4]
+        self.late_y_recv, self.late_z_recv, self.late_z_send, self.late_y_send = sems[4:]
+
+    def source(self, dz, dy, part):
+        return self.own(part) if dz == 0 and dy == 0 else self.place(dz, dy, part)
+
+    def along_z(self, dz, dy, part):
+        for side, step in ((0, 1), (1, -1)):
+            if dz * step <= 0:
+
+                @pl.when(self.spot.has(step))
+                def _(side=side, step=step):
+                    if part:
+                        send = self.late_z_send.at[dz + 3, side, dy]
+                        recv = self.late_z_recv.at[dz + 3 - step, dy]
+                    else:
+                        send = self.z_send.at[dz + 3, side]
+                        recv = self.z_recv.at[dz + 3 - step]
+                    push(
+                        self.source(dz, dy, part), self.place(dz, dy, part), send, recv,
+                        self.spot.device(step),
+                    )
+
+    def along_y(self, dz):
+        push(
+            self.source(dz, 0, 0), self.place(dz, 0, 0), self.y_send, self.y_recv.at[dz + 3],
+            self.spot.device(0, 1),
+        )
+
+    def start(self):
+        self.along_z(0, 0, 0)
+        push(
+            self.own(1), self.place(0, 0, 1), self.late_y_send, self.late_y_recv,
+            self.spot.device(0, 1),
+        )
+        self.along_y(0)
+        self.along_z(0, 0, 1)
+
+    def take_z(self, distance):
+        for dz in (distance, -distance):
+
+            def action(dz=dz):
+                arrive(self.place(dz, 0, 0), self.z_recv.at[dz + 3])
+                self.along_z(dz, 0, 0)
+                self.along_y(dz)
+
+            when_has(self.spot, dz, action)
+
+    def take_late_y(self):
+        arrive(self.place(0, 1, 1), self.late_y_recv)
+        self.along_z(0, 1, 1)
+
+    def take_late_z(self, distance):
+        for dz in (distance, -distance):
+
+            def action(dz=dz):
+                for dy in (0, 1):
+                    arrive(self.place(dz, dy, 1), self.late_z_recv.at[dz + 3, dy])
+                    self.along_z(dz, dy, 1)
+
+            when_has(self.spot, dz, action)
+
+    def drain(self, four):
+        for dz in (0, 1, -1, 2, -2, 3, -3):
+
+            def action(dz=dz):
+                arrive(self.place(dz, 1, 0), self.y_recv.at[dz + 3])
+                for side, step in ((0, 1), (1, -1)):
+                    if dz * step <= 0:
+
+                        @pl.when(self.spot.has(step))
+                        def _(side=side):
+                            arrive(self.place(dz, 0, 0), self.z_send.at[dz + 3, side])
+                            for dy in (0, 1):
+                                arrive(
+                                    self.place(dz, dy, 1), self.late_z_send.at[dz + 3, side, dy]
+                                )
+
+            when_has(self.spot, dz, action)
+        arrive(four, self.y_send)
+        arrive(self.place(0, 0, 1), self.late_y_send)
+
+
+def close_kernel(
+    normed, grad_lin, w_query, w_key, w_value, head_out,
+    reduced, kv_all, query_all, out_all,
+    weight, rows, sums, query_own, kv_part, back, mine, other, from_x_diagonal, from_y, from_x,
+    from_z, kv_mine, kv_y, kv_z, kv_own, row_sem, weight_sem, local_sem,
+    core_send, core_recv, many_send, recv, line_send, line_recv,
+    kv_send, kv_y_recv, kv_line_send, kv_line_recv, *gather_sems,
+):
+    spot = Spot()
+    total, width = normed.shape
+    count, wide = reduced.shape
+    block = 4 * count
+    dim = w_key.shape[1]
+    group = lax.axis_index("expert")
+    to_y, to_x, to_c = spot.device(0, 1), spot.device(0, 0, 1), spot.device(0, 0, 0, 1)
+    cut = 1664
+
+    def parts(part):
+        return pl.ds(cut, total - cut) if part else pl.ds(0, cut)
+
+    def lane_block(dz, dy):
+        return pl.ds(pl.multiple_of(spot.device(dz, dy)[0] * dim, dim), dim)
+
+    weights = [
+        pltpu.make_async_copy(
+            w_query.at[:, pl.ds(pl.multiple_of(group * dim, dim), dim)],
+            weight.at[:, pl.ds(0, dim)], weight_sem.at[0],
+        ),
+        pltpu.make_async_copy(w_key, weight.at[:, pl.ds(dim, dim)], weight_sem.at[1]),
+        pltpu.make_async_copy(w_value, weight.at[:, pl.ds(2 * dim, dim)], weight_sem.at[2]),
+    ]
+
+    def row_copy(step):
+        return pltpu.make_async_copy(
+            normed.at[pl.ds(pl.multiple_of(step * block, block), block), :],
+            rows.at[step % 2], row_sem.at[step % 2],
+        )
+
+    for copy in weights:
+        copy.start()
+    row_copy(0).start()
+    outs = LineGather(
+        spot,
+        lambda dz, dy, part: out_all.at[lane_block(dz, dy), parts(part)],
+        lambda part: head_out.at[:, parts(part)],
+        gather_sems[:8],
+    )
+    queries = LineGather(
+        spot,
+        lambda dz, dy, part: query_all.at[parts(part), lane_block(dz, dy)],
+        lambda part: query_own.at[parts(part), :],
+        gather_sems[8:16],
+    )
+    kv_rows = total // 8
+
+    def kv_span(start, part):
+        return pl.ds(pl.multiple_of(start + part * (kv_rows // 2), kv_rows // 2), kv_rows // 2)
+
+    kvs = LineGather(
+        spot,
+        lambda dz, dy, part: kv_all.at[kv_span(spot.device(dz, dy)[0] * kv_rows, part), :],
+        lambda part: kv_own.at[kv_span(0, part), :],
+        gather_sems[16:],
+    )
+    out_copy = pltpu.make_async_copy(head_out, out_all.at[lane_block(0, 0), :], local_sem.at[0])
+    out_copy.start()
+    spot.greet(line=True)
+    outs.start()
+
+    sums[...] = jnp.zeros_like(sums)
+
+    @pl.loop(0, total // block)
+    def _(step):
+        @pl.when(step < total // block - 1)
+        def _():
+            row_copy(step + 1).start()
+
+        row_copy(step).wait()
+        here = pl.ds(pl.multiple_of(step * block, block), block)
+        sums[...] += mxu(grad_lin[here, :], rows[step % 2], 0, 0)
+
+    query_own[...] = sums[:dim, :].T.astype(BF16)
+    kv_part[...] = sums[dim:, :].T.astype(BF16)
+    query_copy = pltpu.make_async_copy(query_own, query_all.at[:, lane_block(0, 0)], local_sem.at[1])
+    query_copy.start()
+
+    def group_rows(far, dy):
+        y = spot.y + dy * (1 - 2 * spot.y)
+        return pl.ds(pl.multiple_of((far * 2 + y) * block, block), block)
+
+    for k in (3, 2, 1, 0):
+        far = near_first(k, spot.z)
+        push(
+            kv_part.at[group_rows(far, 1), :], kv_y.at[far], kv_send, kv_y_recv.at[far], to_y
+        )
+    for copy in weights:
+        copy.wait()
+
+    def piece(dx, dc):
+        _, part = spot.device(0, 0, dx, dc)
+        return pl.ds(pl.multiple_of(part * count, count), count)
+
+    def core_copy(step, far, dy, dx):
+        return pltpu.make_async_remote_copy(
+            src_ref=back.at[step % 2, piece(dx, 1), :],
+            dst_ref=other.at[far, dy, dx],
+            send_sem=core_send.at[step % 2, dx],
+            recv_sem=core_recv.at[far, dy, dx],
+            device_id=to_c,
+            device_id_type=MESH,
+        )
+
+    def produce(k):
+        far = near_first(k, spot.z)
+        for dy in (1, 0):
+            step = 2 * (3 - k) + 1 - dy
+            if step >= 2:
+                for dx in (1, 0):
+                    core_copy(step, far, dy, dx).wait_send()
+            here = group_rows(far, dy)
+            back[step % 2] = mxu(grad_lin[here, :], weight[...], 1, 1).astype(BF16)
+            for dx in (1, 0):
+                core_copy(step, far, dy, dx).start()
+                mine[far, dy, dx] = back[step % 2, piece(dx, 0), :]
+
+    def merge(far, dy, dx, *terms):
+        arrive(other.at[far, dy, dx], core_recv.at[far, dy, dx])
+        add_into(mine.at[far, dy, dx], 16, other.at[far, dy, dx], *terms)
+        return mine.at[far, dy, dx]
+
+    def merge_diagonal(k):
+        far = near_first(k, spot.z)
+        push(
+            merge(far, 1, 1), from_x_diagonal.at[far], many_send.at[0], recv.at[0, far], to_x
+        )
+
+    def merge_yx(k):
+        far = near_first(k, spot.z)
+        push(merge(far, 0, 1), from_x.at[far], many_send.at[1], recv.at[1, far], to_x)
+        arrive(from_x_diagonal.at[far], recv.at[0, far])
+        push(
+            merge(far, 1, 0, from_x_diagonal.at[far]), from_y.at[far], many_send.at[2],
+            recv.at[2, far], to_y,
+        )
+
+    def far_device(far):
+        return (far * 2 + spot.y, spot.x * 2 + spot.c)
+
+    def merge_kv(k):
+        far = near_first(k, spot.z)
+        kv_mine[far] = kv_part[group_rows(far, 0), :]
+        arrive(kv_y.at[far], kv_y_recv.at[far])
+        add_into(kv_mine.at[far], 64, kv_y.at[far])
+        if k > 0:
+            push(
+                kv_mine.at[far], kv_z.at[spot.z], kv_line_send.at[k], kv_line_recv.at[spot.z],
+                far_device(far),
+            )
+
+    def merge_line(k):
+        far = near_first(k, spot.z)
+        arrive(from_y.at[far], recv.at[2, far])
+        arrive(from_x.at[far], recv.at[1, far])
+        into = merge(far, 0, 0, from_y.at[far], from_x.at[far])
+        if k > 0:
+            push(
+                into, from_z.at[spot.z], line_send.at[k], line_recv.at[spot.z], far_device(far)
+            )
+
+    def sum_kv():
+        sums_kv = kv_mine[spot.z].astype(F32)
+        for k in (1, 2, 3):
+            source = near_first(k, spot.z)
+            arrive(kv_z.at[source], kv_line_recv.at[source])
+            sums_kv = sums_kv + kv_z[source].astype(F32)
+        kv_own[...] = sums_kv.astype(BF16)
+
+    produce(3)
+    produce(2)
+    outs.take_z(1)
+    for k in (3, 2, 1, 0):
+        merge_kv(k)
+    queries.start()
+    merge_diagonal(3)
+    produce(1)
+    merge_diagonal(2)
+    outs.take_late_y()
+    produce(0)
+    merge_diagonal(1)
+    sum_kv()
+    kvs.start()
+    kv_copy = pltpu.make_async_copy(
+        kv_own, kv_all.at[pl.ds(pl.multiple_of(group * kv_rows, kv_rows), kv_rows), :],
+        local_sem.at[2],
+    )
+    kv_copy.start()
+    outs.take_z(2)
+    queries.take_z(1)
+    merge_diagonal(0)
+    merge_yx(3)
+    kvs.take_z(1)
+    kvs.take_late_y()
+    queries.take_late_y()
+    outs.take_late_z(1)
+    merge_yx(2)
+    outs.take_z(3)
+    queries.take_z(2)
+    kvs.take_z(2)
+    kvs.take_late_z(1)
+    merge_line(3)
+    merge_yx(1)
+    queries.take_late_z(1)
+    outs.take_late_z(2)
+    kvs.take_z(3)
+    kvs.take_late_z(2)
+    merge_line(2)
+    merge_yx(0)
+    queries.take_z(3)
+    queries.take_late_z(2)
+    outs.take_late_z(3)
+    merge_line(1)
+    merge_line(0)
+    kvs.take_late_z(3)
+    queries.take_late_z(3)
+    total_rows = mine[spot.z, 0, 0].astype(F32)
+    for k in (1, 2, 3):
+        source = near_first(k, spot.z)
+        arrive(from_z.at[source], line_recv.at[source])
+        total_rows = total_rows + from_z[source].astype(F32)
+    reduced[...] = total_rows
+
+    kvs.drain(kv_all.at[pl.ds(0, 2 * kv_rows), :])
+    kv_copy.wait()
+    outs.drain(out_all.at[pl.ds(0, 4 * dim), parts(0)])
+    queries.drain(query_all.at[parts(0), pl.ds(0, 4 * dim)])
+    out_copy.wait()
+    query_copy.wait()
+    for step in (6, 7):
+        for dx in (0, 1):
+            core_copy(step, near_first(0, spot.z), 0, dx).wait_send()
+    arrive(from_x_diagonal, many_send.at[0])
+    arrive(from_x, many_send.at[1])
+    arrive(from_y, many_send.at[2])
+    arrive(kv_y, kv_send)
+    for k in (1, 2, 3):
+        arrive(from_z.at[0], line_send.at[k])
+        arrive(kv_z.at[0], kv_line_send.at[k])
+
+
+def close(normed, grad_lin, w_query, w_key, w_value, head_out):
+    total, width = normed.shape
+    count, wide, dim = total // 32, width, w_key.shape[1]
+    shape, vmem = jax.ShapeDtypeStruct, pltpu.VMEM
+    line, kv_line = vmem((4, count, wide), BF16), vmem((4, 4 * count, 2 * dim), BF16)
+    return pl.pallas_call(
+        close_kernel,
+        out_shape=(
+            shape((count, wide), F32), shape((total, 2 * dim), BF16),
+            shape((total, 8 * dim), BF16), shape((8 * dim, width), BF16),
+        ),
+        in_specs=[HBM_SPEC, VMEM_SPEC, HBM_SPEC, HBM_SPEC, HBM_SPEC, VMEM_SPEC],
+        out_specs=(VMEM_SPEC, HBM_SPEC, HBM_SPEC, HBM_SPEC),
+        scratch_shapes=[
+            vmem((width, 3 * dim), BF16), vmem((2, 4 * count, width), BF16),
+            vmem((3 * dim, width), F32), vmem((width, dim), BF16), vmem((width, 2 * dim), BF16),
+            vmem((2, 4 * count, wide), BF16),
+            vmem((4, 2, 2, count, wide), BF16), vmem((4, 2, 2, count, wide), BF16),
+            line, line, line, line, kv_line, kv_line, kv_line,
+            vmem((4 * count, 2 * dim), BF16),
+        ]
+        + dma_sems(
+            ((2,), (3,), (3,), (2, 2), (4, 2, 2), (3,), (3, 4), (4,), (4,),
+             None, (4,), (4,), (4,)) + LineGather.SEMS * 3
+        ),
+        compiler_params=pltpu.CompilerParams(
+            collective_id=10, has_side_effects=True, vmem_limit_bytes=60 << 20
+        ),
+        name="close",
+        cost_estimate=cost(7_000_000_000, 110),
+    )(normed, grad_lin, w_query, w_key, w_value, head_out)
+
+
+def cosine_sine(angles):
+    lanes = lax.broadcasted_iota(jnp.int32, angles.shape, 1)
+    turns = jnp.floor(angles * (2.0 / math.pi) + 0.5)
+    rest = angles - turns * 1.5703125
+    rest = rest - turns * 4.837512969970703125e-4
+    rest = rest - turns * 7.54978995489188216e-8
+    square = rest * rest
+    sine = square * (8.3321608736e-3 + square * -1.9515295891e-4) - 1.6666654611e-1
+    sine = rest + rest * square * sine
+    cosine = -1.388731625493765e-3 + square * 2.443315711809948e-5
+    cosine = 1.0 - 0.5 * square + square * square * (4.166664568298827e-2 + square * cosine)
+    turns = jnp.where(lanes < angles.shape[1] // 2, turns, turns - 1.0)
+    turns = turns - 4.0 * jnp.floor(turns * 0.25)
+    odd = (turns == 1.0) | (turns == 3.0)
+    value = jnp.where(odd, sine, cosine)
+    return jnp.where((turns == 1.0) | (turns == 2.0), -value, value)
+
+
+def front_kernel(
+    hidden, cotangent, tag, lengths, gain, w_query, w_key, w_value, q_gain, k_gain, inverse,
+    w_out, second_gain,
+    normed_all, queries, keys, values, lin_out, cosine, sine, attended, log_total,
+    place_row, open_row, place_column, residual, normed, chosen, kept, grad_y_all,
+    rows_all, weight, out_weight, staged, tags, ranks, picks, att_rows,
+    partial_sum, from_core, to_x_sum, from_x,
+    weight_sem, stage_sem, tag_z, tag_y, tag_z_send, tag_y_send, tag_local,
+    send_sem, recv_sem, own_sem, tensor_sems, *gather_sems,
+):
+    spot = Spot()
+    group, part = lax.axis_index("expert"), lax.axis_index("tensor")
+    count, width = residual.shape
+    block = 4 * count
+    total = 32 * count
+    dim = w_key.shape[1]
+    own = pl.ds(pl.multiple_of(part * count, count), count)
+
+    weights = [
+        pltpu.make_async_copy(
+            w_query.at[:, pl.ds(pl.multiple_of(group * dim, dim), dim)],
+            weight.at[:, pl.ds(0, dim)], weight_sem.at[0],
+        ),
+        pltpu.make_async_copy(w_key, weight.at[:, pl.ds(dim, dim)], weight_sem.at[1]),
+        pltpu.make_async_copy(w_value, weight.at[:, pl.ds(2 * dim, dim)], weight_sem.at[2]),
+        pltpu.make_async_copy(w_out, out_weight, weight_sem.at[3]),
+    ]
+    for copy in weights:
+        copy.start()
+    barrier = pltpu.get_barrier_semaphore()
+
+    @pl.loop(1, 8)
+    def _(step):
+        pl.semaphore_signal(
+            barrier, inc=1, device_id=((group + step) % 8, part), device_id_type=MESH
+        )
+
+    for device in (spot.device(0, 0, 1), spot.device(0, 0, 0, 1)):
+        pl.semaphore_signal(barrier, inc=1, device_id=device, device_id_type=MESH)
+
+    def tag_place(dz, dy):
+        return tags.at[spot.device(dz, dy)[0]]
+
+    tag_copy = pltpu.make_async_copy(tag, tag_place(0, 0), tag_local)
+    tag_copy.start()
+    pl.semaphore_wait(barrier, 9)
+
+    def spread_tag(dz):
+        here = tag_place(dz, 0)
+        source = tag if dz == 0 else here
+        for side, step in ((0, 1), (1, -1)):
+            if dz * step <= 0:
+
+                @pl.when(spot.has(step))
+                def _(side=side, step=step):
+                    push(
+                        source, here, tag_z_send.at[dz + 3, side], tag_z.at[dz + 3 - step],
+                        spot.device(step),
+                    )
+
+        push(source, here, tag_y_send.at[dz + 3], tag_y.at[dz + 3], spot.device(0, 1))
+
+    def take_tag(dz):
+        def action():
+            arrive(tag_place(dz, 0), tag_z.at[dz + 3])
+            spread_tag(dz)
+
+        when_has(spot, dz, action)
+
+    def take_tag_y(dz):
+        when_has(spot, dz, lambda: arrive(tag_place(dz, 1), tag_y.at[dz + 3]))
+
+    spread_tag(0)
+    gather = Gather(spot, hidden.at[own, :], rows_all, *gather_sems[:7], full=hidden)
+    gather.start()
+    late = Gather(spot, cotangent.at[own, :], grad_y_all, *gather_sems[7:], full=cotangent)
+    tag_copy.wait()
+    gather.local.wait()
+    for copy in weights:
+        copy.wait()
+
+    def group_of(step):
+        far, dy = near_first(step // 2, spot.z), step % 2
+        return far, dy, far * 2 + spot.y + dy * (1 - 2 * spot.y)
+
+    def stage_copy(step):
+        _, _, index = group_of(step)
+        return pltpu.make_async_copy(
+            staged.at[step % 2],
+            normed_all.at[pl.ds(pl.multiple_of(index * block, block), block), :],
+            stage_sem.at[step % 2],
+        )
+
+    experts_count = chosen.shape[0]
+    names = lax.broadcasted_iota(jnp.int32, (experts_count, block), 0)
+    lanes = lax.broadcasted_iota(jnp.int32, (block, dim), 1)
+
+    def project_group(step):
+        _, _, index = group_of(step)
+        here = pl.ds(pl.multiple_of(index * block, block), block)
+        entries = tags[index]
+        place = entries[0:1, :]
+        segment, opening, bound = jnp.zeros_like(place), jnp.zeros_like(place), 0
+        for at in range(lengths.shape[0]):
+            bound = bound + lengths[at]
+            segment = segment + jnp.where(place >= bound, 1, 0)
+            opening = jnp.where(place >= bound, bound, opening)
+        place_row[:, here] = place.astype(F32)
+        open_row[:, here] = opening.astype(F32)
+        lines = jnp.concatenate(
+            [place.astype(F32), (place - opening).astype(F32), entries[1:2, :].astype(F32),
+             jnp.zeros((5, block), F32)],
+            axis=0,
+        ).T
+        place_column[here, :] = lines[:, 0:1]
+        ranks[here, :] = lines[:, 2:3]
+        named = jnp.zeros((experts_count, block), F32)
+        for at in range(2, 2 + TOPK):
+            named = jnp.where(entries[at : at + 1, :] == names, 1.0, named)
+        chosen[:, here] = named
+        valid = segment < lengths.shape[0]
+        picks[:, here] = jnp.where(valid, named, 0.0).astype(BF16)
+        table = cosine_sine(lines[:, 1:2] * inverse[...])
+        turned_table = pltpu.roll(table, dim // 2, 1)
+        cos = jnp.where(lanes < dim // 2, table, turned_table)
+        sin = jnp.where(lanes < dim // 2, -turned_table, table)
+        cosine[here, :] = cos
+        sine[here, :] = sin
+        rows = rows_all[here, :].astype(F32)
+        root = lax.rsqrt(jnp.mean(rows * rows, axis=-1, keepdims=True) + EPS)
+
+        @pl.when(step >= 2)
+        def _():
+            stage_copy(step - 2).wait()
+
+        staged[step % 2] = (rows * root * gain[...]).astype(BF16)
+        stage_copy(step).start()
+        lin = mxu(staged[step % 2], weight[...])
+        lin_out[here, :] = lin[:, : 2 * dim]
+        values[here, :] = lin[:, 2 * dim :].astype(BF16)
+        for at, head_gain, scale, out in (
+            (0, q_gain, dim**-0.5, queries), (dim, k_gain, 1.0, keys),
+        ):
+            plain, _ = head_norm(lin[:, at : at + dim])
+            plain = plain * head_gain[...]
+            out[here, :] = ((plain * cos + pltpu.roll(plain, dim // 2, 1) * sin) * scale).astype(
+                BF16
+            )
+
+    def both_ways(take, distance):
+        for dz in (distance, -distance) if distance else (0,):
+            take(dz)
+
+    def run(plans, step):
+        for at, plan in plans.items():
+
+            @pl.when(step == at)
+            def _(plan=plan):
+                plan()
+
+    plans = {
+        0: lambda: (both_ways(gather.take_yx, 0), both_ways(take_tag, 1),
+                    both_ways(gather.take_z, 1)),
+        1: lambda: (both_ways(take_tag_y, 0), both_ways(gather.take_diagonal, 0),
+                    both_ways(take_tag, 2), both_ways(gather.take_z, 2),
+                    both_ways(gather.take_late, 0)),
+        2: lambda: (both_ways(gather.take_yx, 1), both_ways(take_tag, 3),
+                    both_ways(gather.take_z, 3), both_ways(gather.take_late, 1)),
+        3: lambda: (both_ways(take_tag_y, 1), both_ways(gather.take_yx, 2),
+                    both_ways(gather.take_diagonal, 1), both_ways(gather.take_late, 2)),
+        4: lambda: (both_ways(gather.take_yx, 3), late.start()),
+        5: lambda: (both_ways(take_tag_y, 2), both_ways(gather.take_diagonal, 2),
+                    both_ways(gather.take_late, 3)),
+        7: lambda: (both_ways(take_tag_y, 3), both_ways(gather.take_diagonal, 3)),
+    }
+
+    @pl.loop(0, 8)
+    def _(step):
+        run(plans, step)
+        far, dy, _ = group_of(step)
+
+        @pl.when(step > 0)
+        def _():
+            for dx in (0, 1):
+                gather.take_core(far, dy, dx)
+
+        project_group(step)
+
+    mine = att_rows.at[:, pl.ds(pl.multiple_of(group * dim, dim), dim)]
+
+    def block_copy(step):
+        target = (group + step) % 8
+        return pltpu.make_async_remote_copy(
+            src_ref=attended.at[pl.ds(pl.multiple_of(target * block, block), block), :],
+            dst_ref=mine,
+            send_sem=send_sem.at[step],
+            recv_sem=recv_sem.at[step],
+            device_id=(target, part),
+            device_id_type=MESH,
+        )
+
+    def attend_block(step):
+        here = pl.ds(pl.multiple_of((group + step) % 8 * block, block), block)
+        scores = mxu(keys[...], queries[here, :], 1, 1)
+        seen = (place_column[...] <= place_row[:, here]) & (place_column[...] >= open_row[:, here])
+        scores = jnp.where(seen, scores, NEG)
+        highest = jnp.max(scores, axis=0, keepdims=True)
+        exps = jnp.exp(scores - highest)
+        totals = jnp.sum(exps, axis=0, keepdims=True)
+        probability = (exps * (1.0 / totals)).astype(BF16)
+        attended[here, :] = mxu(values[...], probability, 0, 0).T.astype(BF16)
+        log_total[:, here] = highest + jnp.log(totals)
+
+    late_plans = {
+        1: lambda: (both_ways(late.take_yx, 0), both_ways(late.take_z, 1)),
+        3: lambda: (both_ways(late.take_z, 2), both_ways(late.take_diagonal, 0),
+                    both_ways(late.take_late, 0)),
+        5: lambda: (both_ways(late.take_yx, 1), both_ways(late.take_z, 3)),
+        7: lambda: (both_ways(late.take_late, 1), both_ways(late.take_yx, 2),
+                    both_ways(late.take_diagonal, 1)),
+    }
+
+    @pl.loop(1, 8)
+    def _(step):
+        run(late_plans, step)
+        attend_block(step)
+        block_copy(step).start()
+
+    attend_block(0)
+    own_copy = pltpu.make_async_copy(
+        attended.at[pl.ds(pl.multiple_of(group * block, block), block), :], mine, own_sem
+    )
+    own_copy.start()
+    both_ways(late.take_yx, 3)
+    both_ways(late.take_late, 2)
+
+    kept[...] = jnp.zeros_like(kept)
+
+    @pl.loop(0, total // block)
+    def _(step):
+        here = pl.ds(pl.multiple_of(step * block, block), block)
+        for at in range(0, total // block):
+            columns = pl.ds(at * block, block)
+            lower = jnp.where(
+                ranks[here, :] < tags[at, 1:2, :].astype(F32), 1.0, 0.0
+            ).astype(BF16)
+            kept[:, columns] += mxu(picks[:, here], lower)
+
+    kept[...] = jnp.where((picks[...].astype(F32) > 0.0) & (kept[...] < CAP), 1.0, 0.0)
+
+    both_ways(late.take_diagonal, 2)
+    both_ways(late.take_late, 3)
+
+    @pl.loop(1, 8)
+    def _(step):
+        block_copy(step).wait_send()
+        source = (group + 8 - step) % 8
+        there = att_rows.at[:, pl.ds(pl.multiple_of(source * dim, dim), dim)]
+        arrive(there, recv_sem.at[step])
+
+    own_copy.wait()
+
+    @pl.loop(0, width // 256)
+    def _(step):
+        columns = pl.ds(pl.multiple_of(step * 256, 256), 256)
+        partial_sum[:, columns] = mxu(att_rows[...], out_weight[:, columns]).astype(BF16)
+
+    def rows_of(dx, dc):
+        _, there = spot.device(0, 0, dx, dc)
+        return partial_sum.at[pl.ds(pl.multiple_of(there * count, count), count), :]
+
+    to_x, to_c = spot.device(0, 0, 1), spot.device(0, 0, 0, 1)
+    for dx in (1, 0):
+        push(rows_of(dx, 1), from_core.at[dx], tensor_sems.at[dx], tensor_sems.at[2 + dx], to_c)
+    arrive(from_core.at[1], tensor_sems.at[3])
+    to_x_sum[...] = (rows_of(1, 0)[...].astype(F32) + from_core[1].astype(F32)).astype(BF16)
+    push(to_x_sum, from_x, tensor_sems.at[4], tensor_sems.at[5], to_x)
+    both_ways(late.take_diagonal, 3)
+    arrive(from_core.at[0], tensor_sems.at[2])
+    arrive(from_x, tensor_sems.at[5])
+    branch = rows_of(0, 0)[...].astype(F32) + from_core[0].astype(F32) + from_x[...].astype(F32)
+    sum_rows = hidden[own, :].astype(F32) + branch
+    residual[...] = sum_rows
+    root = lax.rsqrt(jnp.mean(sum_rows * sum_rows, axis=-1, keepdims=True) + EPS)
+    normed[...] = (sum_rows * root * second_gain[...]).astype(BF16)
+    for at, view in ((0, from_core.at[0]), (1, from_core.at[1]), (4, from_x)):
+        arrive(view, tensor_sems.at[at])
+    for step in (6, 7):
+        stage_copy(step).wait()
+    gather.drain()
+    late.local.wait()
+    for far in range(4):
+        for dx in (0, 1):
+            late.take_core(far, 1, dx)
+
+            @pl.when(spot.z != far)
+            def _(far=far, dx=dx):
+                late.take_core(far, 0, dx)
+
+    late.drain()
+    for dz in range(-3, 4):
+
+        def action(dz=dz):
+            arrive(tag_place(dz, 0), tag_y_send.at[dz + 3])
+            for side, step in ((0, 1), (1, -1)):
+                if dz * step <= 0:
+
+                    @pl.when(spot.has(step))
+                    def _(side=side):
+                        arrive(tag_place(dz, 0), tag_z_send.at[dz + 3, side])
+
+        when_has(spot, dz, action)
+
+
+def front(
+    hidden, cotangent, tag, lengths, gain, w_query, w_key, w_value, q_gain, k_gain, inverse,
+    w_out, second_gain, expert_count,
+):
+    block, width = hidden.shape
+    total, count, dim = 8 * block, block // 4, w_key.shape[1]
+    shape, vmem = jax.ShapeDtypeStruct, pltpu.VMEM
+    smem = pl.BlockSpec(memory_space=pltpu.SMEM)
+    small = (total, dim)
+    return pl.pallas_call(
+        front_kernel,
+        out_shape=(
+            shape((total, width), BF16), shape(small, BF16), shape(small, BF16),
+            shape(small, BF16), shape((total, 2 * dim), F32), shape(small, F32),
+            shape(small, F32), shape(small, BF16), shape((1, total), F32),
+            shape((1, total), F32), shape((1, total), F32), shape((total, 1), F32),
+            shape((count, width), F32), shape((count, width), BF16),
+            shape((expert_count, total), F32), shape((expert_count, total), F32),
+            shape((total, width), BF16),
+        ),
+        in_specs=[VMEM_SPEC, VMEM_SPEC, VMEM_SPEC, smem, VMEM_SPEC, HBM_SPEC, HBM_SPEC, HBM_SPEC,
+                  VMEM_SPEC, VMEM_SPEC, VMEM_SPEC, HBM_SPEC, VMEM_SPEC],
+        out_specs=(HBM_SPEC,) + (VMEM_SPEC,) * 15 + (HBM_SPEC,),
+        scratch_shapes=[
+            vmem((total, width), BF16), vmem((width, 3 * dim), BF16), vmem((8 * dim, width), BF16),
+            vmem((2, block, width), BF16), vmem((8, 16, block), jnp.int32), vmem((total, 1), F32),
+            vmem((expert_count, total), BF16), vmem((block, 8 * dim), BF16),
+            vmem((block, width), BF16), vmem((2, count, width), BF16), vmem((count, width), BF16),
+            vmem((count, width), BF16),
+        ]
+        + dma_sems(
+            ((4,), (2,), (7,), (7,), (7, 2), (7,), None, (8,), (8,), None, (6,)) + Gather.SEMS * 2
+        ),
+        compiler_params=pltpu.CompilerParams(
+            collective_id=1, has_side_effects=True, vmem_limit_bytes=62 << 20
+        ),
+        name="front",
+        cost_estimate=cost(8_000_000_000, 90),
+    )(
+        hidden, cotangent, tag, lengths, gain, w_query, w_key, w_value, q_gain, k_gain, inverse,
+        w_out, second_gain,
+    )
+
+
+def swap(value, bits):
+    return lax.ppermute(
+        value, ("expert", "tensor"), [(device, device ^ bits) for device in range(32)]
+    )
+
+
+def tensor_rows(rows):
+    by_core = swap(rows, 1)
+    by_x = swap(rows, 2)
+    by_both = swap(by_x, 1)
+
+    return in_order(rows, by_core, by_x, by_both)
+
+
+def in_order(rows, by_core, by_x, by_both):
+    part = lax.axis_index("tensor")
+
+    def ordered(first, second, bit):
+        swapped = part // bit % 2 == 1
+        return jnp.concatenate(
+            [jnp.where(swapped, second, first), jnp.where(swapped, first, second)], axis=0
+        )
+
+    return ordered(ordered(rows, by_core, 1), ordered(by_x, by_both, 1), 2)
+
+
+def head_device(
+    hidden_in,
+    cotangent,
+    layout,
+    seq_lengths,
+    expert_ids,
+    drop_rank,
+    norm1_gain,
+    w_query,
+    key_weight,
+    value_weight,
+    query_gain,
+    key_gain,
+    w_out,
+    norm2_gain,
+    w_router,
+    w_gate,
+    w_up,
+    w_down,
+):
+    f32, bf16 = jnp.float32, jnp.bfloat16
+    tok_rows, model_width = hidden_in.shape
+    head_dim = query_gain.shape[0]
+    expert_count = w_router.shape[1]
+    local_count, _, ff_local = w_gate.shape
+    groups = lax.axis_size("expert")
+    tensor_size = lax.axis_size("tensor")
+    total_rows = groups * tok_rows
+    own_rows = tok_rows // tensor_size
+    group = lax.axis_index("expert")
+    part = lax.axis_index("tensor")
+
+    def own(rows):
+        return lax.dynamic_slice_in_dim(rows, part * own_rows, own_rows, 0)
+
+    tag = jnp.concatenate(
+        [layout[None], drop_rank[None], expert_ids.T, jnp.zeros((6, tok_rows), jnp.int32)], axis=0
+    )
+    half_dim = head_dim // 2
+    inverse = THETA ** (-(jnp.arange(half_dim, dtype=f32) * 2.0) / head_dim)
+    q_gain, k_gain = query_gain[None], key_gain[None]
+    (
+        normed1, queries, keys, values, lin, cosine, sine, attended, log_total,
+        place_row, open_row, place_column, residual, normed2, chosen, kept, grad_y_all,
+    ) = front(
+        hidden_in, cotangent, tag, seq_lengths, norm1_gain[None], w_query, key_weight,
+        value_weight, q_gain, k_gain, jnp.concatenate([inverse, inverse])[None], w_out,
+        norm2_gain[None], expert_count,
+    )
+    turn = lambda v: jnp.transpose(v, (0, 2, 1))
+    back, grad_gate, grad_up, grad_down = experts(
+        normed2, grad_y_all, turn(w_gate), turn(w_up), w_down.reshape(-1, model_width),
+        w_router.T, chosen, kept,
+    )
+    out_hidden = tensor_rows((residual + back[:, :model_width]).astype(bf16))
+    back = back[:, model_width:]
+
+    start = group * tok_rows + part * own_rows
+    chosen_own = lax.dynamic_slice_in_dim(chosen, start, own_rows, 1).T
+    logits = jnp.dot(normed2, w_router, preferred_element_type=f32)
+    soft_own = jax.nn.softmax(jnp.where(chosen_own > 0.0, logits, -jnp.inf), axis=1)
+    grad_soft = back[:, model_width : model_width + expert_count]
+    grad_logits = (
+        soft_own * (grad_soft - jnp.sum(soft_own * grad_soft, axis=1, keepdims=True))
+    ).astype(bf16)
+    grad_router = jnp.einsum("td,te->de", normed2, grad_logits, preferred_element_type=f32)
+    grad_normed2 = back[:, :model_width] + jnp.einsum(
+        "te,de->td", grad_logits, w_router, preferred_element_type=f32
+    )
+    norm2_pull = jax.vjp(norm_rows, residual, norm2_gain)[1]
+    grad_resid_norm, grad_norm2 = norm2_pull(grad_normed2)
+    grad_residual = own(cotangent).astype(f32) + grad_resid_norm
+    small = jnp.concatenate([grad_router.T, grad_norm2[None]], axis=0)
+    small = small + swap(small, 16)
+
+    grad_lin, grad_out, grad_qgain, grad_kgain = attend_back(
+        grad_residual.astype(bf16), w_out, queries, keys, values, attended, lin, cosine, sine,
+        place_column, place_row, open_row, log_total, k_gain, q_gain,
+    )
+    grad_lin, small = lax.optimization_barrier((grad_lin, small))
+    small_moved = swap(small, 8)
+    gains = jnp.concatenate(
+        [grad_qgain, grad_kgain, jnp.zeros((1, model_width - 2 * head_dim), f32)], axis=1
+    )
+    reduced, grad_kv, grad_query, grad_out = close(
+        normed1, grad_lin, w_query, key_weight, value_weight, grad_out
+    )
+    reduced, out_hidden, small_moved = lax.optimization_barrier(
+        (reduced, out_hidden, small_moved)
+    )
+    small = small + small_moved
+    norm1_pull = jax.vjp(norm_rows, own(hidden_in).astype(f32), norm1_gain)[1]
+    grad_hidden_norm, grad_norm1 = norm1_pull(reduced)
+    late_sums = jnp.concatenate([grad_norm1[None], gains], axis=0)
+    hidden_rows = (grad_residual + grad_hidden_norm).astype(bf16)
+    grad_query, hidden_rows, late_sums = lax.optimization_barrier(
+        (grad_query, hidden_rows, late_sums)
+    )
+    moved, by_x, by_core = swap(late_sums, 16), swap(hidden_rows, 2), swap(hidden_rows, 1)
+    grad_query = grad_query.astype(f32)
+    grad_query, grad_out, moved = lax.optimization_barrier((grad_query, grad_out, moved))
+    late_sums = late_sums + moved
+    moved = swap(late_sums, 8)
+    grad_out = grad_out.astype(f32)
+    grad_out, grad_kv, moved = lax.optimization_barrier((grad_out, grad_kv, moved))
+    small = jnp.concatenate([small, late_sums + moved], axis=0)
+    moved = swap(small, 4)
+    by_x, moved = lax.optimization_barrier((by_x, moved))
+    by_both = swap(by_x, 1)
+    grad_hidden = in_order(hidden_rows, by_core, by_x, by_both)
+    small = small + moved
+    grad_kv = grad_kv.astype(f32)
+    for bit in (1, 0):
+        small = small + swap(small, 1 << bit)
+    grad_norm1 = small[expert_count + 1]
+    grad_router, grad_norm2 = small[:expert_count].T, small[expert_count]
+    grad_qgain, grad_kgain = jnp.split(small[expert_count + 2, : 2 * head_dim], 2)
+    grad_down = grad_down.reshape(local_count, ff_local, model_width)
+    return (
+        out_hidden,
+        grad_hidden,
+        grad_norm1,
+        grad_query,
+        grad_kv[:, :head_dim],
+        grad_kv[:, head_dim:],
+        grad_qgain,
+        grad_kgain,
+        grad_out,
+        grad_norm2,
+        grad_router,
+        turn(grad_gate),
+        turn(grad_up),
+        grad_down,
+    )
+
+
 def solution(mesh):
+    groups = mesh.shape["expert"]
+
+    def device_fn(*operands):
+        heads = operands[7].shape[1] // operands[10].shape[0]
+        one_head = heads == groups == 8 and operands[8].shape[1] == operands[10].shape[0]
+        one_head = one_head and mesh.shape["tensor"] == 4
+        return (head_device if one_head else per_device)(*operands)
+
     return jax.shard_map(
-        per_device,
+        device_fn,
         mesh=mesh,
         in_specs=(
             P("expert", None),

time: 2410 us -> 480 us (0.20)
  waiting for transfers between devices: 1670 us -> 12.2 us
  Pallas kernels: 0 us -> 422 us
  local copies, waits for them, and re-layouts: 247 us -> 12.5 us
  matrix products: 195 us -> 3.99 us
  blocking collectives: 169 us -> 0 us
  other arithmetic: 78.2 us -> 21 us
    all_to_all x4 -> x0, waiting for transfers between devices: 1290 us -> none  [the longest x2 666 us: bring_back(): lax.all_to_all(payload, 'expert', split_axis=0, concat_axis=0, tiled=True)]
    pallas_call x0 -> x4, Pallas kernels: none -> 422 us  [the longest x1 134 us: experts(): pl.pallas_call(experts_kernel, out_shape=(shape((count, wide), F32), shap...]
    psum x4 -> x0, waiting for transfers between devices: 313 us -> none  [the longest x1 277 us: per_device(): lax.psum(grad_w_query.astype(jnp.bfloat16), 'expert').astype(jnp.float32)]
    dot_general x49 -> x3, matrix products: 195 us -> 3.99 us  [the longest x1 1.7 us: head_device(): jnp.einsum('te,de->td', grad_logits, w_router, preferred_element_type=f32)]
    gather x15 -> x0, local copies, waits for them, and re-layouts: 157 us -> none  [the longest x1 35.8 us: per_device(): pair_grads[slot_pair]]
    all_gather x5 -> x0, blocking collectives: 135 us -> none  [the longest x1 33.2 us: per_device(): lax.all_gather(key_rows, 'expert', axis=0, tiled=True)]
    reduce_scatter x1 -> x0, waiting for transfers between devices: 63.1 us -> none  [per_device(): lax.psum_scatter(stacked.reshape(lax.axis_size('expert') * tok_rows, 2 *...]
    concatenate x6 -> x1, local copies, waits for them, and re-layouts: 37.6 us -> 0.07 us  [head_device(): jnp.concatenate([layout[None], drop_rank[None], expert_ids.T, jnp.zeros((...]
  transfers between devices with their start and end apart: 9 -> 13, of which waited for: 7 -> 3; matrix products, arithmetic and copies ran while one was open for 10% -> 3% of each run, Pallas kernels for 0% -> 39%
where the time goes in v5:
time: 480 us
  Pallas kernels  422 us (88%)
  other arithmetic  21 us (4%)
  local copies, waits for them, and re-layouts  12.5 us (3%)
  waiting for transfers between devices  12.2 us (3%)
  starting transfers between devices  6.88 us (1%)
    pallas_call x1, Pallas kernels, experts(): pl.pallas_call(experts_kernel, out_shape=(shape((count, wide), F32), shap...  134 us
    pallas_call x1, Pallas kernels, close(): pl.pallas_call(close_kernel, out_shape=(shape((count, wide), F32), shape(...  128 us
    pallas_call x1, Pallas kernels, front(): pl.pallas_call(front_kernel, out_shape=(shape((total, width), BF16), shap...  100 us
    pallas_call x1, Pallas kernels, attend_back(): pl.pallas_call(attend_back_kernel, out_shape=[shape((total, 3 * dim), BF1...  59.3 us
    ppermute x13, waiting for transfers between devices, swap(): lax.ppermute(value, ('expert', 'tensor'), [(device, device ^ bits) for de...  12.2 us
  transfers between devices with their start and end apart: 13, of which 3 were waited for; matrix products, arithmetic and copies ran while one was open for 3% of the time, Pallas kernels for 39%

profile of v5, /device:TPU:0, one launch (start us, length us, event | category | flops | bytes accessed | tf_op | source)
XLA Modules:
  0.0 479.6 jit_solution(10974414977591367713)
XLA Ops:
  1.3 1.4 add_add_fusion.2.tag
  2.7 100.3 %front.1 = (bf16[2048,2048]{1,0:T(8,128)(2,1)}, bf16[2048,128]{1,0:T(8,128)(2,1)}, bf16[2048,128]{1,0:T(8,128)(2,1)}, bf16[2048,128]{1,0:T(8,128)(2,1)}, f32[204...) custom-call(bf16[256,2048]{1,0:T(8,128)(2,1)} %hidden.1, ...), custom_call_target="tpu_custom_call" | custom-call | flops 8000000000 | bytes 270000000 | tf_op jit(solution)/shard_map/front/pallas_call | solution.py:1811
  103.1 1.2 multiply_reduce_fusion.2
  104.3 1.1 fusion.3
  105.4 1.2 copy.32
  106.7 1.3 fusion.17
  108.2 134.0 %experts.1 = (f32[64,4224]{1,0:T(8,128)}, f32[2,192,2048]{2,1,0:T(8,128)}, f32[2,192,2048]{2,1,0:T(8,128)}, f32[384,2048]{1,0:T(8,128)}) custom-call(bf16[64,2048]{1,0:T(8,128)(2,1)} %get-tuple-element.60.normed, bf16[2048,2048]{1,0:T(8,128)(2,1)} %get-tuple-element.61.grad_y, bf16[2,192,2048]{2,1,0:T(8,128)(2,1)} %bitcast.48, ...), custom_call_target="tpu_custom_call" | custom-call | flops 28999999488 | bytes 360000000 | tf_op jit(solution)/shard_map/experts/pallas_call | solution.py:943
  242.2 1.0 multiply_reduce_fusion.3
  243.2 1.7 multiply_reduce_fusion
  245.6 1.0 fusion.13
  246.7 1.9 fusion.14.own_rows
  248.6 59.3 %attend_back.1 = (bf16[2048,384]{1,0:T(8,128)(2,1)}, bf16[128,2048]{1,0:T(8,128)(2,1)}, f32[1,128]{1,0:T(1,128)}, f32[1,128]{1,0:T(1,128)}) custom-call(bf16[64,2048]{1,0:T(8,128)(2,1)} %fusion.14.own_rows, bf16[1024,2048]{1,0:T(8,128)(2,1)} %w_out.3, bf16[2048,128]{1,0:T(8,128)(2,1)} %get-tuple-element.66.queries, ...), custom_call_target="tpu_custom_call" | custom-call | flops 8999999488 | bytes 150000000 | tf_op jit(solution)/shard_map/attend_back/pallas_call | solution.py:1076
  308.1 128.2 %close.1 = (f32[64,2048]{1,0:T(8,128)}, bf16[2048,256]{1,0:T(8,128)(2,1)}, bf16[2048,1024]{1,0:T(8,128)(2,1)}, bf16[1024,2048]{1,0:T(8,128)(2,1)}) custom-call(bf16[2048,2048]{1,0:T(8,128)(2,1)} %get-tuple-element.59.normed, bf16[2048,384]{1,0:T(8,128)(2,1)} %get-tuple-element.78.grad_lin, bf16[2048,1024]{1,0:T(8,128)(2,1)} %w_query.3, ...), custom_call_target="tpu_custom_call" | custom-call | flops 7000000000 | bytes 330000000 | tf_op jit(solution)/shard_map/close/pallas_call | solution.py:1442
  436.4 1.5 collective-permute-done.2
  438.2 1.1 pad_maximum_fusion
  439.7 1.6 fusion.2
  441.4 0.9 collective-permute-start.6
  442.3 4.4 convert_element_type.33
  446.7 1.8 collective-permute-start.7
  448.5 1.0 collective-permute-start.5
  449.5 4.4 convert_element_type.34
  454.0 1.1 collective-permute-start.8
  455.1 1.5 fusion.15
  456.6 4.5 collective-permute-done.8
  461.2 1.1 collective-permute-start.11
  462.3 6.2 %collective-permute-done.11 = f32[19,2048]{1,0:T(8,128)S(1)} collective-permute-done((f32[19,2048]{1,0:T(8,128)S(1)}, f32[19,2048]{1,0:T(8,128)S(1)}, u32[]{:S(2)}, u32[]{:S(2)}) %collective-permute-start.11) | collective-permute-done | bytes 155680 | tf_op jit(solution)/shard_map/ppermute | solution.py:1847
  469.0 1.1 pad_maximum_fusion.1
  471.9 1.7 copy.38
  473.6 1.4 copy-done.5
  474.9 1.7 copy.39
  476.6 1.4 copy-done.4
  477.9 1.7 copy.40
  (77 shorter events, 5.0 us)
Async XLA Ops:
  2.7 103.9 %copy-start.10 = (bf16[2048,16]{0,1:T(8,128)(2,1)S(1)}, bf16[2048,16]{0,1:T(8,128)(2,1)}, u32[]{:S(2)}) copy-start(bf16[2048,16]{0,1:T(8,128)(2,1)} %param.32) | copy-start | bytes 196612
  108.1 135.0 %copy-start = (f32[64,2048]{1,0:T(8,128)S(1)}, f32[64,2048]{1,0:T(8,128)}, u32[]{:S(2)}) copy-start(f32[64,2048]{1,0:T(8,128)} %get-tuple-element.65) | copy-start | bytes 1572868
  108.1 135.0 %copy-start.11 = (bf16[2048,16]{0,1:T(8,128)(2,1)S(1)}, bf16[2048,16]{0,1:T(8,128)(2,1)}, u32[]{:S(2)}) copy-start(bf16[2048,16]{0,1:T(8,128)(2,1)} %param.32) | copy-start | bytes 196612
  108.1 135.0 %copy-start.13 = (f32[2048]{0:T(1024)S(1)}, f32[2048]{0:T(1024)}, u32[]{:S(2)}) copy-start(f32[2048]{0:T(1024)} %param.31) | copy-start | bytes 24580
  108.1 137.4 %copy-start.8 = (bf16[64,2048]{1,0:T(8,128)(2,1)S(1)}, bf16[64,2048]{1,0:T(8,128)(2,1)}, u32[]{:S(2)}) copy-start(bf16[64,2048]{1,0:T(8,128)(2,1)} %get-tuple-element.60.normed) | copy-start | bytes 786436
  244.9 191.5 %collective-permute-start.3 = (bf16[64,2048]{1,0:T(8,128)(2,1)S(1)}, bf16[64,2048]{1,0:T(8,128)(2,1)S(1)}, u32[]{:S(2)}, u32[]{:S(2)}) collective-permute-start(bf16[64,2048]{1,0:T(8,128)(2,1)S(1)} %get-tuple-element.122), channel_id=1, source_target_pairs={{0,1},{1,0},{2,3},{3,2},{4,5},{5,4},{6,7},{7,6},{8,9},{9,8},{10,11... | collective-permute-start | bytes 786440 | tf_op jit(solution)/shard_map/ppermute | solution.py:1847
  244.9 191.3 %collective-permute-start.1 = (bf16[64,2048]{1,0:T(8,128)(2,1)S(1)}, bf16[64,2048]{1,0:T(8,128)(2,1)S(1)}, u32[]{:S(2)}, u32[]{:S(2)}) collective-permute-start(bf16[64,2048]{1,0:T(8,128)(2,1)S(1)} %get-tuple-element.122), channel_id=1, source_target_pairs={{0,2},{1,3},{2,0},{3,1},{4,6},{5,7},{6,4},{7,5},{8,10},{9,11},{10,... | collective-permute-start | bytes 786440 | tf_op jit(solution)/shard_map/ppermute | solution.py:1847
  246.6 61.4 %collective-permute-start = (f32[17,2048]{1,0:T(8,128)S(1)}, f32[17,2048]{1,0:T(8,128)S(1)}, u32[]{:S(2)}, u32[]{:S(2)}) collective-permute-start(f32[17,2048]{1,0:T(8,128)S(1)} %pad_maximum_fusion.6), channel_id=1, source_target_pairs={{0,16},{1,17},{2,18},{3,19},{4,20},{5,21},{6,22},{7,23},{8,24},{9,... | collective-permute-start | bytes 417800 | tf_op jit(solution)/shard_map/ppermute | solution.py:1847
  308.0 131.3 %collective-permute-start.4 = (f32[17,2048]{1,0:T(8,128)S(1)}, f32[17,2048]{1,0:T(8,128)S(1)}, u32[]{:S(2)}, u32[]{:S(2)}) collective-permute-start(f32[17,2048]{1,0:T(8,128)S(1)} %fusion.12), channel_id=1, source_target_pairs={{0,8},{1,9},{2,10},{3,11},{4,12},{5,13},{6,14},{7,15},{8,0},{9,1},... | collective-permute-start | bytes 417800 | tf_op jit(solution)/shard_map/ppermute | solution.py:1847
  436.3 1.6 collective-permute-start.2
  437.9 1.4 copy-start.7
  437.9 1.5 copy-start.9
  437.9 1.5 copy-start.12
  438.2 4.1 copy-start.2
  439.3 2.0 copy-start.14
  439.3 2.1 copy-start.15
  441.4 5.3 %collective-permute-start.6 = (f32[2,2048]{1,0:T(2,128)S(1)}, f32[2,2048]{1,0:T(2,128)S(1)}, u32[]{:S(2)}, u32[]{:S(2)}) collective-permute-start(f32[2,2048]{1,0:T(2,128)S(1)} %maximum_maximum_fusion), channel_id=1, source_target_pairs={{0,16},{1,17},{2,18},{3,19},{4,20},{5,21},{6,22},{7,23},{8,24},{9,... | collective-permute-start | bytes 49160 | tf_op jit(solution)/shard_map/ppermute | solution.py:1847
  442.3 7.3 %copy-start.1 = (bf16[1024,2048]{1,0:T(8,128)(2,1)S(1)}, bf16[1024,2048]{1,0:T(8,128)(2,1)}, u32[]{:S(2)}) copy-start(bf16[1024,2048]{1,0:T(8,128)(2,1)} %get-tuple-element.93) | copy-start | bytes 12582916
  446.7 7.3 %collective-permute-start.7 = (f32[2,2048]{1,0:T(2,128)S(1)}, f32[2,2048]{1,0:T(2,128)S(1)}, u32[]{:S(2)}, u32[]{:S(2)}) collective-permute-start(f32[2,2048]{1,0:T(2,128)S(1)} %add.89), channel_id=1, source_target_pairs={{0,8},{1,9},{2,10},{3,11},{4,12},{5,13},{6,14},{7,15},{8,0},{9,1},... | collective-permute-start | bytes 49160 | tf_op jit(solution)/shard_map/ppermute | solution.py:1847
  448.5 13.8 %collective-permute-start.10 = (bf16[64,2048]{1,0:T(8,128)(2,1)S(1)}, bf16[64,2048]{1,0:T(8,128)(2,1)S(1)}, u32[]{:S(2)}, u32[]{:S(2)}) collective-permute-start(bf16[64,2048]{1,0:T(8,128)(2,1)S(1)} %fusion.2), channel_id=1, source_target_pairs={{0,1},{1,0},{2,3},{3,2},{4,5},{5,4},{6,7},{7,6},{8,9},{9,8},{10,11... | collective-permute-start | bytes 786440 | tf_op jit(solution)/shard_map/ppermute | solution.py:1847
  448.5 12.6 %collective-permute-start.5 = (bf16[64,2048]{1,0:T(8,128)(2,1)S(1)}, bf16[64,2048]{1,0:T(8,128)(2,1)S(1)}, u32[]{:S(2)}, u32[]{:S(2)}) collective-permute-start(bf16[64,2048]{1,0:T(8,128)(2,1)S(1)} %fusion.2), channel_id=1, source_target_pairs={{0,2},{1,3},{2,0},{3,1},{4,6},{5,7},{6,4},{7,5},{8,10},{9,11},{10,... | collective-permute-start | bytes 786440 | tf_op jit(solution)/shard_map/ppermute | solution.py:1847
  449.5 5.6 %copy-start.3 = (bf16[2048,256]{1,0:T(8,128)(2,1)S(1)}, bf16[2048,256]{1,0:T(8,128)(2,1)}, u32[]{:S(2)}) copy-start(bf16[2048,256]{1,0:T(8,128)(2,1)} %get-tuple-element.99) | copy-start | bytes 3145732
  454.0 7.1 %collective-permute-start.8 = (f32[19,2048]{1,0:T(8,128)S(1)}, f32[19,2048]{1,0:T(8,128)S(1)}, u32[]{:S(2)}, u32[]{:S(2)}) collective-permute-start(f32[19,2048]{1,0:T(8,128)S(1)} %pad_maximum_fusion.7), channel_id=1, source_target_pairs={{0,4},{1,5},{2,6},{3,7},{4,0},{5,1},{6,2},{7,3},{8,12},{9,13},{10,... | collective-permute-start | bytes 466952 | tf_op jit(solution)/shard_map/ppermute | solution.py:1847
  461.1 7.5 %collective-permute-start.9 = (bf16[64,2048]{1,0:T(8,128)(2,1)S(1)}, bf16[64,2048]{1,0:T(8,128)(2,1)S(1)}, u32[]{:S(2)}, u32[]{:S(2)}) collective-permute-start(bf16[64,2048]{1,0:T(8,128)(2,1)S(1)} %collective-permute-done.5), channel_id=1, source_target_pairs={{0,1},{1,0},{2,3},{3,2},{4,5},{5,4},{6,7},{7,6},{8,9},{9,8},{10,11... | collective-permute-start | bytes 786440 | tf_op jit(solution)/shard_map/ppermute | solution.py:1847
  461.2 7.4 %collective-permute-start.11 = (f32[19,2048]{1,0:T(8,128)S(1)}, f32[19,2048]{1,0:T(8,128)S(1)}, u32[]{:S(2)}, u32[]{:S(2)}) collective-permute-start(f32[19,2048]{1,0:T(8,128)S(1)} %fusion.22), channel_id=1, source_target_pairs={{0,2},{1,3},{2,0},{3,1},{4,6},{5,7},{6,4},{7,5},{8,10},{9,11},{10,... | collective-permute-start | bytes 466952 | tf_op jit(solution)/shard_map/ppermute | solution.py:1847
  468.6 1.5 collective-permute-start.12
  468.7 3.2 copy-start.6
  471.9 3.0 copy-start.5
  474.9 3.0 copy-start.4

commit v6 on v5

--- a/solution.py
+++ b/solution.py
@@ -1843,18 +1843,39 @@
     )
 
 
+def settle_kernel(*refs):
+    half = len(refs) // 2
+    sems = refs[-1]
+    copies = [
+        pltpu.make_async_copy(refs[at], refs[half + at], sems.at[at]) for at in range(half)
+    ]
+    for copy in copies:
+        copy.start()
+    for copy in copies:
+        copy.wait()
+
+
+def settle(*arrays):
+    return pl.pallas_call(
+        settle_kernel,
+        out_shape=tuple(jax.ShapeDtypeStruct(v.shape, v.dtype) for v in arrays),
+        in_specs=[HBM_SPEC] * len(arrays),
+        out_specs=(HBM_SPEC,) * len(arrays),
+        scratch_shapes=dma_sems(((len(arrays),),)),
+        cost_estimate=cost(0, 6),
+        name="settle",
+    )(*arrays)
+
+
 def swap(value, bits):
     return lax.ppermute(
         value, ("expert", "tensor"), [(device, device ^ bits) for device in range(32)]
     )
 
 
-def tensor_rows(rows):
-    by_core = swap(rows, 1)
-    by_x = swap(rows, 2)
-    by_both = swap(by_x, 1)
-
-    return in_order(rows, by_core, by_x, by_both)
+def pair_sums(own, first, second, third):
+    own, first, second, third = (v.astype(jnp.float32) for v in (own, first, second, third))
+    return (own + first) + (second + third)
 
 
 def in_order(rows, by_core, by_x, by_both):
@@ -1923,7 +1944,7 @@
         normed2, grad_y_all, turn(w_gate), turn(w_up), w_down.reshape(-1, model_width),
         w_router.T, chosen, kept,
     )
-    out_hidden = tensor_rows((residual + back[:, :model_width]).astype(bf16))
+    out_own = (residual + back[:, :model_width]).astype(bf16)
     back = back[:, model_width:]
 
     start = group * tok_rows + part * own_rows
@@ -1941,25 +1962,25 @@
     norm2_pull = jax.vjp(norm_rows, residual, norm2_gain)[1]
     grad_resid_norm, grad_norm2 = norm2_pull(grad_normed2)
     grad_residual = own(cotangent).astype(f32) + grad_resid_norm
-    small = jnp.concatenate([grad_router.T, grad_norm2[None]], axis=0)
-    small = small + swap(small, 16)
+    small = jnp.concatenate([grad_router.T, grad_norm2[None]], axis=0).astype(bf16)
+    z_parts = [swap(small, 8 * step) for step in (1, 2, 3)]
 
     grad_lin, grad_out, grad_qgain, grad_kgain = attend_back(
         grad_residual.astype(bf16), w_out, queries, keys, values, attended, lin, cosine, sine,
         place_column, place_row, open_row, log_total, k_gain, q_gain,
     )
-    grad_lin, small = lax.optimization_barrier((grad_lin, small))
-    small_moved = swap(small, 8)
+    small = pair_sums(small, *z_parts).astype(bf16)
+    grad_lin, small, out_own = lax.optimization_barrier((grad_lin, small, out_own))
+    yx_parts = [swap(small, 2 * step) for step in (1, 2, 3)]
+    out_by_x, out_by_core = swap(out_own, 2), swap(out_own, 1)
     gains = jnp.concatenate(
         [grad_qgain, grad_kgain, jnp.zeros((1, model_width - 2 * head_dim), f32)], axis=1
     )
     reduced, grad_kv, grad_query, grad_out = close(
         normed1, grad_lin, w_query, key_weight, value_weight, grad_out
     )
-    reduced, out_hidden, small_moved = lax.optimization_barrier(
-        (reduced, out_hidden, small_moved)
-    )
-    small = small + small_moved
+    reduced, yx_parts, out_by_x = lax.optimization_barrier((reduced, yx_parts, out_by_x))
+    small = pair_sums(small, *yx_parts)
     norm1_pull = jax.vjp(norm_rows, own(hidden_in).astype(f32), norm1_gain)[1]
     grad_hidden_norm, grad_norm1 = norm1_pull(reduced)
     late_sums = jnp.concatenate([grad_norm1[None], gains], axis=0)
@@ -1967,22 +1988,26 @@
     grad_query, hidden_rows, late_sums = lax.optimization_barrier(
         (grad_query, hidden_rows, late_sums)
     )
-    moved, by_x, by_core = swap(late_sums, 16), swap(hidden_rows, 2), swap(hidden_rows, 1)
+    by_x, by_core = swap(hidden_rows, 2), swap(hidden_rows, 1)
+    moved = [swap(late_sums, 8 * step) for step in (1, 2, 3)]
+    out_by_both = swap(out_by_x, 1)
     grad_query = grad_query.astype(f32)
     grad_query, grad_out, moved = lax.optimization_barrier((grad_query, grad_out, moved))
-    late_sums = late_sums + moved
-    moved = swap(late_sums, 8)
-    grad_out = grad_out.astype(f32)
-    grad_out, grad_kv, moved = lax.optimization_barrier((grad_out, grad_kv, moved))
-    small = jnp.concatenate([small, late_sums + moved], axis=0)
-    moved = swap(small, 4)
-    by_x, moved = lax.optimization_barrier((by_x, moved))
-    by_both = swap(by_x, 1)
+    late_sums = pair_sums(late_sums, *moved)
+    moved = [swap(late_sums, 2 * step) for step in (1, 2, 3)]
+    grad_out, grad_kv = grad_out.astype(f32), grad_kv.astype(f32)
+    out_hidden = in_order(out_own, out_by_core, out_by_x, out_by_both)
+    grads = (grad_gate, grad_up, grad_down)
+    grad_out, grad_kv, out_hidden, by_x, moved, grads = lax.optimization_barrier(
+        (grad_out, grad_kv, out_hidden, by_x, moved, grads)
+    )
+    small = jnp.concatenate([small, pair_sums(late_sums, *moved)], axis=0)
+    moved, by_both = swap(small, 1), swap(by_x, 1)
+    grads = settle(*grads)
+    grads, moved, by_both = lax.optimization_barrier((grads, moved, by_both))
+    grad_gate, grad_up, grad_down = grads
+    small = small + moved
     grad_hidden = in_order(hidden_rows, by_core, by_x, by_both)
-    small = small + moved
-    grad_kv = grad_kv.astype(f32)
-    for bit in (1, 0):
-        small = small + swap(small, 1 << bit)
     grad_norm1 = small[expert_count + 1]
     grad_router, grad_norm2 = small[:expert_count].T, small[expert_count]
     grad_qgain, grad_kgain = jnp.split(small[expert_count + 2, : 2 * head_dim], 2)

time: 480 us -> 761 us (1.59)
  Pallas kernels: 422 us -> 707 us
  starting transfers between devices: 6.88 us -> 18.5 us
  waiting for transfers between devices: 12.2 us -> 1.88 us
  local copies, waits for them, and re-layouts: 12.5 us -> 4.72 us
    pallas_call x0 -> x1, Pallas kernels: none -> 287 us  [settle(): pl.pallas_call(settle_kernel, out_shape=tuple((jax.ShapeDtypeStruct(v.sha...]
    ppermute x13 -> x19, starting transfers between devices: 6.88 us -> 18.5 us  [swap(): lax.ppermute(value, ('expert', 'tensor'), [(device, device ^ bits) for de...]
    ppermute x13 -> x19, waiting for transfers between devices: 12.2 us -> 1.88 us  [swap(): lax.ppermute(value, ('expert', 'tensor'), [(device, device ^ bits) for de...]
    unnamed x35 -> x24, local copies, waits for them, and re-layouts: 7.96 us -> 0.15 us
  transfers between devices with their start and end apart: 13 -> 19, of which waited for: 3 -> 1; matrix products, arithmetic and copies ran while one was open for 3% -> 2% of each run, Pallas kernels for 39% -> 62%
where the time goes in v6:
time: 761 us; the launch traced here: 760 us
  Pallas kernels  707 us (93%)
  other arithmetic  22.2 us (3%)
  starting transfers between devices  18.5 us (2%)
    pallas_call x1, Pallas kernels, settle(): pl.pallas_call(settle_kernel, out_shape=tuple((jax.ShapeDtypeStruct(v.sha...  287 us
    pallas_call x1, Pallas kernels, experts(): pl.pallas_call(experts_kernel, out_shape=(shape((count, wide), F32), shap...  134 us
    pallas_call x1, Pallas kernels, close(): pl.pallas_call(close_kernel, out_shape=(shape((count, wide), F32), shape(...  131 us
    pallas_call x1, Pallas kernels, front(): pl.pallas_call(front_kernel, out_shape=(shape((total, width), BF16), shap...  100 us
    pallas_call x1, Pallas kernels, attend_back(): pl.pallas_call(attend_back_kernel, out_shape=[shape((total, 3 * dim), BF1...  54.9 us
    ppermute x19, starting transfers between devices, swap(): lax.ppermute(value, ('expert', 'tensor'), [(device, device ^ bits) for de...  18.5 us
  transfers between devices with their start and end apart: 19, of which 1 were waited for; matrix products, arithmetic and copies ran while one was open for 2% of the time, Pallas kernels for 62%

profile of v6, /device:TPU:0, one launch (start us, length us, event | category | flops | bytes accessed | tf_op | source)
XLA Modules:
  0.0 759.8 jit_solution(7201255049677180710)
XLA Ops:
  1.3 1.4 add_add_fusion.3.tag
  2.7 100.3 %front.1 = (bf16[2048,2048]{1,0:T(8,128)(2,1)}, bf16[2048,128]{1,0:T(8,128)(2,1)}, bf16[2048,128]{1,0:T(8,128)(2,1)}, bf16[2048,128]{1,0:T(8,128)(2,1)}, f32[204...) custom-call(bf16[256,2048]{1,0:T(8,128)(2,1)} %hidden.1, ...), custom_call_target="tpu_custom_call" | custom-call | flops 8000000000 | bytes 270000000 | tf_op jit(solution)/shard_map/front/pallas_call | solution.py:1811
  103.1 1.2 copy.32
  104.3 1.3 fusion.15
  105.8 134.0 %experts.1 = (f32[64,4224]{1,0:T(8,128)}, f32[2,192,2048]{2,1,0:T(8,128)}, f32[2,192,2048]{2,1,0:T(8,128)}, f32[384,2048]{1,0:T(8,128)}) custom-call(bf16[64,2048]{1,0:T(8,128)(2,1)} %get-tuple-element.78.normed, bf16[2048,2048]{1,0:T(8,128)(2,1)} %get-tuple-element.79.grad_y, bf16[2,192,2048]{2,1,0:T(8,128)(2,1)} %bitcast.45, ...), custom_call_target="tpu_custom_call" | custom-call | flops 28999999488 | bytes 360000000 | tf_op jit(solution)/shard_map/experts/pallas_call | solution.py:943
  239.8 1.0 multiply_reduce_fusion.3
  240.8 1.0 convolution_convert_fusion
  241.8 1.1 fusion.3
  243.1 1.7 multiply_reduce_fusion
  244.8 1.9 collective-permute-start
  246.7 3.7 collective-permute-start.1
  250.4 1.9 fusion.12.own_rows
  252.3 54.9 %attend_back.1 = (bf16[2048,384]{1,0:T(8,128)(2,1)}, bf16[128,2048]{1,0:T(8,128)(2,1)}, f32[1,128]{1,0:T(1,128)}, f32[1,128]{1,0:T(1,128)}) custom-call(bf16[64,2048]{1,0:T(8,128)(2,1)} %fusion.12.own_rows, bf16[1024,2048]{1,0:T(8,128)(2,1)} %w_out.3, bf16[2048,128]{1,0:T(8,128)(2,1)} %get-tuple-element.84.queries, ...), custom_call_target="tpu_custom_call" | custom-call | flops 8999999488 | bytes 150000000 | tf_op jit(solution)/shard_map/attend_back/pallas_call | solution.py:1076
  307.4 2.0 collective-permute-start.4
  309.4 1.5 collective-permute-start.5
  311.0 131.2 %close.1 = (f32[64,2048]{1,0:T(8,128)}, bf16[2048,256]{1,0:T(8,128)(2,1)}, bf16[2048,1024]{1,0:T(8,128)(2,1)}, bf16[1024,2048]{1,0:T(8,128)(2,1)}) custom-call(bf16[2048,2048]{1,0:T(8,128)(2,1)} %get-tuple-element.77.normed, bf16[2048,384]{1,0:T(8,128)(2,1)} %get-tuple-element.96.grad_lin, bf16[2048,1024]{1,0:T(8,128)(2,1)} %w_query.3, ...), custom_call_target="tpu_custom_call" | custom-call | flops 7000000000 | bytes 330000000 | tf_op jit(solution)/shard_map/close/pallas_call | solution.py:1442
  442.2 1.5 convert_element_type.68
  444.1 1.5 fusion.2
  445.7 2.0 collective-permute-start.8
  447.7 2.4 collective-permute-start.9
  450.3 1.0 broadcast_select_fusion.9
  451.3 4.4 convert_element_type.66
  456.3 1.9 collective-permute-start.13
  458.4 4.4 convert_element_type.67
  462.8 1.5 collective-permute-start.15
  464.6 1.0 pad_maximum_fusion
  465.7 1.8 collective-permute-done.15
  468.1 1.4 fusion.13
  469.6 287.0 %settle.1 = (f32[2,192,2048]{2,1,0:T(8,128)}, f32[2,192,2048]{2,1,0:T(8,128)}, f32[384,2048]{1,0:T(8,128)}) custom-call(f32[2,192,2048]{2,1,0:T(8,128)} %get-tuple-element.119.refs_0_, f32[2,192,2048]{2,1,0:T(8,128)} %get-tuple-element.120.refs_1_, f32[384,2048]{1,0:T(8,128)} %get-tuple-element.121.refs_2_), custom_call_target="tpu_custom_call" | custom-call | bytes 18000000 | tf_op jit(solution)/shard_map/settle/pallas_call | solution.py:1859
  756.7 0.7 slice_bitcast_fusion
  757.3 0.6 fusion.14
  758.8 1.1 pad_maximum_fusion.1
  (79 shorter events, 4.4 us)
Async XLA Ops:
  2.7 101.6 %copy-start.6 = (bf16[2048,16]{0,1:T(8,128)(2,1)S(1)}, bf16[2048,16]{0,1:T(8,128)(2,1)}, u32[]{:S(2)}) copy-start(bf16[2048,16]{0,1:T(8,128)(2,1)} %param.32) | copy-start | bytes 196612
  105.8 135.0 %copy-start.4 = (bf16[64,2048]{1,0:T(8,128)(2,1)S(1)}, bf16[64,2048]{1,0:T(8,128)(2,1)}, u32[]{:S(2)}) copy-start(bf16[64,2048]{1,0:T(8,128)(2,1)} %get-tuple-element.78.normed) | copy-start | bytes 786436
  105.8 137.1 %copy-start = (f32[64,2048]{1,0:T(8,128)S(1)}, f32[64,2048]{1,0:T(8,128)}, u32[]{:S(2)}) copy-start(f32[64,2048]{1,0:T(8,128)} %get-tuple-element.83) | copy-start | bytes 1572868
  105.8 137.3 %copy-start.7 = (bf16[2048,16]{0,1:T(8,128)(2,1)S(1)}, bf16[2048,16]{0,1:T(8,128)(2,1)}, u32[]{:S(2)}) copy-start(bf16[2048,16]{0,1:T(8,128)(2,1)} %param.32) | copy-start | bytes 196612
  105.8 137.3 %copy-start.9 = (f32[2048]{0:T(1024)S(1)}, f32[2048]{0:T(1024)}, u32[]{:S(2)}) copy-start(f32[2048]{0:T(1024)} %param.31) | copy-start | bytes 24580
  244.8 62.4 %collective-permute-start = (bf16[17,2048]{1,0:T(8,128)(2,1)S(1)}, bf16[17,2048]{1,0:T(8,128)(2,1)S(1)}, u32[]{:S(2)}, u32[]{:S(2)}) collective-permute-start(bf16[17,2048]{1,0:T(8,128)(2,1)S(1)} %pad_maximum_fusion.7), channel_id=1, source_target_pairs={{0,8},{1,9},{2,10},{3,11},{4,12},{5,13},{6,14},{7,15},{8,0},{9,1},... | collective-permute-start | bytes 208904 | tf_op jit(solution)/shard_map/ppermute | solution.py:1871
  246.7 60.5 %collective-permute-start.1 = (bf16[17,2048]{1,0:T(8,128)(2,1)S(1)}, bf16[17,2048]{1,0:T(8,128)(2,1)S(1)}, u32[]{:S(2)}, u32[]{:S(2)}) collective-permute-start(bf16[17,2048]{1,0:T(8,128)(2,1)S(1)} %pad_maximum_fusion.7), channel_id=1, source_target_pairs={{0,16},{1,17},{2,18},{3,19},{4,20},{5,21},{6,22},{7,23},{8,24},{9,... | collective-permute-start | bytes 208904 | tf_op jit(solution)/shard_map/ppermute | solution.py:1871
  250.4 56.8 %collective-permute-start.2 = (bf16[17,2048]{1,0:T(8,128)(2,1)S(1)}, bf16[17,2048]{1,0:T(8,128)(2,1)S(1)}, u32[]{:S(2)}, u32[]{:S(2)}) collective-permute-start(bf16[17,2048]{1,0:T(8,128)(2,1)S(1)} %pad_maximum_fusion.7), channel_id=1, source_target_pairs={{0,24},{1,25},{2,26},{3,27},{4,28},{5,29},{6,30},{7,31},{8,16},{9,... | collective-permute-start | bytes 208904 | tf_op jit(solution)/shard_map/ppermute | solution.py:1871
  307.3 136.4 %collective-permute-start.3 = (bf16[17,2048]{1,0:T(8,128)(2,1)S(1)}, bf16[17,2048]{1,0:T(8,128)(2,1)S(1)}, u32[]{:S(2)}, u32[]{:S(2)}) collective-permute-start(bf16[17,2048]{1,0:T(8,128)(2,1)S(1)} %add_convert_fusion.1), channel_id=1, source_target_pairs={{0,2},{1,3},{2,0},{3,1},{4,6},{5,7},{6,4},{7,5},{8,10},{9,11},{10,... | collective-permute-start | bytes 208904 | tf_op jit(solution)/shard_map/ppermute | solution.py:1871
  307.4 136.3 %collective-permute-start.4 = (bf16[17,2048]{1,0:T(8,128)(2,1)S(1)}, bf16[17,2048]{1,0:T(8,128)(2,1)S(1)}, u32[]{:S(2)}, u32[]{:S(2)}) collective-permute-start(bf16[17,2048]{1,0:T(8,128)(2,1)S(1)} %add_convert_fusion.1), channel_id=1, source_target_pairs={{0,4},{1,5},{2,6},{3,7},{4,0},{5,1},{6,2},{7,3},{8,12},{9,13},{10,... | collective-permute-start | bytes 208904 | tf_op jit(solution)/shard_map/ppermute | solution.py:1871
  309.4 134.3 %collective-permute-start.5 = (bf16[17,2048]{1,0:T(8,128)(2,1)S(1)}, bf16[17,2048]{1,0:T(8,128)(2,1)S(1)}, u32[]{:S(2)}, u32[]{:S(2)}) collective-permute-start(bf16[17,2048]{1,0:T(8,128)(2,1)S(1)} %add_convert_fusion.1), channel_id=1, source_target_pairs={{0,6},{1,7},{2,4},{3,5},{4,2},{5,3},{6,0},{7,1},{8,14},{9,15},{10,... | collective-permute-start | bytes 208904 | tf_op jit(solution)/shard_map/ppermute | solution.py:1871
  310.9 132.9 %collective-permute-start.6 = (bf16[64,2048]{1,0:T(8,128)(2,1)S(1)}, bf16[64,2048]{1,0:T(8,128)(2,1)S(1)}, u32[]{:S(2)}, u32[]{:S(2)}) collective-permute-start(bf16[64,2048]{1,0:T(8,128)(2,1)S(1)} %get-tuple-element.101), channel_id=1, source_target_pairs={{0,2},{1,3},{2,0},{3,1},{4,6},{5,7},{6,4},{7,5},{8,10},{9,11},{10,... | collective-permute-start | bytes 786440 | tf_op jit(solution)/shard_map/ppermute | solution.py:1871
  311.0 139.3 %collective-permute-start.11 = (bf16[64,2048]{1,0:T(8,128)(2,1)S(1)}, bf16[64,2048]{1,0:T(8,128)(2,1)}, u32[]{:S(2)}, u32[]{:S(2)}) collective-permute-start(bf16[64,2048]{1,0:T(8,128)(2,1)S(1)} %get-tuple-element.101), channel_id=1, source_target_pairs={{0,1},{1,0},{2,3},{3,2},{4,5},{5,4},{6,7},{7,6},{8,9},{9,8},{10,11... | collective-permute-start | bytes 786440 | tf_op jit(solution)/shard_map/ppermute | solution.py:1871
  442.2 1.6 copy-start.3
  442.2 1.7 copy-start.5
  442.2 1.7 copy-start.8
  443.7 1.9 copy-start.10
  443.7 1.9 copy-start.11
  443.9 7.4 copy-start.2
  445.6 10.1 %collective-permute-start.7 = (f32[2,2048]{1,0:T(2,128)S(1)}, f32[2,2048]{1,0:T(2,128)S(1)}, u32[]{:S(2)}, u32[]{:S(2)}) collective-permute-start(f32[2,2048]{1,0:T(2,128)S(1)} %maximum_maximum_fusion), channel_id=1, source_target_pairs={{0,8},{1,9},{2,10},{3,11},{4,12},{5,13},{6,14},{7,15},{8,0},{9,1},... | collective-permute-start | bytes 49160 | tf_op jit(solution)/shard_map/ppermute | solution.py:1871
  445.7 10.6 %collective-permute-start.8 = (f32[2,2048]{1,0:T(2,128)S(1)}, f32[2,2048]{1,0:T(2,128)S(1)}, u32[]{:S(2)}, u32[]{:S(2)}) collective-permute-start(f32[2,2048]{1,0:T(2,128)S(1)} %maximum_maximum_fusion), channel_id=1, source_target_pairs={{0,16},{1,17},{2,18},{3,19},{4,20},{5,21},{6,22},{7,23},{8,24},{9,... | collective-permute-start | bytes 49160 | tf_op jit(solution)/shard_map/ppermute | solution.py:1871
  447.7 8.6 %collective-permute-start.9 = (f32[2,2048]{1,0:T(2,128)S(1)}, f32[2,2048]{1,0:T(2,128)S(1)}, u32[]{:S(2)}, u32[]{:S(2)}) collective-permute-start(f32[2,2048]{1,0:T(2,128)S(1)} %maximum_maximum_fusion), channel_id=1, source_target_pairs={{0,24},{1,25},{2,26},{3,27},{4,28},{5,29},{6,30},{7,31},{8,16},{9,... | collective-permute-start | bytes 49160 | tf_op jit(solution)/shard_map/ppermute | solution.py:1871
  450.1 17.4 %collective-permute-start.12 = (bf16[64,2048]{1,0:T(8,128)(2,1)S(1)}, bf16[64,2048]{1,0:T(8,128)(2,1)S(1)}, u32[]{:S(2)}, u32[]{:S(2)}) collective-permute-start(bf16[64,2048]{1,0:T(8,128)(2,1)S(1)} %fusion.2), channel_id=1, source_target_pairs={{0,2},{1,3},{2,0},{3,1},{4,6},{5,7},{6,4},{7,5},{8,10},{9,11},{10,... | collective-permute-start | bytes 786440 | tf_op jit(solution)/shard_map/ppermute | solution.py:1871
  450.3 19.3 %collective-permute-start.18 = (bf16[64,2048]{1,0:T(8,128)(2,1)S(1)}, bf16[64,2048]{1,0:T(8,128)(2,1)S(1)}, u32[]{:S(2)}, u32[]{:S(2)}) collective-permute-start(bf16[64,2048]{1,0:T(8,128)(2,1)S(1)} %fusion.2), channel_id=1, source_target_pairs={{0,1},{1,0},{2,3},{3,2},{4,5},{5,4},{6,7},{7,6},{8,9},{9,8},{10,11... | collective-permute-start | bytes 786440 | tf_op jit(solution)/shard_map/ppermute | solution.py:1871
  451.3 7.1 copy-start.1
  455.8 7.1 collective-permute-start.10
  456.3 9.3 %collective-permute-start.13 = (f32[2,2048]{1,0:T(2,128)S(1)}, f32[2,2048]{1,0:T(2,128)S(1)}, u32[]{:S(2)}, u32[]{:S(2)}) collective-permute-start(f32[2,2048]{1,0:T(2,128)S(1)} %add_add_fusion.5), channel_id=1, source_target_pairs={{0,2},{1,3},{2,0},{3,1},{4,6},{5,7},{6,4},{7,5},{8,10},{9,11},{10,... | collective-permute-start | bytes 49160 | tf_op jit(solution)/shard_map/ppermute | solution.py:1871
  458.2 7.4 collective-permute-start.14
  462.8 4.6 collective-permute-start.15
  467.5 289.1 %collective-permute-start.16 = (f32[19,2048]{1,0:T(8,128)S(1)}, f32[19,2048]{1,0:T(8,128)S(1)}, u32[]{:S(2)}, u32[]{:S(2)}) collective-permute-start(f32[19,2048]{1,0:T(8,128)S(1)} %pad_maximum_fusion.6), channel_id=1, source_target_pairs={{0,1},{1,0},{2,3},{3,2},{4,5},{5,4},{6,7},{7,6},{8,9},{9,8},{10,11... | collective-permute-start | bytes 466952 | tf_op jit(solution)/shard_map/ppermute | solution.py:1871
  467.6 289.0 %collective-permute-start.17 = (bf16[64,2048]{1,0:T(8,128)(2,1)S(1)}, bf16[64,2048]{1,0:T(8,128)(2,1)S(1)}, u32[]{:S(2)}, u32[]{:S(2)}) collective-permute-start(bf16[64,2048]{1,0:T(8,128)(2,1)S(1)} %collective-permute-done.12), channel_id=1, source_target_pairs={{0,1},{1,0},{2,3},{3,2},{4,5},{5,4},{6,7},{7,6},{8,9},{9,8},{10,11... | collective-permute-start | bytes 786440 | tf_op jit(solution)/shard_map/ppermute | solution.py:1871

commit v7 on v6

--- a/solution.py
+++ b/solution.py
@@ -1845,26 +1845,26 @@
 
 def settle_kernel(*refs):
     half = len(refs) // 2
-    sems = refs[-1]
-    copies = [
-        pltpu.make_async_copy(refs[at], refs[half + at], sems.at[at]) for at in range(half)
-    ]
-    for copy in copies:
-        copy.start()
-    for copy in copies:
-        copy.wait()
+    for source, target in zip(refs[:half], refs[half:]):
+        target[...] = source[...]
 
 
 def settle(*arrays):
-    return pl.pallas_call(
+    width = arrays[0].shape[-1]
+    flat = [v.reshape(-1, width) for v in arrays]
+    steps = 6
+    blocks = [pl.BlockSpec((v.shape[0] // steps, width), lambda i: (i, 0)) for v in flat]
+    out = pl.pallas_call(
         settle_kernel,
-        out_shape=tuple(jax.ShapeDtypeStruct(v.shape, v.dtype) for v in arrays),
-        in_specs=[HBM_SPEC] * len(arrays),
-        out_specs=(HBM_SPEC,) * len(arrays),
-        scratch_shapes=dma_sems(((len(arrays),),)),
+        grid=(steps,),
+        out_shape=tuple(jax.ShapeDtypeStruct(v.shape, v.dtype) for v in flat),
+        in_specs=blocks,
+        out_specs=tuple(blocks),
         cost_estimate=cost(0, 6),
+        compiler_params=pltpu.CompilerParams(vmem_limit_bytes=32 << 20),
         name="settle",
-    )(*arrays)
+    )(*flat)
+    return tuple(v.reshape(w.shape) for v, w in zip(out, arrays))
 
 
 def swap(value, bits):
@@ -1963,15 +1963,16 @@
     grad_resid_norm, grad_norm2 = norm2_pull(grad_normed2)
     grad_residual = own(cotangent).astype(f32) + grad_resid_norm
     small = jnp.concatenate([grad_router.T, grad_norm2[None]], axis=0).astype(bf16)
-    z_parts = [swap(small, 8 * step) for step in (1, 2, 3)]
+    small = lax.optimization_barrier(small)
+    far_part = swap(small, 16)
 
     grad_lin, grad_out, grad_qgain, grad_kgain = attend_back(
         grad_residual.astype(bf16), w_out, queries, keys, values, attended, lin, cosine, sine,
         place_column, place_row, open_row, log_total, k_gain, q_gain,
     )
-    small = pair_sums(small, *z_parts).astype(bf16)
+    small = (small.astype(f32) + far_part.astype(f32)).astype(bf16)
     grad_lin, small, out_own = lax.optimization_barrier((grad_lin, small, out_own))
-    yx_parts = [swap(small, 2 * step) for step in (1, 2, 3)]
+    near_part = swap(small, 8)
     out_by_x, out_by_core = swap(out_own, 2), swap(out_own, 1)
     gains = jnp.concatenate(
         [grad_qgain, grad_kgain, jnp.zeros((1, model_width - 2 * head_dim), f32)], axis=1
@@ -1979,8 +1980,8 @@
     reduced, grad_kv, grad_query, grad_out = close(
         normed1, grad_lin, w_query, key_weight, value_weight, grad_out
     )
-    reduced, yx_parts, out_by_x = lax.optimization_barrier((reduced, yx_parts, out_by_x))
-    small = pair_sums(small, *yx_parts)
+    reduced, near_part, out_by_x = lax.optimization_barrier((reduced, near_part, out_by_x))
+    small = small.astype(f32) + near_part.astype(f32)
     norm1_pull = jax.vjp(norm_rows, own(hidden_in).astype(f32), norm1_gain)[1]
     grad_hidden_norm, grad_norm1 = norm1_pull(reduced)
     late_sums = jnp.concatenate([grad_norm1[None], gains], axis=0)
@@ -1993,15 +1994,16 @@
     out_by_both = swap(out_by_x, 1)
     grad_query = grad_query.astype(f32)
     grad_query, grad_out, moved = lax.optimization_barrier((grad_query, grad_out, moved))
-    late_sums = pair_sums(late_sums, *moved)
-    moved = [swap(late_sums, 2 * step) for step in (1, 2, 3)]
+    small = jnp.concatenate([small, pair_sums(late_sums, *moved)], axis=0).astype(bf16)
+    small = lax.optimization_barrier(small)
+    moved = [swap(small, 2 * step) for step in (1, 2, 3)]
     grad_out, grad_kv = grad_out.astype(f32), grad_kv.astype(f32)
     out_hidden = in_order(out_own, out_by_core, out_by_x, out_by_both)
     grads = (grad_gate, grad_up, grad_down)
     grad_out, grad_kv, out_hidden, by_x, moved, grads = lax.optimization_barrier(
         (grad_out, grad_kv, out_hidden, by_x, moved, grads)
     )
-    small = jnp.concatenate([small, pair_sums(late_sums, *moved)], axis=0)
+    small = pair_sums(small, *moved)
     moved, by_both = swap(small, 1), swap(by_x, 1)
     grads = settle(*grads)
     grads, moved, by_both = lax.optimization_barrier((grads, moved, by_both))

time: 761 us -> 472 us (0.62)
  Pallas kernels: 707 us -> 427 us
  starting transfers between devices: 18.5 us -> 10.8 us
    pallas_call x1, Pallas kernels: 287 us -> 4.17 us  [settle(): pl.pallas_call(settle_kernel, grid=(steps,), out_shape=tuple((jax.ShapeDt...]
    ppermute x19 -> x15, starting transfers between devices: 18.5 us -> 10.8 us  [swap(): lax.ppermute(value, ('expert', 'tensor'), [(device, device ^ bits) for de...]
  transfers between devices with their start and end apart: 19 -> 15, of which waited for: 1 -> 1; matrix products, arithmetic and copies ran while one was open for 2% -> 4% of each run, Pallas kernels for 62% -> 41%
where the time goes in v7:
time: 472 us; the launch traced here: 471 us
  Pallas kernels  427 us (90%)
  other arithmetic  20.6 us (4%)
  starting transfers between devices  10.8 us (2%)
  local copies, waits for them, and re-layouts  5.42 us (1%)
    pallas_call x1, Pallas kernels, experts(): pl.pallas_call(experts_kernel, out_shape=(shape((count, wide), F32), shap...  134 us
    pallas_call x1, Pallas kernels, close(): pl.pallas_call(close_kernel, out_shape=(shape((count, wide), F32), shape(...  129 us
    pallas_call x1, Pallas kernels, front(): pl.pallas_call(front_kernel, out_shape=(shape((total, width), BF16), shap...  100 us
    pallas_call x1, Pallas kernels, attend_back(): pl.pallas_call(attend_back_kernel, out_shape=[shape((total, 3 * dim), BF1...  59.6 us
    ppermute x15, starting transfers between devices, swap(): lax.ppermute(value, ('expert', 'tensor'), [(device, device ^ bits) for de...  10.8 us
  transfers between devices with their start and end apart: 15, of which 1 were waited for; matrix products, arithmetic and copies ran while one was open for 4% of the time, Pallas kernels for 41%

profile of v7, /device:TPU:0, one launch (start us, length us, event | category | flops | bytes accessed | tf_op | source)
XLA Modules:
  0.0 470.9 jit_solution(10729162110929540248)
XLA Ops:
  0.8 0.6 maximum_bitcast_fusion.inverse
  1.3 1.4 add_add_fusion.3.tag
  2.7 100.3 %front.1 = (bf16[2048,2048]{1,0:T(8,128)(2,1)}, bf16[2048,128]{1,0:T(8,128)(2,1)}, bf16[2048,128]{1,0:T(8,128)(2,1)}, bf16[2048,128]{1,0:T(8,128)(2,1)}, f32[204...) custom-call(bf16[256,2048]{1,0:T(8,128)(2,1)} %hidden.1, ...), custom_call_target="tpu_custom_call" | custom-call | flops 8000000000 | bytes 270000000 | tf_op jit(solution)/shard_map/front/pallas_call | solution.py:1811
  103.0 1.2 copy.32
  104.3 1.3 fusion.15
  105.8 134.0 %experts.1 = (f32[64,4224]{1,0:T(8,128)}, f32[2,192,2048]{2,1,0:T(8,128)}, f32[2,192,2048]{2,1,0:T(8,128)}, f32[384,2048]{1,0:T(8,128)}) custom-call(bf16[64,2048]{1,0:T(8,128)(2,1)} %get-tuple-element.76.normed, bf16[2048,2048]{1,0:T(8,128)(2,1)} %get-tuple-element.77.grad_y, bf16[2,192,2048]{2,1,0:T(8,128)(2,1)} %bitcast.51, ...), custom_call_target="tpu_custom_call" | custom-call | flops 28999999488 | bytes 360000000 | tf_op jit(solution)/shard_map/experts/pallas_call | solution.py:943
  239.8 1.0 multiply_reduce_fusion.3
  240.9 1.0 convolution_convert_fusion
  242.1 1.7 multiply_reduce_fusion
  244.1 1.9 fusion.12.own_rows
  246.0 59.6 %attend_back.1 = (bf16[2048,384]{1,0:T(8,128)(2,1)}, bf16[128,2048]{1,0:T(8,128)(2,1)}, f32[1,128]{1,0:T(1,128)}, f32[1,128]{1,0:T(1,128)}) custom-call(bf16[64,2048]{1,0:T(8,128)(2,1)} %fusion.12.own_rows, bf16[1024,2048]{1,0:T(8,128)(2,1)} %w_out.3, bf16[2048,128]{1,0:T(8,128)(2,1)} %get-tuple-element.82.queries, ...), custom_call_target="tpu_custom_call" | custom-call | flops 8999999488 | bytes 150000000 | tf_op jit(solution)/shard_map/attend_back/pallas_call | solution.py:1076
  306.0 128.9 %close.1 = (f32[64,2048]{1,0:T(8,128)}, bf16[2048,256]{1,0:T(8,128)(2,1)}, bf16[2048,1024]{1,0:T(8,128)(2,1)}, bf16[1024,2048]{1,0:T(8,128)(2,1)}) custom-call(bf16[2048,2048]{1,0:T(8,128)(2,1)} %get-tuple-element.75.normed, bf16[2048,384]{1,0:T(8,128)(2,1)} %get-tuple-element.94.grad_lin, bf16[2048,1024]{1,0:T(8,128)(2,1)} %w_query.3, ...), custom_call_target="tpu_custom_call" | custom-call | flops 7000000000 | bytes 330000000 | tf_op jit(solution)/shard_map/close/pallas_call | solution.py:1442
  434.9 1.4 convert_element_type.67
  437.1 1.7 fusion.2
  438.9 2.7 collective-permute-start.4
  441.6 1.7 collective-permute-start.5
  443.3 1.3 collective-permute-start.8
  444.7 4.4 convert_element_type.65
  449.1 0.5 collective-permute-start.6
  449.7 0.8 collective-permute-start.10
  450.5 1.5 collective-permute-start.11
  452.0 4.4 convert_element_type.66
  456.4 1.3 collective-permute-start.9
  458.0 1.1 pad_maximum_fusion
  459.1 2.0 collective-permute-done.9
  461.2 0.5 collective-permute-start.13
  461.7 1.4 fusion.13
  463.5 4.2 settle.1
  467.7 0.7 slice_bitcast_fusion
  468.4 0.6 fusion.14
  469.0 0.5 slice_bitcast_fusion.1
  469.8 1.1 pad_maximum_fusion.1
  (81 shorter events, 3.1 us)
Async XLA Ops:
  2.7 101.5 %copy-start.11 = (bf16[2048,16]{0,1:T(8,128)(2,1)S(1)}, bf16[2048,16]{0,1:T(8,128)(2,1)}, u32[]{:S(2)}) copy-start(bf16[2048,16]{0,1:T(8,128)(2,1)} %param.32) | copy-start | bytes 196612
  105.8 135.1 %copy-start.7 = (bf16[64,2048]{1,0:T(8,128)(2,1)S(1)}, bf16[64,2048]{1,0:T(8,128)(2,1)}, u32[]{:S(2)}) copy-start(bf16[64,2048]{1,0:T(8,128)(2,1)} %get-tuple-element.76.normed) | copy-start | bytes 786436
  105.8 136.2 %copy-start.3 = (f32[64,2048]{1,0:T(8,128)S(1)}, f32[64,2048]{1,0:T(8,128)}, u32[]{:S(2)}) copy-start(f32[64,2048]{1,0:T(8,128)} %get-tuple-element.81) | copy-start | bytes 1572868
  105.8 136.3 %copy-start.12 = (bf16[2048,16]{0,1:T(8,128)(2,1)S(1)}, bf16[2048,16]{0,1:T(8,128)(2,1)}, u32[]{:S(2)}) copy-start(bf16[2048,16]{0,1:T(8,128)(2,1)} %param.32) | copy-start | bytes 196612
  105.8 136.3 %copy-start.14 = (f32[2048]{0:T(1024)S(1)}, f32[2048]{0:T(1024)}, u32[]{:S(2)}) copy-start(f32[2048]{0:T(1024)} %param.31) | copy-start | bytes 24580
  239.8 4.1 copy-start.8
  243.8 61.7 %collective-permute-start = (bf16[17,2048]{1,0:T(8,128)(2,1)S(1)}, bf16[17,2048]{1,0:T(8,128)(2,1)S(1)}, u32[]{:S(2)}, u32[]{:S(2)}) collective-permute-start(bf16[17,2048]{1,0:T(8,128)(2,1)S(1)} %pad_maximum_fusion.6), channel_id=1, source_target_pairs={{0,16},{1,17},{2,18},{3,19},{4,20},{5,21},{6,22},{7,23},{8,24},{9,... | collective-permute-start | bytes 208904 | tf_op jit(solution)/shard_map/ppermute | solution.py:1871
  305.6 130.7 %collective-permute-start.2 = (bf16[64,2048]{1,0:T(8,128)(2,1)S(1)}, bf16[64,2048]{1,0:T(8,128)(2,1)S(1)}, u32[]{:S(2)}, u32[]{:S(2)}) collective-permute-start(bf16[64,2048]{1,0:T(8,128)(2,1)S(1)} %get-tuple-element.99), channel_id=1, source_target_pairs={{0,2},{1,3},{2,0},{3,1},{4,6},{5,7},{6,4},{7,5},{8,10},{9,11},{10,... | collective-permute-start | bytes 786440 | tf_op jit(solution)/shard_map/ppermute | solution.py:1871
  306.0 138.6 %collective-permute-start.7 = (bf16[64,2048]{1,0:T(8,128)(2,1)S(1)}, bf16[64,2048]{1,0:T(8,128)(2,1)S(1)}, u32[]{:S(2)}, u32[]{:S(2)}) collective-permute-start(bf16[64,2048]{1,0:T(8,128)(2,1)S(1)} %get-tuple-element.99), channel_id=1, source_target_pairs={{0,1},{1,0},{2,3},{3,2},{4,5},{5,4},{6,7},{7,6},{8,9},{9,8},{10,11... | collective-permute-start | bytes 786440 | tf_op jit(solution)/shard_map/ppermute | solution.py:1871
  306.0 130.4 %collective-permute-start.1 = (bf16[17,2048]{1,0:T(8,128)(2,1)S(1)}, bf16[17,2048]{1,0:T(8,128)(2,1)S(1)}, u32[]{:S(2)}, u32[]{:S(2)}) collective-permute-start(bf16[17,2048]{1,0:T(8,128)(2,1)S(1)} %add_convert_fusion.2), channel_id=1, source_target_pairs={{0,8},{1,9},{2,10},{3,11},{4,12},{5,13},{6,14},{7,15},{8,0},{9,1},... | collective-permute-start | bytes 208904 | tf_op jit(solution)/shard_map/ppermute | solution.py:1871
  434.8 1.5 copy-start.6
  434.9 1.5 copy-start.13
  436.3 2.5 copy-start.15
  436.3 2.5 copy-start.16
  436.4 0.7 copy-start.9
  436.4 8.3 %copy-start.5 = (bf16[2048,1024]{1,0:T(8,128)(2,1)S(1)}, bf16[2048,1024]{1,0:T(8,128)(2,1)}, u32[]{:S(2)}) copy-start(bf16[2048,1024]{1,0:T(8,128)(2,1)} %get-tuple-element.103) | copy-start | bytes 12582916
  438.8 10.3 %collective-permute-start.3 = (f32[2,2048]{1,0:T(2,128)S(1)}, f32[2,2048]{1,0:T(2,128)S(1)}, u32[]{:S(2)}, u32[]{:S(2)}) collective-permute-start(f32[2,2048]{1,0:T(2,128)S(1)} %maximum_maximum_fusion), channel_id=1, source_target_pairs={{0,8},{1,9},{2,10},{3,11},{4,12},{5,13},{6,14},{7,15},{8,0},{9,1},... | collective-permute-start | bytes 49160 | tf_op jit(solution)/shard_map/ppermute | solution.py:1871
  438.9 10.7 %collective-permute-start.4 = (f32[2,2048]{1,0:T(2,128)S(1)}, f32[2,2048]{1,0:T(2,128)S(1)}, u32[]{:S(2)}, u32[]{:S(2)}) collective-permute-start(f32[2,2048]{1,0:T(2,128)S(1)} %maximum_maximum_fusion), channel_id=1, source_target_pairs={{0,16},{1,17},{2,18},{3,19},{4,20},{5,21},{6,22},{7,23},{8,24},{9,... | collective-permute-start | bytes 49160 | tf_op jit(solution)/shard_map/ppermute | solution.py:1871
  441.6 8.0 %collective-permute-start.5 = (f32[2,2048]{1,0:T(2,128)S(1)}, f32[2,2048]{1,0:T(2,128)S(1)}, u32[]{:S(2)}, u32[]{:S(2)}) collective-permute-start(f32[2,2048]{1,0:T(2,128)S(1)} %maximum_maximum_fusion), channel_id=1, source_target_pairs={{0,24},{1,25},{2,26},{3,27},{4,28},{5,29},{6,30},{7,31},{8,16},{9,... | collective-permute-start | bytes 49160 | tf_op jit(solution)/shard_map/ppermute | solution.py:1871
  443.3 17.8 %collective-permute-start.8 = (bf16[64,2048]{1,0:T(8,128)(2,1)S(1)}, bf16[64,2048]{1,0:T(8,128)(2,1)S(1)}, u32[]{:S(2)}, u32[]{:S(2)}) collective-permute-start(bf16[64,2048]{1,0:T(8,128)(2,1)S(1)} %fusion.2), channel_id=1, source_target_pairs={{0,2},{1,3},{2,0},{3,1},{4,6},{5,7},{6,4},{7,5},{8,10},{9,11},{10,... | collective-permute-start | bytes 786440 | tf_op jit(solution)/shard_map/ppermute | solution.py:1871
  444.6 18.6 %collective-permute-start.14 = (bf16[64,2048]{1,0:T(8,128)(2,1)S(1)}, bf16[64,2048]{1,0:T(8,128)(2,1)S(1)}, u32[]{:S(2)}, u32[]{:S(2)}) collective-permute-start(bf16[64,2048]{1,0:T(8,128)(2,1)S(1)} %fusion.2), channel_id=1, source_target_pairs={{0,1},{1,0},{2,3},{3,2},{4,5},{5,4},{6,7},{7,6},{8,9},{9,8},{10,11... | collective-permute-start | bytes 786440 | tf_op jit(solution)/shard_map/ppermute | solution.py:1871
  444.6 4.5 copy-start.10
  444.7 7.3 %copy-start.4 = (bf16[1024,2048]{1,0:T(8,128)(2,1)S(1)}, bf16[1024,2048]{1,0:T(8,128)(2,1)}, u32[]{:S(2)}) copy-start(bf16[1024,2048]{1,0:T(8,128)(2,1)} %get-tuple-element.106) | copy-start | bytes 12582916
  449.1 7.3 %collective-permute-start.6 = (bf16[64,2048]{1,0:T(8,128)(2,1)S(1)}, bf16[64,2048]{1,0:T(8,128)(2,1)S(1)}, u32[]{:S(2)}, u32[]{:S(2)}) collective-permute-start(bf16[64,2048]{1,0:T(8,128)(2,1)S(1)} %copy-done.10), channel_id=1, source_target_pairs={{0,1},{1,0},{2,3},{3,2},{4,5},{5,4},{6,7},{7,6},{8,9},{9,8},{10,11... | collective-permute-start | bytes 786440 | tf_op jit(solution)/shard_map/ppermute | solution.py:1871
  449.7 9.4 %collective-permute-start.10 = (bf16[19,2048]{1,0:T(8,128)(2,1)S(1)}, bf16[19,2048]{1,0:T(8,128)(2,1)S(1)}, u32[]{:S(2)}, u32[]{:S(2)}) collective-permute-start(bf16[19,2048]{1,0:T(8,128)(2,1)S(1)} %pad_maximum_fusion.7), channel_id=1, source_target_pairs={{0,4},{1,5},{2,6},{3,7},{4,0},{5,1},{6,2},{7,3},{8,12},{9,13},{10,... | collective-permute-start | bytes 233480 | tf_op jit(solution)/shard_map/ppermute | solution.py:1871
  450.5 8.6 %collective-permute-start.11 = (bf16[19,2048]{1,0:T(8,128)(2,1)S(1)}, bf16[19,2048]{1,0:T(8,128)(2,1)S(1)}, u32[]{:S(2)}, u32[]{:S(2)}) collective-permute-start(bf16[19,2048]{1,0:T(8,128)(2,1)S(1)} %pad_maximum_fusion.7), channel_id=1, source_target_pairs={{0,6},{1,7},{2,4},{3,5},{4,2},{5,3},{6,0},{7,1},{8,14},{9,15},{10,... | collective-permute-start | bytes 233480 | tf_op jit(solution)/shard_map/ppermute | solution.py:1871
  456.4 4.6 collective-permute-start.9
  457.7 5.5 %copy-start.2 = (f32[384,2048]{1,0:T(8,128)S(1)}, f32[384,2048]{1,0:T(8,128)}, u32[]{:S(2)}) copy-start(f32[384,2048]{1,0:T(8,128)} %get-tuple-element.120.refs_2_) | copy-start | bytes 9437188
  458.0 5.2 %copy-start.1 = (f32[2,192,2048]{2,1,0:T(8,128)S(1)}, f32[2,192,2048]{2,1,0:T(8,128)}, u32[]{:S(2)}) copy-start(f32[2,192,2048]{2,1,0:T(8,128)} %get-tuple-element.119) | copy-start | bytes 9437188
  461.1 2.4 copy-start
  461.1 6.6 %collective-permute-start.12 = (f32[19,2048]{1,0:T(8,128)S(1)}, f32[19,2048]{1,0:T(8,128)S(1)}, u32[]{:S(2)}, u32[]{:S(2)}) collective-permute-start(f32[19,2048]{1,0:T(8,128)S(1)} %add_add_fusion.2), channel_id=1, source_target_pairs={{0,1},{1,0},{2,3},{3,2},{4,5},{5,4},{6,7},{7,6},{8,9},{9,8},{10,11... | collective-permute-start | bytes 466952 | tf_op jit(solution)/shard_map/ppermute | solution.py:1871
  461.2 6.5 %collective-permute-start.13 = (bf16[64,2048]{1,0:T(8,128)(2,1)S(1)}, bf16[64,2048]{1,0:T(8,128)(2,1)S(1)}, u32[]{:S(2)}, u32[]{:S(2)}) collective-permute-start(bf16[64,2048]{1,0:T(8,128)(2,1)S(1)} %collective-permute-done.8), channel_id=1, source_target_pairs={{0,1},{1,0},{2,3},{3,2},{4,5},{5,4},{6,7},{7,6},{8,9},{9,8},{10,11... | collective-permute-start | bytes 786440 | tf_op jit(solution)/shard_map/ppermute | solution.py:1871

commit v8 on v7

--- a/solution.py
+++ b/solution.py
@@ -531,13 +531,14 @@
     SEMS = ((5, 7), (7, 2), (6,), (7, 2, 2), None, (7, 2), (7, 2, 2))
 
     def __init__(
-        self, spot, src, out, recv, z_send, sends, c_recv, local_sem, late_recv, late_send, full=None
+        self, spot, src, out, recv, z_send, sends, c_recv, local_sem, late_recv, late_send, full=None, share=5
     ):
         self.spot, self.src, self.out, self.full = spot, src, out, full
         self.recv, self.z_send, self.sends, self.c_recv = recv, z_send, sends, c_recv
         self.late_recv, self.late_send = late_recv, late_send
         self.count, self.width = src.shape
-        width, late = self.width, self.width * 5 // 16
+        width, late = self.width, self.width * share // 16
+        self.share = share
         half = width * 5 // 8 if full is not None else width // 2
         self.first, self.second = pl.ds(0, half), pl.ds(half, width - half)
         self.whole = pl.ds(0, width)
@@ -642,12 +643,13 @@
         def action():
             for dy, dx in ((1, 0), (0, 1)):
                 columns = self.late[dx]
-                if dz != 0:
+                if self.share and dz != 0:
                     arrive(self.place(dz, dy, dx, 0, columns), self.late_recv.at[dz + 3, dx])
-                self.along_z(
-                    dz, dy, dx, columns, lambda side: self.late_send.at[dz + 3, side, dx],
-                    lambda at: self.late_recv.at[at, dx],
-                )
+                if self.share:
+                    self.along_z(
+                        dz, dy, dx, columns, lambda side: self.late_send.at[dz + 3, side, dx],
+                        lambda at: self.late_recv.at[at, dx],
+                    )
                 self.to_core(dz, dy, dx)
 
         when_has(self.spot, dz, action)
@@ -680,7 +682,7 @@
                     @pl.when(spot.has(dz) & spot.has(step))
                     def _(dz=dz, side=side):
                         arrive(self.place(0, 0, 0), self.z_send.at[dz + 3, side])
-                        for at in (0, 1):
+                        for at in (0, 1) if self.share else ():
                             arrive(
                                 self.place(0, 0, 0, 0, self.late[at]),
                                 self.late_send.at[dz + 3, side, at],
@@ -728,7 +730,7 @@
     for copy in weights:
         copy.start()
     y_copy(0).start()
-    gather = Gather(spot, normed, rows_all, *gather_sems)
+    gather = Gather(spot, normed, rows_all, *gather_sems, share=7)
     spot.greet()
     gather.start()
     grad_in[...] = jnp.zeros_like(grad_in)
@@ -989,7 +991,7 @@
         w_out.at[pl.ds(pl.multiple_of(group * dim, dim), dim), :], head_out, head_sem
     )
     head_copy.start()
-    gather = Gather(spot, own_rows, rows_all, *gather_sems)
+    gather = Gather(spot, own_rows, rows_all, *gather_sems, share=3)
     spot.greet()
     gather.start()
     grad_keys[...] = jnp.zeros_like(grad_keys)
@@ -1033,13 +1035,13 @@
             take(dz)
 
     plans = {
-        0: lambda: (both_ways(gather.take_yx, 0), both_ways(gather.take_z, 1),
-                    both_ways(gather.take_late, 0)),
+        0: lambda: (both_ways(gather.take_yx, 0), both_ways(gather.take_late, 0),
+                    both_ways(gather.take_z, 1)),
         1: lambda: (both_ways(gather.take_diagonal, 0), both_ways(gather.take_z, 2)),
-        2: lambda: (both_ways(gather.take_yx, 1), both_ways(gather.take_z, 3),
-                    both_ways(gather.take_late, 1)),
-        3: lambda: (both_ways(gather.take_yx, 2), both_ways(gather.take_diagonal, 1),
-                    both_ways(gather.take_late, 2)),
+        2: lambda: (both_ways(gather.take_yx, 1), both_ways(gather.take_late, 1),
+                    both_ways(gather.take_z, 3)),
+        3: lambda: (both_ways(gather.take_yx, 2), both_ways(gather.take_late, 2),
+                    both_ways(gather.take_diagonal, 1)),
         4: lambda: (both_ways(gather.take_yx, 3), both_ways(gather.take_late, 3)),
         5: lambda: both_ways(gather.take_diagonal, 2),
         7: lambda: both_ways(gather.take_diagonal, 3),

time: 472 us -> 467 us (0.989)
  Pallas kernels: 427 us -> 420 us
  transfers between devices with their start and end apart: 15 -> 15, of which waited for: 1 -> 1; matrix products, arithmetic and copies ran while one was open for 4% -> 4% of each run, Pallas kernels for 41% -> 40%
where the time goes in v8:
time: 467 us
  Pallas kernels  420 us (90%)
  other arithmetic  20.6 us (4%)
  starting transfers between devices  14.4 us (3%)
  local copies, waits for them, and re-layouts  5.36 us (1%)
    pallas_call x1, Pallas kernels, experts(): pl.pallas_call(experts_kernel, out_shape=(shape((count, wide), F32), shap...  133 us
    pallas_call x1, Pallas kernels, close(): pl.pallas_call(close_kernel, out_shape=(shape((count, wide), F32), shape(...  127 us
    pallas_call x1, Pallas kernels, front(): pl.pallas_call(front_kernel, out_shape=(shape((total, width), BF16), shap...  100 us
    pallas_call x1, Pallas kernels, attend_back(): pl.pallas_call(attend_back_kernel, out_shape=[shape((total, 3 * dim), BF1...  54.9 us
    ppermute x15, starting transfers between devices, swap(): lax.ppermute(value, ('expert', 'tensor'), [(device, device ^ bits) for de...  14.4 us
  transfers between devices with their start and end apart: 15, of which 1 were waited for; matrix products, arithmetic and copies ran while one was open for 4% of the time, Pallas kernels for 40%

profile of v8, /device:TPU:0, one launch (start us, length us, event | category | flops | bytes accessed | tf_op | source)
XLA Modules:
  0.0 466.8 jit_solution(5056462652190681904)
XLA Ops:
  0.8 0.6 maximum_bitcast_fusion.inverse
  1.3 1.4 add_add_fusion.3.tag
  2.7 100.3 %front.1 = (bf16[2048,2048]{1,0:T(8,128)(2,1)}, bf16[2048,128]{1,0:T(8,128)(2,1)}, bf16[2048,128]{1,0:T(8,128)(2,1)}, bf16[2048,128]{1,0:T(8,128)(2,1)}, f32[204...) custom-call(bf16[256,2048]{1,0:T(8,128)(2,1)} %hidden.1, ...), custom_call_target="tpu_custom_call" | custom-call | flops 8000000000 | bytes 270000000 | tf_op jit(solution)/shard_map/front/pallas_call | solution.py:1813
  103.0 1.2 copy.32
  104.3 1.3 fusion.15
  105.8 132.9 %experts.1 = (f32[64,4224]{1,0:T(8,128)}, f32[2,192,2048]{2,1,0:T(8,128)}, f32[2,192,2048]{2,1,0:T(8,128)}, f32[384,2048]{1,0:T(8,128)}) custom-call(bf16[64,2048]{1,0:T(8,128)(2,1)} %get-tuple-element.76.normed, bf16[2048,2048]{1,0:T(8,128)(2,1)} %get-tuple-element.77.grad_y, bf16[2,192,2048]{2,1,0:T(8,128)(2,1)} %bitcast.51, ...), custom_call_target="tpu_custom_call" | custom-call | flops 28999999488 | bytes 360000000 | tf_op jit(solution)/shard_map/experts/pallas_call | solution.py:945
  238.7 1.0 multiply_reduce_fusion.3
  239.7 1.0 convolution_convert_fusion
  241.0 1.7 multiply_reduce_fusion
  242.9 1.9 fusion.12.own_rows
  244.8 54.9 %attend_back.1 = (bf16[2048,384]{1,0:T(8,128)(2,1)}, bf16[128,2048]{1,0:T(8,128)(2,1)}, f32[1,128]{1,0:T(1,128)}, f32[1,128]{1,0:T(1,128)}) custom-call(bf16[64,2048]{1,0:T(8,128)(2,1)} %fusion.12.own_rows, bf16[1024,2048]{1,0:T(8,128)(2,1)} %w_out.3, bf16[2048,128]{1,0:T(8,128)(2,1)} %get-tuple-element.82.queries, ...), custom_call_target="tpu_custom_call" | custom-call | flops 8999999488 | bytes 150000000 | tf_op jit(solution)/shard_map/attend_back/pallas_call | solution.py:1078
  299.8 0.5 collective-permute-start.2
  300.3 1.1 collective-permute-start.7
  301.4 2.1 collective-permute-start.1
  303.6 127.3 %close.1 = (f32[64,2048]{1,0:T(8,128)}, bf16[2048,256]{1,0:T(8,128)(2,1)}, bf16[2048,1024]{1,0:T(8,128)(2,1)}, bf16[1024,2048]{1,0:T(8,128)(2,1)}) custom-call(bf16[2048,2048]{1,0:T(8,128)(2,1)} %get-tuple-element.75.normed, bf16[2048,384]{1,0:T(8,128)(2,1)} %get-tuple-element.94.grad_lin, bf16[2048,1024]{1,0:T(8,128)(2,1)} %w_query.3, ...), custom_call_target="tpu_custom_call" | custom-call | flops 7000000000 | bytes 330000000 | tf_op jit(solution)/shard_map/close/pallas_call | solution.py:1444
  430.9 1.4 convert_element_type.67
  433.1 1.7 fusion.2
  435.2 2.6 collective-permute-start.4
  437.8 1.5 collective-permute-start.5
  439.3 1.5 collective-permute-start.8
  440.9 4.4 convert_element_type.65
  445.9 0.6 collective-permute-start.10
  446.5 1.5 collective-permute-start.11
  448.0 4.4 convert_element_type.66
  452.4 1.5 collective-permute-start.9
  454.2 1.1 pad_maximum_fusion
  455.3 1.8 collective-permute-done.9
  457.7 1.4 fusion.13
  459.5 4.2 settle.1
  463.7 0.7 slice_bitcast_fusion
  464.3 0.6 fusion.14
  465.7 1.1 pad_maximum_fusion.1
  (81 shorter events, 4.5 us)
Async XLA Ops:
  2.7 101.5 %copy-start.11 = (bf16[2048,16]{0,1:T(8,128)(2,1)S(1)}, bf16[2048,16]{0,1:T(8,128)(2,1)}, u32[]{:S(2)}) copy-start(bf16[2048,16]{0,1:T(8,128)(2,1)} %param.32) | copy-start | bytes 196612
  105.8 134.0 %copy-start.7 = (bf16[64,2048]{1,0:T(8,128)(2,1)S(1)}, bf16[64,2048]{1,0:T(8,128)(2,1)}, u32[]{:S(2)}) copy-start(bf16[64,2048]{1,0:T(8,128)(2,1)} %get-tuple-element.76.normed) | copy-start | bytes 786436
  105.8 135.0 %copy-start.3 = (f32[64,2048]{1,0:T(8,128)S(1)}, f32[64,2048]{1,0:T(8,128)}, u32[]{:S(2)}) copy-start(f32[64,2048]{1,0:T(8,128)} %get-tuple-element.81) | copy-start | bytes 1572868
  105.8 135.2 %copy-start.12 = (bf16[2048,16]{0,1:T(8,128)(2,1)S(1)}, bf16[2048,16]{0,1:T(8,128)(2,1)}, u32[]{:S(2)}) copy-start(bf16[2048,16]{0,1:T(8,128)(2,1)} %param.32) | copy-start | bytes 196612
  105.8 135.2 %copy-start.14 = (f32[2048]{0:T(1024)S(1)}, f32[2048]{0:T(1024)}, u32[]{:S(2)}) copy-start(f32[2048]{0:T(1024)} %param.31) | copy-start | bytes 24580
  238.7 4.1 copy-start.8
  242.7 57.1 %collective-permute-start = (bf16[17,2048]{1,0:T(8,128)(2,1)S(1)}, bf16[17,2048]{1,0:T(8,128)(2,1)S(1)}, u32[]{:S(2)}, u32[]{:S(2)}) collective-permute-start(bf16[17,2048]{1,0:T(8,128)(2,1)S(1)} %pad_maximum_fusion.6), channel_id=1, source_target_pairs={{0,16},{1,17},{2,18},{3,19},{4,20},{5,21},{6,22},{7,23},{8,24},{9,... | collective-permute-start | bytes 208904 | tf_op jit(solution)/shard_map/ppermute | solution.py:1873
  299.8 132.5 %collective-permute-start.2 = (bf16[64,2048]{1,0:T(8,128)(2,1)S(1)}, bf16[64,2048]{1,0:T(8,128)(2,1)S(1)}, u32[]{:S(2)}, u32[]{:S(2)}) collective-permute-start(bf16[64,2048]{1,0:T(8,128)(2,1)S(1)} %get-tuple-element.99), channel_id=1, source_target_pairs={{0,2},{1,3},{2,0},{3,1},{4,6},{5,7},{6,4},{7,5},{8,10},{9,11},{10,... | collective-permute-start | bytes 786440 | tf_op jit(solution)/shard_map/ppermute | solution.py:1873
  300.3 140.5 %collective-permute-start.7 = (bf16[64,2048]{1,0:T(8,128)(2,1)S(1)}, bf16[64,2048]{1,0:T(8,128)(2,1)S(1)}, u32[]{:S(2)}, u32[]{:S(2)}) collective-permute-start(bf16[64,2048]{1,0:T(8,128)(2,1)S(1)} %get-tuple-element.99), channel_id=1, source_target_pairs={{0,1},{1,0},{2,3},{3,2},{4,5},{5,4},{6,7},{7,6},{8,9},{9,8},{10,11... | collective-permute-start | bytes 786440 | tf_op jit(solution)/shard_map/ppermute | solution.py:1873
  301.4 130.9 %collective-permute-start.1 = (bf16[17,2048]{1,0:T(8,128)(2,1)S(1)}, bf16[17,2048]{1,0:T(8,128)(2,1)S(1)}, u32[]{:S(2)}, u32[]{:S(2)}) collective-permute-start(bf16[17,2048]{1,0:T(8,128)(2,1)S(1)} %add_convert_fusion.2), channel_id=1, source_target_pairs={{0,8},{1,9},{2,10},{3,11},{4,12},{5,13},{6,14},{7,15},{8,0},{9,1},... | collective-permute-start | bytes 208904 | tf_op jit(solution)/shard_map/ppermute | solution.py:1873
  430.8 1.5 copy-start.6
  430.8 1.5 copy-start.13
  432.3 2.5 copy-start.15
  432.3 2.5 copy-start.16
  432.3 0.7 copy-start.9
  432.4 8.5 %copy-start.5 = (bf16[2048,1024]{1,0:T(8,128)(2,1)S(1)}, bf16[2048,1024]{1,0:T(8,128)(2,1)}, u32[]{:S(2)}) copy-start(bf16[2048,1024]{1,0:T(8,128)(2,1)} %get-tuple-element.103) | copy-start | bytes 12582916
  434.8 10.5 %collective-permute-start.3 = (f32[2,2048]{1,0:T(2,128)S(1)}, f32[2,2048]{1,0:T(2,128)S(1)}, u32[]{:S(2)}, u32[]{:S(2)}) collective-permute-start(f32[2,2048]{1,0:T(2,128)S(1)} %maximum_maximum_fusion), channel_id=1, source_target_pairs={{0,8},{1,9},{2,10},{3,11},{4,12},{5,13},{6,14},{7,15},{8,0},{9,1},... | collective-permute-start | bytes 49160 | tf_op jit(solution)/shard_map/ppermute | solution.py:1873
  435.2 10.6 %collective-permute-start.4 = (f32[2,2048]{1,0:T(2,128)S(1)}, f32[2,2048]{1,0:T(2,128)S(1)}, u32[]{:S(2)}, u32[]{:S(2)}) collective-permute-start(f32[2,2048]{1,0:T(2,128)S(1)} %maximum_maximum_fusion), channel_id=1, source_target_pairs={{0,16},{1,17},{2,18},{3,19},{4,20},{5,21},{6,22},{7,23},{8,24},{9,... | collective-permute-start | bytes 49160 | tf_op jit(solution)/shard_map/ppermute | solution.py:1873
  437.8 8.0 %collective-permute-start.5 = (f32[2,2048]{1,0:T(2,128)S(1)}, f32[2,2048]{1,0:T(2,128)S(1)}, u32[]{:S(2)}, u32[]{:S(2)}) collective-permute-start(f32[2,2048]{1,0:T(2,128)S(1)} %maximum_maximum_fusion), channel_id=1, source_target_pairs={{0,24},{1,25},{2,26},{3,27},{4,28},{5,29},{6,30},{7,31},{8,16},{9,... | collective-permute-start | bytes 49160 | tf_op jit(solution)/shard_map/ppermute | solution.py:1873
  439.3 17.8 %collective-permute-start.8 = (bf16[64,2048]{1,0:T(8,128)(2,1)S(1)}, bf16[64,2048]{1,0:T(8,128)(2,1)S(1)}, u32[]{:S(2)}, u32[]{:S(2)}) collective-permute-start(bf16[64,2048]{1,0:T(8,128)(2,1)S(1)} %fusion.2), channel_id=1, source_target_pairs={{0,2},{1,3},{2,0},{3,1},{4,6},{5,7},{6,4},{7,5},{8,10},{9,11},{10,... | collective-permute-start | bytes 786440 | tf_op jit(solution)/shard_map/ppermute | solution.py:1873
  440.8 18.4 %collective-permute-start.14 = (bf16[64,2048]{1,0:T(8,128)(2,1)S(1)}, bf16[64,2048]{1,0:T(8,128)(2,1)S(1)}, u32[]{:S(2)}, u32[]{:S(2)}) collective-permute-start(bf16[64,2048]{1,0:T(8,128)(2,1)S(1)} %fusion.2), channel_id=1, source_target_pairs={{0,1},{1,0},{2,3},{3,2},{4,5},{5,4},{6,7},{7,6},{8,9},{9,8},{10,11... | collective-permute-start | bytes 786440 | tf_op jit(solution)/shard_map/ppermute | solution.py:1873
  440.9 4.5 copy-start.10
  440.9 7.1 %copy-start.4 = (bf16[1024,2048]{1,0:T(8,128)(2,1)S(1)}, bf16[1024,2048]{1,0:T(8,128)(2,1)}, u32[]{:S(2)}) copy-start(bf16[1024,2048]{1,0:T(8,128)(2,1)} %get-tuple-element.106) | copy-start | bytes 12582916
  445.3 7.1 %collective-permute-start.6 = (bf16[64,2048]{1,0:T(8,128)(2,1)S(1)}, bf16[64,2048]{1,0:T(8,128)(2,1)S(1)}, u32[]{:S(2)}, u32[]{:S(2)}) collective-permute-start(bf16[64,2048]{1,0:T(8,128)(2,1)S(1)} %copy-done.10), channel_id=1, source_target_pairs={{0,1},{1,0},{2,3},{3,2},{4,5},{5,4},{6,7},{7,6},{8,9},{9,8},{10,11... | collective-permute-start | bytes 786440 | tf_op jit(solution)/shard_map/ppermute | solution.py:1873
  445.9 9.4 %collective-permute-start.10 = (bf16[19,2048]{1,0:T(8,128)(2,1)S(1)}, bf16[19,2048]{1,0:T(8,128)(2,1)S(1)}, u32[]{:S(2)}, u32[]{:S(2)}) collective-permute-start(bf16[19,2048]{1,0:T(8,128)(2,1)S(1)} %pad_maximum_fusion.7), channel_id=1, source_target_pairs={{0,4},{1,5},{2,6},{3,7},{4,0},{5,1},{6,2},{7,3},{8,12},{9,13},{10,... | collective-permute-start | bytes 233480 | tf_op jit(solution)/shard_map/ppermute | solution.py:1873
  446.5 8.8 %collective-permute-start.11 = (bf16[19,2048]{1,0:T(8,128)(2,1)S(1)}, bf16[19,2048]{1,0:T(8,128)(2,1)S(1)}, u32[]{:S(2)}, u32[]{:S(2)}) collective-permute-start(bf16[19,2048]{1,0:T(8,128)(2,1)S(1)} %pad_maximum_fusion.7), channel_id=1, source_target_pairs={{0,6},{1,7},{2,4},{3,5},{4,2},{5,3},{6,0},{7,1},{8,14},{9,15},{10,... | collective-permute-start | bytes 233480 | tf_op jit(solution)/shard_map/ppermute | solution.py:1873
  452.4 4.6 collective-permute-start.9
  454.0 5.2 %copy-start.2 = (f32[384,2048]{1,0:T(8,128)S(1)}, f32[384,2048]{1,0:T(8,128)}, u32[]{:S(2)}) copy-start(f32[384,2048]{1,0:T(8,128)} %get-tuple-element.120.refs_2_) | copy-start | bytes 9437188
  454.2 5.0 %copy-start.1 = (f32[2,192,2048]{2,1,0:T(8,128)S(1)}, f32[2,192,2048]{2,1,0:T(8,128)}, u32[]{:S(2)}) copy-start(f32[2,192,2048]{2,1,0:T(8,128)} %get-tuple-element.119) | copy-start | bytes 9437188
  457.1 2.3 copy-start
  457.1 6.5 %collective-permute-start.12 = (f32[19,2048]{1,0:T(8,128)S(1)}, f32[19,2048]{1,0:T(8,128)S(1)}, u32[]{:S(2)}, u32[]{:S(2)}) collective-permute-start(f32[19,2048]{1,0:T(8,128)S(1)} %add_add_fusion.2), channel_id=1, source_target_pairs={{0,1},{1,0},{2,3},{3,2},{4,5},{5,4},{6,7},{7,6},{8,9},{9,8},{10,11... | collective-permute-start | bytes 466952 | tf_op jit(solution)/shard_map/ppermute | solution.py:1873
  457.2 6.4 %collective-permute-start.13 = (bf16[64,2048]{1,0:T(8,128)(2,1)S(1)}, bf16[64,2048]{1,0:T(8,128)(2,1)S(1)}, u32[]{:S(2)}, u32[]{:S(2)}) collective-permute-start(bf16[64,2048]{1,0:T(8,128)(2,1)S(1)} %collective-permute-done.8), channel_id=1, source_target_pairs={{0,1},{1,0},{2,3},{3,2},{4,5},{5,4},{6,7},{7,6},{8,9},{9,8},{10,11... | collective-permute-start | bytes 786440 | tf_op jit(solution)/shard_map/ppermute | solution.py:1873

commit v9 on v8

--- a/solution.py
+++ b/solution.py
@@ -730,7 +730,7 @@
     for copy in weights:
         copy.start()
     y_copy(0).start()
-    gather = Gather(spot, normed, rows_all, *gather_sems, share=7)
+    gather = Gather(spot, normed, rows_all, *gather_sems, share=8)
     spot.greet()
     gather.start()
     grad_in[...] = jnp.zeros_like(grad_in)

time: 467 us -> 468 us (level)
  no operation moved by 1% of the time
where the time goes in v9:
time: 468 us
  Pallas kernels  420 us (90%)
  other arithmetic  20.6 us (4%)
  starting transfers between devices  14.3 us (3%)
  local copies, waits for them, and re-layouts  5.42 us (1%)
    pallas_call x1, Pallas kernels, experts(): pl.pallas_call(experts_kernel, out_shape=(shape((count, wide), F32), shap...  134 us
    pallas_call x1, Pallas kernels, close(): pl.pallas_call(close_kernel, out_shape=(shape((count, wide), F32), shape(...  127 us
    pallas_call x1, Pallas kernels, front(): pl.pallas_call(front_kernel, out_shape=(shape((total, width), BF16), shap...  100 us
    pallas_call x1, Pallas kernels, attend_back(): pl.pallas_call(attend_back_kernel, out_shape=[shape((total, 3 * dim), BF1...  55.1 us
    ppermute x15, starting transfers between devices, swap(): lax.ppermute(value, ('expert', 'tensor'), [(device, device ^ bits) for de...  14.3 us
  transfers between devices with their start and end apart: 15, of which 1 were waited for; matrix products, arithmetic and copies ran while one was open for 4% of the time, Pallas kernels for 40%

profile of v9, /device:TPU:0, one launch (start us, length us, event | category | flops | bytes accessed | tf_op | source)
XLA Modules:
  0.0 467.8 jit_solution(15400208905437935091)
XLA Ops:
  0.8 0.6 maximum_bitcast_fusion.inverse
  1.3 1.4 add_add_fusion.3.tag
  2.7 100.3 %front.1 = (bf16[2048,2048]{1,0:T(8,128)(2,1)}, bf16[2048,128]{1,0:T(8,128)(2,1)}, bf16[2048,128]{1,0:T(8,128)(2,1)}, bf16[2048,128]{1,0:T(8,128)(2,1)}, f32[204...) custom-call(bf16[256,2048]{1,0:T(8,128)(2,1)} %hidden.1, ...), custom_call_target="tpu_custom_call" | custom-call | flops 8000000000 | bytes 270000000 | tf_op jit(solution)/shard_map/front/pallas_call | solution.py:1813
  103.0 1.2 copy.32
  104.3 1.3 fusion.15
  105.8 133.5 %experts.1 = (f32[64,4224]{1,0:T(8,128)}, f32[2,192,2048]{2,1,0:T(8,128)}, f32[2,192,2048]{2,1,0:T(8,128)}, f32[384,2048]{1,0:T(8,128)}) custom-call(bf16[64,2048]{1,0:T(8,128)(2,1)} %get-tuple-element.76.normed, bf16[2048,2048]{1,0:T(8,128)(2,1)} %get-tuple-element.77.grad_y, bf16[2,192,2048]{2,1,0:T(8,128)(2,1)} %bitcast.51, ...), custom_call_target="tpu_custom_call" | custom-call | flops 28999999488 | bytes 360000000 | tf_op jit(solution)/shard_map/experts/pallas_call | solution.py:945
  239.4 1.0 multiply_reduce_fusion.3
  240.4 1.0 convolution_convert_fusion
  241.6 1.7 multiply_reduce_fusion
  243.6 1.9 fusion.12.own_rows
  245.5 55.1 %attend_back.1 = (bf16[2048,384]{1,0:T(8,128)(2,1)}, bf16[128,2048]{1,0:T(8,128)(2,1)}, f32[1,128]{1,0:T(1,128)}, f32[1,128]{1,0:T(1,128)}) custom-call(bf16[64,2048]{1,0:T(8,128)(2,1)} %fusion.12.own_rows, bf16[1024,2048]{1,0:T(8,128)(2,1)} %w_out.3, bf16[2048,128]{1,0:T(8,128)(2,1)} %get-tuple-element.82.queries, ...), custom_call_target="tpu_custom_call" | custom-call | flops 8999999488 | bytes 150000000 | tf_op jit(solution)/shard_map/attend_back/pallas_call | solution.py:1078
  301.0 1.1 collective-permute-start.7
  302.2 2.3 collective-permute-start.1
  304.4 127.3 %close.1 = (f32[64,2048]{1,0:T(8,128)}, bf16[2048,256]{1,0:T(8,128)(2,1)}, bf16[2048,1024]{1,0:T(8,128)(2,1)}, bf16[1024,2048]{1,0:T(8,128)(2,1)}) custom-call(bf16[2048,2048]{1,0:T(8,128)(2,1)} %get-tuple-element.75.normed, bf16[2048,384]{1,0:T(8,128)(2,1)} %get-tuple-element.94.grad_lin, bf16[2048,1024]{1,0:T(8,128)(2,1)} %w_query.3, ...), custom_call_target="tpu_custom_call" | custom-call | flops 7000000000 | bytes 330000000 | tf_op jit(solution)/shard_map/close/pallas_call | solution.py:1444
  431.7 1.4 convert_element_type.67
  433.9 1.7 fusion.2
  436.1 2.6 collective-permute-start.4
  438.7 1.5 collective-permute-start.5
  440.2 1.3 collective-permute-start.8
  441.6 4.4 convert_element_type.65
  446.6 0.7 collective-permute-start.10
  447.4 1.5 collective-permute-start.11
  448.8 4.4 convert_element_type.66
  453.3 1.3 collective-permute-start.9
  454.9 1.1 pad_maximum_fusion
  456.0 1.9 collective-permute-done.9
  458.6 1.4 fusion.13
  460.4 4.2 settle.1
  464.6 0.7 slice_bitcast_fusion
  465.3 0.6 fusion.14
  465.9 0.5 slice_bitcast_fusion.1
  466.7 1.1 pad_maximum_fusion.1
  (81 shorter events, 4.5 us)
Async XLA Ops:
  2.7 101.5 %copy-start.11 = (bf16[2048,16]{0,1:T(8,128)(2,1)S(1)}, bf16[2048,16]{0,1:T(8,128)(2,1)}, u32[]{:S(2)}) copy-start(bf16[2048,16]{0,1:T(8,128)(2,1)} %param.32) | copy-start | bytes 196612
  105.8 134.7 %copy-start.7 = (bf16[64,2048]{1,0:T(8,128)(2,1)S(1)}, bf16[64,2048]{1,0:T(8,128)(2,1)}, u32[]{:S(2)}) copy-start(bf16[64,2048]{1,0:T(8,128)(2,1)} %get-tuple-element.76.normed) | copy-start | bytes 786436
  105.8 135.7 %copy-start.3 = (f32[64,2048]{1,0:T(8,128)S(1)}, f32[64,2048]{1,0:T(8,128)}, u32[]{:S(2)}) copy-start(f32[64,2048]{1,0:T(8,128)} %get-tuple-element.81) | copy-start | bytes 1572868
  105.8 135.8 %copy-start.12 = (bf16[2048,16]{0,1:T(8,128)(2,1)S(1)}, bf16[2048,16]{0,1:T(8,128)(2,1)}, u32[]{:S(2)}) copy-start(bf16[2048,16]{0,1:T(8,128)(2,1)} %param.32) | copy-start | bytes 196612
  105.8 135.8 %copy-start.14 = (f32[2048]{0:T(1024)S(1)}, f32[2048]{0:T(1024)}, u32[]{:S(2)}) copy-start(f32[2048]{0:T(1024)} %param.31) | copy-start | bytes 24580
  239.3 4.1 copy-start.8
  243.4 57.3 %collective-permute-start = (bf16[17,2048]{1,0:T(8,128)(2,1)S(1)}, bf16[17,2048]{1,0:T(8,128)(2,1)S(1)}, u32[]{:S(2)}, u32[]{:S(2)}) collective-permute-start(bf16[17,2048]{1,0:T(8,128)(2,1)S(1)} %pad_maximum_fusion.6), channel_id=1, source_target_pairs={{0,16},{1,17},{2,18},{3,19},{4,20},{5,21},{6,22},{7,23},{8,24},{9,... | collective-permute-start | bytes 208904 | tf_op jit(solution)/shard_map/ppermute | solution.py:1873
  300.7 132.5 %collective-permute-start.2 = (bf16[64,2048]{1,0:T(8,128)(2,1)S(1)}, bf16[64,2048]{1,0:T(8,128)(2,1)S(1)}, u32[]{:S(2)}, u32[]{:S(2)}) collective-permute-start(bf16[64,2048]{1,0:T(8,128)(2,1)S(1)} %get-tuple-element.99), channel_id=1, source_target_pairs={{0,2},{1,3},{2,0},{3,1},{4,6},{5,7},{6,4},{7,5},{8,10},{9,11},{10,... | collective-permute-start | bytes 786440 | tf_op jit(solution)/shard_map/ppermute | solution.py:1873
  301.0 140.5 %collective-permute-start.7 = (bf16[64,2048]{1,0:T(8,128)(2,1)S(1)}, bf16[64,2048]{1,0:T(8,128)(2,1)S(1)}, u32[]{:S(2)}, u32[]{:S(2)}) collective-permute-start(bf16[64,2048]{1,0:T(8,128)(2,1)S(1)} %get-tuple-element.99), channel_id=1, source_target_pairs={{0,1},{1,0},{2,3},{3,2},{4,5},{5,4},{6,7},{7,6},{8,9},{9,8},{10,11... | collective-permute-start | bytes 786440 | tf_op jit(solution)/shard_map/ppermute | solution.py:1873
  302.2 131.0 %collective-permute-start.1 = (bf16[17,2048]{1,0:T(8,128)(2,1)S(1)}, bf16[17,2048]{1,0:T(8,128)(2,1)S(1)}, u32[]{:S(2)}, u32[]{:S(2)}) collective-permute-start(bf16[17,2048]{1,0:T(8,128)(2,1)S(1)} %add_convert_fusion.2), channel_id=1, source_target_pairs={{0,8},{1,9},{2,10},{3,11},{4,12},{5,13},{6,14},{7,15},{8,0},{9,1},... | collective-permute-start | bytes 208904 | tf_op jit(solution)/shard_map/ppermute | solution.py:1873
  431.7 1.5 copy-start.6
  431.7 1.5 copy-start.13
  433.2 2.5 copy-start.15
  433.2 2.5 copy-start.16
  433.2 0.7 copy-start.9
  433.2 8.3 %copy-start.5 = (bf16[2048,1024]{1,0:T(8,128)(2,1)S(1)}, bf16[2048,1024]{1,0:T(8,128)(2,1)}, u32[]{:S(2)}) copy-start(bf16[2048,1024]{1,0:T(8,128)(2,1)} %get-tuple-element.103) | copy-start | bytes 12582916
  435.7 10.4 %collective-permute-start.3 = (f32[2,2048]{1,0:T(2,128)S(1)}, f32[2,2048]{1,0:T(2,128)S(1)}, u32[]{:S(2)}, u32[]{:S(2)}) collective-permute-start(f32[2,2048]{1,0:T(2,128)S(1)} %maximum_maximum_fusion), channel_id=1, source_target_pairs={{0,8},{1,9},{2,10},{3,11},{4,12},{5,13},{6,14},{7,15},{8,0},{9,1},... | collective-permute-start | bytes 49160 | tf_op jit(solution)/shard_map/ppermute | solution.py:1873
  436.1 10.5 %collective-permute-start.4 = (f32[2,2048]{1,0:T(2,128)S(1)}, f32[2,2048]{1,0:T(2,128)S(1)}, u32[]{:S(2)}, u32[]{:S(2)}) collective-permute-start(f32[2,2048]{1,0:T(2,128)S(1)} %maximum_maximum_fusion), channel_id=1, source_target_pairs={{0,16},{1,17},{2,18},{3,19},{4,20},{5,21},{6,22},{7,23},{8,24},{9,... | collective-permute-start | bytes 49160 | tf_op jit(solution)/shard_map/ppermute | solution.py:1873
  438.7 7.9 %collective-permute-start.5 = (f32[2,2048]{1,0:T(2,128)S(1)}, f32[2,2048]{1,0:T(2,128)S(1)}, u32[]{:S(2)}, u32[]{:S(2)}) collective-permute-start(f32[2,2048]{1,0:T(2,128)S(1)} %maximum_maximum_fusion), channel_id=1, source_target_pairs={{0,24},{1,25},{2,26},{3,27},{4,28},{5,29},{6,30},{7,31},{8,16},{9,... | collective-permute-start | bytes 49160 | tf_op jit(solution)/shard_map/ppermute | solution.py:1873
  440.2 17.8 %collective-permute-start.8 = (bf16[64,2048]{1,0:T(8,128)(2,1)S(1)}, bf16[64,2048]{1,0:T(8,128)(2,1)S(1)}, u32[]{:S(2)}, u32[]{:S(2)}) collective-permute-start(bf16[64,2048]{1,0:T(8,128)(2,1)S(1)} %fusion.2), channel_id=1, source_target_pairs={{0,2},{1,3},{2,0},{3,1},{4,6},{5,7},{6,4},{7,5},{8,10},{9,11},{10,... | collective-permute-start | bytes 786440 | tf_op jit(solution)/shard_map/ppermute | solution.py:1873
  441.5 18.5 %collective-permute-start.14 = (bf16[64,2048]{1,0:T(8,128)(2,1)S(1)}, bf16[64,2048]{1,0:T(8,128)(2,1)S(1)}, u32[]{:S(2)}, u32[]{:S(2)}) collective-permute-start(bf16[64,2048]{1,0:T(8,128)(2,1)S(1)} %fusion.2), channel_id=1, source_target_pairs={{0,1},{1,0},{2,3},{3,2},{4,5},{5,4},{6,7},{7,6},{8,9},{9,8},{10,11... | collective-permute-start | bytes 786440 | tf_op jit(solution)/shard_map/ppermute | solution.py:1873
  441.6 4.5 copy-start.10
  441.6 7.2 %copy-start.4 = (bf16[1024,2048]{1,0:T(8,128)(2,1)S(1)}, bf16[1024,2048]{1,0:T(8,128)(2,1)}, u32[]{:S(2)}) copy-start(bf16[1024,2048]{1,0:T(8,128)(2,1)} %get-tuple-element.106) | copy-start | bytes 12582916
  446.1 7.2 %collective-permute-start.6 = (bf16[64,2048]{1,0:T(8,128)(2,1)S(1)}, bf16[64,2048]{1,0:T(8,128)(2,1)S(1)}, u32[]{:S(2)}, u32[]{:S(2)}) collective-permute-start(bf16[64,2048]{1,0:T(8,128)(2,1)S(1)} %copy-done.10), channel_id=1, source_target_pairs={{0,1},{1,0},{2,3},{3,2},{4,5},{5,4},{6,7},{7,6},{8,9},{9,8},{10,11... | collective-permute-start | bytes 786440 | tf_op jit(solution)/shard_map/ppermute | solution.py:1873
  446.6 9.4 %collective-permute-start.10 = (bf16[19,2048]{1,0:T(8,128)(2,1)S(1)}, bf16[19,2048]{1,0:T(8,128)(2,1)S(1)}, u32[]{:S(2)}, u32[]{:S(2)}) collective-permute-start(bf16[19,2048]{1,0:T(8,128)(2,1)S(1)} %pad_maximum_fusion.7), channel_id=1, source_target_pairs={{0,4},{1,5},{2,6},{3,7},{4,0},{5,1},{6,2},{7,3},{8,12},{9,13},{10,... | collective-permute-start | bytes 233480 | tf_op jit(solution)/shard_map/ppermute | solution.py:1873
  447.4 8.7 %collective-permute-start.11 = (bf16[19,2048]{1,0:T(8,128)(2,1)S(1)}, bf16[19,2048]{1,0:T(8,128)(2,1)S(1)}, u32[]{:S(2)}, u32[]{:S(2)}) collective-permute-start(bf16[19,2048]{1,0:T(8,128)(2,1)S(1)} %pad_maximum_fusion.7), channel_id=1, source_target_pairs={{0,6},{1,7},{2,4},{3,5},{4,2},{5,3},{6,0},{7,1},{8,14},{9,15},{10,... | collective-permute-start | bytes 233480 | tf_op jit(solution)/shard_map/ppermute | solution.py:1873
  453.3 4.6 collective-permute-start.9
  454.7 5.4 %copy-start.2 = (f32[384,2048]{1,0:T(8,128)S(1)}, f32[384,2048]{1,0:T(8,128)}, u32[]{:S(2)}) copy-start(f32[384,2048]{1,0:T(8,128)} %get-tuple-element.120.refs_2_) | copy-start | bytes 9437188
  454.9 5.1 %copy-start.1 = (f32[2,192,2048]{2,1,0:T(8,128)S(1)}, f32[2,192,2048]{2,1,0:T(8,128)}, u32[]{:S(2)}) copy-start(f32[2,192,2048]{2,1,0:T(8,128)} %get-tuple-element.119) | copy-start | bytes 9437188
  458.0 2.4 copy-start
  458.0 6.6 %collective-permute-start.12 = (f32[19,2048]{1,0:T(8,128)S(1)}, f32[19,2048]{1,0:T(8,128)S(1)}, u32[]{:S(2)}, u32[]{:S(2)}) collective-permute-start(f32[19,2048]{1,0:T(8,128)S(1)} %add_add_fusion.2), channel_id=1, source_target_pairs={{0,1},{1,0},{2,3},{3,2},{4,5},{5,4},{6,7},{7,6},{8,9},{9,8},{10,11... | collective-permute-start | bytes 466952 | tf_op jit(solution)/shard_map/ppermute | solution.py:1873
  458.1 6.5 %collective-permute-start.13 = (bf16[64,2048]{1,0:T(8,128)(2,1)S(1)}, bf16[64,2048]{1,0:T(8,128)(2,1)S(1)}, u32[]{:S(2)}, u32[]{:S(2)}) collective-permute-start(bf16[64,2048]{1,0:T(8,128)(2,1)S(1)} %collective-permute-done.8), channel_id=1, source_target_pairs={{0,1},{1,0},{2,3},{3,2},{4,5},{5,4},{6,7},{7,6},{8,9},{9,8},{10,11... | collective-permute-start | bytes 786440 | tf_op jit(solution)/shard_map/ppermute | solution.py:1873
